TPU v7x, 32 devices: a whole 2x2x4 slice. The times are simulated.
32 devices in a mesh: req: 8 (over y, x, core), mdl: 4 (over z).
Axes of the slice: x: 2, y: 2, z: 4, core: 2. Of those that a mesh axis runs over, the one named last changes fastest.
Arguments:
- tokens: bfloat16 [256, 4, 2048], P('req', None, 'mdl'), may hold values from -6 to 6
- counts: int32 [256], P('req'), may hold values from 1 to 4
- new_owner: int32 [256], replicated, may hold values from 0 to 255, as said below
- wkv_state: float32 [256, 32, 4096], P('req', 'mdl'), may hold values from -12 to 12
- att_shift: bfloat16 [256, 2048], P('req', 'mdl'), may hold values from -6 to 6
- ffn_shift: bfloat16 [256, 2048], P('req', 'mdl'), may hold values from -6 to 6
- norm_params: float32 [4, 2048], replicated, may hold values from 0.25 to 1.75
- mix_coeffs: float32 [7, 2048], replicated, may hold values from 0 to 1
- head_params: float32 [7, 2048], P(None, 'mdl'), may hold values from -6 to 2
- recept_weight: bfloat16 [2048, 2048], P(None, 'mdl'), may hold values from -0.125 to 0.125
- key_weight: bfloat16 [2048, 2048], P(None, 'mdl'), may hold values from -0.125 to 0.125
- value_weight: bfloat16 [2048, 2048], P(None, 'mdl'), may hold values from -0.125 to 0.125
- output_weight: bfloat16 [2048, 2048], P('mdl'), may hold values from -0.125 to 0.125
- decay_down: bfloat16 [2048, 96], P('mdl'), may hold values from -0.125 to 0.125
- decay_up: bfloat16 [96, 2048], P(None, 'mdl'), may hold values from -0.625 to 0.625
- alpha_down: bfloat16 [2048, 96], P('mdl'), may hold values from -0.125 to 0.125
- alpha_up: bfloat16 [96, 2048], P(None, 'mdl'), may hold values from -0.625 to 0.625
- gate_down: bfloat16 [2048, 256], P('mdl'), may hold values from -0.125 to 0.125
- gate_up: bfloat16 [256, 2048], P(None, 'mdl'), may hold values from -0.375 to 0.375
- ffn_key_weight: bfloat16 [2048, 4096], P(None, 'mdl'), may hold values from -0.125 to 0.125
- ffn_value_weight: bfloat16 [4096, 2048], P('mdl'), may hold values from -0.09375 to 0.09375
Outputs:
- block_output: bfloat16 [256, 4, 2048], P('req', None, 'mdl')
- new_state: float32 [256, 32, 4096], P('req', 'mdl')
- new_att_shift: bfloat16 [256, 2048], P('req', 'mdl')
- new_ffn_shift: bfloat16 [256, 2048], P('req', 'mdl')
Inputs may be any that keep to these rules, and one draw needn't show every extreme that they name: new_owner is a permutation: the states of request i move to position new_owner[i]. Of the 32 requests of each aligned block of positions, exactly 4 move into each aligned block.
All inputs are finite; a program needn't handle non-finite values.
Results may differ from a plain program's by a relative error of at most 0.0095.
Values may be sent and summed in bfloat16 or wider, within the bound.
No kernel may reach another device: no remote copies, remote signals or barrier semaphores. Data moves between devices by JAX's collectives and lax.ppermute only.
A program may use at most 256 MiB of HBM per device.

v0:
```python
import jax
import jax.numpy as jnp
from jax import lax
from jax.sharding import PartitionSpec as P


def layer_norm(stream, gain_row, offset):
    center = stream - jnp.mean(stream, axis=-1, keepdims=True)
    spread = jnp.mean(center * center, axis=-1, keepdims=True)
    return center / jnp.sqrt(spread + 1e-05) * gain_row + offset


def project(inputs, weight):
    return jnp.dot(inputs, weight, preferred_element_type=jnp.float32)


def split_heads(source, head_size):
    sequence_batch_count, decode_loop_steps_count, feature_count = source.shape
    return source.reshape(
        sequence_batch_count, decode_loop_steps_count, feature_count // head_size, head_size
    )


def advance(wkv_square, decay_now, key_now, value_now, unit_now, alpha_now, recept_now, is_valid):
    removal = -jnp.sum(wkv_square * unit_now[:, :, None, :], axis=-1)
    updated = (
        wkv_square * decay_now[:, :, None, :]
        + removal[..., None] * (unit_now * alpha_now)[:, :, None, :]
        + value_now[..., None] * key_now[:, :, None, :]
    )
    memory_matrix_product = jnp.sum(updated * recept_now[:, :, None, :], axis=-1)
    return (jnp.where(is_valid[:, None, None, None], updated, wkv_square), memory_matrix_product)


def prepare_keys(key_proj, in_context, learned_weights, head_size):
    scaled = split_heads(key_proj * learned_weights[2], head_size)
    key_unit = scaled / jnp.sqrt(jnp.sum(scaled * scaled, axis=-1, keepdims=True) + 1e-06)
    lookup_adjust_factor = key_proj * (1.0 + (in_context - 1.0) * learned_weights[3])
    return (key_unit.reshape(key_proj.shape), lookup_adjust_factor)


def run_heads(
    wkv_flat,
    decay_rate,
    lookup_adjust_factor,
    values,
    key_unit,
    in_context,
    acceptance_matrix_lines,
    live_mask,
    head_size,
):
    sequence_batch_count, decode_loop_steps_count, feature_count = acceptance_matrix_lines.shape
    head_count = feature_count // head_size
    decay_heads = split_heads(decay_rate, head_size)
    keymod_heads = split_heads(lookup_adjust_factor, head_size)
    payload_each_group = split_heads(values, head_size)
    unit_heads = split_heads(key_unit, head_size)
    alpha_heads = split_heads(in_context, head_size)
    recept_heads = split_heads(acceptance_matrix_lines, head_size)
    wkv_square = wkv_flat.reshape(sequence_batch_count, head_count, head_size, head_size)
    readouts = []
    for position in range(decode_loop_steps_count):
        wkv_square, memory_matrix_product = advance(
            wkv_square,
            decay_heads[:, position],
            keymod_heads[:, position],
            payload_each_group[:, position],
            unit_heads[:, position],
            alpha_heads[:, position],
            recept_heads[:, position],
            live_mask[:, position] > 0.5,
        )
        readouts.append(memory_matrix_product)
    stacked = jnp.stack(readouts, axis=1).reshape(
        sequence_batch_count, decode_loop_steps_count, feature_count
    )
    return (stacked, wkv_square.reshape(sequence_batch_count, head_count, head_size * head_size))


def finish_heads(
    memory_matrix_product,
    acceptance_matrix_lines,
    lookup_adjust_factor,
    values,
    sigmoid_scaling_entries,
    learned_weights,
    head_size,
):
    stacked = split_heads(memory_matrix_product, head_size)
    center = stacked - jnp.mean(stacked, axis=-1, keepdims=True)
    spread = jnp.mean(center * center, axis=-1, keepdims=True)
    layernormed_activations = (center / jnp.sqrt(spread + 0.00064)).reshape(
        memory_matrix_product.shape
    ) * learned_weights[5] + learned_weights[6]
    extra_term_share = jnp.sum(
        split_heads(acceptance_matrix_lines * lookup_adjust_factor * learned_weights[4], head_size),
        axis=-1,
        keepdims=True,
    ) * split_heads(values, head_size)
    return (
        (layernormed_activations + extra_term_share.reshape(memory_matrix_product.shape))
        * sigmoid_scaling_entries
    ).astype(jnp.bfloat16)


def per_device(
    tokens,
    counts,
    new_owner,
    wkv_state,
    att_shift,
    ffn_shift,
    norm_params,
    mix_coeffs,
    head_params,
    recept_weight,
    key_weight,
    value_weight,
    output_weight,
    decay_down,
    decay_up,
    alpha_down,
    alpha_up,
    gate_down,
    gate_up,
    ffn_key_weight,
    ffn_value_weight,
):
    groups = lax.axis_size("req")
    sequence_batch_count, decode_loop_steps_count, local_width = tokens.shape
    per_pair = sequence_batch_count // groups
    req_rank = lax.axis_index("req")
    column_start = lax.axis_index("mdl") * local_width
    head_size = local_width // wkv_state.shape[1]
    row_count = sequence_batch_count * decode_loop_steps_count
    shape_three = (sequence_batch_count, decode_loop_steps_count, local_width)
    slot_ids = jnp.arange(decode_loop_steps_count, dtype=jnp.int32)
    live_mask = (slot_ids[None, :] < counts[:, None]).astype(jnp.float32)
    own_block = lax.dynamic_slice_in_dim(
        new_owner, req_rank * sequence_batch_count, sequence_batch_count
    )
    sending = jnp.argsort(own_block)
    sorted_rows = jnp.sort(new_owner.reshape(groups, sequence_batch_count), axis=1)
    arriving = (
        lax.dynamic_slice_in_dim(sorted_rows, req_rank * per_pair, per_pair, 1)
        - req_rank * sequence_batch_count
    )
    placing = jnp.argsort(arriving.reshape(-1))
    sent_state = wkv_state[sending].reshape((groups, per_pair) + wkv_state.shape[1:])
    sent_att = att_shift[sending].astype(jnp.float32).reshape(groups, per_pair, local_width)
    sent_ffn = ffn_shift[sending].astype(jnp.float32).reshape(groups, per_pair, local_width)
    got_state, got_att, got_ffn = (
        lax.all_to_all(sent_state, "req", split_axis=0, concat_axis=0, tiled=True),
        lax.all_to_all(sent_att, "req", split_axis=0, concat_axis=0, tiled=True),
        lax.all_to_all(sent_ffn, "req", split_axis=0, concat_axis=0, tiled=True),
    )
    moved_state = got_state.reshape((sequence_batch_count,) + wkv_state.shape[1:])[placing]
    moved_att = got_att.reshape(sequence_batch_count, local_width)[placing].astype(jnp.bfloat16)
    moved_ffn = got_ffn.reshape(sequence_batch_count, local_width)[placing].astype(jnp.bfloat16)
    full_tokens = lax.all_gather(tokens, "mdl", axis=2, tiled=True)
    full_stream = full_tokens.astype(jnp.float32)
    entire_channel_count = full_tokens.shape[2]
    prev_att, prev_ffn = (
        lax.all_gather(moved_att, "mdl", axis=1, tiled=True),
        lax.all_gather(moved_ffn, "mdl", axis=1, tiled=True),
    )
    normed_one = layer_norm(full_stream, norm_params[0], norm_params[1])
    before_one = jnp.concatenate(
        [prev_att.astype(jnp.float32)[:, None], normed_one[:, :-1]], axis=1
    )
    delta_one = before_one - normed_one
    normed_local = lax.dynamic_slice_in_dim(normed_one, column_start, local_width, 2)

    def mixed_input(mix_index):
        return (
            (normed_one + delta_one * mix_coeffs[mix_index])
            .astype(jnp.bfloat16)
            .reshape(row_count, entire_channel_count)
        )

    decay_full, alpha_full, gate_full = (
        lax.all_gather(decay_down, "mdl", axis=0, tiled=True),
        lax.all_gather(alpha_down, "mdl", axis=0, tiled=True),
        lax.all_gather(gate_down, "mdl", axis=0, tiled=True),
    )
    decay_sum = project(mixed_input(1), decay_full)
    alpha_sum = project(mixed_input(4), alpha_full)
    gate_sum = project(mixed_input(5), gate_full)
    decay_low = jnp.tanh(decay_sum).astype(jnp.bfloat16)
    alpha_low = alpha_sum.astype(jnp.bfloat16)
    gate_low = jax.nn.sigmoid(gate_sum).astype(jnp.bfloat16)
    decay_rate = jnp.exp(
        -0.606531 * jax.nn.sigmoid(head_params[0] + project(decay_low, decay_up))
    ).reshape(shape_three)
    in_context = jax.nn.sigmoid(head_params[1] + project(alpha_low, alpha_up)).reshape(shape_three)
    sigmoid_scaling_entries = project(gate_low, gate_up).reshape(shape_three)
    acceptance_matrix_lines = project(mixed_input(0), recept_weight).reshape(shape_three)
    key_proj = project(mixed_input(2), key_weight).reshape(shape_three)
    values = project(mixed_input(3), value_weight).reshape(shape_three)
    key_unit, lookup_adjust_factor = prepare_keys(key_proj, in_context, head_params, head_size)
    memory_matrix_product, new_state = run_heads(
        moved_state,
        decay_rate,
        lookup_adjust_factor,
        values,
        key_unit,
        in_context,
        acceptance_matrix_lines,
        live_mask,
        head_size,
    )
    attention_group_result = finish_heads(
        memory_matrix_product,
        acceptance_matrix_lines,
        lookup_adjust_factor,
        values,
        sigmoid_scaling_entries,
        head_params,
        head_size,
    )
    attended_term = project(attention_group_result.reshape(row_count, local_width), output_weight)
    attended = lax.psum_scatter(attended_term, "mdl", scatter_dimension=1, tiled=True).reshape(
        shape_three
    )
    midstream = (tokens.astype(jnp.float32) + attended).astype(jnp.bfloat16)
    full_mid = lax.all_gather(midstream, "mdl", axis=2, tiled=True)
    normed_two = layer_norm(full_mid.astype(jnp.float32), norm_params[2], norm_params[3])
    before_two = jnp.concatenate(
        [prev_ffn.astype(jnp.float32)[:, None], normed_two[:, :-1]], axis=1
    )
    ffn_in = (
        (normed_two + (before_two - normed_two) * mix_coeffs[6])
        .astype(jnp.bfloat16)
        .reshape(row_count, entire_channel_count)
    )
    hidden = jnp.square(jax.nn.relu(project(ffn_in, ffn_key_weight))).astype(jnp.bfloat16)
    ffn_out = (
        lax.psum_scatter(
            project(hidden, ffn_value_weight).astype(jnp.bfloat16),
            "mdl",
            scatter_dimension=1,
            tiled=True,
        )
        .astype(jnp.float32)
        .reshape(shape_three)
    )
    block_output = jnp.where(
        live_mask[..., None] > 0.5, midstream.astype(jnp.float32) + ffn_out, 0.0
    ).astype(jnp.bfloat16)
    chosen = (slot_ids[None, :] == (counts - 1)[:, None]).astype(jnp.float32)
    normed_two_local = lax.dynamic_slice_in_dim(normed_two, column_start, local_width, 2)
    new_att_shift = jnp.sum(normed_local * chosen[..., None], axis=1).astype(jnp.bfloat16)
    new_ffn_shift = jnp.sum(normed_two_local * chosen[..., None], axis=1).astype(jnp.bfloat16)
    return (block_output, new_state, new_att_shift, new_ffn_shift)


def solution(mesh):
    return jax.shard_map(
        per_device,
        mesh=mesh,
        in_specs=(
            P("req", None, "mdl"),
            P("req"),
            P(),
            P("req", "mdl", None),
            P("req", "mdl"),
            P("req", "mdl"),
            P(),
            P(),
            P(None, "mdl"),
            P(None, "mdl"),
            P(None, "mdl"),
            P(None, "mdl"),
            P("mdl", None),
            P("mdl", None),
            P(None, "mdl"),
            P("mdl", None),
            P(None, "mdl"),
            P("mdl", None),
            P(None, "mdl"),
            P(None, "mdl"),
            P("mdl", None),
        ),
        out_specs=(P("req", None, "mdl"), P("req", "mdl", None), P("req", "mdl"), P("req", "mdl")),
        check_vma=False,
    )
```

profile of v0, /device:TPU:0, one launch (start us, length us, event | category | flops | bytes accessed | tf_op | source)
XLA Modules:
  0.0 439.1 jit_solution(6680961267923316029)
XLA Ops:
  8.7 1.6 sort.46
  10.3 1.4 gather_fusion.2
  12.3 5.2 %all-to-all-start.1 = ((bf16[8,4,512]{2,1,0:T(4,128)(2,1)}), bf16[8,4,512]{2,1,0:T(4,128)(2,1)S(1)}, u32[]{:S(2)}, u32[]{:S(2)}) async-start(bf16[8,4,512]{2,1,0:T(4,128)(2,1)} %reshape.354), calls=%async_computation.1 | async-start | bytes 65536 | tf_op jit(solution)/shard_map/all_to_all | solution.py:155
  18.3 1.2 broadcast_compare_fusion
  20.2 1.6 fusion.60
  22.7 1.6 sort.48
  24.4 1.5 fusion.59
  25.9 1.8 fusion.58
  27.7 20.2 %all_gather.23 = bf16[2048,96]{0,1:T(8,128)(2,1)} all-gather(bf16[512,96]{0,1:T(8,128)(2,1)} %param.34), channel_id=1, replica_groups=mesh['req'=8,'mdl'=4] {'mdl'}, dimensions={0}, use_global_device_ids=true | all-gather | bytes 491520 | tf_op jit(solution)/shard_map/all_gather | solution.py:183
  47.9 15.2 %all_gather.24 = bf16[2048,96]{0,1:T(8,128)(2,1)S(1)} all-gather(bf16[512,96]{0,1:T(8,128)(2,1)} %param.36), channel_id=1, replica_groups=mesh['req'=8,'mdl'=4] {'mdl'}, dimensions={0}, use_global_device_ids=true | all-gather | bytes 491520 | tf_op jit(solution)/shard_map/all_gather | solution.py:184
  63.2 14.9 %all_gather.21 = bf16[32,4,2048]{2,1,0:T(4,128)(2,1)S(1)} all-gather(bf16[32,4,512]{2,1,0:T(4,128)(2,1)} %param.21), channel_id=1, replica_groups=mesh['req'=8,'mdl'=4] {'mdl'}, dimensions={2}, use_global_device_ids=true | all-gather | bytes 655360 | tf_op jit(solution)/shard_map/all_gather | solution.py:161
  78.9 1.5 fusion.28
  80.4 3.9 copy.89
  84.3 5.0 %gather_fusion = f32[32,8,4096]{2,1,0:T(8,128)} fusion(f32[32,8,4096]{2,1,0:T(8,128)} %param.24, s32[1024]{0:T(1024)S(1)} %pad_clamp_fusion.1), kind=kCustom, calls=%fused_computation | custom fusion | bytes 8388736 | tf_op jit(solution)/shard_map/gather | solution.py:150
  89.4 4.8 %all-to-all-start = ((f32[8,4,8,4096]{3,2,1,0:T(8,128)}), f32[8,4,8,4096]{3,2,1,0:T(8,128)}, u32[]{:S(2)}, u32[]{:S(2)}) async-start(f32[8,4,8,4096]{3,2,1,0:T(8,128)} %bitcast.175), calls=%async_computation | async-start | bytes 8388608 | tf_op jit(solution)/shard_map/all_to_all | solution.py:154
  94.9 13.9 %all_gather.22 = bf16[32,2048]{1,0:T(8,128)(2,1)S(1)} all-gather(bf16[32,512]{1,0:T(8,128)(2,1)S(1)} %gather_fusion.3), channel_id=1, replica_groups=mesh['req'=8,'mdl'=4] {'mdl'}, dimensions={1}, use_global_device_ids=true | all-gather | bytes 163840 | tf_op jit(solution)/shard_map/all_gather | solution.py:165
  109.1 3.5 add_convert_fusion.1
  112.6 2.0 reshape.344
  114.5 2.2 fusion.61
  118.5 1.9 reshape.348
  120.4 4.4 %add_convert_fusion.5 = (bf16[32,4,2048]{2,1,0:T(4,128)(2,1)}, bf16[32,4,2048]{2,1,0:T(4,128)(2,1)}, bf16[32,4,2048]{2,1,0:T(4,128)(2,1)}, bf16[32,4,2048,1]{2,1,0,3:T(4,128)(2,1)}) fusion(f32[2048]{0:T(1024)} %bitcast.202, f32[32,3,2048]{2,1,0:T(4,128)} %bitcast.177, f32[32,1,2048]{2,1,0:T(1,128)S(1)} %copy.86, f32[2048]{0:T(1024)} %bitcast.190, ...), kind=kLoop, calls=%fused_computation.82 | loop fusion | flops 4980736 | bytes 3720192 | tf_op jit(solution)/shard_map/convert_element_type | solution.py:178
  124.8 1.2 reshape.340
  126.0 1.7 fusion.17
  128.6 1.2 reshape.342
  129.8 2.2 broadcast_add_fusion
  132.1 2.5 fusion.39
  137.2 3.8 broadcast_multiply_fusion.8
  142.1 1.9 reshape.347
  148.3 1.9 slice_bitcast_fusion.12
  150.2 1.9 slice_bitcast_fusion.11
  153.0 1.9 slice_bitcast_fusion.1
  155.0 2.3 fusion.23
  157.3 5.1 %gather_fusion.1 = f32[32,8,4096]{2,1,0:T(8,128)} fusion(f32[32,8,4096]{2,1,0:T(8,128)} %bitcast.1, s32[1024]{0:T(1024)} %copy-done.21), kind=kCustom, calls=%fused_computation.1 | custom fusion | bytes 8388736 | tf_op jit(solution)/shard_map/gather | solution.py:158
  162.4 8.0 %reshape.338 = f32[32,8,64,64]{3,2,1,0:T(8,128)} reshape(f32[32,8,4096]{2,1,0:T(8,128)} %gather_fusion.1) | data formatting | bytes 8388608 | tf_op jit(solution)/shard_map/reshape | solution.py:61
  170.4 5.8 %multiply_reduce_fusion.7 = f32[32,8,64]{2,1,0:T(8,128)S(1)} fusion(f32[32,8,64,64]{3,2,1,0:T(8,128)} %reshape.338, f32[32,8,64]{2,1,0:T(8,128)S(1)} %get-tuple-element.90), kind=kLoop, calls=%fused_computation.16 | loop fusion | flops 2080768 | bytes 4325376 | tf_op jit(solution)/shard_map/reduce_sum | solution.py:25
  176.3 11.0 %multiply_reduce_fusion.6 = (f32[32,8,64]{2,1,0:T(8,128)S(1)}, f32[32,8,64]{2,1,0:T(8,128)S(1)}) fusion(f32[32,8,64]{2,1,0:T(8,128)S(1)} %copy-done.8, f32[32,8,64,64]{3,2,1,0:T(8,128)S(1)} %copy-done.2, f32[32,8,64]{2,1,0:T(8,128)S(1)} %get-tuple-element.51, f32[32,8,64]{2,1,0:T(8,128)S(1)} %get-tuple-element.30, f32[32,8,64]{2,1,0:T(8,128)S(1)} %neg.38, ...), kind=kLoop, calls=%fused_computation.14 | loop fusion | flops 10452992 | bytes 4784160 | tf_op jit(solution)/shard_map/reduce_sum | solution.py:31
  188.6 18.7 %multiply_reduce_fusion.3 = (f32[32,8,64]{2,1,0:T(8,128)S(1)}, f32[32,8,64,64]{3,2,1,0:T(8,128)}, f32[32,8,64]{2,1,0:T(8,128)S(1)}, f32[32,8,64,64]{3,2,1,0:T(8,...) fusion(f32[32,8,64]{2,1,0:T(8,128)} %get-tuple-element.92, ...), kind=kLoop, calls=%fused_computation.10 | loop fusion | flops 16744448 | bytes 26083392 | tf_op jit(solution)/shard_map/reduce_sum | solution.py:25
  208.1 12.5 %multiply_reduce_fusion.2 = (f32[32,8,64]{2,1,0:T(8,128)S(1)}, f32[32,8,64]{2,1,0:T(8,128)S(1)}, f32[32,8,64,64]{3,2,1,0:T(8,128)}, f32[32,8,64,64]{3,2,1,0:T(8,128)}) fusion(f32[32,8,64]{2,1,0:T(8,128)} %get-tuple-element.34, f32[32,8,64,64]{3,2,1,0:T(8,128)} %get-tuple-element.18, f32[32,8,64]{2,1,0:T(8,128)S(1)} %get-tuple-element.48, ...), kind=kLoop, calls=%fused_computation.8 | loop fusion | flops 10452992 | bytes 13172768 | tf_op jit(solution)/shard_map/reduce_sum | solution.py:31
  222.0 15.5 %broadcast_multiply_fusion.1 = (f32[32,8,64,64]{3,2,1,0:T(8,128)}, f32[32,8,64]{2,1,0:T(8,128)S(1)}, f32[32,8,64,64]{3,2,1,0:T(8,128)}) fusion(f32[32,8,64]{2,1,0:T(8,128)} %get-tuple-element.31, f32[32,8,64]{2,1,0:T(8,128)} %neg.42, f32[32,8,64]{2,1,0:T(8,128)} %get-tuple-element.33, f32[32,8,64]{2,1,0:T(8,128)} %get-tuple-element.40, ...), kind=kLoop, calls=%fused_computation.19 | loop fusion | flops 13615104 | bytes 13369376 | tf_op jit(solution)/shard_map/mul | solution.py:28
  238.5 1.2 pad_maximum_fusion.1
  241.9 2.8 fusion.19
  246.1 4.5 %all-to-all-start.2 = ((bf16[8,4,512]{2,1,0:T(4,128)(2,1)}), bf16[8,4,512]{2,1,0:T(4,128)(2,1)S(1)}, u32[]{:S(2)}, u32[]{:S(2)}) async-start(bf16[8,4,512]{2,1,0:T(4,128)(2,1)} %reshape.356), calls=%async_computation.3 | async-start | bytes 65536 | tf_op jit(solution)/shard_map/all_to_all | solution.py:156
  250.8 4.6 %all-to-all-done.2 = bf16[8,4,512]{2,1,0:T(4,128)(2,1)S(1)} async-done(((bf16[8,4,512]{2,1,0:T(4,128)(2,1)}), bf16[8,4,512]{2,1,0:T(4,128)(2,1)S(1)}, u32[]{:S(2)}, u32[]{:S(2)}) %all-to-all-start.2) | async-done | bytes 32800 | tf_op jit(solution)/shard_map/all_to_all | solution.py:156
  256.2 14.6 %all_gather.27 = bf16[32,2048]{1,0:T(8,128)(2,1)S(1)} all-gather(bf16[32,512]{1,0:T(8,128)(2,1)S(1)} %gather_fusion.5), channel_id=1, replica_groups=mesh['req'=8,'mdl'=4] {'mdl'}, dimensions={1}, use_global_device_ids=true | all-gather | bytes 163840 | tf_op jit(solution)/shard_map/all_gather | solution.py:166
  271.1 3.7 mul.597
  274.8 8.1 %mul.647 = f32[32,8,4096]{2,1,0:T(8,128)} reshape(f32[32,8,64,64]{3,2,1,0:T(8,128)} %mul.597) | data formatting | bytes 8388608 | tf_op jit(solution)/shard_map/mul | solution.py:27
  282.9 3.7 mul.561
  286.6 7.9 %mul.639 = f32[32,8,4096]{2,1,0:T(8,128)} reshape(f32[32,8,64,64]{3,2,1,0:T(8,128)} %mul.561) | data formatting | bytes 8388608 | tf_op jit(solution)/shard_map/mul | solution.py:27
  294.5 3.7 mul.579
  298.3 7.9 %mul.643 = f32[32,8,4096]{2,1,0:T(8,128)} reshape(f32[32,8,64,64]{3,2,1,0:T(8,128)} %mul.579) | data formatting | bytes 8388608 | tf_op jit(solution)/shard_map/mul | solution.py:27
  306.2 3.7 mul.523
  309.9 7.9 %mul.635 = f32[32,8,4096]{2,1,0:T(8,128)} reshape(f32[32,8,64,64]{3,2,1,0:T(8,128)} %mul.523) | data formatting | bytes 8388608 | tf_op jit(solution)/shard_map/mul | solution.py:27
  317.8 7.9 %mul.637 = f32[32,8,4096]{2,1,0:T(8,128)} reshape(f32[32,8,64,64]{3,2,1,0:T(8,128)} %get-tuple-element.52) | data formatting | bytes 8388608 | tf_op jit(solution)/shard_map/mul | solution.py:28
  325.7 7.9 %mul.638 = f32[32,8,4096]{2,1,0:T(8,128)} reshape(f32[32,8,64,64]{3,2,1,0:T(8,128)} %get-tuple-element.53) | data formatting | bytes 8388608 | tf_op jit(solution)/shard_map/mul | solution.py:29
  333.6 7.9 %mul.641 = f32[32,8,4096]{2,1,0:T(8,128)} reshape(f32[32,8,64,64]{3,2,1,0:T(8,128)} %get-tuple-element.54) | data formatting | bytes 8388608 | tf_op jit(solution)/shard_map/mul | solution.py:28
  341.5 7.9 %mul.642 = f32[32,8,4096]{2,1,0:T(8,128)} reshape(f32[32,8,64,64]{3,2,1,0:T(8,128)} %get-tuple-element.55) | data formatting | bytes 8388608 | tf_op jit(solution)/shard_map/mul | solution.py:29
  349.3 7.9 %mul.645 = f32[32,8,4096]{2,1,0:T(8,128)} reshape(f32[32,8,64,64]{3,2,1,0:T(8,128)} %get-tuple-element.56) | data formatting | bytes 8388608 | tf_op jit(solution)/shard_map/mul | solution.py:28
  357.3 7.9 %mul.646 = f32[32,8,4096]{2,1,0:T(8,128)} reshape(f32[32,8,64,64]{3,2,1,0:T(8,128)} %get-tuple-element.57) | data formatting | bytes 8388608 | tf_op jit(solution)/shard_map/mul | solution.py:29
  365.2 7.9 %mul.649 = f32[32,8,4096]{2,1,0:T(8,128)} reshape(f32[32,8,64,64]{3,2,1,0:T(8,128)} %get-tuple-element.58) | data formatting | bytes 8388608 | tf_op jit(solution)/shard_map/mul | solution.py:28
  373.1 7.9 %mul.650 = f32[32,8,4096]{2,1,0:T(8,128)} reshape(f32[32,8,64,64]{3,2,1,0:T(8,128)} %get-tuple-element.60) | data formatting | bytes 8388608 | tf_op jit(solution)/shard_map/mul | solution.py:29
  382.1 16.0 %all_gather.26 = bf16[32,4,2048]{2,1,0:T(4,128)(2,1)S(1)} all-gather(bf16[32,4,512]{2,1,0:T(4,128)(2,1)S(1)} %add_convert_fusion.6), channel_id=1, replica_groups=mesh['req'=8,'mdl'=4] {'mdl'}, dimensions={2}, use_global_device_ids=true | all-gather | bytes 655360 | tf_op jit(solution)/shard_map/all_gather | solution.py:227
  400.6 5.6 %convolution_convert_fusion = bf16[128,2048]{1,0:T(8,128)(2,1)} fusion(bf16[1024,2048]{1,0:T(8,128)(2,1)} %param.41, bf16[128,2048]{1,0:T(8,128)(2,1)S(1)} %reshape.351, bf16[2048,1024]{1,0:T(8,128)(2,1)} %param.40), kind=kOutput, calls=%fused_computation.29 | convolution fusion | flops 1074397184 | bytes 9437184 | tf_op jit(solution)/shard_map/dot_general | solution.py:14
  406.3 22.3 %add_select_fusion = f32[32,8,4096]{2,1,0:T(8,128)} fusion(f32[32,8,4096]{2,1,0:T(8,128)} %mul.650, f32[32,8,4096]{2,1,0:T(8,128)} %mul.649, f32[32,8,4096]{2,1,0:T(8,128)} %mul.647, f32[32,8,4096]{2,1,0:T(8,128)} %mul.646, f32[32,8,4096]{2,1,0:T(8,128)} %mul.645, f32[32,8,4096]{2,1,0:T(8,128)} %mul.643, f32[32,8,4096]{2,1,0:T(8,128)} %mul.642, ...), kind=kLoop, calls=%fused_computation.17 | loop fusion | flops 16777216 | bytes 58720384 | tf_op jit(solution)/shard_map/jit(_where)/select_n | solution.py:32
  428.5 2.0 multiply_reduce_fusion.10
  (146 shorter events, 32.7 us)
Async XLA Ops:
  7.2 234.7 %copy-start = (bf16[512,2048]{1,0:T(8,128)(2,1)S(1)}, bf16[512,2048]{1,0:T(8,128)(2,1)}, u32[]{:S(2)}) copy-start(bf16[512,2048]{1,0:T(8,128)(2,1)} %param.33) | copy-start | bytes 6291460
  7.2 147.8 %all-gather.2.cloned.1.call-start = ((), (), s32[]{:S(2)}) async-start(), calls=%async_computation.5 | async-start | bytes 1310720 | tf_op jit(solution)/shard_map/all_gather | solution.py:185
  10.3 79.1 %copy-start.20 = (s32[1024]{0:T(1024)}, s32[1024]{0:T(1024)S(1)}, u32[]{:S(2)}) copy-start(s32[1024]{0:T(1024)S(1)} %pad_clamp_fusion.1) | copy-start | bytes 12292
  12.3 77.0 %all-to-all-start.1 = ((bf16[8,4,512]{2,1,0:T(4,128)(2,1)}), bf16[8,4,512]{2,1,0:T(4,128)(2,1)S(1)}, u32[]{:S(2)}, u32[]{:S(2)}) async-start(bf16[8,4,512]{2,1,0:T(4,128)(2,1)} %reshape.354), calls=%async_computation.1 | async-start | bytes 65536 | tf_op jit(solution)/shard_map/all_to_all | solution.py:155
  25.9 63.5 %copy-start.11 = (f32[1,2048]{1,0:T(1,128)}, f32[1,2048]{1,0:T(1,128)S(1)}, u32[]{:S(2)}) copy-start(f32[1,2048]{1,0:T(1,128)S(1)} %get-tuple-element.70) | copy-start | bytes 24580
  25.9 63.5 %copy-start.12 = (f32[1,2048]{1,0:T(1,128)}, f32[1,2048]{1,0:T(1,128)S(1)}, u32[]{:S(2)}) copy-start(f32[1,2048]{1,0:T(1,128)S(1)} %get-tuple-element.71) | copy-start | bytes 24580
  78.9 10.5 %copy-start.10 = (f32[32,4]{1,0:T(8,128)}, f32[32,4]{1,0:T(8,128)S(1)}, u32[]{:S(2)}) copy-start(f32[32,4]{1,0:T(8,128)S(1)} %add_sqrt_fusion.3) | copy-start | bytes 1540
  80.4 13.8 %copy-start.21 = (s32[1024]{0:T(1024)}, s32[1024]{0:T(1024)S(1)}, u32[]{:S(2)}) copy-start(s32[1024]{0:T(1024)S(1)} %pad_clamp_fusion) | copy-start | bytes 12292
  89.4 67.9 %all-to-all-start = ((f32[8,4,8,4096]{3,2,1,0:T(8,128)}), f32[8,4,8,4096]{3,2,1,0:T(8,128)}, u32[]{:S(2)}, u32[]{:S(2)}) async-start(f32[8,4,8,4096]{3,2,1,0:T(8,128)} %bitcast.175), calls=%async_computation | async-start | bytes 8388608 | tf_op jit(solution)/shard_map/all_to_all | solution.py:154
  94.2 286.8 %reduce-scatter.3.cloned.1.call-start = ((), (), s32[]{:S(2)}) async-start(), calls=%async_computation.6 | async-start | bytes 1310720 | tf_op jit(solution)/shard_map/reduce_scatter | solution.py:223
  162.4 13.8 %copy-start.5 = (f32[32,8,64]{2,1,0:T(8,128)S(1)}, f32[32,8,64]{2,1,0:T(8,128)}, u32[]{:S(2)}) copy-start(f32[32,8,64]{2,1,0:T(8,128)} %copy.91) | copy-start | bytes 196612
  162.4 13.8 %copy-start.19 = (pred[32]{0:T(512)(128)(4,1)S(1)}, pred[32]{0:T(512)(128)(4,1)}, u32[]{:S(2)}) copy-start(pred[32]{0:T(512)(128)(4,1)} %get-tuple-element.83) | copy-start | bytes 100
  170.4 5.8 %copy-start.2 = (f32[32,8,64,64]{3,2,1,0:T(8,128)S(1)}, f32[32,8,64,64]{3,2,1,0:T(8,128)}, u32[]{:S(2)}) copy-start(f32[32,8,64,64]{3,2,1,0:T(8,128)} %reshape.338) | copy-start | bytes 12582916
  170.4 5.8 %copy-start.8 = (f32[32,8,64]{2,1,0:T(8,128)S(1)}, f32[32,8,64]{2,1,0:T(8,128)}, u32[]{:S(2)}) copy-start(f32[32,8,64]{2,1,0:T(8,128)} %get-tuple-element.35) | copy-start | bytes 196612
  170.4 18.2 %copy-start.22 = (pred[32]{0:T(512)(128)(4,1)S(1)}, pred[32]{0:T(512)(128)(4,1)}, u32[]{:S(2)}) copy-start(pred[32]{0:T(512)(128)(4,1)} %get-tuple-element.82) | copy-start | bytes 100
  188.6 19.5 %copy-start.4 = (f32[32,8,64]{2,1,0:T(8,128)S(1)}, f32[32,8,64]{2,1,0:T(8,128)}, u32[]{:S(2)}) copy-start(f32[32,8,64]{2,1,0:T(8,128)} %copy.96) | copy-start | bytes 196612
  188.6 19.5 %copy-start.18 = (pred[32]{0:T(512)(128)(4,1)S(1)}, pred[32]{0:T(512)(128)(4,1)}, u32[]{:S(2)}) copy-start(pred[32]{0:T(512)(128)(4,1)} %get-tuple-element.81) | copy-start | bytes 100
  208.1 13.9 %copy-start.7 = (f32[32,8,64]{2,1,0:T(8,128)S(1)}, f32[32,8,64]{2,1,0:T(8,128)}, u32[]{:S(2)}) copy-start(f32[32,8,64]{2,1,0:T(8,128)} %get-tuple-element.49) | copy-start | bytes 196612
  222.0 19.8 %copy-start.16 = (f32[1,512]{1,0:T(1,128)S(1)}, f32[1,512]{1,0:T(1,128)}, u32[]{:S(2)}) copy-start(f32[1,512]{1,0:T(1,128)} %get-tuple-element.73) | copy-start | bytes 6148
  222.0 19.8 %copy-start.17 = (f32[1,512]{1,0:T(1,128)S(1)}, f32[1,512]{1,0:T(1,128)}, u32[]{:S(2)}) copy-start(f32[1,512]{1,0:T(1,128)} %get-tuple-element.79) | copy-start | bytes 6148
  237.6 7.1 %copy-start.3 = (bf16[32,512]{1,0:T(8,128)(2,1)S(1)}, bf16[32,512]{1,0:T(8,128)(2,1)}, u32[]{:S(2)}) copy-start(bf16[32,512]{1,0:T(8,128)(2,1)} %param.26) | copy-start | bytes 98308
  237.6 13.0 %copy-start.26 = (s32[32]{0:T(128)S(1)}, s32[32]{0:T(128)}, u32[]{:S(2)}) copy-start(s32[32]{0:T(128)} %param.22) | copy-start | bytes 388
  237.6 13.1 %copy-start.24 = (pred[32,4]{0,1:T(4,128)(4,1)S(1)}, pred[32,4]{0,1:T(4,128)(4,1)}, u32[]{:S(2)}) copy-start(pred[32,4]{0,1:T(4,128)(4,1)} %get-tuple-element.84) | copy-start | bytes 388
  246.1 9.4 %all-to-all-start.2 = ((bf16[8,4,512]{2,1,0:T(4,128)(2,1)}), bf16[8,4,512]{2,1,0:T(4,128)(2,1)S(1)}, u32[]{:S(2)}, u32[]{:S(2)}) async-start(bf16[8,4,512]{2,1,0:T(4,128)(2,1)} %reshape.356), calls=%async_computation.3 | async-start | bytes 65536 | tf_op jit(solution)/shard_map/all_to_all | solution.py:156
  250.6 179.9 %reduce-scatter.5.cloned.1.call-start = ((), (), s32[]{:S(2)}) async-start(), calls=%async_computation.7 | async-start | bytes 655360 | tf_op jit(solution)/shard_map/reduce_scatter | solution.py:239
  274.8 8.1 %copy-start.6 = (f32[32,8,64]{2,1,0:T(8,128)S(1)}, f32[32,8,64]{2,1,0:T(8,128)}, u32[]{:S(2)}) copy-start(f32[32,8,64]{2,1,0:T(8,128)} %get-tuple-element.50) | copy-start | bytes 196612
  373.1 9.0 %copy-start.9 = (bf16[32,4,512]{2,1,0:T(4,128)(2,1)S(1)}, bf16[32,4,512]{2,1,0:T(4,128)(2,1)}, u32[]{:S(2)}) copy-start(bf16[32,4,512]{2,1,0:T(4,128)(2,1)} %param.21) | copy-start | bytes 393220
  373.1 25.9 %copy-start.13 = (f32[1,2048]{1,0:T(1,128)S(1)}, f32[1,2048]{1,0:T(1,128)}, u32[]{:S(2)}) copy-start(f32[1,2048]{1,0:T(1,128)} %get-tuple-element.69) | copy-start | bytes 24580
  373.1 25.9 %copy-start.14 = (f32[1,2048]{1,0:T(1,128)S(1)}, f32[1,2048]{1,0:T(1,128)}, u32[]{:S(2)}) copy-start(f32[1,2048]{1,0:T(1,128)} %get-tuple-element.72) | copy-start | bytes 24580
  373.1 26.4 %copy-start.15 = (f32[1,2048]{1,0:T(1,128)S(1)}, f32[1,2048]{1,0:T(1,128)}, u32[]{:S(2)}) copy-start(f32[1,2048]{1,0:T(1,128)} %get-tuple-element.62) | copy-start | bytes 24580
  382.1 24.1 %copy-start.23 = (pred[32]{0:T(512)(128)(4,1)S(1)}, pred[32]{0:T(512)(128)(4,1)}, u32[]{:S(2)}) copy-start(pred[32]{0:T(512)(128)(4,1)} %get-tuple-element.82) | copy-start | bytes 100
  382.1 24.1 %copy-start.25 = (pred[32]{0:T(512)(128)(4,1)S(1)}, pred[32]{0:T(512)(128)(4,1)}, u32[]{:S(2)}) copy-start(pred[32]{0:T(512)(128)(4,1)} %get-tuple-element.80) | copy-start | bytes 100
  406.2 26.0 %copy-start.1 = (bf16[512,2048]{1,0:T(8,128)(2,1)S(1)}, bf16[512,2048]{1,0:T(8,128)(2,1)}, u32[]{:S(2)}) copy-start(bf16[512,2048]{1,0:T(8,128)(2,1)} %param.33) | copy-start | bytes 6291460
Sparse Core Ops, SparseCore 0:
  9.6 36.9 all-gather.1
  244.8 30.9 reduce-scatter.2
  406.4 20.1 reduce-scatter.4
where the time goes:
time: 445 us; the launch traced here: 439 us
  local copies, waits for them, and re-layouts  175 us (39%)
  other arithmetic  112 us (25%)
  blocking collectives  94.9 us (21%)
  matrix products  23 us (5%)
  starting transfers between devices  14.6 us (3%)
  between operations  14.5 us (3%)
  waiting for transfers between devices  5.32 us (1%)
    mul x9, local copies, waits for them, and re-layouts, advance(): wkv_square * decay_now[:, :, None, :]  48.6 us
    mul x10, local copies, waits for them, and re-layouts, advance(): value_now[..., None] * key_now[:, :, None, :]  37.6 us
    mul x4, local copies, waits for them, and re-layouts, advance(): removal[..., None] * (unit_now * alpha_now)[:, :, None, :]  31.6 us
    reduce_sum x2, other arithmetic, advance(): removal = -jnp.sum(wkv_square * unit_now[:, :, None, :], axis=-1)  24.5 us
    reduce_sum x2, other arithmetic, advance(): jnp.sum(updated * recept_now[:, :, None, :], axis=-1)  23.4 us
    dot_general x8, matrix products, project(): return jnp.dot(inputs, weight, preferred_element_type=jnp.float32)  23 us
    select_n x1, other arithmetic, advance(): jnp.where(is_valid[:, None, None, None], updated, wkv_square)  22.3 us
    all_gather x1, blocking collectives, per_device(): lax.all_gather(decay_down, 'mdl', axis=0, tiled=True)  20.2 us
  transfers between devices with their start and end apart: 6, of which 1 were waited for; matrix products, arithmetic and copies ran while one was open for 48% of the time, Pallas kernels for 0%

commit v1 on v0

v1 whole, which is shorter than its diff:
```python
import functools

import jax
import jax.numpy as jnp
from jax import lax
from jax.experimental import pallas as pl
from jax.experimental.pallas import tpu as pltpu
from jax.sharding import PartitionSpec as P

F32 = jnp.float32
BF16 = jnp.bfloat16
VMEM_LIMIT = 56 * 1024 * 1024


def xor_permute(x, axis, size, k):
    return lax.ppermute(x, axis, [(a, a ^ k) for a in range(size)])


def params(limit=VMEM_LIMIT):
    return pltpu.CompilerParams(vmem_limit_bytes=limit)


def full_spec(shape):
    return pl.BlockSpec(shape, lambda *_: (0,) * len(shape))


def dot32(a, b):
    return jnp.dot(a, b, preferred_element_type=F32)


def pack_states(wkv_state, order, per_pair, groups):
    heads, cells = wkv_state.shape[1:]

    def body(order_ref, in_ref, *out_refs):
        step = pl.program_id(0)
        for k in range(groups):

            @pl.when(step // per_pair == k)
            def _():
                out_refs[k][...] = in_ref[...].astype(BF16)

    def out_map(k, step, order_ref):
        return (jnp.clip(step - k * per_pair, 0, per_pair - 1), 0, 0)

    return pl.pallas_call(
        body,
        grid_spec=pltpu.PrefetchScalarGridSpec(
            num_scalar_prefetch=1,
            grid=(groups * per_pair,),
            in_specs=[pl.BlockSpec((1, heads, cells), lambda s, o: (o[s], 0, 0))],
            out_specs=[
                pl.BlockSpec((1, heads, cells), functools.partial(out_map, k))
                for k in range(groups)
            ],
        ),
        out_shape=[jax.ShapeDtypeStruct((per_pair, heads, cells), BF16) for _ in range(groups)],
        compiler_params=params(),
        name="pack_states",
    )(order, wkv_state)


def states_to_lanes(rank, payloads, requests, lanes):
    groups = len(payloads)
    per_pair, heads, cells = payloads[0].shape
    head_size = 64
    step_chunks = 4
    steps = cells // (128 * step_chunks)
    half = lanes // requests
    halves = heads // half

    def body(rank_ref, *refs):
        ins, out_ref, rows = refs[:groups], refs[groups], refs[groups + 1]
        for c in range(step_chunks):
            for k in range(groups):
                base = (rank_ref[0] ^ k) * (per_pair * heads)
                for j in range(per_pair):
                    tile = ins[k][j, :, c * 128 : (c + 1) * 128].astype(F32)
                    rows[c, pl.ds(pl.multiple_of(base + j * heads, heads), heads), :] = tile
        for c in range(step_chunks):
            for g in range(halves):
                block = jnp.concatenate(
                    [
                        rows[c, pl.ds(g * half + h, requests, stride=heads), :]
                        for h in range(half)
                    ],
                    axis=0,
                )
                turned = block.T
                out_ref[g, 2 * c] = turned[:head_size]
                out_ref[g, 2 * c + 1] = turned[head_size:]

    return pl.pallas_call(
        body,
        grid_spec=pltpu.PrefetchScalarGridSpec(
            num_scalar_prefetch=1,
            grid=(steps,),
            in_specs=[
                pl.BlockSpec((per_pair, heads, 128 * step_chunks), lambda s, r: (0, 0, s))
                for _ in range(groups)
            ],
            out_specs=pl.BlockSpec(
                (halves, 2 * step_chunks, head_size, lanes), lambda s, r: (0, s, 0, 0)
            ),
            scratch_shapes=[pltpu.VMEM((step_chunks, requests * heads, 128), F32)],
        ),
        out_shape=jax.ShapeDtypeStruct((halves, cells // head_size, head_size, lanes), F32),
        compiler_params=params(),
        name="states_to_lanes",
    )(rank, *payloads)


def first_norm(place, toks, atts, row_source, count_col, back_col, norm, mix, downs):
    rows, width = toks[0].shape
    parts = len(toks)
    total = parts * width
    requests = count_col.shape[0]
    slots = rows // requests
    rank_d, rank_a, rank_g = [w.shape[1] for w in downs]

    def body(place_ref, *refs):
        tok = refs[:parts]
        att = refs[parts : 2 * parts]
        src, cnt, back, nrm, mx, dd, ad, gd = refs[2 * parts : 2 * parts + 8]
        normed_ref, low_ref, lowsend_ref, shift_ref = refs[2 * parts + 8 :]
        pick = (lax.broadcasted_iota(jnp.int32, (rows, rows), 1) == src[...]).astype(BF16)
        xs = [dot32(pick, t[...]) for t in tok]
        mean = sum(jnp.sum(x, axis=1, keepdims=True) for x in xs) / total
        cs = [x - mean for x in xs]
        var = sum(jnp.sum(c * c, axis=1, keepdims=True) for c in cs) / total
        scale = lax.rsqrt(var + 1e-05)
        for k in range(parts):
            at = pl.ds(pl.multiple_of((place_ref[0] ^ k) * width, 128), width)
            normed_ref[k] = cs[k] * scale * nrm[0:1, at] + nrm[1:2, at]
        at = pl.ds(pl.multiple_of(place_ref[0] * width, 128), width)
        now = normed_ref[0]
        before = jnp.concatenate([att[0][0:requests].astype(F32), now[: rows - requests]], axis=0)
        delta = before - now
        low_ref[...] = jnp.zeros(low_ref.shape, F32)
        low_ref[:, 0:rank_d] = dot32((now + delta * mx[1:2, at]).astype(BF16), dd[...])
        low_ref[:, 128 : 128 + rank_a] = dot32((now + delta * mx[4:5, at]).astype(BF16), ad[...])
        low_ref[:, 256 : 256 + rank_g] = dot32((now + delta * mx[5:6, at]).astype(BF16), gd[...])
        lowsend_ref[...] = low_ref[...].astype(BF16)
        chosen = jnp.zeros((requests, width), F32)
        for t in range(slots):
            chosen = jnp.where(cnt[...] == t + 1, now[t * requests : (t + 1) * requests], chosen)
        unpick = (
            lax.broadcasted_iota(jnp.int32, (requests, requests), 1) == back[...]
        ).astype(BF16)
        shift_ref[...] = dot32(unpick, chosen.astype(BF16)).astype(BF16)

    low_width = 256 + rank_g
    args = (*toks, *atts, row_source, count_col, back_col, norm, mix, *downs)
    return pl.pallas_call(
        body,
        grid_spec=pltpu.PrefetchScalarGridSpec(
            num_scalar_prefetch=1,
            grid=(1,),
            in_specs=[full_spec(a.shape) for a in args],
            out_specs=[
                full_spec((parts, rows, width)),
                full_spec((rows, low_width)),
                full_spec((rows, low_width)),
                full_spec((requests, width)),
            ],
        ),
        out_shape=[
            jax.ShapeDtypeStruct((parts, rows, width), F32),
            jax.ShapeDtypeStruct((rows, low_width), F32),
            jax.ShapeDtypeStruct((rows, low_width), BF16),
            jax.ShapeDtypeStruct((requests, width), BF16),
        ],
        compiler_params=params(),
        name="first_norm",
    )(place, *args)


def projections(place, normed, atts, mix, weights, requests):
    parts, rows, width = normed.shape
    out_width = weights[0].shape[1]

    def body(place_ref, n_ref, *refs):
        att = refs[:parts]
        mx = refs[parts]
        w = refs[parts + 1 : parts + 4]
        outs = refs[parts + 4 : parts + 7]
        k = pl.program_id(0)
        at = pl.ds(pl.multiple_of((place_ref[0] ^ k) * width, 128), width)
        now = n_ref[0]
        prev = att[0][0:requests]
        for other in range(1, parts):
            prev = jnp.where(k == other, att[other][0:requests], prev)
        before = jnp.concatenate([prev.astype(F32), now[: rows - requests]], axis=0)
        delta = before - now
        for which, c in enumerate((0, 2, 3)):
            term = dot32((now + delta * mx[c : c + 1, at]).astype(BF16), w[which][...])

            @pl.when(k == 0)
            def _():
                outs[which][...] = term

            @pl.when(k > 0)
            def _():
                outs[which][...] += term

    return pl.pallas_call(
        body,
        grid_spec=pltpu.PrefetchScalarGridSpec(
            num_scalar_prefetch=1,
            grid=(parts,),
            in_specs=[pl.BlockSpec((1, rows, width), lambda k, p: (k, 0, 0))]
            + [full_spec(a.shape) for a in atts]
            + [full_spec(mix.shape)]
            + [pl.BlockSpec((width, out_width), lambda k, p: (p[0] ^ k, 0)) for _ in weights],
            out_specs=[full_spec((rows, out_width)) for _ in weights],
        ),
        out_shape=[jax.ShapeDtypeStruct((rows, out_width), F32) for _ in weights],
        compiler_params=params(),
        name="projections",
    )(place, normed, *atts, mix, *weights)


def swap_groups(arrays, lane_group, flag_one, flag_two):
    a0, a1, a2, a3 = arrays
    lanes = 4 * lane_group
    up = lambda x: pltpu.roll(x, lane_group, 1)
    down = lambda x: pltpu.roll(x, lanes - lane_group, 1)
    far = lambda x: pltpu.roll(x, 2 * lane_group, 1)
    b0 = jnp.where(flag_one, a0, up(a1))
    b1 = jnp.where(flag_one, down(a0), a1)
    b2 = jnp.where(flag_one, a2, up(a3))
    b3 = jnp.where(flag_one, down(a2), a3)
    return [
        jnp.where(flag_two, b0, far(b2)),
        jnp.where(flag_two, b1, far(b3)),
        jnp.where(flag_two, far(b0), b2),
        jnp.where(flag_two, far(b1), b3),
    ]


def fold_eight(items, flags):
    shift = 1
    for flag in flags:
        items = [
            jnp.where(flag, a, b) + pltpu.roll(jnp.where(flag, b, a), shift, 0)
            for a, b in zip(items[0::2], items[1::2])
        ]
        shift *= 2
    return items[0]


def heads_step(
    place, low_own, low_others, recept, key, value, states, head_params, ups, out_weight, count_row
):
    rows, width = recept.shape
    halves, size, _, lanes = states.shape
    parts = len(low_others) + 1
    slots = 4
    requests = rows // slots
    half = lanes // requests
    n_groups = width // 128
    rank_d, rank_a, rank_g = [w.shape[0] for w in ups]

    def body(place_ref, *refs):
        low = refs[0]
        others = refs[1:parts]
        (r_ref, k_ref, v_ref, st_hbm, hp, du, au, gu, wo_hbm, cnt) = refs[parts : parts + 10]
        outs = refs[parts + 10 : 2 * parts + 10]
        p_out, v_out, kq_out, uq_out, d_out = refs[2 * parts + 10 : 2 * parts + 15]
        st, wo, vec, wvec, prod, normed, sems = refs[2 * parts + 15 :]
        copy_states = pltpu.make_async_copy(st_hbm, st, sems.at[0])
        copy_weight = pltpu.make_async_copy(wo_hbm, wo, sems.at[1])
        copy_states.start()
        copy_weight.start()

        total = low[...]
        for o in others:
            total = total + o[...].astype(F32)
        dlow = jnp.tanh(total[:, 0:rank_d]).astype(BF16)
        alow = total[:, 128 : 128 + rank_a].astype(BF16)
        glow = jax.nn.sigmoid(total[:, 256 : 256 + rank_g]).astype(BF16)
        decay = jnp.exp(-0.606531 * jax.nn.sigmoid(hp[0:1] + dot32(dlow, du[...])))
        context = jax.nn.sigmoid(hp[1:2] + dot32(alow, au[...]))
        gate = dot32(glow, gu[...])
        r = r_ref[...]
        k = k_ref[...]
        v = v_ref[...]
        scaled = k * hp[2:3]
        kmod = k * (1.0 + (context - 1.0) * hp[3:4])
        rk = r * kmod * hp[4:5]

        lane = lax.broadcasted_iota(jnp.int32, (size, lanes), 1)
        flag_one = (lane // requests) % 2 == 0
        flag_two = (lane // requests) // 2 == 0
        for index, array in enumerate((r, kmod, scaled, decay, context, v)):
            pieces = []
            for g in range(n_groups):
                turned = array[:, g * 128 : (g + 1) * 128].T
                pieces += [turned[:size], turned[size:]]
            for g in range(halves):
                swapped = swap_groups(pieces[g * half : (g + 1) * half], requests, flag_one, flag_two)
                for t in range(slots):
                    vec[index, g, t] = swapped[t]

        sub = lax.broadcasted_iota(jnp.int32, (8, lanes), 0)
        folds = [(sub // s) % 2 == 0 for s in (1, 2, 4)]
        valid = [cnt[...] > t for t in range(slots)]
        ksum = lambda x, y: jnp.sum(x * y, axis=0, keepdims=True)

        coefs = []
        for g in range(halves):
            for t in range(slots):
                s = vec[2, g, t]
                unit = s * lax.rsqrt(jnp.sum(s * s, axis=0, keepdims=True) + 1e-06)
                vec[2, g, t] = unit
                vec[4, g, t] = unit * vec[4, g, t]
            cu, cr = {}, {}

            def back_through(x, top, into, s):
                for b in range(top, -1, -1):
                    into[s, b] = jnp.where(valid[b], ksum(vec[1, g, b], x), 0.0)
                    moved = vec[3, g, b] * x - vec[2, g, b] * ksum(vec[4, g, b], x)
                    x = jnp.where(valid[b], moved, x)
                return x

            for t in range(slots):
                wvec[g, t] = back_through(vec[2, g, t], t - 1, cu, t)
                x = vec[0, g, t]
                cr[t, t] = ksum(vec[1, g, t], x)
                x = vec[3, g, t] * x - vec[2, g, t] * ksum(vec[4, g, t], x)
                wvec[g, slots + t] = back_through(x, t - 1, cr, t)
            coefs.append((cu, cr))
            run = jnp.ones((size, lanes), F32)
            for t in range(slots - 1, -1, -1):
                kq_out[g, t] = jnp.where(valid[t], vec[1, g, t] * run, 0.0)
                uq_out[g, t] = jnp.where(valid[t], -(vec[4, g, t] * run), 0.0)
                run = jnp.where(valid[t], run * vec[3, g, t], run)
                v_out[g, t] = vec[5, g, t]
            d_out[g] = run

        copy_states.wait()
        quad = 4
        for g in range(halves):
            for part in range(2 * slots // quad):

                def products(block, _):
                    ws = [wvec[g, part * quad + w] for w in range(quad)]
                    sums = [[] for _ in range(quad)]
                    for i in range(8):
                        s = st[g, block * 8 + i]
                        for w in range(quad):
                            term = s * ws[w]
                            acc = term[0:8]
                            for jv in range(1, size // 8):
                                acc = acc + term[jv * 8 : (jv + 1) * 8]
                            sums[w].append(acc)
                    for w in range(quad):
                        prod[g, part * quad + w, pl.ds(pl.multiple_of(block * 8, 8), 8), :] = (
                            fold_eight(sums[w], folds)
                        )
                    return 0

                lax.fori_loop(0, size // 8, products, 0)

        backs = []
        for g in range(halves):
            cu, cr = coefs[g]
            outs_t = []
            for t in range(slots):
                removed = prod[g, t]
                y = prod[g, slots + t] + cr[t, t] * vec[5, g, t]
                for b in range(t):
                    removed = removed + cu[t, b] * vec[5, g, b]
                    y = y + cr[t, b] * vec[5, g, b]
                p_out[g, t] = removed
                center = y - jnp.mean(y, axis=0, keepdims=True)
                spread = jnp.mean(center * center, axis=0, keepdims=True)
                outs_t.append(center * lax.rsqrt(spread + 0.00064))
            backs += swap_groups(outs_t, requests, flag_one, flag_two)
        lane_r = lax.broadcasted_iota(jnp.int32, (128, 128), 0)
        lane_c = lax.broadcasted_iota(jnp.int32, (128, 128), 1)
        ones = ((lane_r // size) == (lane_c // size)).astype(BF16)
        for g in range(n_groups):
            cols = slice(g * 128, (g + 1) * 128)
            turned = jnp.concatenate([backs[2 * g], backs[2 * g + 1]], axis=0).T
            rkg = rk[:, cols]
            high = rkg.astype(BF16)
            bonus = dot32(high, ones) + dot32((rkg - high.astype(F32)).astype(BF16), ones)
            done = (turned * hp[5:6, cols] + hp[6:7, cols] + bonus * v[:, cols]) * gate[:, cols]
            normed[:, cols] = done.astype(BF16)
        copy_weight.wait()
        for q in range(parts):
            at = pl.ds(pl.multiple_of((place_ref[0] ^ q) * width, 128), width)
            outs[q][...] = dot32(normed[...], wo[:, at]).astype(outs[q].dtype)

    vector = lambda n: jax.ShapeDtypeStruct((halves, n, size, lanes), F32)
    args = (low_own, *low_others, recept, key, value)
    out_shape = (
        [jax.ShapeDtypeStruct((rows, width), F32)]
        + [jax.ShapeDtypeStruct((rows, width), BF16) for _ in range(parts - 1)]
        + [vector(slots) for _ in range(4)]
        + [jax.ShapeDtypeStruct((halves, size, lanes), F32)]
    )
    anywhere = pl.BlockSpec(memory_space=pl.ANY)
    return pl.pallas_call(
        body,
        grid_spec=pltpu.PrefetchScalarGridSpec(
            num_scalar_prefetch=1,
            grid=(1,),
            in_specs=[full_spec(a.shape) for a in args]
            + [anywhere, full_spec(head_params.shape)]
            + [full_spec(u.shape) for u in ups]
            + [anywhere, full_spec(count_row.shape)],
            out_specs=[full_spec(o.shape) for o in out_shape],
            scratch_shapes=[
                pltpu.VMEM(states.shape, F32),
                pltpu.VMEM(out_weight.shape, BF16),
                pltpu.VMEM((6, halves, slots, size, lanes), F32),
                pltpu.VMEM((halves, 2 * slots, size, lanes), F32),
                pltpu.VMEM((halves, 2 * slots, size, lanes), F32),
                pltpu.VMEM((rows, width), BF16),
                pltpu.SemaphoreType.DMA((2,)),
            ],
        ),
        out_shape=out_shape,
        compiler_params=params(),
        name="heads_step",
    )(place, *args, states, head_params, *ups, out_weight, count_row)


def final_states(arriving, states, removed, values, keys, units, decay, heads):
    halves, size, _, lanes = states.shape
    slots = removed.shape[1]
    requests = arriving.shape[0]
    half = lanes // requests
    step_chunks = 4
    steps = size // (2 * step_chunks)
    cells = size * size

    def body(arr_ref, st, p_ref, v_ref, kq_ref, uq_ref, d_ref, out_ref, new, rows):
        for g in range(halves):

            def update(block, _):
                first = block * 4
                lefts = []
                for i in range(4):
                    row = [v_ref[g, t, pl.ds(first + i, 1), :] for t in range(slots)]
                    row += [p_ref[g, t, pl.ds(first + i, 1), :] for t in range(slots)]
                    lefts.append([jnp.broadcast_to(x, (8, lanes)) for x in row])
                for jv in range(size // 8):
                    at = slice(jv * 8, (jv + 1) * 8)
                    rights = [kq_ref[g, t, at, :] for t in range(slots)]
                    rights += [uq_ref[g, t, at, :] for t in range(slots)]
                    decayed = d_ref[g, at, :]
                    for i in range(4):
                        acc = st[g, first + i, at, :] * decayed
                        for left, right in zip(lefts[i], rights):
                            acc = acc + left * right
                        new[g, first + i, at, :] = acc
                return 0

            lax.fori_loop(0, 2 * step_chunks // 4, update, 0)
        for c in range(step_chunks):
            for g in range(halves):
                turned = jnp.concatenate([new[g, 2 * c], new[g, 2 * c + 1]], axis=0).T
                for h in range(half):
                    rows[c, pl.ds(g * half + h, requests, stride=heads), :] = turned[
                        h * requests : (h + 1) * requests
                    ]
        for c in range(step_chunks):
            for q in range(requests):
                out_ref[arr_ref[q], :, c * 128 : (c + 1) * 128] = rows[
                    c, q * heads : (q + 1) * heads, :
                ]

    per_step = lambda s, a: (0, 0, s, 0)
    return pl.pallas_call(
        body,
        grid_spec=pltpu.PrefetchScalarGridSpec(
            num_scalar_prefetch=1,
            grid=(steps,),
            in_specs=[
                pl.BlockSpec((halves, 2 * step_chunks, size, lanes), lambda s, a: (0, s, 0, 0)),
                pl.BlockSpec((halves, slots, 2 * step_chunks, lanes), per_step),
                pl.BlockSpec((halves, slots, 2 * step_chunks, lanes), per_step),
                full_spec(keys.shape),
                full_spec(units.shape),
                full_spec(decay.shape),
            ],
            out_specs=pl.BlockSpec((requests, heads, 128 * step_chunks), lambda s, a: (0, 0, s)),
            scratch_shapes=[
                pltpu.VMEM((halves, 2 * step_chunks, size, lanes), F32),
                pltpu.VMEM((step_chunks, requests * heads, 128), F32),
            ],
        ),
        out_shape=jax.ShapeDtypeStruct((requests, heads, cells), F32),
        compiler_params=params(),
        name="final_states",
    )(arriving, states, removed, values, keys, units, decay)


def middle(tok, row_source, own, others):
    rows, width = tok.shape

    def body(tok_ref, src, own_ref, *refs):
        out = refs[-1]
        pick = (lax.broadcasted_iota(jnp.int32, (rows, rows), 1) == src[...]).astype(BF16)
        total = dot32(pick, tok_ref[...]) + own_ref[...]
        for o in refs[:-1]:
            total = total + o[...].astype(F32)
        out[...] = total.astype(BF16)

    args = (tok, row_source, own, *others)
    return pl.pallas_call(
        body,
        grid=(1,),
        in_specs=[full_spec(a.shape) for a in args],
        out_specs=full_spec((rows, width)),
        out_shape=jax.ShapeDtypeStruct((rows, width), BF16),
        compiler_params=params(),
        name="middle",
    )(*args)


def channel_mix(place, mids, prevs, count_col, back_col, norm, mix, key_weight, value_weight):
    parts = len(mids)
    rows, width = mids[0].shape
    total = parts * width
    hidden_width = key_weight.shape[1]
    requests = count_col.shape[0]
    slots = rows // requests

    def body(place_ref, *refs):
        mid = refs[:parts]
        prev = refs[parts : 2 * parts]
        cnt, back, nrm, mx, kw, vw = refs[2 * parts : 2 * parts + 6]
        outs = refs[2 * parts + 6 : 3 * parts + 6]
        shift_ref, inputs, acc, hidden = refs[3 * parts + 6 :]
        step = pl.program_id(0)

        @pl.when(step == 0)
        def _():
            xs = [m[...].astype(F32) for m in mid]
            mean = sum(jnp.sum(x, axis=1, keepdims=True) for x in xs) / total
            cs = [x - mean for x in xs]
            var = sum(jnp.sum(c * c, axis=1, keepdims=True) for c in cs) / total
            scale = lax.rsqrt(var + 1e-05)
            for k in range(parts):
                at = pl.ds(pl.multiple_of((place_ref[0] ^ k) * width, 128), width)
                now = cs[k] * scale * nrm[2:3, at] + nrm[3:4, at]
                before = jnp.concatenate(
                    [prev[k][requests:].astype(F32), now[: rows - requests]], axis=0
                )
                inputs[k] = (now + (before - now) * mx[6:7, at]).astype(BF16)
                if k == 0:
                    chosen = jnp.zeros((requests, width), F32)
                    for t in range(slots):
                        chosen = jnp.where(
                            cnt[...] == t + 1, now[t * requests : (t + 1) * requests], chosen
                        )
                    unpick = (
                        lax.broadcasted_iota(jnp.int32, (requests, requests), 1) == back[...]
                    ).astype(BF16)
                    shift_ref[...] = dot32(unpick, chosen.astype(BF16)).astype(BF16)
            acc[...] = dot32(inputs[0], kw[...])

        @pl.when((step > 0) & (step < parts))
        def _():
            acc[...] += dot32(inputs[step], kw[...])

        @pl.when(step == parts - 1)
        def _():
            h = jnp.maximum(acc[...], 0.0)
            hidden[...] = (h * h).astype(BF16)

        for q in range(parts):

            @pl.when(step == parts + q)
            def _():
                outs[q][...] = dot32(hidden[...], vw[...]).astype(outs[q].dtype)

    args = (*mids, *prevs, count_col, back_col, norm, mix)
    return pl.pallas_call(
        body,
        grid_spec=pltpu.PrefetchScalarGridSpec(
            num_scalar_prefetch=1,
            grid=(2 * parts,),
            in_specs=[full_spec(a.shape) for a in args]
            + [
                pl.BlockSpec(
                    (width, hidden_width), lambda s, p: (p[0] ^ jnp.minimum(s, parts - 1), 0)
                ),
                pl.BlockSpec(
                    (hidden_width, width), lambda s, p: (0, p[0] ^ jnp.maximum(s - parts, 0))
                ),
            ],
            out_specs=[full_spec((rows, width)) for _ in range(parts)]
            + [full_spec((requests, width))],
            scratch_shapes=[
                pltpu.VMEM((parts, rows, width), BF16),
                pltpu.VMEM((rows, hidden_width), F32),
                pltpu.VMEM((rows, hidden_width), BF16),
            ],
        ),
        out_shape=[jax.ShapeDtypeStruct((rows, width), F32)]
        + [jax.ShapeDtypeStruct((rows, width), BF16) for _ in range(parts - 1)]
        + [jax.ShapeDtypeStruct((requests, width), BF16)],
        compiler_params=params(),
        name="channel_mix",
    )(place, *args, key_weight, value_weight)


def finish(mid, own, others, live_col, row_back):
    rows, width = mid.shape

    def body(mid_ref, own_ref, *refs):
        out = refs[-1]
        live, back = refs[-3:-1]
        total = own_ref[...]
        for o in refs[:-3]:
            total = total + o[...].astype(F32)
        total = jnp.where(live[...] > 0, mid_ref[...].astype(F32) + total, 0.0).astype(BF16)
        pick = (lax.broadcasted_iota(jnp.int32, (rows, rows), 1) == back[...]).astype(BF16)
        out[...] = dot32(pick, total).astype(BF16)

    args = (mid, own, *others, live_col, row_back)
    return pl.pallas_call(
        body,
        grid=(1,),
        in_specs=[full_spec(a.shape) for a in args],
        out_specs=full_spec((rows, width)),
        out_shape=jax.ShapeDtypeStruct((rows, width), BF16),
        compiler_params=params(),
        name="finish",
    )(*args)


def per_device(
    groups,
    parts,
    tokens,
    counts,
    new_owner,
    wkv_state,
    att_shift,
    ffn_shift,
    norm_params,
    mix_coeffs,
    head_params,
    recept_weight,
    key_weight,
    value_weight,
    output_weight,
    decay_down,
    decay_up,
    alpha_down,
    alpha_up,
    gate_down,
    gate_up,
    ffn_key_weight,
    ffn_value_weight,
):
    requests, slots, width = tokens.shape
    heads = wkv_state.shape[1]
    per_pair = requests // groups
    rows = requests * slots
    rank = lax.axis_index("req").astype(jnp.int32)
    place = lax.axis_index("mdl").astype(jnp.int32)
    rank_one, place_one = rank.reshape(1), place.reshape(1)

    blocks = new_owner.reshape(groups, requests)
    target = blocks // requests
    ids = jnp.arange(requests, dtype=jnp.int32)
    own = lax.dynamic_slice_in_dim(new_owner, rank * requests, requests)
    own_target = own // requests
    own_turn = jnp.sum(
        (own_target[:, None] == own_target[None, :]) & (ids[None, :] < ids[:, None]), axis=1
    ).astype(jnp.int32)
    own_slot = own_target * per_pair + own_turn
    sending = jnp.sum(jnp.where(own_slot[None, :] == ids[:, None], ids[None, :], 0), axis=1)
    partner_slot = (own_target ^ rank) * per_pair + own_turn
    order = jnp.sum(jnp.where(partner_slot[None, :] == ids[:, None], ids[None, :], 0), axis=1)
    mine = target == rank
    turn = jnp.cumsum(mine.astype(jnp.int32), axis=1) - 1
    arrival = jnp.where(
        mine, jnp.arange(groups, dtype=jnp.int32)[:, None] * per_pair + turn, -1
    ).reshape(-1)
    local = new_owner - rank * requests
    arriving = jnp.sum(jnp.where(arrival[None, :] == ids[:, None], local[None, :], 0), axis=1)
    hit = arriving[None, :] == ids[:, None]
    inverse = jnp.sum(jnp.where(hit, ids[None, :], 0), axis=1)
    count_arr = jnp.sum(jnp.where(hit, counts[:, None], 0), axis=0)

    slot_ids = jnp.arange(slots, dtype=jnp.int32)
    row_source = (arriving[None, :] * slots + slot_ids[:, None]).reshape(rows, 1)
    row_back = (inverse[:, None] + slot_ids[None, :] * requests).reshape(rows, 1)
    live_col = (slot_ids[:, None] < count_arr[None, :]).astype(jnp.int32).reshape(rows, 1)
    count_col, back_col = count_arr[:, None], inverse[:, None]
    lanes = rows
    count_row = jnp.tile(count_arr, lanes // requests)[None, :]

    gather = lambda x: [x] + [xor_permute(x, "mdl", parts, k) for k in range(1, parts)]
    scatter = lambda xs: [xor_permute(xs[k], "mdl", parts, k) for k in range(1, parts)]

    toks = gather(tokens.reshape(rows, width))
    shifts = jnp.concatenate(
        [
            att_shift[sending].reshape(groups, per_pair, width),
            ffn_shift[sending].reshape(groups, per_pair, width),
        ],
        axis=1,
    )
    shifts = lax.all_to_all(shifts, "req", split_axis=0, concat_axis=0, tiled=True)
    shifts = jnp.concatenate(
        [
            shifts[:, :per_pair].reshape(requests, width),
            shifts[:, per_pair:].reshape(requests, width),
        ],
        axis=0,
    )
    prevs = gather(shifts)

    packed = pack_states(wkv_state, order, per_pair, groups)
    payloads = [packed[0]] + [xor_permute(packed[k], "req", groups, k) for k in range(1, groups)]
    states = states_to_lanes(rank_one, payloads, requests, lanes)

    normed, low, low_send, new_att = first_norm(
        place_one,
        toks,
        prevs,
        row_source,
        count_col,
        back_col,
        norm_params,
        mix_coeffs,
        (decay_down, alpha_down, gate_down),
    )
    low_others = gather(low_send)[1:]
    recept, key, value = projections(
        place_one, normed, prevs, mix_coeffs, (recept_weight, key_weight, value_weight), requests
    )
    results = heads_step(
        place_one,
        low,
        low_others,
        recept,
        key,
        value,
        states,
        head_params,
        (decay_up, alpha_up, gate_up),
        output_weight,
        count_row,
    )
    outs, (removed, vals, keys, units, decay) = results[:parts], results[parts:]
    mid = middle(toks[0], row_source, outs[0], scatter(outs))
    new_state = final_states(arriving, states, removed, vals, keys, units, decay, heads)
    mids = gather(mid)
    results = channel_mix(
        place_one,
        mids,
        prevs,
        count_col,
        back_col,
        norm_params,
        mix_coeffs,
        ffn_key_weight,
        ffn_value_weight,
    )
    outs, new_ffn = results[:parts], results[parts]
    block = finish(mid, outs[0], scatter(outs), live_col, row_back)
    return (block.reshape(requests, slots, width), new_state, new_att, new_ffn)


def solution(mesh):
    return jax.shard_map(
        functools.partial(per_device, mesh.shape["req"], mesh.shape["mdl"]),
        mesh=mesh,
        in_specs=(
            P("req", None, "mdl"),
            P("req"),
            P(),
            P("req", "mdl", None),
            P("req", "mdl"),
            P("req", "mdl"),
            P(),
            P(),
            P(None, "mdl"),
            P(None, "mdl"),
            P(None, "mdl"),
            P(None, "mdl"),
            P("mdl", None),
            P("mdl", None),
            P(None, "mdl"),
            P("mdl", None),
            P(None, "mdl"),
            P("mdl", None),
            P(None, "mdl"),
            P(None, "mdl"),
            P("mdl", None),
        ),
        out_specs=(P("req", None, "mdl"), P("req", "mdl", None), P("req", "mdl"), P("req", "mdl")),
        check_vma=False,
    )
```

time: 445 us -> 164 us (0.37)
  local copies, waits for them, and re-layouts: 175 us -> 13.8 us
  other arithmetic: 112 us -> 3.71 us
  blocking collectives: 94.9 us -> 0 us
  Pallas kernels: 0 us -> 65.8 us
  waiting for transfers between devices: 5.32 us -> 39.7 us
  starting transfers between devices: 14.6 us -> 37.9 us
  matrix products: 23 us -> 0 us
  between operations: 14.5 us -> 1.1 us
    mul x25 -> x0, local copies, waits for them, and re-layouts: 121 us -> none  [the longest x9 48.6 us: advance(): wkv_square * decay_now[:, :, None, :]]
    all_gather x6 -> x0, blocking collectives: 94.9 us -> none  [the longest x1 20.2 us: per_device(): lax.all_gather(decay_down, 'mdl', axis=0, tiled=True)]
    pallas_call x0 -> x9, Pallas kernels: none -> 65.8 us  [the longest x1 18.2 us: pack_states(): pl.pallas_call(body, grid_spec=pltpu.PrefetchScalarGridSpec(num_scalar_pr...]
    reduce_sum x13 -> x4, other arithmetic: 52.6 us -> 1.04 us  [the longest x1 0.63 us: per_device(): jnp.sum(jnp.where(partner_slot[None, :] == ids[:, None], ids[None, :], 0)...]
    ppermute x0 -> x25, waiting for transfers between devices: none -> 39.7 us  [xor_permute(): return lax.ppermute(x, axis, [(a, a ^ k) for a in range(size)])]
    ppermute x0 -> x25, starting transfers between devices: none -> 32.7 us  [xor_permute(): return lax.ppermute(x, axis, [(a, a ^ k) for a in range(size)])]
    dot_general x8 -> x0, matrix products: 23 us -> none  [project(): return jnp.dot(inputs, weight, preferred_element_type=jnp.float32)]
    select_n x3, other arithmetic: 22.3 us -> 0.87 us  [the longest x1 0.86 us: per_device(): own_target = own // requests]
  transfers between devices with their start and end apart: 6 -> 26, of which waited for: 1 -> 9; matrix products, arithmetic and copies ran while one was open for 48% -> 4% of each run, Pallas kernels for 0% -> 27%
where the time goes in v1:
time: 164 us; the launch traced here: 162 us
  Pallas kernels  65.8 us (40%)
  waiting for transfers between devices  39.7 us (24%)
  starting transfers between devices  37.9 us (23%)
  local copies, waits for them, and re-layouts  13.8 us (8%)
  other arithmetic  3.71 us (2%)
    ppermute x25, waiting for transfers between devices, xor_permute(): return lax.ppermute(x, axis, [(a, a ^ k) for a in range(size)])  39.7 us
    ppermute x25, starting transfers between devices, xor_permute(): return lax.ppermute(x, axis, [(a, a ^ k) for a in range(size)])  32.7 us
    pallas_call x1, Pallas kernels, pack_states(): pl.pallas_call(body, grid_spec=pltpu.PrefetchScalarGridSpec(num_scalar_pr...  18.2 us
    pallas_call x1, Pallas kernels, final_states(): pl.pallas_call(body, grid_spec=pltpu.PrefetchScalarGridSpec(num_scalar_pr...  9.56 us
    pallas_call x1, Pallas kernels, channel_mix(): pl.pallas_call(body, grid_spec=pltpu.PrefetchScalarGridSpec(num_scalar_pr...  8.94 us
    pallas_call x1, Pallas kernels, heads_step(): pl.pallas_call(body, grid_spec=pltpu.PrefetchScalarGridSpec(num_scalar_pr...  8.67 us
    pallas_call x1, Pallas kernels, states_to_lanes(): pl.pallas_call(body, grid_spec=pltpu.PrefetchScalarGridSpec(num_scalar_pr...  6.63 us
    pallas_call x1, Pallas kernels, projections(): pl.pallas_call(body, grid_spec=pltpu.PrefetchScalarGridSpec(num_scalar_pr...  6.45 us
  transfers between devices with their start and end apart: 26, of which 9 were waited for; matrix products, arithmetic and copies ran while one was open for 4% of the time, Pallas kernels for 27%

profile of v1, /device:TPU:0, one launch (start us, length us, event | category | flops | bytes accessed | tf_op | source)
XLA Modules:
  0.0 162.1 jit_solution(12435223584831975202)
XLA Ops:
  0.7 0.9 and_select_fusion
  1.6 0.2 convert_reduce_fusion
  1.7 0.8 multiply_add_fusion
  2.5 0.6 select_reduce_fusion.1
  3.2 0.6 gather_fusion.1
  3.8 1.4 gather_fusion
  5.2 0.7 pad_maximum_fusion
  5.9 5.2 %all-to-all-start = ((bf16[8,8,512]{2,1,0:T(8,128)(2,1)}), bf16[8,8,512]{2,1,0:T(8,128)(2,1)S(1)}, u32[]{:S(2)}, u32[]{:S(2)}) async-start(bf16[8,8,512]{2,1,0:T(8,128)(2,1)} %pad_maximum_fusion), calls=%async_computation | async-start | bytes 131072 | tf_op jit(solution)/shard_map/all_to_all | solution.py:712
  11.1 18.2 %pack_states.1 = (bf16[4,8,4096]{2,1,0:T(8,128)(2,1)}, bf16[4,8,4096]{2,1,0:T(8,128)(2,1)}, bf16[4,8,4096]{2,1,0:T(8,128)(2,1)}, bf16[4,8,4096]{2,1,0:T(8,128)(2...) custom-call(s32[32]{0:T(128)} %get-tuple-element.70.order_ref, ...), custom_call_target="tpu_custom_call" | custom-call | tf_op jit(solution)/shard_map/pack_states/pallas_call | solution.py:45
  29.2 0.5 collective-permute-start.9
  29.8 1.7 %collective-permute-start.10 = (bf16[4,8,4096]{2,1,0:T(8,128)(2,1)}, bf16[4,8,4096]{2,1,0:T(8,128)(2,1)S(1)}, u32[]{:S(2)}, u32[]{:S(2)}) collective-permute-start(bf16[4,8,4096]{2,1,0:T(8,128)(2,1)} %get-tuple-element.41), channel_id=1, source_target_pairs={{0,8},{4,12},{8,0},{12,4},{16,24},{20,28},{24,16},{28,20},{1,9},{5... | collective-permute-start | bytes 786440 | tf_op jit(solution)/shard_map/ppermute | solution.py:16
  31.5 0.2 reduce_window_sum.11
  32.0 1.6 %collective-permute-start.3 = (bf16[64,512]{1,0:T(8,128)(2,1)S(1)}, bf16[64,512]{1,0:T(8,128)(2,1)S(1)}, u32[]{:S(2)}, u32[]{:S(2)}) collective-permute-start(bf16[64,512]{1,0:T(8,128)(2,1)S(1)} %constant_dynamic-update-slice_fusion.refs_4_.refs_0_), channel_id=1, source_target_pairs={{0,1},{1,0},{2,3},{3,2},{4,5},{5,4},{6,7},{7,6},{8,9},{9,8},{10,11... | collective-permute-start | bytes 196616 | tf_op jit(solution)/shard_map/ppermute | solution.py:16
  33.6 2.6 %collective-permute-start.4 = (bf16[64,512]{1,0:T(8,128)(2,1)S(1)}, bf16[64,512]{1,0:T(8,128)(2,1)S(1)}, u32[]{:S(2)}, u32[]{:S(2)}) collective-permute-start(bf16[64,512]{1,0:T(8,128)(2,1)S(1)} %constant_dynamic-update-slice_fusion.refs_4_.refs_0_), channel_id=1, source_target_pairs={{0,2},{1,3},{2,0},{3,1},{4,6},{5,7},{6,4},{7,5},{8,10},{9,11},{10,... | collective-permute-start | bytes 196616 | tf_op jit(solution)/shard_map/ppermute | solution.py:16
  36.2 0.2 collective-permute-start.5
  36.7 1.3 collective-permute-start
  37.9 3.2 %collective-permute-done.4.refs_6_.refs_2_ = bf16[64,512]{1,0:T(8,128)(2,1)S(1)} collective-permute-done((bf16[64,512]{1,0:T(8,128)(2,1)S(1)}, bf16[64,512]{1,0:T(8,128)(2,1)S(1)}, u32[]{:S(2)}, u32[]{:S(2)}) %collective-permute-start.4) | collective-permute-done | bytes 65568 | tf_op jit(solution)/shard_map/ppermute | solution.py:16
  41.1 1.0 collective-permute-start.1
  42.1 1.0 collective-permute-done.5.refs_7_.refs_3_
  43.2 1.6 collective-permute-start.2
  44.8 7.6 %collective-permute-done.1.refs_2_ = bf16[128,512]{1,0:T(8,128)(2,1)S(1)} collective-permute-done((bf16[128,512]{1,0:T(8,128)(2,1)S(1)}, bf16[128,512]{1,0:T(8,128)(2,1)S(1)}, u32[]{:S(2)}, u32[]{:S(2)}) %collective-permute-start.1) | collective-permute-done | bytes 131104 | tf_op jit(solution)/shard_map/ppermute | solution.py:16
  52.4 1.5 collective-permute-start.12
  53.9 0.3 collective-permute-start.14
  54.3 2.6 %collective-permute-start.15 = (bf16[4,8,4096]{2,1,0:T(8,128)(2,1)}, bf16[4,8,4096]{2,1,0:T(8,128)(2,1)S(1)}, u32[]{:S(2)}, u32[]{:S(2)}) collective-permute-start(bf16[4,8,4096]{2,1,0:T(8,128)(2,1)} %get-tuple-element.46), channel_id=1, source_target_pairs={{0,28},{4,24},{8,20},{12,16},{16,12},{20,8},{24,4},{28,0},{1,29},{... | collective-permute-start | bytes 786440 | tf_op jit(solution)/shard_map/ppermute | solution.py:16
  56.9 0.7 add.105.refs_8_.src
  57.6 0.1 select_reduce_fusion.2
  57.7 0.7 copy.46.refs_9_.refs_8_
  58.4 0.7 copy.47.refs_10_.refs_9_
  59.1 0.8 copy.48.refs_13_
  59.8 0.8 copy.49.refs_14_
  60.7 3.3 %first_norm.1 = (f32[4,128,512]{2,1,0:T(8,128)}, f32[128,512]{1,0:T(8,128)}, bf16[128,512]{1,0:T(8,128)(2,1)}, bf16[32,512]{1,0:T(8,128)(2,1)}) custom-call(s32[1]{0:T(128)} %bitcast.place_ref, bf16[128,512]{1,0:T(8,128)(2,1)} %copy-done.1, bf16[128,512]{1,0:T(8,128)(2,1)} %copy-done.23, bf16[128,512]{1,0:T(8,128)(2,1)} %copy-done.24, ...), custom_call_target="tpu_custom_call" | custom-call | tf_op jit(solution)/shard_map/first_norm/pallas_call | solution.py:153
  63.9 1.5 collective-permute-start.6
  65.4 6.8 %collective-permute-done.12.refs_4_ = bf16[4,8,4096]{2,1,0:T(8,128)(2,1)S(1)} collective-permute-done((bf16[4,8,4096]{2,1,0:T(8,128)(2,1)}, bf16[4,8,4096]{2,1,0:T(8,128)(2,1)S(1)}, u32[]{:S(2)}, u32[]{:S(2)}) %collective-permute-start.12) | collective-permute-done | bytes 262176 | tf_op jit(solution)/shard_map/ppermute | solution.py:16
  72.2 2.8 %collective-permute-done.13.refs_5_ = bf16[4,8,4096]{2,1,0:T(8,128)(2,1)S(1)} collective-permute-done((bf16[4,8,4096]{2,1,0:T(8,128)(2,1)}, bf16[4,8,4096]{2,1,0:T(8,128)(2,1)S(1)}, u32[]{:S(2)}, u32[]{:S(2)}) %collective-permute-start.13) | collective-permute-done | bytes 262176 | tf_op jit(solution)/shard_map/ppermute | solution.py:16
  75.0 2.2 %collective-permute-start.8 = (bf16[128,512]{1,0:T(8,128)(2,1)}, bf16[128,512]{1,0:T(8,128)(2,1)S(1)}, u32[]{:S(2)}, u32[]{:S(2)}) collective-permute-start(bf16[128,512]{1,0:T(8,128)(2,1)} %get-tuple-element.34), channel_id=1, source_target_pairs={{0,3},{1,2},{2,1},{3,0},{4,7},{5,6},{6,5},{7,4},{8,11},{9,10},{10,... | collective-permute-start | bytes 393224 | tf_op jit(solution)/shard_map/ppermute | solution.py:16
  77.2 0.6 broadcast_in_dim_tile.3.refs_13_
  77.8 6.4 %projections.1 = (f32[128,512]{1,0:T(8,128)}, f32[128,512]{1,0:T(8,128)}, f32[128,512]{1,0:T(8,128)}) custom-call(s32[1]{0:T(128)} %bitcast.place_ref, f32[4,128,512]{2,1,0:T(8,128)} %get-tuple-element.35.n_ref, bf16[64,512]{1,0:T(8,128)(2,1)} %copy-done.2, bf16[64,512]{1,0:T(8,128)(2,1)} %copy-done.3, bf16[64,512]{1,0:T(8,128)(2,1)} %copy-done.4, ...), custom_call_target="tpu_custom_call" | custom-call | tf_op jit(solution)/shard_map/projections/pallas_call | solution.py:205
  84.3 0.6 copy-done.11
  85.0 6.6 %states_to_lanes.1.refs_7_.st = f32[2,64,64,128]{3,2,1,0:T(8,128)} custom-call(s32[1]{0:T(128)} %bitcast.5.rank_ref, bf16[4,8,4096]{2,1,0:T(8,128)(2,1)} %get-tuple-element.39.refs_0_, bf16[4,8,4096]{2,1,0:T(8,128)(2,1)} %copy-done.6, bf16[4,8,4096]{2,1,0:T(8,128)(2,1)} %copy-done.7, bf16[4,8,4096]{2,1,0:T(8,128)(2,1)} %copy-done.8, ...), custom_call_target="tpu_custom_call" | custom-call | tf_op jit(solution)/shard_map/states_to_lanes/pallas_call | solution.py:92
  91.7 0.6 copy-done.13
  92.4 8.7 %heads_step.1 = (f32[128,512]{1,0:T(8,128)}, bf16[128,512]{1,0:T(8,128)(2,1)}, bf16[128,512]{1,0:T(8,128)(2,1)}, bf16[128,512]{1,0:T(8,128)(2,1)}, f32[2,4,64,12...) custom-call(s32[1]{0:T(128)} %bitcast.place_ref, ...), custom_call_target="tpu_custom_call" | custom-call | tf_op jit(solution)/shard_map/heads_step/pallas_call | solution.py:404
  101.2 2.2 %collective-permute-start.17 = (bf16[128,512]{1,0:T(8,128)(2,1)}, bf16[128,512]{1,0:T(8,128)(2,1)S(1)}, u32[]{:S(2)}, u32[]{:S(2)}) collective-permute-start(bf16[128,512]{1,0:T(8,128)(2,1)} %get-tuple-element.49), channel_id=1, source_target_pairs={{0,2},{1,3},{2,0},{3,1},{4,6},{5,7},{6,4},{7,5},{8,10},{9,11},{10,... | collective-permute-start | bytes 393224 | tf_op jit(solution)/shard_map/ppermute | solution.py:16
  103.3 2.2 %collective-permute-start.18 = (bf16[128,512]{1,0:T(8,128)(2,1)}, bf16[128,512]{1,0:T(8,128)(2,1)S(1)}, u32[]{:S(2)}, u32[]{:S(2)}) collective-permute-start(bf16[128,512]{1,0:T(8,128)(2,1)} %get-tuple-element.50), channel_id=1, source_target_pairs={{0,3},{1,2},{2,1},{3,0},{4,7},{5,6},{6,5},{7,4},{8,11},{9,10},{10,... | collective-permute-start | bytes 393224 | tf_op jit(solution)/shard_map/ppermute | solution.py:16
  105.6 3.4 %collective-permute-done.16.refs_0_ = bf16[128,512]{1,0:T(8,128)(2,1)S(1)} collective-permute-done((bf16[128,512]{1,0:T(8,128)(2,1)}, bf16[128,512]{1,0:T(8,128)(2,1)S(1)}, u32[]{:S(2)}, u32[]{:S(2)}) %collective-permute-start.16) | collective-permute-done | bytes 131104 | tf_op jit(solution)/shard_map/ppermute | solution.py:16
  109.0 5.3 %collective-permute-done.17.refs_1_ = bf16[128,512]{1,0:T(8,128)(2,1)S(1)} collective-permute-done((bf16[128,512]{1,0:T(8,128)(2,1)}, bf16[128,512]{1,0:T(8,128)(2,1)S(1)}, u32[]{:S(2)}, u32[]{:S(2)}) %collective-permute-start.17) | collective-permute-done | bytes 131104 | tf_op jit(solution)/shard_map/ppermute | solution.py:16
  114.3 0.6 copy-done.20
  115.0 2.1 %middle.1.refs_0_.mid_ref = bf16[128,512]{1,0:T(8,128)(2,1)} custom-call(bf16[128,512]{1,0:T(8,128)(2,1)} %copy-done.1, s32[128,1]{1,0:T(8,128)} %add.105.refs_8_.src, f32[128,512]{1,0:T(8,128)} %get-tuple-element.47.own_ref, bf16[128,512]{1,0:T(8,128)(2,1)} %copy-done.19, bf16[128,512]{1,0:T(8,128)(2,1)} %copy-done.20, bf16[128,512]{1,0:T(8,128)(2,1)} %copy-done.21), custom_call_target="tpu_custom_call" | custom-call | tf_op jit(solution)/shard_map/middle/pallas_call | solution.py:513
  117.2 2.9 %collective-permute-start.19 = (bf16[128,512]{1,0:T(8,128)(2,1)}, bf16[128,512]{1,0:T(8,128)(2,1)S(1)}, u32[]{:S(2)}, u32[]{:S(2)}) collective-permute-start(bf16[128,512]{1,0:T(8,128)(2,1)} %middle.1.refs_0_.mid_ref), channel_id=1, source_target_pairs={{0,1},{1,0},{2,3},{3,2},{4,5},{5,4},{6,7},{7,6},{8,9},{9,8},{10,11... | collective-permute-start | bytes 393224 | tf_op jit(solution)/shard_map/ppermute | solution.py:16
  120.0 0.1 collective-permute-start.20
  120.2 2.2 %collective-permute-start.21 = (bf16[128,512]{1,0:T(8,128)(2,1)}, bf16[128,512]{1,0:T(8,128)(2,1)S(1)}, u32[]{:S(2)}, u32[]{:S(2)}) collective-permute-start(bf16[128,512]{1,0:T(8,128)(2,1)} %middle.1.refs_0_.mid_ref), channel_id=1, source_target_pairs={{0,3},{1,2},{2,1},{3,0},{4,7},{5,6},{6,5},{7,4},{8,11},{9,10},{10,... | collective-permute-start | bytes 393224 | tf_op jit(solution)/shard_map/ppermute | solution.py:16
  122.4 0.7 reshape.201.refs_3_
  123.1 1.3 collective-permute-done.19.refs_1_
  124.4 8.2 %collective-permute-done.20.refs_2_ = bf16[128,512]{1,0:T(8,128)(2,1)S(1)} collective-permute-done((bf16[128,512]{1,0:T(8,128)(2,1)}, bf16[128,512]{1,0:T(8,128)(2,1)S(1)}, u32[]{:S(2)}, u32[]{:S(2)}) %collective-permute-start.20) | collective-permute-done | bytes 131104 | tf_op jit(solution)/shard_map/ppermute | solution.py:16
  132.6 0.6 copy-done.17
  133.3 0.7 copy-done.18
  133.9 8.9 %channel_mix.1 = (f32[128,512]{1,0:T(8,128)}, bf16[128,512]{1,0:T(8,128)(2,1)}, bf16[128,512]{1,0:T(8,128)(2,1)}, bf16[128,512]{1,0:T(8,128)(2,1)}, bf16[32,512]{1,0:T(8,128)(2,1)}) custom-call(s32[1]{0:T(128)} %bitcast.place_ref, bf16[128,512]{1,0:T(8,128)(2,1)} %middle.1.refs_0_.mid_ref, bf16[128,512]{1,0:T(8,128)(2,1)} %copy-done.16, ...), custom_call_target="tpu_custom_call" | custom-call | tf_op jit(solution)/shard_map/channel_mix/pallas_call | solution.py:582
  142.9 1.8 %collective-permute-start.22 = (bf16[128,512]{1,0:T(8,128)(2,1)}, bf16[128,512]{1,0:T(8,128)(2,1)S(1)}, u32[]{:S(2)}, u32[]{:S(2)}) collective-permute-start(bf16[128,512]{1,0:T(8,128)(2,1)} %get-tuple-element.52), channel_id=1, source_target_pairs={{0,1},{1,0},{2,3},{3,2},{4,5},{5,4},{6,7},{7,6},{8,9},{9,8},{10,11... | collective-permute-start | bytes 393224 | tf_op jit(solution)/shard_map/ppermute | solution.py:16
  144.6 0.8 collective-permute-start.23
  145.4 1.9 %collective-permute-start.24 = (bf16[128,512]{1,0:T(8,128)(2,1)}, bf16[128,512]{1,0:T(8,128)(2,1)S(1)}, u32[]{:S(2)}, u32[]{:S(2)}) collective-permute-start(bf16[128,512]{1,0:T(8,128)(2,1)} %get-tuple-element.54), channel_id=1, source_target_pairs={{0,3},{1,2},{2,1},{3,0},{4,7},{5,6},{6,5},{7,4},{8,11},{9,10},{10,... | collective-permute-start | bytes 393224 | tf_op jit(solution)/shard_map/ppermute | solution.py:16
  147.4 0.7 add.106.refs_4_
  148.1 9.6 %final_states.1 = f32[32,8,4096]{2,1,0:T(8,128)} custom-call(s32[32]{0:T(128)} %copy-done.32, f32[2,64,64,128]{3,2,1,0:T(8,128)} %states_to_lanes.1.refs_7_.st, f32[2,4,64,128]{3,2,1,0:T(8,128)} %get-tuple-element.55.p_ref, f32[2,4,64,128]{3,2,1,0:T(8,128)} %get-tuple-element.56.v_ref, f32[2,4,64,128]{3,2,1,0:T(8,128)} %get-tuple-element.57.kq_ref, ...), custom_call_target="tpu_custom_call" | custom-call | tf_op jit(solution)/shard_map/final_states/pallas_call | solution.py:476
  157.7 0.6 copy-done.26
  158.4 2.1 %finish.1 = bf16[128,512]{1,0:T(8,128)(2,1)} custom-call(bf16[128,512]{1,0:T(8,128)(2,1)} %middle.1.refs_0_.mid_ref, f32[128,512]{1,0:T(8,128)} %get-tuple-element.51.own_ref, bf16[128,512]{1,0:T(8,128)(2,1)} %copy-done.26, bf16[128,512]{1,0:T(8,128)(2,1)} %copy-done.27, bf16[128,512]{1,0:T(8,128)(2,1)} %copy-done.28, s32[128,1]{1,0:T(8,128)} %reshape.201.refs_3_, ...), custom_call_target="tpu_custom_call" | custom-call | tf_op jit(solution)/shard_map/finish/pallas_call | solution.py:626
  160.5 1.6 reshape.183
  (106 shorter events, 1.3 us)
Async XLA Ops:
  0.6 2.5 %copy-start = (bf16[32,512]{1,0:T(8,128)(2,1)S(1)}, bf16[32,512]{1,0:T(8,128)(2,1)}, u32[]{:S(2)}) copy-start(bf16[32,512]{1,0:T(8,128)(2,1)} %param.26) | copy-start | bytes 98308
  0.6 30.8 %copy-start.31 = (s32[256]{0:T(256)S(1)}, s32[256]{0:T(256)}, u32[]{:S(2)}) copy-start(s32[256]{0:T(256)} %param.23) | copy-start | bytes 3076
  0.7 35.9 %copy-start.22 = (bf16[32,4,512]{2,1,0:T(4,128)(2,1)S(1)}, bf16[32,4,512]{2,1,0:T(4,128)(2,1)}, u32[]{:S(2)}) copy-start(bf16[32,4,512]{2,1,0:T(4,128)(2,1)} %param.21) | copy-start | bytes 393220
  0.7 56.9 %copy-start.33 = (s32[32]{0:T(128)S(1)}, s32[32]{0:T(128)}, u32[]{:S(2)}) copy-start(s32[32]{0:T(128)} %param.22) | copy-start | bytes 388
  0.7 58.4 %copy-start.29 = (bf16[512,96]{0,1:T(8,128)(2,1)S(1)}, bf16[512,96]{0,1:T(8,128)(2,1)}, u32[]{:S(2)}) copy-start(bf16[512,96]{0,1:T(8,128)(2,1)} %param.34) | copy-start | bytes 294916
  0.7 59.2 %copy-start.30 = (bf16[512,96]{0,1:T(8,128)(2,1)S(1)}, bf16[512,96]{0,1:T(8,128)(2,1)}, u32[]{:S(2)}) copy-start(bf16[512,96]{0,1:T(8,128)(2,1)} %param.36) | copy-start | bytes 294916
  5.9 26.0 %all-to-all-start = ((bf16[8,8,512]{2,1,0:T(8,128)(2,1)}), bf16[8,8,512]{2,1,0:T(8,128)(2,1)S(1)}, u32[]{:S(2)}, u32[]{:S(2)}) async-start(bf16[8,8,512]{2,1,0:T(8,128)(2,1)} %pad_maximum_fusion), calls=%async_computation | async-start | bytes 131072 | tf_op jit(solution)/shard_map/all_to_all | solution.py:712
  29.2 24.7 %collective-permute-start.9 = (bf16[4,8,4096]{2,1,0:T(8,128)(2,1)}, bf16[4,8,4096]{2,1,0:T(8,128)(2,1)S(1)}, u32[]{:S(2)}, u32[]{:S(2)}) collective-permute-start(bf16[4,8,4096]{2,1,0:T(8,128)(2,1)} %get-tuple-element.40), channel_id=1, source_target_pairs={{0,4},{4,0},{8,12},{12,8},{16,20},{20,16},{24,28},{28,24},{1,5},{5... | collective-permute-start | bytes 786440 | tf_op jit(solution)/shard_map/ppermute | solution.py:16
  29.8 24.5 %collective-permute-start.10 = (bf16[4,8,4096]{2,1,0:T(8,128)(2,1)}, bf16[4,8,4096]{2,1,0:T(8,128)(2,1)S(1)}, u32[]{:S(2)}, u32[]{:S(2)}) collective-permute-start(bf16[4,8,4096]{2,1,0:T(8,128)(2,1)} %get-tuple-element.41), channel_id=1, source_target_pairs={{0,8},{4,12},{8,0},{12,4},{16,24},{20,28},{24,16},{28,20},{1,9},{5... | collective-permute-start | bytes 786440 | tf_op jit(solution)/shard_map/ppermute | solution.py:16
  32.0 28.6 %copy-start.2 = (bf16[64,512]{1,0:T(8,128)(2,1)}, bf16[64,512]{1,0:T(8,128)(2,1)S(1)}, u32[]{:S(2)}) copy-start(bf16[64,512]{1,0:T(8,128)(2,1)S(1)} %constant_dynamic-update-slice_fusion.refs_4_.refs_0_) | copy-start | bytes 196612
  32.0 4.6 %collective-permute-start.3 = (bf16[64,512]{1,0:T(8,128)(2,1)S(1)}, bf16[64,512]{1,0:T(8,128)(2,1)S(1)}, u32[]{:S(2)}, u32[]{:S(2)}) collective-permute-start(bf16[64,512]{1,0:T(8,128)(2,1)S(1)} %constant_dynamic-update-slice_fusion.refs_4_.refs_0_), channel_id=1, source_target_pairs={{0,1},{1,0},{2,3},{3,2},{4,5},{5,4},{6,7},{7,6},{8,9},{9,8},{10,11... | collective-permute-start | bytes 196616 | tf_op jit(solution)/shard_map/ppermute | solution.py:16
  33.6 7.5 %collective-permute-start.4 = (bf16[64,512]{1,0:T(8,128)(2,1)S(1)}, bf16[64,512]{1,0:T(8,128)(2,1)S(1)}, u32[]{:S(2)}, u32[]{:S(2)}) collective-permute-start(bf16[64,512]{1,0:T(8,128)(2,1)S(1)} %constant_dynamic-update-slice_fusion.refs_4_.refs_0_), channel_id=1, source_target_pairs={{0,2},{1,3},{2,0},{3,1},{4,6},{5,7},{6,4},{7,5},{8,10},{9,11},{10,... | collective-permute-start | bytes 196616 | tf_op jit(solution)/shard_map/ppermute | solution.py:16
  36.2 6.9 %collective-permute-start.5 = (bf16[64,512]{1,0:T(8,128)(2,1)S(1)}, bf16[64,512]{1,0:T(8,128)(2,1)S(1)}, u32[]{:S(2)}, u32[]{:S(2)}) collective-permute-start(bf16[64,512]{1,0:T(8,128)(2,1)S(1)} %constant_dynamic-update-slice_fusion.refs_4_.refs_0_), channel_id=1, source_target_pairs={{0,3},{1,2},{2,1},{3,0},{4,7},{5,6},{6,5},{7,4},{8,11},{9,10},{10,... | collective-permute-start | bytes 196616 | tf_op jit(solution)/shard_map/ppermute | solution.py:16
  36.6 47.6 %copy-start.32 = (s32[32]{0:T(128)}, s32[32]{0:T(128)S(1)}, u32[]{:S(2)}) copy-start(s32[32]{0:T(128)S(1)} %select_reduce_fusion.arr_ref) | copy-start | bytes 388
  36.6 24.0 %copy-start.1 = (bf16[128,512]{1,0:T(8,128)(2,1)}, bf16[128,512]{1,0:T(8,128)(2,1)S(1)}, u32[]{:S(2)}) copy-start(bf16[128,512]{1,0:T(8,128)(2,1)S(1)} %reshape.175.refs_0_.tok_ref) | copy-start | bytes 393220
  36.6 24.0 %copy-start.3 = (bf16[64,512]{1,0:T(8,128)(2,1)}, bf16[64,512]{1,0:T(8,128)(2,1)S(1)}, u32[]{:S(2)}) copy-start(bf16[64,512]{1,0:T(8,128)(2,1)S(1)} %collective-permute-done.3.refs_5_.refs_1_) | copy-start | bytes 196612
  36.7 8.1 %collective-permute-start = (bf16[128,512]{1,0:T(8,128)(2,1)S(1)}, bf16[128,512]{1,0:T(8,128)(2,1)S(1)}, u32[]{:S(2)}, u32[]{:S(2)}) collective-permute-start(bf16[128,512]{1,0:T(8,128)(2,1)S(1)} %reshape.175.refs_0_.tok_ref), channel_id=1, source_target_pairs={{0,1},{1,0},{2,3},{3,2},{4,5},{5,4},{6,7},{7,6},{8,9},{9,8},{10,11... | collective-permute-start | bytes 393224 | tf_op jit(solution)/shard_map/ppermute | solution.py:16
  41.1 19.5 %copy-start.4 = (bf16[64,512]{1,0:T(8,128)(2,1)}, bf16[64,512]{1,0:T(8,128)(2,1)S(1)}, u32[]{:S(2)}) copy-start(bf16[64,512]{1,0:T(8,128)(2,1)S(1)} %collective-permute-done.4.refs_6_.refs_2_) | copy-start | bytes 196612
  41.1 11.3 %collective-permute-start.1 = (bf16[128,512]{1,0:T(8,128)(2,1)S(1)}, bf16[128,512]{1,0:T(8,128)(2,1)S(1)}, u32[]{:S(2)}, u32[]{:S(2)}) collective-permute-start(bf16[128,512]{1,0:T(8,128)(2,1)S(1)} %reshape.175.refs_0_.tok_ref), channel_id=1, source_target_pairs={{0,2},{1,3},{2,0},{3,1},{4,6},{5,7},{6,4},{7,5},{8,10},{9,11},{10,... | collective-permute-start | bytes 393224 | tf_op jit(solution)/shard_map/ppermute | solution.py:16
  43.2 17.5 %copy-start.5 = (bf16[64,512]{1,0:T(8,128)(2,1)}, bf16[64,512]{1,0:T(8,128)(2,1)S(1)}, u32[]{:S(2)}) copy-start(bf16[64,512]{1,0:T(8,128)(2,1)S(1)} %collective-permute-done.5.refs_7_.refs_3_) | copy-start | bytes 196612
  43.2 10.7 %collective-permute-start.2 = (bf16[128,512]{1,0:T(8,128)(2,1)S(1)}, bf16[128,512]{1,0:T(8,128)(2,1)S(1)}, u32[]{:S(2)}, u32[]{:S(2)}) collective-permute-start(bf16[128,512]{1,0:T(8,128)(2,1)S(1)} %reshape.175.refs_0_.tok_ref), channel_id=1, source_target_pairs={{0,3},{1,2},{2,1},{3,0},{4,7},{5,6},{6,5},{7,4},{8,11},{9,10},{10,... | collective-permute-start | bytes 393224 | tf_op jit(solution)/shard_map/ppermute | solution.py:16
  44.7 15.9 %copy-start.23 = (bf16[128,512]{1,0:T(8,128)(2,1)}, bf16[128,512]{1,0:T(8,128)(2,1)S(1)}, u32[]{:S(2)}) copy-start(bf16[128,512]{1,0:T(8,128)(2,1)S(1)} %collective-permute-done.refs_1_) | copy-start | bytes 393220
  44.7 19.2 %collective-permute-start.11 = (bf16[4,8,4096]{2,1,0:T(8,128)(2,1)}, bf16[4,8,4096]{2,1,0:T(8,128)(2,1)S(1)}, u32[]{:S(2)}, u32[]{:S(2)}) collective-permute-start(bf16[4,8,4096]{2,1,0:T(8,128)(2,1)} %get-tuple-element.42), channel_id=1, source_target_pairs={{0,12},{4,8},{8,4},{12,0},{16,28},{20,24},{24,20},{28,16},{1,13},{... | collective-permute-start | bytes 786440 | tf_op jit(solution)/shard_map/ppermute | solution.py:16
  52.4 8.2 %copy-start.24 = (bf16[128,512]{1,0:T(8,128)(2,1)}, bf16[128,512]{1,0:T(8,128)(2,1)S(1)}, u32[]{:S(2)}) copy-start(bf16[128,512]{1,0:T(8,128)(2,1)S(1)} %collective-permute-done.1.refs_2_) | copy-start | bytes 393220
  52.4 19.7 %collective-permute-start.12 = (bf16[4,8,4096]{2,1,0:T(8,128)(2,1)}, bf16[4,8,4096]{2,1,0:T(8,128)(2,1)S(1)}, u32[]{:S(2)}, u32[]{:S(2)}) collective-permute-start(bf16[4,8,4096]{2,1,0:T(8,128)(2,1)} %get-tuple-element.43), channel_id=1, source_target_pairs={{0,16},{4,20},{8,24},{12,28},{16,0},{20,4},{24,8},{28,12},{1,17},{... | collective-permute-start | bytes 786440 | tf_op jit(solution)/shard_map/ppermute | solution.py:16
  53.9 6.7 %copy-start.25 = (bf16[128,512]{1,0:T(8,128)(2,1)}, bf16[128,512]{1,0:T(8,128)(2,1)S(1)}, u32[]{:S(2)}) copy-start(bf16[128,512]{1,0:T(8,128)(2,1)S(1)} %collective-permute-done.2.refs_3_) | copy-start | bytes 393220
  53.9 21.0 %collective-permute-start.13 = (bf16[4,8,4096]{2,1,0:T(8,128)(2,1)}, bf16[4,8,4096]{2,1,0:T(8,128)(2,1)S(1)}, u32[]{:S(2)}, u32[]{:S(2)}) collective-permute-start(bf16[4,8,4096]{2,1,0:T(8,128)(2,1)} %get-tuple-element.44), channel_id=1, source_target_pairs={{0,20},{4,16},{8,28},{12,24},{16,4},{20,0},{24,12},{28,8},{1,21},{... | collective-permute-start | bytes 786440 | tf_op jit(solution)/shard_map/ppermute | solution.py:16
  53.9 30.3 %copy-start.6 = (bf16[4,8,4096]{2,1,0:T(8,128)(2,1)}, bf16[4,8,4096]{2,1,0:T(8,128)(2,1)S(1)}, u32[]{:S(2)}) copy-start(bf16[4,8,4096]{2,1,0:T(8,128)(2,1)S(1)} %collective-permute-done.9.refs_1_) | copy-start | bytes 786436
  53.9 30.3 %collective-permute-start.14 = (bf16[4,8,4096]{2,1,0:T(8,128)(2,1)}, bf16[4,8,4096]{2,1,0:T(8,128)(2,1)S(1)}, u32[]{:S(2)}, u32[]{:S(2)}) collective-permute-start(bf16[4,8,4096]{2,1,0:T(8,128)(2,1)} %get-tuple-element.45), channel_id=1, source_target_pairs={{0,24},{4,28},{8,16},{12,20},{16,8},{20,12},{24,0},{28,4},{1,25},{... | collective-permute-start | bytes 786440 | tf_op jit(solution)/shard_map/ppermute | solution.py:16
  54.3 29.9 %copy-start.7 = (bf16[4,8,4096]{2,1,0:T(8,128)(2,1)}, bf16[4,8,4096]{2,1,0:T(8,128)(2,1)S(1)}, u32[]{:S(2)}) copy-start(bf16[4,8,4096]{2,1,0:T(8,128)(2,1)S(1)} %collective-permute-done.10.refs_2_) | copy-start | bytes 786436
  54.3 30.0 %collective-permute-start.15 = (bf16[4,8,4096]{2,1,0:T(8,128)(2,1)}, bf16[4,8,4096]{2,1,0:T(8,128)(2,1)S(1)}, u32[]{:S(2)}, u32[]{:S(2)}) collective-permute-start(bf16[4,8,4096]{2,1,0:T(8,128)(2,1)} %get-tuple-element.46), channel_id=1, source_target_pairs={{0,28},{4,24},{8,20},{12,16},{16,12},{20,8},{24,4},{28,0},{1,29},{... | collective-permute-start | bytes 786440 | tf_op jit(solution)/shard_map/ppermute | solution.py:16
  63.9 20.4 %copy-start.8 = (bf16[4,8,4096]{2,1,0:T(8,128)(2,1)}, bf16[4,8,4096]{2,1,0:T(8,128)(2,1)S(1)}, u32[]{:S(2)}) copy-start(bf16[4,8,4096]{2,1,0:T(8,128)(2,1)S(1)} %collective-permute-done.11.refs_3_) | copy-start | bytes 786436
  63.9 27.7 %collective-permute-start.6 = (bf16[128,512]{1,0:T(8,128)(2,1)}, bf16[128,512]{1,0:T(8,128)(2,1)S(1)}, u32[]{:S(2)}, u32[]{:S(2)}) collective-permute-start(bf16[128,512]{1,0:T(8,128)(2,1)} %get-tuple-element.34), channel_id=1, source_target_pairs={{0,1},{1,0},{2,3},{3,2},{4,5},{5,4},{6,7},{7,6},{8,9},{9,8},{10,11... | collective-permute-start | bytes 393224 | tf_op jit(solution)/shard_map/ppermute | solution.py:16
  72.2 12.1 %copy-start.9 = (bf16[4,8,4096]{2,1,0:T(8,128)(2,1)}, bf16[4,8,4096]{2,1,0:T(8,128)(2,1)S(1)}, u32[]{:S(2)}) copy-start(bf16[4,8,4096]{2,1,0:T(8,128)(2,1)S(1)} %collective-permute-done.12.refs_4_) | copy-start | bytes 786436
  72.2 19.5 %collective-permute-start.7 = (bf16[128,512]{1,0:T(8,128)(2,1)}, bf16[128,512]{1,0:T(8,128)(2,1)S(1)}, u32[]{:S(2)}, u32[]{:S(2)}) collective-permute-start(bf16[128,512]{1,0:T(8,128)(2,1)} %get-tuple-element.34), channel_id=1, source_target_pairs={{0,2},{1,3},{2,0},{3,1},{4,6},{5,7},{6,4},{7,5},{8,10},{9,11},{10,... | collective-permute-start | bytes 393224 | tf_op jit(solution)/shard_map/ppermute | solution.py:16
  75.0 9.3 %copy-start.10 = (bf16[4,8,4096]{2,1,0:T(8,128)(2,1)}, bf16[4,8,4096]{2,1,0:T(8,128)(2,1)S(1)}, u32[]{:S(2)}) copy-start(bf16[4,8,4096]{2,1,0:T(8,128)(2,1)S(1)} %collective-permute-done.13.refs_5_) | copy-start | bytes 786436
  75.0 16.7 %collective-permute-start.8 = (bf16[128,512]{1,0:T(8,128)(2,1)}, bf16[128,512]{1,0:T(8,128)(2,1)S(1)}, u32[]{:S(2)}, u32[]{:S(2)}) collective-permute-start(bf16[128,512]{1,0:T(8,128)(2,1)} %get-tuple-element.34), channel_id=1, source_target_pairs={{0,3},{1,2},{2,1},{3,0},{4,7},{5,6},{6,5},{7,4},{8,11},{9,10},{10,... | collective-permute-start | bytes 393224 | tf_op jit(solution)/shard_map/ppermute | solution.py:16
  84.2 0.7 copy-start.11
  84.3 0.8 copy-start.12
  91.7 0.7 copy-start.13
  91.7 0.7 copy-start.14
  91.7 0.7 copy-start.15
  101.1 7.9 %collective-permute-start.16 = (bf16[128,512]{1,0:T(8,128)(2,1)}, bf16[128,512]{1,0:T(8,128)(2,1)S(1)}, u32[]{:S(2)}, u32[]{:S(2)}) collective-permute-start(bf16[128,512]{1,0:T(8,128)(2,1)} %get-tuple-element.48), channel_id=1, source_target_pairs={{0,1},{1,0},{2,3},{3,2},{4,5},{5,4},{6,7},{7,6},{8,9},{9,8},{10,11... | collective-permute-start | bytes 393224 | tf_op jit(solution)/shard_map/ppermute | solution.py:16
  101.2 13.1 %collective-permute-start.17 = (bf16[128,512]{1,0:T(8,128)(2,1)}, bf16[128,512]{1,0:T(8,128)(2,1)S(1)}, u32[]{:S(2)}, u32[]{:S(2)}) collective-permute-start(bf16[128,512]{1,0:T(8,128)(2,1)} %get-tuple-element.49), channel_id=1, source_target_pairs={{0,2},{1,3},{2,0},{3,1},{4,6},{5,7},{6,4},{7,5},{8,10},{9,11},{10,... | collective-permute-start | bytes 393224 | tf_op jit(solution)/shard_map/ppermute | solution.py:16
  103.3 11.0 %collective-permute-start.18 = (bf16[128,512]{1,0:T(8,128)(2,1)}, bf16[128,512]{1,0:T(8,128)(2,1)S(1)}, u32[]{:S(2)}, u32[]{:S(2)}) collective-permute-start(bf16[128,512]{1,0:T(8,128)(2,1)} %get-tuple-element.50), channel_id=1, source_target_pairs={{0,3},{1,2},{2,1},{3,0},{4,7},{5,6},{6,5},{7,4},{8,11},{9,10},{10,... | collective-permute-start | bytes 393224 | tf_op jit(solution)/shard_map/ppermute | solution.py:16
  109.0 5.3 %copy-start.19 = (bf16[128,512]{1,0:T(8,128)(2,1)}, bf16[128,512]{1,0:T(8,128)(2,1)S(1)}, u32[]{:S(2)}) copy-start(bf16[128,512]{1,0:T(8,128)(2,1)S(1)} %collective-permute-done.16.refs_0_) | copy-start | bytes 393220
  114.3 0.7 copy-start.20
  114.3 0.7 copy-start.21
  117.2 7.3 %collective-permute-start.19 = (bf16[128,512]{1,0:T(8,128)(2,1)}, bf16[128,512]{1,0:T(8,128)(2,1)S(1)}, u32[]{:S(2)}, u32[]{:S(2)}) collective-permute-start(bf16[128,512]{1,0:T(8,128)(2,1)} %middle.1.refs_0_.mid_ref), channel_id=1, source_target_pairs={{0,1},{1,0},{2,3},{3,2},{4,5},{5,4},{6,7},{7,6},{8,9},{9,8},{10,11... | collective-permute-start | bytes 393224 | tf_op jit(solution)/shard_map/ppermute | solution.py:16
  120.0 12.6 %collective-permute-start.20 = (bf16[128,512]{1,0:T(8,128)(2,1)}, bf16[128,512]{1,0:T(8,128)(2,1)S(1)}, u32[]{:S(2)}, u32[]{:S(2)}) collective-permute-start(bf16[128,512]{1,0:T(8,128)(2,1)} %middle.1.refs_0_.mid_ref), channel_id=1, source_target_pairs={{0,2},{1,3},{2,0},{3,1},{4,6},{5,7},{6,4},{7,5},{8,10},{9,11},{10,... | collective-permute-start | bytes 393224 | tf_op jit(solution)/shard_map/ppermute | solution.py:16
  120.2 12.4 %collective-permute-start.21 = (bf16[128,512]{1,0:T(8,128)(2,1)}, bf16[128,512]{1,0:T(8,128)(2,1)S(1)}, u32[]{:S(2)}, u32[]{:S(2)}) collective-permute-start(bf16[128,512]{1,0:T(8,128)(2,1)} %middle.1.refs_0_.mid_ref), channel_id=1, source_target_pairs={{0,3},{1,2},{2,1},{3,0},{4,7},{5,6},{6,5},{7,4},{8,11},{9,10},{10,... | collective-permute-start | bytes 393224 | tf_op jit(solution)/shard_map/ppermute | solution.py:16
  124.4 8.2 %copy-start.16 = (bf16[128,512]{1,0:T(8,128)(2,1)}, bf16[128,512]{1,0:T(8,128)(2,1)S(1)}, u32[]{:S(2)}) copy-start(bf16[128,512]{1,0:T(8,128)(2,1)S(1)} %collective-permute-done.19.refs_1_) | copy-start | bytes 393220
  132.6 0.7 copy-start.17
  133.3 0.7 copy-start.18
  142.9 14.8 %collective-permute-start.22 = (bf16[128,512]{1,0:T(8,128)(2,1)}, bf16[128,512]{1,0:T(8,128)(2,1)S(1)}, u32[]{:S(2)}, u32[]{:S(2)}) collective-permute-start(bf16[128,512]{1,0:T(8,128)(2,1)} %get-tuple-element.52), channel_id=1, source_target_pairs={{0,1},{1,0},{2,3},{3,2},{4,5},{5,4},{6,7},{7,6},{8,9},{9,8},{10,11... | collective-permute-start | bytes 393224 | tf_op jit(solution)/shard_map/ppermute | solution.py:16
  144.6 13.1 %collective-permute-start.23 = (bf16[128,512]{1,0:T(8,128)(2,1)}, bf16[128,512]{1,0:T(8,128)(2,1)S(1)}, u32[]{:S(2)}, u32[]{:S(2)}) collective-permute-start(bf16[128,512]{1,0:T(8,128)(2,1)} %get-tuple-element.53), channel_id=1, source_target_pairs={{0,2},{1,3},{2,0},{3,1},{4,6},{5,7},{6,4},{7,5},{8,10},{9,11},{10,... | collective-permute-start | bytes 393224 | tf_op jit(solution)/shard_map/ppermute | solution.py:16
  145.4 12.3 %collective-permute-start.24 = (bf16[128,512]{1,0:T(8,128)(2,1)}, bf16[128,512]{1,0:T(8,128)(2,1)S(1)}, u32[]{:S(2)}, u32[]{:S(2)}) collective-permute-start(bf16[128,512]{1,0:T(8,128)(2,1)} %get-tuple-element.54), channel_id=1, source_target_pairs={{0,3},{1,2},{2,1},{3,0},{4,7},{5,6},{6,5},{7,4},{8,11},{9,10},{10,... | collective-permute-start | bytes 393224 | tf_op jit(solution)/shard_map/ppermute | solution.py:16
  157.7 0.7 copy-start.26
  157.7 0.7 copy-start.27
  157.7 0.7 copy-start.28

commit v2 on v0

v2 whole, which is shorter than its diff:
```python
import functools

import jax
import jax.numpy as jnp
from jax import lax
from jax.experimental import pallas as pl
from jax.experimental.pallas import tpu as pltpu
from jax.sharding import PartitionSpec as P

F32 = jnp.float32
BF16 = jnp.bfloat16
I32 = jnp.int32
SCRATCH_LIMIT = 16 * 1024 * 1024


def xor_permute(x, axis, size, k):
    return lax.ppermute(x, axis, [(a, a ^ k) for a in range(size)])


def dot32(a, b):
    return jnp.dot(a, b, preferred_element_type=F32)


def dot32_turned(a, b):
    return lax.dot_general(a, b, (((1,), (1,)), ((), ())), preferred_element_type=F32)


def vmem(shape, dtype):
    return pltpu.VMEM(shape, dtype)


def run(body, name, scalars, args, outs, scratch=(), in_hbm=(), out_hbm=()):
    anywhere = pl.BlockSpec(memory_space=pl.ANY)
    near = pl.BlockSpec(memory_space=pltpu.VMEM)
    return pl.pallas_call(
        body,
        grid_spec=pltpu.PrefetchScalarGridSpec(
            num_scalar_prefetch=len(scalars),
            grid=(1,),
            in_specs=[anywhere if i in in_hbm else near for i in range(len(args))],
            out_specs=[
                pl.BlockSpec(memory_space=pltpu.SMEM)
                if o.memory_space == pltpu.SMEM
                else anywhere if i in out_hbm else near
                for i, o in enumerate(outs)
            ],
            scratch_shapes=scratch,
        ),
        out_shape=[
            jax.ShapeDtypeStruct(o.shape, o.dtype)
            if o.memory_space == pltpu.SMEM or i in out_hbm
            else o
            for i, o in enumerate(outs)
        ],
        compiler_params=pltpu.CompilerParams(vmem_limit_bytes=SCRATCH_LIMIT),
        name=name,
    )(
        *scalars,
        *[
            a if i in in_hbm else pltpu.with_memory_space_constraint(a, pltpu.VMEM)
            for i, a in enumerate(args)
        ],
    )


def positions(groups):
    return list(range(0, groups, 2)) + list(range(1, groups, 2))


SOURCE, BACK, LIVE, COUNT, UNSORT, ATT, FFN = range(7)


def make_plan(rank, new_owner, counts, att, ffn, groups, slots):
    requests, width = att.shape
    per_pair = requests // groups
    rows = requests * slots
    sent_rows = 2 * requests

    def body(
        rank_ref, owner, cnt, att_ref, ffn_ref, order, arriving, cols, lanes_ref, sent_ref,
        turn, inverse, att_f, ffn_f, sent_f,
    ):
        me = rank_ref[0]

        def place_of(k):
            return k // 2 + (k % 2) * (groups // 2)

        for g in range(groups):
            turn[g] = 0

        def own(i, _):
            spot = place_of((owner[me * requests + i] // requests) ^ me)
            order[spot * per_pair + turn[spot]] = i
            turn[spot] = turn[spot] + 1
            return 0

        lax.fori_loop(0, requests, own, 0)

        def source(s, _):
            base = place_of(s ^ me) * per_pair

            def one(i, found):
                v = owner[s * requests + i]
                mine = v // requests == me

                @pl.when(mine)
                def _():
                    arriving[base + found] = v % requests
                    inverse[v % requests] = base + found

                return found + mine.astype(I32)

            lax.fori_loop(0, requests, one, jnp.int32(0))
            return 0

        lax.fori_loop(0, groups, source, 0)

        att_f[...] = att_ref[...].astype(F32)
        ffn_f[...] = ffn_ref[...].astype(F32)
        for d in range(groups):
            base = place_of(me ^ d) * per_pair
            for j in range(per_pair):
                i = order[base + j]
                to = d * 2 * per_pair + j
                sent_f[to : to + 1, :] = att_f[pl.ds(i, 1), :]
                sent_f[to + per_pair : to + per_pair + 1, :] = ffn_f[pl.ds(i, 1), :]
        sent_ref[...] = sent_f[...].astype(BF16)

        row = lax.broadcasted_iota(I32, (requests, 128), 0)
        long_row = lax.broadcasted_iota(I32, (rows, 128), 0)
        lane = lax.broadcasted_iota(I32, (requests, 128), 1)
        long_lane = lax.broadcasted_iota(I32, (rows, 128), 1)
        arr = jnp.zeros((requests, 128), I32)
        inv = jnp.zeros((requests, 128), I32)
        num = jnp.zeros((requests, 128), I32)
        got = jnp.zeros((requests, 128), I32)
        back = jnp.zeros((rows, 128), I32)
        lane_row = lax.broadcasted_iota(I32, (8, 128), 1)
        sub_row = lax.broadcasted_iota(I32, (8, 128), 0)
        lane_counts = jnp.zeros((8, 128), I32)
        half = requests // 2
        partners = positions(groups)
        for q in range(requests):
            at = row == q
            a = arriving[q]
            n = cnt[a]
            arr = jnp.where(at, a, arr)
            num = jnp.where(at, n, num)
            inv = jnp.where(at, inverse[q], inv)
            got = jnp.where(
                at, (me ^ partners[q // per_pair]) * 2 * per_pair + q % per_pair, got
            )
            back = jnp.where(long_row // slots == q, inverse[q], back)
            lane_counts = jnp.where(
                (lane_row % half == q % half) & (sub_row == q // half), n, lane_counts
            )
        lanes_ref[...] = lane_counts
        blocks = []
        for t in range(slots):
            block = jnp.where(lane == SOURCE, arr * slots + t, 0)
            block = jnp.where(lane == LIVE, (num > t).astype(I32), block)
            block = jnp.where(lane == COUNT, num, block)
            block = jnp.where(lane == UNSORT, inv, block)
            block = jnp.where(lane == ATT, got, block)
            block = jnp.where(lane == FFN, got + per_pair, block)
            blocks.append(block)
        table = jnp.concatenate(blocks, axis=0)
        cols[...] = jnp.where(long_lane == BACK, back + (long_row % slots) * requests, table)

    return run(
        body,
        "make_plan",
        (rank, new_owner, counts),
        (att, ffn),
        [
            pltpu.SMEM((requests,), I32),
            pltpu.SMEM((requests,), I32),
            vmem((rows, 128), I32),
            vmem((8, 128), I32),
            vmem((sent_rows, width), BF16),
        ],
        scratch=[
            pltpu.SMEM((groups,), I32),
            pltpu.SMEM((requests,), I32),
            vmem((requests, width), F32),
            vmem((requests, width), F32),
            vmem((sent_rows, width), F32),
        ],
    )


def chooser(cols, lane, rows, columns):
    return (lax.broadcasted_iota(I32, (rows, columns), 1) == cols[0:rows, lane : lane + 1]).astype(
        BF16
    )


def sort_shifts(cols, got):
    sent_rows, width = got.shape
    requests = sent_rows // 2

    def body(cols_ref, got_ref, att, ffn):
        for lane, out in ((ATT, att), (FFN, ffn)):
            out[...] = dot32(chooser(cols_ref, lane, requests, sent_rows), got_ref[...]).astype(BF16)

    return run(body, "sort_shifts", (), (cols, got), [vmem((requests, width), BF16)] * 2)


def pack_states(order, wkv_state, groups):
    requests, heads, cells = wkv_state.shape
    per_pair = requests // groups

    def body(order_ref, src, *refs):
        outs, (stage, sems) = refs[:groups], refs[groups:]
        copies = [
            pltpu.make_async_copy(src.at[order_ref[q]], stage.at[q], sems.at[q])
            for q in range(requests)
        ]
        for c in copies:
            c.start()
        for q in range(requests):
            copies[q].wait()
            outs[q // per_pair][q % per_pair] = stage[q].astype(BF16)

    return run(
        body,
        "pack_states",
        (order,),
        (wkv_state,),
        [vmem((per_pair, heads, cells), BF16) for _ in range(groups)],
        scratch=[vmem(wkv_state.shape, F32), pltpu.SemaphoreType.DMA((requests,))],
        in_hbm=(0,),
    )


def states_to_lanes(payloads, size):
    per_pair, heads, cells = payloads[0].shape
    requests = per_pair * len(payloads)
    lanes = heads * requests
    together = 4

    def body(*refs):
        ins, out_ref, rows = refs[: len(payloads)], refs[len(payloads)], refs[len(payloads) + 1]

        def some(step, _):
            for c in range(together):
                at = pl.ds(pl.multiple_of((step * together + c) * 128, 128), 128)
                for k in range(len(payloads)):
                    for j in range(per_pair):
                        first = (k * per_pair + j) * heads
                        rows[c, first : first + heads, :] = ins[k][j, :, at].astype(F32)
            for c in range(together):
                block = jnp.concatenate(
                    [rows[c, pl.ds(h, requests, stride=heads), :] for h in range(heads)], axis=0
                )
                turned = block.T
                chunk = step * together + c
                for e in range(128 // size):
                    out_ref[chunk * (128 // size) + e] = turned[e * size : (e + 1) * size]
            return 0

        lax.fori_loop(0, cells // (128 * together), some, 0)

    return run(
        body,
        "states_to_lanes",
        (),
        payloads,
        [vmem((cells // size, size, lanes), F32)],
        scratch=[vmem((together, requests * heads, 128), F32)],
    )[0]


def first_norm(place, toks, att, cols, norm, mix, down_d, down_a, down_g):
    rows, width = toks[0].shape
    parts = len(toks)
    total = parts * width
    requests = att.shape[0]
    slots = rows // requests
    small = down_d.shape[0]
    rank_g = down_g.shape[1]
    low_width = rank_g + 2 * small

    def body(place_ref, *refs):
        tok = refs[:parts]
        att_ref, col, nrm, mx, dd, da, dg, normed, low, low_send, shift = refs[parts:]
        pick = chooser(col, SOURCE, rows, rows)
        xs = [dot32(pick, t[...]) for t in tok]
        mean = sum(jnp.sum(x, axis=1, keepdims=True) for x in xs) / total
        cs = [x - mean for x in xs]
        var = sum(jnp.sum(c * c, axis=1, keepdims=True) for c in cs) / total
        scale = lax.rsqrt(var + 1e-05)
        for k in range(parts):
            at = pl.ds(pl.multiple_of((place_ref[0] ^ k) * width, 128), width)
            normed[k] = cs[k] * scale * nrm[0:1, at] + nrm[1:2, at]
        at = pl.ds(pl.multiple_of(place_ref[0] * width, 128), width)
        now = normed[0]
        before = jnp.concatenate([att_ref[...].astype(F32), now[: rows - requests]], axis=0)
        delta = before - now
        mixed = lambda c: (now + delta * mx[c : c + 1, at]).astype(BF16)
        nothing = jnp.zeros((small, width), BF16)
        low[:, 0:rank_g] = dot32(mixed(5), dg[...])
        low[:, rank_g:low_width] = dot32_turned(
            mixed(1), jnp.concatenate([dd[...], nothing], axis=0)
        ) + dot32_turned(mixed(4), jnp.concatenate([nothing, da[...]], axis=0))
        low_send[...] = low[...].astype(BF16)
        chosen = jnp.zeros((requests, width), F32)
        number = col[0:requests, COUNT : COUNT + 1]
        for t in range(slots):
            chosen = jnp.where(number == t + 1, now[t * requests : (t + 1) * requests], chosen)
        unsort = chooser(col, UNSORT, requests, requests)
        shift[...] = dot32(unsort, chosen.astype(BF16)).astype(BF16)

    return run(
        body,
        "first_norm",
        (place,),
        (*toks, att, cols, norm, mix, down_d, down_a, down_g),
        [
            vmem((parts, rows, width), F32),
            vmem((rows, low_width), F32),
            vmem((rows, low_width), BF16),
            vmem((requests, width), BF16),
        ],
    )


def projections(place, normed, atts, mix, weights):
    parts, rows, width = normed.shape
    requests = atts[0].shape[0]
    out_width = weights[0].shape[1]

    def body(place_ref, n_ref, *refs):
        att, mx, w, outs = refs[:parts], refs[parts], refs[parts + 1 : parts + 4], refs[parts + 4 :]
        sums = [None] * 3
        for k in range(parts):
            at = pl.ds(pl.multiple_of((place_ref[0] ^ k) * width, 128), width)
            now = n_ref[k]
            before = jnp.concatenate([att[k][...].astype(F32), now[: rows - requests]], axis=0)
            delta = before - now
            for which, c in enumerate((0, 2, 3)):
                term = dot32((now + delta * mx[c : c + 1, at]).astype(BF16), w[which][at, :])
                sums[which] = term if k == 0 else sums[which] + term
        for out, value in zip(outs, sums):
            out[...] = value

    return run(
        body,
        "projections",
        (place,),
        (normed, *atts, mix, *weights),
        [vmem((rows, out_width), F32) for _ in weights],
    )


def swap_groups(arrays, group):
    arrays = list(arrays)
    lanes = arrays[0].shape[1]
    where = lax.broadcasted_iota(I32, arrays[0].shape, 1) // group
    bit = 1
    while bit < len(arrays):
        low = (where // bit) % 2 == 0
        out = list(arrays)
        for a in range(len(arrays)):
            if a & bit == 0:
                first, second = arrays[a], arrays[a | bit]
                out[a] = jnp.where(low, first, pltpu.roll(second, bit * group, 1))
                out[a | bit] = jnp.where(low, pltpu.roll(first, lanes - bit * group, 1), second)
        arrays = out
        bit *= 2
    return arrays


def fold_eight(items, flags):
    shift = 1
    for flag in flags:
        items = [
            jnp.where(flag, a, b) + pltpu.roll(jnp.where(flag, b, a), shift, 0)
            for a, b in zip(items[0::2], items[1::2])
        ]
        shift *= 2
    return items[0]


def head_vectors(low_own, low_others, recept, key, value, head_params, ups, lane_counts, size):
    rows, width = recept.shape
    lanes = 128
    heads = width // size
    group = lanes // heads
    slots = 4
    halves = rows // slots // group
    n_groups = width // 128
    small = ups[0].shape[0]
    rank_g = ups[2].shape[0]
    n_others = len(low_others)
    pairs = [(t, b) for t in range(slots) for b in range(t + 1)]

    def body(low, *refs):
        others = refs[:n_others]
        (r_ref, k_ref, v_ref, hp, du, au, gu, cnt) = refs[n_others : n_others + 8]
        (w_out, c_out, v_out, kq_out, uq_out, d_out, g_out, b_out, vec) = refs[n_others + 8 :]
        total = low[...]
        for o in others:
            total = total + o[...].astype(F32)
        glow = jax.nn.sigmoid(total[:, 0:rank_g]).astype(BF16)
        pair = total[:, rank_g : rank_g + 2 * small]
        nothing = jnp.zeros((small, width), BF16)
        decay_in = dot32(
            jnp.tanh(pair).astype(BF16), jnp.concatenate([du[...], nothing], axis=0)
        )
        context_in = dot32(pair.astype(BF16), jnp.concatenate([nothing, au[...]], axis=0))
        decay = jnp.exp(-0.606531 * jax.nn.sigmoid(hp[0:1] + decay_in))
        context = jax.nn.sigmoid(hp[1:2] + context_in)
        g_out[...] = dot32(glow, gu[...])
        r = r_ref[...]
        k = k_ref[...]
        v = v_ref[...]
        scaled = k * hp[2:3]
        kmod = k * (1.0 + (context - 1.0) * hp[3:4])
        rk = r * kmod * hp[4:5]
        lane_r = lax.broadcasted_iota(I32, (128, 128), 0)
        lane_c = lax.broadcasted_iota(I32, (128, 128), 1)
        ones = ((lane_r // size) == (lane_c // size)).astype(BF16)
        for g in range(n_groups):
            at = slice(g * 128, (g + 1) * 128)
            high = rk[:, at].astype(BF16)
            rest = (rk[:, at] - high.astype(F32)).astype(BF16)
            b_out[:, at] = (dot32(high, ones) + dot32(rest, ones)) * v[:, at]

        for index, array in enumerate((r, kmod, scaled, decay, context, v)):
            pieces = []
            for g in range(n_groups):
                turned = array[:, g * 128 : (g + 1) * 128].T
                pieces += [turned[e * size : (e + 1) * size] for e in range(128 // size)]
            for at, piece in enumerate(swap_groups(pieces, group)):
                vec[index, at % halves, at // halves] = piece

        ksum = lambda x, y: jnp.sum(x * y, axis=0, keepdims=True)
        for g in range(halves):
            valid = [cnt[g : g + 1, :] > t for t in range(slots)]
            for t in range(slots):
                s = vec[2, g, t]
                unit = s * lax.rsqrt(jnp.sum(s * s, axis=0, keepdims=True) + 1e-06)
                vec[2, g, t] = unit
                vec[4, g, t] = unit * vec[4, g, t]

            def back_through(x, top, base):
                for b in range(top, -1, -1):
                    at = base + pairs.index((top + 1, b))
                    c_out[g, at : at + 1, :] = jnp.where(valid[b], ksum(vec[1, g, b], x), 0.0)
                    moved = vec[3, g, b] * x - vec[2, g, b] * ksum(vec[4, g, b], x)
                    x = jnp.where(valid[b], moved, x)
                return x

            for t in range(slots):
                w_out[g, t] = back_through(vec[2, g, t], t - 1, 0)
                x = vec[0, g, t]
                at = len(pairs) + pairs.index((t, t))
                c_out[g, at : at + 1, :] = ksum(vec[1, g, t], x)
                x = vec[3, g, t] * x - vec[2, g, t] * ksum(vec[4, g, t], x)
                w_out[g, slots + t] = back_through(x, t - 1, len(pairs))
            run_decay = jnp.ones((size, lanes), F32)
            for t in range(slots - 1, -1, -1):
                kq_out[g, t] = jnp.where(valid[t], vec[1, g, t] * run_decay, 0.0)
                uq_out[g, t] = jnp.where(valid[t], -(vec[4, g, t] * run_decay), 0.0)
                run_decay = jnp.where(valid[t], run_decay * vec[3, g, t], run_decay)
                v_out[g, t] = vec[5, g, t]
            d_out[g] = run_decay

    return run(
        body,
        "head_vectors",
        (),
        (low_own, *low_others, recept, key, value, head_params, *ups, lane_counts),
        [
            vmem((halves, 2 * slots, size, lanes), F32),
            vmem((halves, 2 * len(pairs), lanes), F32),
            vmem((halves, slots, size, lanes), F32),
            vmem((halves, slots, size, lanes), F32),
            vmem((halves, slots, size, lanes), F32),
            vmem((halves, size, lanes), F32),
            vmem((rows, width), F32),
            vmem((rows, width), F32),
        ],
        scratch=[vmem((6, halves, slots, size, lanes), F32)],
    )


def head_outputs(place, states, weights, coefs, values, gate, bonus, head_params, out_weight, parts):
    rows, width = gate.shape
    halves = len(states)
    size, lanes = states[0].shape[1:]
    slots = values.shape[1]
    group = rows // slots // halves
    n_groups = width // 128
    pairs = [(t, b) for t in range(slots) for b in range(t + 1)]
    quad = 4

    def body(place_ref, *refs):
        st = refs[:halves]
        w_ref, c_ref, v_ref, gate_ref, bonus_ref, hp, wo = refs[halves : halves + 7]
        outs = refs[halves + 7 : halves + 7 + parts]
        p_out, prod, done = refs[halves + 7 + parts :]
        sub = lax.broadcasted_iota(I32, (8, lanes), 0)
        folds = [(sub // s) % 2 == 0 for s in (1, 2, 4)]
        for g in range(halves):
            for part in range(2 * slots // quad):

                def products(block, _):
                    ws = [w_ref[g, part * quad + w] for w in range(quad)]
                    sums = [[] for _ in range(quad)]
                    for i in range(8):
                        s = st[g][block * 8 + i]
                        for w in range(quad):
                            term = s * ws[w]
                            acc = term[0:8]
                            for jv in range(1, size // 8):
                                acc = acc + term[jv * 8 : (jv + 1) * 8]
                            sums[w].append(acc)
                    at = pl.ds(pl.multiple_of(block * 8, 8), 8)
                    for w in range(quad):
                        prod[g, part * quad + w, at, :] = fold_eight(sums[w], folds)
                    return 0

                lax.fori_loop(0, size // 8, products, 0)

        by_group = [None] * (halves * slots)
        for g in range(halves):
            for t in range(slots):
                removed = prod[g, t]
                y = prod[g, slots + t]
                for b in range(t + 1):
                    at = pairs.index((t, b))
                    if b < t:
                        removed = removed + c_ref[g, at : at + 1, :] * v_ref[g, b]
                    at += len(pairs)
                    y = y + c_ref[g, at : at + 1, :] * v_ref[g, b]
                p_out[g, t] = removed
                center = y - jnp.mean(y, axis=0, keepdims=True)
                spread = jnp.mean(center * center, axis=0, keepdims=True)
                by_group[t * halves + g] = center * lax.rsqrt(spread + 0.00064)
        backs = swap_groups(by_group, group)
        each = 128 // size
        for g in range(n_groups):
            at = slice(g * 128, (g + 1) * 128)
            turned = jnp.concatenate(backs[each * g : each * (g + 1)], axis=0).T
            full = (turned * hp[5:6, at] + hp[6:7, at] + bonus_ref[:, at]) * gate_ref[:, at]
            done[:, at] = full.astype(BF16)
        for q in range(parts):
            at = pl.ds(pl.multiple_of((place_ref[0] ^ q) * width, 128), width)
            outs[q][...] = dot32(done[...], wo[:, at]).astype(outs[q].dtype)

    return run(
        body,
        "head_outputs",
        (place,),
        (*states, weights, coefs, values, gate, bonus, head_params, out_weight),
        [vmem((rows, width), F32)]
        + [vmem((rows, width), BF16) for _ in range(parts - 1)]
        + [vmem(values.shape, F32)],
        scratch=[vmem(weights.shape, F32), vmem((rows, width), BF16)],
    )


def final_states(arriving, states, removed, values, keys, units, decay, heads):
    halves = len(states)
    size, _, lanes = states[0].shape
    slots = removed.shape[1]
    requests = arriving.shape[0]
    half = requests // halves
    step_chunks = 4
    per_chunk = 128 // size
    steps = size // (per_chunk * step_chunks)
    cells = size * size

    def body(arr_ref, *refs):
        st = refs[:halves]
        p_ref, v_ref, kq_ref, uq_ref, d_ref, out_ref, new, rows = refs[halves:]
        step = pl.program_id(0)
        for g in range(halves):

            def update(block, _):
                first = block * 4
                real = step * (per_chunk * step_chunks) + first
                lefts = []
                for i in range(4):
                    row = [v_ref[g, t, pl.ds(real + i, 1), :] for t in range(slots)]
                    row += [p_ref[g, t, pl.ds(real + i, 1), :] for t in range(slots)]
                    lefts.append([jnp.broadcast_to(x, (8, lanes)) for x in row])
                for jv in range(size // 8):
                    at = slice(jv * 8, (jv + 1) * 8)
                    rights = [kq_ref[g, t, at, :] for t in range(slots)]
                    rights += [uq_ref[g, t, at, :] for t in range(slots)]
                    decayed = d_ref[g, at, :]
                    for i in range(4):
                        acc = st[g][real + i, at, :] * decayed
                        for left, right in zip(lefts[i], rights):
                            acc = acc + left * right
                        new[g, first + i, at, :] = acc
                return 0

            lax.fori_loop(0, per_chunk * step_chunks // 4, update, 0)
        for c in range(step_chunks):
            for g in range(halves):
                block = [new[g, per_chunk * c + e] for e in range(per_chunk)]
                turned = jnp.concatenate(block, axis=0).T
                for h in range(heads):
                    rows[c, pl.ds(g * half * heads + h, half, stride=heads), :] = turned[
                        h * half : (h + 1) * half
                    ]
        for c in range(step_chunks):
            for q in range(requests):
                out_ref[arr_ref[q], :, c * 128 : (c + 1) * 128] = rows[
                    c, q * heads : (q + 1) * heads, :
                ]

    args = (*states, removed, values, keys, units, decay)
    return pl.pallas_call(
        body,
        grid_spec=pltpu.PrefetchScalarGridSpec(
            num_scalar_prefetch=1,
            grid=(steps,),
            in_specs=[pl.BlockSpec(memory_space=pltpu.VMEM) for _ in args],
            out_specs=pl.BlockSpec((requests, heads, 128 * step_chunks), lambda s, a: (0, 0, s)),
            scratch_shapes=[
                vmem((halves, per_chunk * step_chunks, size, lanes), F32),
                vmem((step_chunks, requests * heads, 128), F32),
            ],
        ),
        out_shape=jax.ShapeDtypeStruct((requests, heads, cells), F32),
        compiler_params=pltpu.CompilerParams(vmem_limit_bytes=SCRATCH_LIMIT),
        name="final_states",
    )(arriving, *[pltpu.with_memory_space_constraint(a, pltpu.VMEM) for a in args])


def middle(tok, cols, own, others):
    rows, width = tok.shape

    def body(tok_ref, col, own_ref, *refs):
        out = refs[-1]
        total = dot32(chooser(col, SOURCE, rows, rows), tok_ref[...]) + own_ref[...]
        for o in refs[:-1]:
            total = total + o[...].astype(F32)
        out[...] = total.astype(BF16)

    return run(body, "middle", (), (tok, cols, own, *others), [vmem((rows, width), BF16)])[0]


def channel_mix(place, mids, prevs, cols, norm, mix, key_weight, value_weight):
    parts = len(mids)
    rows, width = mids[0].shape
    total = parts * width
    requests = prevs[0].shape[0]
    slots = rows // requests

    def body(place_ref, *refs):
        mid, prev = refs[:parts], refs[parts : 2 * parts]
        col, nrm, mx, kw, vw = refs[2 * parts : 2 * parts + 5]
        outs, shift = refs[2 * parts + 5 : 3 * parts + 5], refs[3 * parts + 5]
        xs = [m[...].astype(F32) for m in mid]
        mean = sum(jnp.sum(x, axis=1, keepdims=True) for x in xs) / total
        cs = [x - mean for x in xs]
        var = sum(jnp.sum(c * c, axis=1, keepdims=True) for c in cs) / total
        scale = lax.rsqrt(var + 1e-05)
        acc = None
        for k in range(parts):
            at = pl.ds(pl.multiple_of((place_ref[0] ^ k) * width, 128), width)
            now = cs[k] * scale * nrm[2:3, at] + nrm[3:4, at]
            before = jnp.concatenate([prev[k][...].astype(F32), now[: rows - requests]], axis=0)
            term = dot32((now + (before - now) * mx[6:7, at]).astype(BF16), kw[at, :])
            acc = term if k == 0 else acc + term
            if k == 0:
                chosen = jnp.zeros((requests, width), F32)
                number = col[0:requests, COUNT : COUNT + 1]
                for t in range(slots):
                    chosen = jnp.where(
                        number == t + 1, now[t * requests : (t + 1) * requests], chosen
                    )
                unsort = chooser(col, UNSORT, requests, requests)
                shift[...] = dot32(unsort, chosen.astype(BF16)).astype(BF16)
        h = jnp.maximum(acc, 0.0)
        hidden = (h * h).astype(BF16)
        for q in range(parts):
            at = pl.ds(pl.multiple_of((place_ref[0] ^ q) * width, 128), width)
            outs[q][...] = dot32(hidden, vw[:, at]).astype(outs[q].dtype)

    return run(
        body,
        "channel_mix",
        (place,),
        (*mids, *prevs, cols, norm, mix, key_weight, value_weight),
        [vmem((rows, width), F32)]
        + [vmem((rows, width), BF16) for _ in range(parts - 1)]
        + [vmem((requests, width), BF16)],
    )


def finish(mid, own, others, cols):
    rows, width = mid.shape

    def body(mid_ref, own_ref, *refs):
        col, out = refs[-2:]
        total = own_ref[...]
        for o in refs[:-2]:
            total = total + o[...].astype(F32)
        live = col[:, LIVE : LIVE + 1] > 0
        total = jnp.where(live, mid_ref[...].astype(F32) + total, 0.0).astype(BF16)
        out[...] = dot32(chooser(col, BACK, rows, rows), total).astype(BF16)

    return run(body, "finish", (), (mid, own, *others, cols), [vmem((rows, width), BF16)])[0]


def per_device(
    groups,
    parts,
    tokens,
    counts,
    new_owner,
    wkv_state,
    att_shift,
    ffn_shift,
    norm_params,
    mix_coeffs,
    head_params,
    recept_weight,
    key_weight,
    value_weight,
    output_weight,
    decay_down,
    decay_up,
    alpha_down,
    alpha_up,
    gate_down,
    gate_up,
    ffn_key_weight,
    ffn_value_weight,
):
    requests, slots, width = tokens.shape
    heads = wkv_state.shape[1]
    size = width // heads
    rows = requests * slots
    rank = lax.axis_index("req").astype(I32).reshape(1)
    place = lax.axis_index("mdl").astype(I32).reshape(1)
    gather = lambda x: [x] + [xor_permute(x, "mdl", parts, k) for k in range(1, parts)]
    scatter = lambda xs: [xor_permute(xs[k], "mdl", parts, k) for k in range(1, parts)]

    toks = gather(tokens.reshape(rows, width))
    order, arriving, cols, lane_counts, sent = make_plan(
        rank, new_owner, counts, att_shift, ffn_shift, groups, slots
    )
    got = lax.all_to_all(
        sent.reshape(groups, -1, width), "req", split_axis=0, concat_axis=0, tiled=True
    )
    att, ffn = sort_shifts(cols, got.reshape(2 * requests, width))
    atts = gather(att)

    first = toks[1]
    order, first = lax.optimization_barrier((order, first))
    toks = [toks[0], first] + toks[2:]
    packed = pack_states(order, wkv_state, groups)
    payloads = [
        packed[at] if k == 0 else xor_permute(packed[at], "req", groups, k)
        for at, k in enumerate(positions(groups))
    ]
    split = groups // 2
    states = [states_to_lanes(payloads[:split], size), states_to_lanes(payloads[split:], size)]

    normed, low, low_send, new_att = first_norm(
        place,
        toks,
        att,
        cols,
        norm_params,
        mix_coeffs,
        decay_down.T,
        alpha_down.T,
        gate_down,
    )
    low_others = gather(low_send)[1:]
    ffns = gather(ffn)
    recept, key, value = projections(
        place, normed, atts, mix_coeffs, (recept_weight, key_weight, value_weight)
    )
    weights, coefs, vals, keys, units, decay, gate, bonus = head_vectors(
        low,
        low_others,
        recept,
        key,
        value,
        head_params,
        (decay_up, alpha_up, gate_up),
        lane_counts,
        size,
    )
    results = head_outputs(
        place, states, weights, coefs, vals, gate, bonus, head_params, output_weight, parts
    )
    outs, removed = results[:parts], results[parts]
    mid = middle(toks[0], cols, outs[0], scatter(outs))
    new_state = final_states(arriving, states, removed, vals, keys, units, decay, heads)
    results = channel_mix(
        place,
        gather(mid),
        ffns,
        cols,
        norm_params,
        mix_coeffs,
        ffn_key_weight,
        ffn_value_weight,
    )
    outs, new_ffn = results[:parts], results[parts]
    block = finish(mid, outs[0], scatter(outs), cols)
    return (block.reshape(requests, slots, width), new_state, new_att, new_ffn)


def solution(mesh):
    return jax.shard_map(
        functools.partial(per_device, mesh.shape["req"], mesh.shape["mdl"]),
        mesh=mesh,
        in_specs=(
            P("req", None, "mdl"),
            P("req"),
            P(),
            P("req", "mdl", None),
            P("req", "mdl"),
            P("req", "mdl"),
            P(),
            P(),
            P(None, "mdl"),
            P(None, "mdl"),
            P(None, "mdl"),
            P(None, "mdl"),
            P("mdl", None),
            P("mdl", None),
            P(None, "mdl"),
            P("mdl", None),
            P(None, "mdl"),
            P("mdl", None),
            P(None, "mdl"),
            P(None, "mdl"),
            P("mdl", None),
        ),
        out_specs=(P("req", None, "mdl"), P("req", "mdl", None), P("req", "mdl"), P("req", "mdl")),
        check_vma=False,
    )
```

time: 445 us -> 131 us (0.29); the launches traced: 439 us -> 130 us
  local copies, waits for them, and re-layouts: 175 us -> 15.9 us
  other arithmetic: 112 us -> 0 us
  blocking collectives: 94.9 us -> 7.39 us
  Pallas kernels: 0 us -> 35.7 us
  starting transfers between devices: 14.6 us -> 41.7 us
  waiting for transfers between devices: 5.32 us -> 28.6 us
  matrix products: 23 us -> 0 us
  between operations: 14.5 us -> 0.93 us
    mul x25 -> x0, local copies, waits for them, and re-layouts: 121 us -> none  [the longest x9 48.6 us: advance(): wkv_square * decay_now[:, :, None, :]]
    all_gather x6 -> x0, blocking collectives: 94.9 us -> none  [the longest x1 20.2 us: per_device(): lax.all_gather(decay_down, 'mdl', axis=0, tiled=True)]
    reduce_sum x13 -> x0, other arithmetic: 52.6 us -> none  [the longest x2 24.5 us: advance(): removal = -jnp.sum(wkv_square * unit_now[:, :, None, :], axis=-1)]
    ppermute x0 -> x28, starting transfers between devices: none -> 41.7 us  [xor_permute(): return lax.ppermute(x, axis, [(a, a ^ k) for a in range(size)])]
    pallas_call x0 -> x13, Pallas kernels: none -> 35.7 us  [the longest x12 28.8 us: run(): pl.pallas_call(body, grid_spec=pltpu.PrefetchScalarGridSpec(num_scalar_pr...]
    ppermute x0 -> x28, waiting for transfers between devices: none -> 28.6 us  [xor_permute(): return lax.ppermute(x, axis, [(a, a ^ k) for a in range(size)])]
    dot_general x8 -> x0, matrix products: 23 us -> none  [project(): return jnp.dot(inputs, weight, preferred_element_type=jnp.float32)]
    select_n x3 -> x0, other arithmetic: 22.3 us -> none  [the longest x1 22.3 us: advance(): jnp.where(is_valid[:, None, None, None], updated, wkv_square)]
  transfers between devices with their start and end apart: 6 -> 28, of which waited for: 1 -> 8; matrix products, arithmetic and copies ran while one was open for 48% -> 1% of each run, Pallas kernels for 0% -> 22%
where the time goes in v2:
time: 131 us; the launch traced here: 130 us
  starting transfers between devices  41.7 us (32%)
  Pallas kernels  35.7 us (27%)
  waiting for transfers between devices  28.6 us (22%)
  local copies, waits for them, and re-layouts  15.9 us (12%)
  blocking collectives  7.39 us (6%)
    ppermute x28, starting transfers between devices, xor_permute(): return lax.ppermute(x, axis, [(a, a ^ k) for a in range(size)])  41.7 us
    pallas_call x12, Pallas kernels, run(): pl.pallas_call(body, grid_spec=pltpu.PrefetchScalarGridSpec(num_scalar_pr...  28.8 us
    ppermute x28, waiting for transfers between devices, xor_permute(): return lax.ppermute(x, axis, [(a, a ^ k) for a in range(size)])  28.6 us
    unnamed x56, local copies, waits for them, and re-layouts  14.3 us
    all_to_all x1, blocking collectives, per_device(): lax.all_to_all(sent.reshape(groups, -1, width), 'req', split_axis=0, conc...  7.39 us
    pallas_call x1, Pallas kernels, final_states(): pl.pallas_call(body, grid_spec=pltpu.PrefetchScalarGridSpec(num_scalar_pr...  6.96 us
  transfers between devices with their start and end apart: 28, of which 8 were waited for; matrix products, arithmetic and copies ran while one was open for 1% of the time, Pallas kernels for 22%

profile of v2, /device:TPU:0, one launch (start us, length us, event | category | flops | bytes accessed | tf_op | source)
XLA Modules:
  0.0 130.3 jit_solution(3971490039600777192)
XLA Ops:
  0.6 0.9 reshape.26.refs_0_.tok_ref
  1.6 3.1 %collective-permute-start = (bf16[128,512]{1,0:T(8,128)(2,1)S(1)}, bf16[128,512]{1,0:T(8,128)(2,1)S(1)}, u32[]{:S(2)}, u32[]{:S(2)}) collective-permute-start(bf16[128,512]{1,0:T(8,128)(2,1)S(1)} %reshape.26.refs_0_.tok_ref), channel_id=1, source_target_pairs={{0,1},{1,0},{2,3},{3,2},{4,5},{5,4},{6,7},{7,6},{8,9},{9,8},{10,11... | collective-permute-start | bytes 393224 | tf_op jit(solution)/shard_map/ppermute | solution.py:17
  4.7 2.6 %collective-permute-start.8 = (bf16[128,512]{1,0:T(8,128)(2,1)S(1)}, bf16[128,512]{1,0:T(8,128)(2,1)}, u32[]{:S(2)}, u32[]{:S(2)}) collective-permute-start(bf16[128,512]{1,0:T(8,128)(2,1)S(1)} %reshape.26.refs_0_.tok_ref), channel_id=1, source_target_pairs={{0,2},{1,3},{2,0},{3,1},{4,6},{5,7},{6,4},{7,5},{8,10},{9,11},{10,... | collective-permute-start | bytes 393224 | tf_op jit(solution)/shard_map/ppermute | solution.py:17
  7.3 0.8 copy-done.18
  8.0 0.8 copy-done.19
  8.8 0.7 copy-done.20
  9.5 0.7 copy-done.21
  10.1 5.9 %make_plan.1 = (s32[32]{0:T(128)S(1)}, s32[32]{0:T(128)S(1)}, s32[128,128]{1,0:T(8,128)S(1)}, s32[8,128]{1,0:T(8,128)S(1)}, bf16[64,512]{1,0:T(8,128)(2,1)S(1)}) custom-call(s32[1]{0:T(128)} %bitcast.rank_ref, s32[256]{0:T(256)S(1)} %copy-done.20, s32[32]{0:T(128)S(1)} %copy-done.21, bf16[32,512]{1,0:T(8,128)(2,1)S(1)} %copy-done.18, ...), custom_call_target="tpu_custom_call" | custom-call | tf_op jit(solution)/shard_map/make_plan/pallas_call | solution.py:35
  16.1 0.6 copy-done.11
  16.7 2.2 %copy-done.2 = f32[32,8,4096]{2,1,0:T(8,128)S(1)} copy-done((f32[32,8,4096]{2,1,0:T(8,128)S(1)}, f32[32,8,4096]{2,1,0:T(8,128)}, u32[]{:S(2)}) %copy-start.2) | copy-done | bytes 4194328
  18.9 7.4 %pack_states.1 = (bf16[4,8,4096]{2,1,0:T(8,128)(2,1)S(1)}, bf16[4,8,4096]{2,1,0:T(8,128)(2,1)}, bf16[4,8,4096]{2,1,0:T(8,128)(2,1)}, bf16[4,8,4096]{2,1,0:T(8,12...) custom-call(s32[32]{0:T(128)S(1)} %get-tuple-element.48.order_ref, ...), custom_call_target="tpu_custom_call" | custom-call | tf_op jit(solution)/shard_map/pack_states/pallas_call | solution.py:35
  26.3 0.7 copy-done.22
  27.0 0.7 copy-done.26
  27.7 1.7 %collective-permute-start.1 = (bf16[4,8,4096]{2,1,0:T(8,128)(2,1)}, bf16[4,8,4096]{2,1,0:T(8,128)(2,1)S(1)}, u32[]{:S(2)}, u32[]{:S(2)}) collective-permute-start(bf16[4,8,4096]{2,1,0:T(8,128)(2,1)} %get-tuple-element.50), channel_id=1, source_target_pairs={{0,8},{4,12},{8,0},{12,4},{16,24},{20,28},{24,16},{28,20},{1,9},{5... | collective-permute-start | bytes 786440 | tf_op jit(solution)/shard_map/ppermute | solution.py:17
  29.5 1.5 %collective-permute-start.2 = (bf16[4,8,4096]{2,1,0:T(8,128)(2,1)}, bf16[4,8,4096]{2,1,0:T(8,128)(2,1)S(1)}, u32[]{:S(2)}, u32[]{:S(2)}) collective-permute-start(bf16[4,8,4096]{2,1,0:T(8,128)(2,1)} %get-tuple-element.51), channel_id=1, source_target_pairs={{0,16},{4,20},{8,24},{12,28},{16,0},{20,4},{24,8},{28,12},{1,17},{... | collective-permute-start | bytes 786440 | tf_op jit(solution)/shard_map/ppermute | solution.py:17
  31.0 7.4 %all_to_all.5 = bf16[8,8,512]{2,1,0:T(8,128)(2,1)S(1)} all-to-all(bf16[8,8,512]{2,1,0:T(8,128)(2,1)S(1)} %bitcast.9), channel_id=1, replica_groups=mesh['req'=8,'mdl'=4] {'req'}, dimensions={0} | all-to-all | bytes 131072 | tf_op jit(solution)/shard_map/all_to_all | solution.py:751
  38.6 0.7 collective-permute-start.13
  39.3 3.5 %collective-permute-start.14 = (bf16[32,512]{1,0:T(8,128)(2,1)S(1)}, bf16[32,512]{1,0:T(8,128)(2,1)}, u32[]{:S(2)}, u32[]{:S(2)}) collective-permute-start(bf16[32,512]{1,0:T(8,128)(2,1)S(1)} %get-tuple-element.59.refs_4_.refs_0_), channel_id=1, source_target_pairs={{0,2},{1,3},{2,0},{3,1},{4,6},{5,7},{6,4},{7,5},{8,10},{9,11},{10,... | collective-permute-start | bytes 98312 | tf_op jit(solution)/shard_map/ppermute | solution.py:17
  42.8 0.3 collective-permute-start.15
  43.1 0.9 copy-done.12
  44.0 0.9 copy-done.13
  44.9 0.9 copy-done.14
  45.8 2.0 %first_norm.1 = (f32[4,128,512]{2,1,0:T(8,128)S(1)}, f32[128,448]{1,0:T(8,128)S(1)}, bf16[128,448]{1,0:T(8,128)(2,1)S(1)}, bf16[32,512]{1,0:T(8,128)(2,1)S(1)}) custom-call(s32[1]{0:T(128)} %bitcast.1.place_ref, bf16[128,512]{1,0:T(8,128)(2,1)S(1)} %reshape.26.refs_0_.tok_ref, bf16[128,512]{1,0:T(8,128)(2,1)S(1)} %copy-done.12, ...), custom_call_target="tpu_custom_call" | custom-call | tf_op jit(solution)/shard_map/first_norm/pallas_call | solution.py:35
  47.8 0.4 collective-permute-start.10
  48.2 3.8 %collective-permute-start.11 = (bf16[128,448]{1,0:T(8,128)(2,1)S(1)}, bf16[128,448]{1,0:T(8,128)(2,1)S(1)}, u32[]{:S(2)}, u32[]{:S(2)}) collective-permute-start(bf16[128,448]{1,0:T(8,128)(2,1)S(1)} %get-tuple-element.61), channel_id=1, source_target_pairs={{0,2},{1,3},{2,0},{3,1},{4,6},{5,7},{6,4},{7,5},{8,10},{9,11},{10,... | collective-permute-start | bytes 344072 | tf_op jit(solution)/shard_map/ppermute | solution.py:17
  52.0 0.2 collective-permute-start.12
  52.3 2.1 %collective-permute-done.10.refs_0_ = bf16[128,448]{1,0:T(8,128)(2,1)S(1)} collective-permute-done((bf16[128,448]{1,0:T(8,128)(2,1)S(1)}, bf16[128,448]{1,0:T(8,128)(2,1)S(1)}, u32[]{:S(2)}, u32[]{:S(2)}) %collective-permute-start.10) | collective-permute-done | bytes 114720 | tf_op jit(solution)/shard_map/ppermute | solution.py:17
  54.4 1.0 collective-permute-start.3
  55.4 5.9 %collective-permute-done.11.refs_1_ = bf16[128,448]{1,0:T(8,128)(2,1)S(1)} collective-permute-done((bf16[128,448]{1,0:T(8,128)(2,1)S(1)}, bf16[128,448]{1,0:T(8,128)(2,1)S(1)}, u32[]{:S(2)}, u32[]{:S(2)}) %collective-permute-start.11) | collective-permute-done | bytes 114720 | tf_op jit(solution)/shard_map/ppermute | solution.py:17
  61.2 1.0 collective-permute-start.5
  62.2 0.5 collective-permute-start.6
  62.7 1.8 %collective-permute-start.7 = (bf16[4,8,4096]{2,1,0:T(8,128)(2,1)}, bf16[4,8,4096]{2,1,0:T(8,128)(2,1)S(1)}, u32[]{:S(2)}, u32[]{:S(2)}) collective-permute-start(bf16[4,8,4096]{2,1,0:T(8,128)(2,1)} %copy-done.22), channel_id=1, source_target_pairs={{0,28},{4,24},{8,20},{12,16},{16,12},{20,8},{24,4},{28,0},{1,29},{... | collective-permute-start | bytes 786440 | tf_op jit(solution)/shard_map/ppermute | solution.py:17
  64.6 1.6 %copy-done.5 = bf16[2048,512]{1,0:T(8,128)(2,1)S(1)} copy-done((bf16[2048,512]{1,0:T(8,128)(2,1)S(1)}, bf16[2048,512]{1,0:T(8,128)(2,1)}, u32[]{:S(2)}) %copy-start.5) | copy-done | bytes 2097176
  66.2 1.6 %copy-done.6 = bf16[2048,512]{1,0:T(8,128)(2,1)S(1)} copy-done((bf16[2048,512]{1,0:T(8,128)(2,1)S(1)}, bf16[2048,512]{1,0:T(8,128)(2,1)}, u32[]{:S(2)}) %copy-start.6) | copy-done | bytes 2097176
  67.8 1.9 %projections.1 = (f32[128,512]{1,0:T(8,128)S(1)}, f32[128,512]{1,0:T(8,128)S(1)}, f32[128,512]{1,0:T(8,128)S(1)}) custom-call(s32[1]{0:T(128)} %bitcast.1.place_ref, f32[4,128,512]{2,1,0:T(8,128)S(1)} %get-tuple-element.62.n_ref, bf16[32,512]{1,0:T(8,128)(2,1)S(1)} %get-tuple-element.59.refs_4_.refs_0_, bf16[32,512]{1,0:T(8,128)(2,1)S(1)} %collective-permute-done.13.refs_1_, ...), custom_call_target="tpu_custom_call" | custom-call | tf_op jit(solution)/shard_map/projections/pallas_call | solution.py:35
  69.7 2.5 %head_vectors.1 = (f32[2,8,64,128]{3,2,1,0:T(8,128)S(1)}, f32[2,20,128]{2,1,0:T(8,128)S(1)}, f32[2,4,64,128]{3,2,1,0:T(8,128)S(1)}, f32[2,4,64,128]{3,2,1,0:T(8,...) custom-call(f32[128,448]{1,0:T(8,128)S(1)} %get-tuple-element.60.low, ...), custom_call_target="tpu_custom_call" | custom-call | tf_op jit(solution)/shard_map/head_vectors/pallas_call | solution.py:35
  72.2 1.3 %states_to_lanes.2.refs_0_ = f32[64,64,128]{2,1,0:T(8,128)S(1)} custom-call(bf16[4,8,4096]{2,1,0:T(8,128)(2,1)S(1)} %get-tuple-element.49.refs_0_, bf16[4,8,4096]{2,1,0:T(8,128)(2,1)S(1)} %collective-permute-done.1.refs_1_, bf16[4,8,4096]{2,1,0:T(8,128)(2,1)S(1)} %collective-permute-done.2.refs_2_, bf16[4,8,4096]{2,1,0:T(8,128)(2,1)S(1)} %collective-permute-done.3.refs_3_), custom_call_target="tpu_custom_call" | custom-call | tf_op jit(solution)/shard_map/states_to_lanes/pallas_call | solution.py:35
  73.6 2.9 %collective-permute-done.6.refs_2_ = bf16[4,8,4096]{2,1,0:T(8,128)(2,1)S(1)} collective-permute-done((bf16[4,8,4096]{2,1,0:T(8,128)(2,1)}, bf16[4,8,4096]{2,1,0:T(8,128)(2,1)S(1)}, u32[]{:S(2)}, u32[]{:S(2)}) %collective-permute-start.6) | collective-permute-done | bytes 262176 | tf_op jit(solution)/shard_map/ppermute | solution.py:17
  76.5 1.3 %states_to_lanes.3.refs_1_ = f32[64,64,128]{2,1,0:T(8,128)S(1)} custom-call(bf16[4,8,4096]{2,1,0:T(8,128)(2,1)S(1)} %collective-permute-done.4.refs_0_, bf16[4,8,4096]{2,1,0:T(8,128)(2,1)S(1)} %collective-permute-done.5.refs_1_, bf16[4,8,4096]{2,1,0:T(8,128)(2,1)S(1)} %collective-permute-done.6.refs_2_, bf16[4,8,4096]{2,1,0:T(8,128)(2,1)S(1)} %collective-permute-done.7.refs_3_), custom_call_target="tpu_custom_call" | custom-call | tf_op jit(solution)/shard_map/states_to_lanes/pallas_call | solution.py:35
  77.9 3.9 %head_outputs.1 = (f32[128,512]{1,0:T(8,128)S(1)}, bf16[128,512]{1,0:T(8,128)(2,1)S(1)}, bf16[128,512]{1,0:T(8,128)(2,1)S(1)}, bf16[128,512]{1,0:T(8,128)(2,1)S(1)}, f32[2,4,64,128]{3,2,1,0:T(8,128)S(1)}) custom-call(s32[1]{0:T(128)} %bitcast.1.place_ref, f32[64,64,128]{2,1,0:T(8,128)S(1)} %states_to_lanes.2.refs_0_, ...), custom_call_target="tpu_custom_call" | custom-call | tf_op jit(solution)/shard_map/head_outputs/pallas_call | solution.py:35
  81.8 1.1 collective-permute-start.16
  82.9 1.8 %collective-permute-start.17 = (bf16[128,512]{1,0:T(8,128)(2,1)S(1)}, bf16[128,512]{1,0:T(8,128)(2,1)S(1)}, u32[]{:S(2)}, u32[]{:S(2)}) collective-permute-start(bf16[128,512]{1,0:T(8,128)(2,1)S(1)} %get-tuple-element.74), channel_id=1, source_target_pairs={{0,2},{1,3},{2,0},{3,1},{4,6},{5,7},{6,4},{7,5},{8,10},{9,11},{10,... | collective-permute-start | bytes 393224 | tf_op jit(solution)/shard_map/ppermute | solution.py:17
  84.7 1.6 %collective-permute-start.18 = (bf16[128,512]{1,0:T(8,128)(2,1)S(1)}, bf16[128,512]{1,0:T(8,128)(2,1)S(1)}, u32[]{:S(2)}, u32[]{:S(2)}) collective-permute-start(bf16[128,512]{1,0:T(8,128)(2,1)S(1)} %get-tuple-element.75), channel_id=1, source_target_pairs={{0,3},{1,2},{2,1},{3,0},{4,7},{5,6},{6,5},{7,4},{8,11},{9,10},{10,... | collective-permute-start | bytes 393224 | tf_op jit(solution)/shard_map/ppermute | solution.py:17
  86.2 3.2 %collective-permute-done.16.refs_0_ = bf16[128,512]{1,0:T(8,128)(2,1)S(1)} collective-permute-done((bf16[128,512]{1,0:T(8,128)(2,1)S(1)}, bf16[128,512]{1,0:T(8,128)(2,1)S(1)}, u32[]{:S(2)}, u32[]{:S(2)}) %collective-permute-start.16) | collective-permute-done | bytes 131104 | tf_op jit(solution)/shard_map/ppermute | solution.py:17
  89.4 6.4 %collective-permute-done.17.refs_1_ = bf16[128,512]{1,0:T(8,128)(2,1)S(1)} collective-permute-done((bf16[128,512]{1,0:T(8,128)(2,1)S(1)}, bf16[128,512]{1,0:T(8,128)(2,1)S(1)}, u32[]{:S(2)}, u32[]{:S(2)}) %collective-permute-start.17) | collective-permute-done | bytes 131104 | tf_op jit(solution)/shard_map/ppermute | solution.py:17
  95.8 0.3 middle.1.refs_0_.mid_ref
  96.1 2.3 %collective-permute-start.19 = (bf16[128,512]{1,0:T(8,128)(2,1)S(1)}, bf16[128,512]{1,0:T(8,128)(2,1)S(1)}, u32[]{:S(2)}, u32[]{:S(2)}) collective-permute-start(bf16[128,512]{1,0:T(8,128)(2,1)S(1)} %middle.1.refs_0_.mid_ref), channel_id=1, source_target_pairs={{0,1},{1,0},{2,3},{3,2},{4,5},{5,4},{6,7},{7,6},{8,9},{9,8},{10,11... | collective-permute-start | bytes 393224 | tf_op jit(solution)/shard_map/ppermute | solution.py:17
  98.3 1.0 collective-permute-start.20
  99.3 1.4 %collective-permute-start.21 = (bf16[128,512]{1,0:T(8,128)(2,1)S(1)}, bf16[128,512]{1,0:T(8,128)(2,1)S(1)}, u32[]{:S(2)}, u32[]{:S(2)}) collective-permute-start(bf16[128,512]{1,0:T(8,128)(2,1)S(1)} %middle.1.refs_0_.mid_ref), channel_id=1, source_target_pairs={{0,3},{1,2},{2,1},{3,0},{4,7},{5,6},{6,5},{7,4},{8,11},{9,10},{10,... | collective-permute-start | bytes 393224 | tf_op jit(solution)/shard_map/ppermute | solution.py:17
  100.8 1.0 collective-permute-start.22
  101.8 1.9 %collective-permute-start.23 = (bf16[32,512]{1,0:T(8,128)(2,1)S(1)}, bf16[32,512]{1,0:T(8,128)(2,1)S(1)}, u32[]{:S(2)}, u32[]{:S(2)}) collective-permute-start(bf16[32,512]{1,0:T(8,128)(2,1)S(1)} %get-tuple-element.76.refs_4_), channel_id=1, source_target_pairs={{0,2},{1,3},{2,0},{3,1},{4,6},{5,7},{6,4},{7,5},{8,10},{9,11},{10,... | collective-permute-start | bytes 98312 | tf_op jit(solution)/shard_map/ppermute | solution.py:17
  103.7 3.1 %collective-permute-done.22.refs_5_ = bf16[32,512]{1,0:T(8,128)(2,1)S(1)} collective-permute-done((bf16[32,512]{1,0:T(8,128)(2,1)S(1)}, bf16[32,512]{1,0:T(8,128)(2,1)S(1)}, u32[]{:S(2)}, u32[]{:S(2)}) %collective-permute-start.22) | collective-permute-done | bytes 32800 | tf_op jit(solution)/shard_map/ppermute | solution.py:17
  106.9 3.0 %collective-permute-start.24 = (bf16[32,512]{1,0:T(8,128)(2,1)S(1)}, bf16[32,512]{1,0:T(8,128)(2,1)S(1)}, u32[]{:S(2)}, u32[]{:S(2)}) collective-permute-start(bf16[32,512]{1,0:T(8,128)(2,1)S(1)} %get-tuple-element.76.refs_4_), channel_id=1, source_target_pairs={{0,3},{1,2},{2,1},{3,0},{4,7},{5,6},{6,5},{7,4},{8,11},{9,10},{10,... | collective-permute-start | bytes 98312 | tf_op jit(solution)/shard_map/ppermute | solution.py:17
  109.8 4.4 %collective-permute-done.23.refs_6_ = bf16[32,512]{1,0:T(8,128)(2,1)S(1)} collective-permute-done((bf16[32,512]{1,0:T(8,128)(2,1)S(1)}, bf16[32,512]{1,0:T(8,128)(2,1)S(1)}, u32[]{:S(2)}, u32[]{:S(2)}) %collective-permute-start.23) | collective-permute-done | bytes 32800 | tf_op jit(solution)/shard_map/ppermute | solution.py:17
  114.3 1.8 %channel_mix.1 = (f32[128,512]{1,0:T(8,128)S(1)}, bf16[128,512]{1,0:T(8,128)(2,1)S(1)}, bf16[128,512]{1,0:T(8,128)(2,1)S(1)}, bf16[128,512]{1,0:T(8,128)(2,1)S(1)}, bf16[32,512]{1,0:T(8,128)(2,1)S(1)}) custom-call(s32[1]{0:T(128)} %bitcast.1.place_ref, bf16[128,512]{1,0:T(8,128)(2,1)S(1)} %middle.1.refs_0_.mid_ref, ...), custom_call_target="tpu_custom_call" | custom-call | tf_op jit(solution)/shard_map/channel_mix/pallas_call | solution.py:35
  116.1 1.0 collective-permute-start.25
  117.0 2.2 %collective-permute-start.26 = (bf16[128,512]{1,0:T(8,128)(2,1)S(1)}, bf16[128,512]{1,0:T(8,128)(2,1)S(1)}, u32[]{:S(2)}, u32[]{:S(2)}) collective-permute-start(bf16[128,512]{1,0:T(8,128)(2,1)S(1)} %get-tuple-element.79), channel_id=1, source_target_pairs={{0,2},{1,3},{2,0},{3,1},{4,6},{5,7},{6,4},{7,5},{8,10},{9,11},{10,... | collective-permute-start | bytes 393224 | tf_op jit(solution)/shard_map/ppermute | solution.py:17
  119.2 1.3 collective-permute-start.27
  120.5 0.6 copy.25
  121.1 7.0 %final_states.1 = f32[32,8,4096]{2,1,0:T(8,128)} custom-call(s32[32]{0:T(128)S(1)} %get-tuple-element.81.arr_ref, f32[64,64,128]{2,1,0:T(8,128)S(1)} %states_to_lanes.2.refs_0_, f32[64,64,128]{2,1,0:T(8,128)S(1)} %states_to_lanes.3.refs_1_, f32[2,4,64,128]{3,2,1,0:T(8,128)S(1)} %get-tuple-element.82.refs_2_, ...), custom_call_target="tpu_custom_call" | custom-call | tf_op jit(solution)/shard_map/final_states/pallas_call | solution.py:618
  128.1 0.6 copy.26
  128.7 0.6 collective-permute-done.26.refs_1_
  129.3 0.2 finish.1
  129.6 0.7 reshape.31
  (64 shorter events, 0.3 us)
Async XLA Ops:
  1.6 14.5 %collective-permute-start = (bf16[128,512]{1,0:T(8,128)(2,1)S(1)}, bf16[128,512]{1,0:T(8,128)(2,1)S(1)}, u32[]{:S(2)}, u32[]{:S(2)}) collective-permute-start(bf16[128,512]{1,0:T(8,128)(2,1)S(1)} %reshape.26.refs_0_.tok_ref), channel_id=1, source_target_pairs={{0,1},{1,0},{2,3},{3,2},{4,5},{5,4},{6,7},{7,6},{8,9},{9,8},{10,11... | collective-permute-start | bytes 393224 | tf_op jit(solution)/shard_map/ppermute | solution.py:17
  4.7 34.7 %collective-permute-start.8 = (bf16[128,512]{1,0:T(8,128)(2,1)S(1)}, bf16[128,512]{1,0:T(8,128)(2,1)}, u32[]{:S(2)}, u32[]{:S(2)}) collective-permute-start(bf16[128,512]{1,0:T(8,128)(2,1)S(1)} %reshape.26.refs_0_.tok_ref), channel_id=1, source_target_pairs={{0,2},{1,3},{2,0},{3,1},{4,6},{5,7},{6,4},{7,5},{8,10},{9,11},{10,... | collective-permute-start | bytes 393224 | tf_op jit(solution)/shard_map/ppermute | solution.py:17
  7.3 35.6 %collective-permute-start.9 = (bf16[128,512]{1,0:T(8,128)(2,1)S(1)}, bf16[128,512]{1,0:T(8,128)(2,1)}, u32[]{:S(2)}, u32[]{:S(2)}) collective-permute-start(bf16[128,512]{1,0:T(8,128)(2,1)S(1)} %reshape.26.refs_0_.tok_ref), channel_id=1, source_target_pairs={{0,3},{1,2},{2,1},{3,0},{4,7},{5,6},{6,5},{7,4},{8,11},{9,10},{10,... | collective-permute-start | bytes 393224 | tf_op jit(solution)/shard_map/ppermute | solution.py:17
  7.3 0.8 copy-start.18
  8.0 0.8 copy-start.19
  8.8 0.7 copy-start.20
  9.5 0.7 copy-start.21
  16.0 0.7 copy-start.11
  16.7 2.2 %copy-start.2 = (f32[32,8,4096]{2,1,0:T(8,128)S(1)}, f32[32,8,4096]{2,1,0:T(8,128)}, u32[]{:S(2)}) copy-start(f32[32,8,4096]{2,1,0:T(8,128)} %src.1) | copy-start | bytes 12582916
  18.9 24.2 %copy-start.7 = (f32[7,2048]{1,0:T(8,128)S(1)}, f32[7,2048]{1,0:T(8,128)}, u32[]{:S(2)}) copy-start(f32[7,2048]{1,0:T(8,128)} %refs_10_.3) | copy-start | bytes 172036
  18.9 24.2 %copy-start.8 = (bf16[512,256]{1,0:T(8,128)(2,1)S(1)}, bf16[512,256]{1,0:T(8,128)(2,1)}, u32[]{:S(2)}) copy-start(bf16[512,256]{1,0:T(8,128)(2,1)} %refs_10_.2) | copy-start | bytes 786436
  18.9 24.2 %copy-start.10 = (f32[4,2048]{1,0:T(4,128)S(1)}, f32[4,2048]{1,0:T(4,128)}, u32[]{:S(2)}) copy-start(f32[4,2048]{1,0:T(4,128)} %refs_9_.3) | copy-start | bytes 98308
  18.9 45.7 %copy-start.4 = (bf16[2048,512]{1,0:T(8,128)(2,1)S(1)}, bf16[2048,512]{1,0:T(8,128)(2,1)}, u32[]{:S(2)}) copy-start(bf16[2048,512]{1,0:T(8,128)(2,1)} %refs_5_.1) | copy-start | bytes 6291460
  26.3 0.7 copy-start.22
  27.0 0.7 copy-start.26
  27.7 1.7 %copy-start.23 = (bf16[4,8,4096]{2,1,0:T(8,128)(2,1)}, bf16[4,8,4096]{2,1,0:T(8,128)(2,1)S(1)}, u32[]{:S(2)}) copy-start(bf16[4,8,4096]{2,1,0:T(8,128)(2,1)S(1)} %get-tuple-element.55) | copy-start | bytes 786436
  27.7 15.1 %copy-start.24 = (bf16[4,8,4096]{2,1,0:T(8,128)(2,1)}, bf16[4,8,4096]{2,1,0:T(8,128)(2,1)S(1)}, u32[]{:S(2)}) copy-start(bf16[4,8,4096]{2,1,0:T(8,128)(2,1)S(1)} %get-tuple-element.54) | copy-start | bytes 786436
  27.7 15.1 %copy-start.25 = (bf16[4,8,4096]{2,1,0:T(8,128)(2,1)}, bf16[4,8,4096]{2,1,0:T(8,128)(2,1)S(1)}, u32[]{:S(2)}) copy-start(bf16[4,8,4096]{2,1,0:T(8,128)(2,1)S(1)} %get-tuple-element.53) | copy-start | bytes 786436
  27.7 34.5 %collective-permute-start.1 = (bf16[4,8,4096]{2,1,0:T(8,128)(2,1)}, bf16[4,8,4096]{2,1,0:T(8,128)(2,1)S(1)}, u32[]{:S(2)}, u32[]{:S(2)}) collective-permute-start(bf16[4,8,4096]{2,1,0:T(8,128)(2,1)} %get-tuple-element.50), channel_id=1, source_target_pairs={{0,8},{4,12},{8,0},{12,4},{16,24},{20,28},{24,16},{28,20},{1,9},{5... | collective-permute-start | bytes 786440 | tf_op jit(solution)/shard_map/ppermute | solution.py:17
  29.5 33.3 %collective-permute-start.2 = (bf16[4,8,4096]{2,1,0:T(8,128)(2,1)}, bf16[4,8,4096]{2,1,0:T(8,128)(2,1)S(1)}, u32[]{:S(2)}, u32[]{:S(2)}) collective-permute-start(bf16[4,8,4096]{2,1,0:T(8,128)(2,1)} %get-tuple-element.51), channel_id=1, source_target_pairs={{0,16},{4,20},{8,24},{12,28},{16,0},{20,4},{24,8},{28,12},{1,17},{... | collective-permute-start | bytes 786440 | tf_op jit(solution)/shard_map/ppermute | solution.py:17
  38.6 9.2 %collective-permute-start.13 = (bf16[32,512]{1,0:T(8,128)(2,1)S(1)}, bf16[32,512]{1,0:T(8,128)(2,1)S(1)}, u32[]{:S(2)}, u32[]{:S(2)}) collective-permute-start(bf16[32,512]{1,0:T(8,128)(2,1)S(1)} %get-tuple-element.59.refs_4_.refs_0_), channel_id=1, source_target_pairs={{0,1},{1,0},{2,3},{3,2},{4,5},{5,4},{6,7},{7,6},{8,9},{9,8},{10,11... | collective-permute-start | bytes 98312 | tf_op jit(solution)/shard_map/ppermute | solution.py:17
  39.3 8.9 %collective-permute-start.14 = (bf16[32,512]{1,0:T(8,128)(2,1)S(1)}, bf16[32,512]{1,0:T(8,128)(2,1)}, u32[]{:S(2)}, u32[]{:S(2)}) collective-permute-start(bf16[32,512]{1,0:T(8,128)(2,1)S(1)} %get-tuple-element.59.refs_4_.refs_0_), channel_id=1, source_target_pairs={{0,2},{1,3},{2,0},{3,1},{4,6},{5,7},{6,4},{7,5},{8,10},{9,11},{10,... | collective-permute-start | bytes 98312 | tf_op jit(solution)/shard_map/ppermute | solution.py:17
  42.8 9.2 %collective-permute-start.15 = (bf16[32,512]{1,0:T(8,128)(2,1)S(1)}, bf16[32,512]{1,0:T(8,128)(2,1)}, u32[]{:S(2)}, u32[]{:S(2)}) collective-permute-start(bf16[32,512]{1,0:T(8,128)(2,1)S(1)} %get-tuple-element.59.refs_4_.refs_0_), channel_id=1, source_target_pairs={{0,3},{1,2},{2,1},{3,0},{4,7},{5,6},{6,5},{7,4},{8,11},{9,10},{10,... | collective-permute-start | bytes 98312 | tf_op jit(solution)/shard_map/ppermute | solution.py:17
  43.1 0.9 copy-start.12
  44.0 0.9 copy-start.13
  44.9 0.9 copy-start.14
  47.8 6.6 %collective-permute-start.10 = (bf16[128,448]{1,0:T(8,128)(2,1)S(1)}, bf16[128,448]{1,0:T(8,128)(2,1)S(1)}, u32[]{:S(2)}, u32[]{:S(2)}) collective-permute-start(bf16[128,448]{1,0:T(8,128)(2,1)S(1)} %get-tuple-element.61), channel_id=1, source_target_pairs={{0,1},{1,0},{2,3},{3,2},{4,5},{5,4},{6,7},{7,6},{8,9},{9,8},{10,11... | collective-permute-start | bytes 344072 | tf_op jit(solution)/shard_map/ppermute | solution.py:17
  48.2 13.0 %collective-permute-start.11 = (bf16[128,448]{1,0:T(8,128)(2,1)S(1)}, bf16[128,448]{1,0:T(8,128)(2,1)S(1)}, u32[]{:S(2)}, u32[]{:S(2)}) collective-permute-start(bf16[128,448]{1,0:T(8,128)(2,1)S(1)} %get-tuple-element.61), channel_id=1, source_target_pairs={{0,2},{1,3},{2,0},{3,1},{4,6},{5,7},{6,4},{7,5},{8,10},{9,11},{10,... | collective-permute-start | bytes 344072 | tf_op jit(solution)/shard_map/ppermute | solution.py:17
  52.0 9.2 %collective-permute-start.12 = (bf16[128,448]{1,0:T(8,128)(2,1)S(1)}, bf16[128,448]{1,0:T(8,128)(2,1)S(1)}, u32[]{:S(2)}, u32[]{:S(2)}) collective-permute-start(bf16[128,448]{1,0:T(8,128)(2,1)S(1)} %get-tuple-element.61), channel_id=1, source_target_pairs={{0,3},{1,2},{2,1},{3,0},{4,7},{5,6},{6,5},{7,4},{8,11},{9,10},{10,... | collective-permute-start | bytes 344072 | tf_op jit(solution)/shard_map/ppermute | solution.py:17
  54.4 17.8 %collective-permute-start.3 = (bf16[4,8,4096]{2,1,0:T(8,128)(2,1)}, bf16[4,8,4096]{2,1,0:T(8,128)(2,1)S(1)}, u32[]{:S(2)}, u32[]{:S(2)}) collective-permute-start(bf16[4,8,4096]{2,1,0:T(8,128)(2,1)} %copy-done.26), channel_id=1, source_target_pairs={{0,24},{4,28},{8,16},{12,20},{16,8},{20,12},{24,0},{28,4},{1,25},{... | collective-permute-start | bytes 786440 | tf_op jit(solution)/shard_map/ppermute | solution.py:17
  61.2 12.4 %collective-permute-start.4 = (bf16[4,8,4096]{2,1,0:T(8,128)(2,1)}, bf16[4,8,4096]{2,1,0:T(8,128)(2,1)S(1)}, u32[]{:S(2)}, u32[]{:S(2)}) collective-permute-start(bf16[4,8,4096]{2,1,0:T(8,128)(2,1)} %copy-done.25), channel_id=1, source_target_pairs={{0,4},{4,0},{8,12},{12,8},{16,20},{20,16},{24,28},{28,24},{1,5},{5... | collective-permute-start | bytes 786440 | tf_op jit(solution)/shard_map/ppermute | solution.py:17
  61.2 12.4 %collective-permute-start.5 = (bf16[4,8,4096]{2,1,0:T(8,128)(2,1)}, bf16[4,8,4096]{2,1,0:T(8,128)(2,1)S(1)}, u32[]{:S(2)}, u32[]{:S(2)}) collective-permute-start(bf16[4,8,4096]{2,1,0:T(8,128)(2,1)} %copy-done.24), channel_id=1, source_target_pairs={{0,12},{4,8},{8,4},{12,0},{16,28},{20,24},{24,20},{28,16},{1,13},{... | collective-permute-start | bytes 786440 | tf_op jit(solution)/shard_map/ppermute | solution.py:17
  62.2 14.2 %collective-permute-start.6 = (bf16[4,8,4096]{2,1,0:T(8,128)(2,1)}, bf16[4,8,4096]{2,1,0:T(8,128)(2,1)S(1)}, u32[]{:S(2)}, u32[]{:S(2)}) collective-permute-start(bf16[4,8,4096]{2,1,0:T(8,128)(2,1)} %copy-done.23), channel_id=1, source_target_pairs={{0,20},{4,16},{8,28},{12,24},{16,4},{20,0},{24,12},{28,8},{1,21},{... | collective-permute-start | bytes 786440 | tf_op jit(solution)/shard_map/ppermute | solution.py:17
  62.7 13.8 %collective-permute-start.7 = (bf16[4,8,4096]{2,1,0:T(8,128)(2,1)}, bf16[4,8,4096]{2,1,0:T(8,128)(2,1)S(1)}, u32[]{:S(2)}, u32[]{:S(2)}) collective-permute-start(bf16[4,8,4096]{2,1,0:T(8,128)(2,1)} %copy-done.22), channel_id=1, source_target_pairs={{0,28},{4,24},{8,20},{12,16},{16,12},{20,8},{24,4},{28,0},{1,29},{... | collective-permute-start | bytes 786440 | tf_op jit(solution)/shard_map/ppermute | solution.py:17
  64.6 1.6 %copy-start.5 = (bf16[2048,512]{1,0:T(8,128)(2,1)S(1)}, bf16[2048,512]{1,0:T(8,128)(2,1)}, u32[]{:S(2)}) copy-start(bf16[2048,512]{1,0:T(8,128)(2,1)} %refs_6_.4) | copy-start | bytes 6291460
  66.2 1.6 %copy-start.6 = (bf16[2048,512]{1,0:T(8,128)(2,1)S(1)}, bf16[2048,512]{1,0:T(8,128)(2,1)}, u32[]{:S(2)}) copy-start(bf16[2048,512]{1,0:T(8,128)(2,1)} %refs_7_.5) | copy-start | bytes 6291460
  67.8 1.9 %copy-start.9 = (bf16[256,512]{1,0:T(8,128)(2,1)S(1)}, bf16[256,512]{1,0:T(8,128)(2,1)}, u32[]{:S(2)}) copy-start(bf16[256,512]{1,0:T(8,128)(2,1)} %refs_9_.2) | copy-start | bytes 786436
  67.8 1.9 %copy-start.15 = (bf16[96,512]{1,0:T(8,128)(2,1)S(1)}, bf16[96,512]{1,0:T(8,128)(2,1)}, u32[]{:S(2)}) copy-start(bf16[96,512]{1,0:T(8,128)(2,1)} %refs_7_.6) | copy-start | bytes 294916
  67.8 2.0 %copy-start.16 = (bf16[96,512]{1,0:T(8,128)(2,1)S(1)}, bf16[96,512]{1,0:T(8,128)(2,1)}, u32[]{:S(2)}) copy-start(bf16[96,512]{1,0:T(8,128)(2,1)} %refs_8_.2) | copy-start | bytes 294916
  67.8 2.0 %copy-start.17 = (f32[7,512]{1,0:T(8,128)S(1)}, f32[7,512]{1,0:T(8,128)}, u32[]{:S(2)}) copy-start(f32[7,512]{1,0:T(8,128)} %refs_7_.7) | copy-start | bytes 43012
  73.6 4.2 %copy-start.3 = (bf16[512,2048]{1,0:T(8,128)(2,1)S(1)}, bf16[512,2048]{1,0:T(8,128)(2,1)}, u32[]{:S(2)}) copy-start(bf16[512,2048]{1,0:T(8,128)(2,1)} %refs_8_.3) | copy-start | bytes 6291460
  77.8 36.4 %copy-start = (bf16[2048,1024]{1,0:T(8,128)(2,1)S(1)}, bf16[2048,1024]{1,0:T(8,128)(2,1)}, u32[]{:S(2)}) copy-start(bf16[2048,1024]{1,0:T(8,128)(2,1)} %refs_11_.1) | copy-start | bytes 12582916
  77.9 36.4 %copy-start.1 = (bf16[1024,2048]{1,0:T(8,128)(2,1)S(1)}, bf16[1024,2048]{1,0:T(8,128)(2,1)}, u32[]{:S(2)}) copy-start(bf16[1024,2048]{1,0:T(8,128)(2,1)} %refs_12_.1) | copy-start | bytes 12582916
  81.8 7.6 %collective-permute-start.16 = (bf16[128,512]{1,0:T(8,128)(2,1)S(1)}, bf16[128,512]{1,0:T(8,128)(2,1)S(1)}, u32[]{:S(2)}, u32[]{:S(2)}) collective-permute-start(bf16[128,512]{1,0:T(8,128)(2,1)S(1)} %get-tuple-element.73), channel_id=1, source_target_pairs={{0,1},{1,0},{2,3},{3,2},{4,5},{5,4},{6,7},{7,6},{8,9},{9,8},{10,11... | collective-permute-start | bytes 393224 | tf_op jit(solution)/shard_map/ppermute | solution.py:17
  82.9 12.9 %collective-permute-start.17 = (bf16[128,512]{1,0:T(8,128)(2,1)S(1)}, bf16[128,512]{1,0:T(8,128)(2,1)S(1)}, u32[]{:S(2)}, u32[]{:S(2)}) collective-permute-start(bf16[128,512]{1,0:T(8,128)(2,1)S(1)} %get-tuple-element.74), channel_id=1, source_target_pairs={{0,2},{1,3},{2,0},{3,1},{4,6},{5,7},{6,4},{7,5},{8,10},{9,11},{10,... | collective-permute-start | bytes 393224 | tf_op jit(solution)/shard_map/ppermute | solution.py:17
  84.7 11.1 %collective-permute-start.18 = (bf16[128,512]{1,0:T(8,128)(2,1)S(1)}, bf16[128,512]{1,0:T(8,128)(2,1)S(1)}, u32[]{:S(2)}, u32[]{:S(2)}) collective-permute-start(bf16[128,512]{1,0:T(8,128)(2,1)S(1)} %get-tuple-element.75), channel_id=1, source_target_pairs={{0,3},{1,2},{2,1},{3,0},{4,7},{5,6},{6,5},{7,4},{8,11},{9,10},{10,... | collective-permute-start | bytes 393224 | tf_op jit(solution)/shard_map/ppermute | solution.py:17
  96.1 18.2 %collective-permute-start.19 = (bf16[128,512]{1,0:T(8,128)(2,1)S(1)}, bf16[128,512]{1,0:T(8,128)(2,1)S(1)}, u32[]{:S(2)}, u32[]{:S(2)}) collective-permute-start(bf16[128,512]{1,0:T(8,128)(2,1)S(1)} %middle.1.refs_0_.mid_ref), channel_id=1, source_target_pairs={{0,1},{1,0},{2,3},{3,2},{4,5},{5,4},{6,7},{7,6},{8,9},{9,8},{10,11... | collective-permute-start | bytes 393224 | tf_op jit(solution)/shard_map/ppermute | solution.py:17
  98.3 15.9 %collective-permute-start.20 = (bf16[128,512]{1,0:T(8,128)(2,1)S(1)}, bf16[128,512]{1,0:T(8,128)(2,1)S(1)}, u32[]{:S(2)}, u32[]{:S(2)}) collective-permute-start(bf16[128,512]{1,0:T(8,128)(2,1)S(1)} %middle.1.refs_0_.mid_ref), channel_id=1, source_target_pairs={{0,2},{1,3},{2,0},{3,1},{4,6},{5,7},{6,4},{7,5},{8,10},{9,11},{10,... | collective-permute-start | bytes 393224 | tf_op jit(solution)/shard_map/ppermute | solution.py:17
  99.3 14.9 %collective-permute-start.21 = (bf16[128,512]{1,0:T(8,128)(2,1)S(1)}, bf16[128,512]{1,0:T(8,128)(2,1)S(1)}, u32[]{:S(2)}, u32[]{:S(2)}) collective-permute-start(bf16[128,512]{1,0:T(8,128)(2,1)S(1)} %middle.1.refs_0_.mid_ref), channel_id=1, source_target_pairs={{0,3},{1,2},{2,1},{3,0},{4,7},{5,6},{6,5},{7,4},{8,11},{9,10},{10,... | collective-permute-start | bytes 393224 | tf_op jit(solution)/shard_map/ppermute | solution.py:17
  100.8 6.1 %collective-permute-start.22 = (bf16[32,512]{1,0:T(8,128)(2,1)S(1)}, bf16[32,512]{1,0:T(8,128)(2,1)S(1)}, u32[]{:S(2)}, u32[]{:S(2)}) collective-permute-start(bf16[32,512]{1,0:T(8,128)(2,1)S(1)} %get-tuple-element.76.refs_4_), channel_id=1, source_target_pairs={{0,1},{1,0},{2,3},{3,2},{4,5},{5,4},{6,7},{7,6},{8,9},{9,8},{10,11... | collective-permute-start | bytes 98312 | tf_op jit(solution)/shard_map/ppermute | solution.py:17
  101.8 12.4 %collective-permute-start.23 = (bf16[32,512]{1,0:T(8,128)(2,1)S(1)}, bf16[32,512]{1,0:T(8,128)(2,1)S(1)}, u32[]{:S(2)}, u32[]{:S(2)}) collective-permute-start(bf16[32,512]{1,0:T(8,128)(2,1)S(1)} %get-tuple-element.76.refs_4_), channel_id=1, source_target_pairs={{0,2},{1,3},{2,0},{3,1},{4,6},{5,7},{6,4},{7,5},{8,10},{9,11},{10,... | collective-permute-start | bytes 98312 | tf_op jit(solution)/shard_map/ppermute | solution.py:17
  106.9 7.4 %collective-permute-start.24 = (bf16[32,512]{1,0:T(8,128)(2,1)S(1)}, bf16[32,512]{1,0:T(8,128)(2,1)S(1)}, u32[]{:S(2)}, u32[]{:S(2)}) collective-permute-start(bf16[32,512]{1,0:T(8,128)(2,1)S(1)} %get-tuple-element.76.refs_4_), channel_id=1, source_target_pairs={{0,3},{1,2},{2,1},{3,0},{4,7},{5,6},{6,5},{7,4},{8,11},{9,10},{10,... | collective-permute-start | bytes 98312 | tf_op jit(solution)/shard_map/ppermute | solution.py:17
  116.1 12.6 %collective-permute-start.25 = (bf16[128,512]{1,0:T(8,128)(2,1)S(1)}, bf16[128,512]{1,0:T(8,128)(2,1)S(1)}, u32[]{:S(2)}, u32[]{:S(2)}) collective-permute-start(bf16[128,512]{1,0:T(8,128)(2,1)S(1)} %get-tuple-element.78), channel_id=1, source_target_pairs={{0,1},{1,0},{2,3},{3,2},{4,5},{5,4},{6,7},{7,6},{8,9},{9,8},{10,11... | collective-permute-start | bytes 393224 | tf_op jit(solution)/shard_map/ppermute | solution.py:17
  117.0 12.3 %collective-permute-start.26 = (bf16[128,512]{1,0:T(8,128)(2,1)S(1)}, bf16[128,512]{1,0:T(8,128)(2,1)S(1)}, u32[]{:S(2)}, u32[]{:S(2)}) collective-permute-start(bf16[128,512]{1,0:T(8,128)(2,1)S(1)} %get-tuple-element.79), channel_id=1, source_target_pairs={{0,2},{1,3},{2,0},{3,1},{4,6},{5,7},{6,4},{7,5},{8,10},{9,11},{10,... | collective-permute-start | bytes 393224 | tf_op jit(solution)/shard_map/ppermute | solution.py:17
  119.2 10.1 %collective-permute-start.27 = (bf16[128,512]{1,0:T(8,128)(2,1)S(1)}, bf16[128,512]{1,0:T(8,128)(2,1)S(1)}, u32[]{:S(2)}, u32[]{:S(2)}) collective-permute-start(bf16[128,512]{1,0:T(8,128)(2,1)S(1)} %get-tuple-element.80), channel_id=1, source_target_pairs={{0,3},{1,2},{2,1},{3,0},{4,7},{5,6},{6,5},{7,4},{8,11},{9,10},{10,... | collective-permute-start | bytes 393224 | tf_op jit(solution)/shard_map/ppermute | solution.py:17

commit v3 on v2

--- a/solution.py
+++ b/solution.py
@@ -29,35 +29,58 @@
     return pltpu.VMEM(shape, dtype)
 
 
-def run(body, name, scalars, args, outs, scratch=(), in_hbm=(), out_hbm=()):
-    anywhere = pl.BlockSpec(memory_space=pl.ANY)
+def run(body, name, scalars, args, outs, scratch=(), fetch=(), in_hbm=()):
+    far = set(fetch) | set(in_hbm)
+    anywhere = pl.BlockSpec(memory_space=pltpu.HBM)
     near = pl.BlockSpec(memory_space=pltpu.VMEM)
+    n_scalars, n_args, n_outs = len(scalars), len(args), len(outs)
+
+    def whole(*refs):
+        refs = list(refs)
+        if not fetch:
+            return body(*refs)
+        sems = refs.pop()
+        first = len(refs) - len(fetch)
+        buffers = refs[first:]
+        refs = refs[:first]
+        copies = []
+        for at, (i, buffer) in enumerate(zip(fetch, buffers)):
+            copies.append(pltpu.make_async_copy(refs[n_scalars + i], buffer, sems.at[at]))
+            refs[n_scalars + i] = buffer
+        for c in copies:
+            c.start()
+
+        def ready(which=None):
+            for c in copies if which is None else [copies[which]]:
+                c.wait()
+
+        return body(ready, *refs)
+
+    extra = [pltpu.VMEM(args[i].shape, args[i].dtype) for i in fetch]
+    if fetch:
+        extra.append(pltpu.SemaphoreType.DMA((len(fetch),)))
     return pl.pallas_call(
-        body,
+        whole,
         grid_spec=pltpu.PrefetchScalarGridSpec(
-            num_scalar_prefetch=len(scalars),
+            num_scalar_prefetch=n_scalars,
             grid=(1,),
-            in_specs=[anywhere if i in in_hbm else near for i in range(len(args))],
+            in_specs=[anywhere if i in far else near for i in range(n_args)],
             out_specs=[
-                pl.BlockSpec(memory_space=pltpu.SMEM)
-                if o.memory_space == pltpu.SMEM
-                else anywhere if i in out_hbm else near
-                for i, o in enumerate(outs)
+                pl.BlockSpec(memory_space=pltpu.SMEM) if o.memory_space == pltpu.SMEM else near
+                for o in outs
             ],
-            scratch_shapes=scratch,
+            scratch_shapes=list(scratch) + extra,
         ),
         out_shape=[
-            jax.ShapeDtypeStruct(o.shape, o.dtype)
-            if o.memory_space == pltpu.SMEM or i in out_hbm
-            else o
-            for i, o in enumerate(outs)
+            jax.ShapeDtypeStruct(o.shape, o.dtype) if o.memory_space == pltpu.SMEM else o
+            for o in outs
         ],
         compiler_params=pltpu.CompilerParams(vmem_limit_bytes=SCRATCH_LIMIT),
         name=name,
     )(
         *scalars,
         *[
-            a if i in in_hbm else pltpu.with_memory_space_constraint(a, pltpu.VMEM)
+            pltpu.with_memory_space_constraint(a, pltpu.HBM if i in far else pltpu.VMEM)
             for i, a in enumerate(args)
         ],
     )
@@ -67,64 +90,60 @@
     return list(range(0, groups, 2)) + list(range(1, groups, 2))
 
 
+def place_of(k, groups):
+    return k // 2 + (k % 2) * (groups // 2)
+
+
 SOURCE, BACK, LIVE, COUNT, UNSORT, ATT, FFN = range(7)
 
 
-def make_plan(rank, new_owner, counts, att, ffn, groups, slots):
-    requests, width = att.shape
+def plan_and_pack(rank, new_owner, counts, wkv_state, groups, slots):
+    requests, heads, cells = wkv_state.shape
     per_pair = requests // groups
     rows = requests * slots
-    sent_rows = 2 * requests
 
     def body(
-        rank_ref, owner, cnt, att_ref, ffn_ref, order, arriving, cols, lanes_ref, sent_ref,
-        turn, inverse, att_f, ffn_f, sent_f,
+        rank_ref, owner_far, cnt_far, wkv, arriving, cols, lanes_ref, *rest
     ):
+        packed = rest[:groups]
+        owner, cnt, turn, order, inverse, stage, sems, small = rest[groups:]
         me = rank_ref[0]
-
-        def place_of(k):
-            return k // 2 + (k % 2) * (groups // 2)
-
+        get_owner = pltpu.make_async_copy(owner_far, owner, small.at[0])
+        get_counts = pltpu.make_async_copy(cnt_far, cnt, small.at[1])
+        get_owner.start()
+        get_counts.start()
+        get_owner.wait()
+        get_counts.wait()
         for g in range(groups):
             turn[g] = 0
 
         def own(i, _):
-            spot = place_of((owner[me * requests + i] // requests) ^ me)
+            spot = place_of((owner[me * requests + i] // requests) ^ me, groups)
             order[spot * per_pair + turn[spot]] = i
             turn[spot] = turn[spot] + 1
             return 0
 
-        lax.fori_loop(0, requests, own, 0)
+        lax.fori_loop(0, requests, own, 0, unroll=4)
+        copies = []
+        for q in range(requests):
+            copies.append(pltpu.make_async_copy(wkv.at[order[q]], stage.at[q], sems.at[q]))
+            copies[q].start()
 
         def source(s, _):
-            base = place_of(s ^ me) * per_pair
+            base = place_of(s ^ me, groups) * per_pair
 
             def one(i, found):
                 v = owner[s * requests + i]
                 mine = v // requests == me
-
-                @pl.when(mine)
-                def _():
-                    arriving[base + found] = v % requests
-                    inverse[v % requests] = base + found
-
+                spot = v % requests
+                arriving[jnp.where(mine, base + found, requests)] = spot
+                inverse[jnp.where(mine, spot, requests)] = base + found
                 return found + mine.astype(I32)
 
-            lax.fori_loop(0, requests, one, jnp.int32(0))
+            lax.fori_loop(0, requests, one, jnp.int32(0), unroll=8)
             return 0
 
         lax.fori_loop(0, groups, source, 0)
-
-        att_f[...] = att_ref[...].astype(F32)
-        ffn_f[...] = ffn_ref[...].astype(F32)
-        for d in range(groups):
-            base = place_of(me ^ d) * per_pair
-            for j in range(per_pair):
-                i = order[base + j]
-                to = d * 2 * per_pair + j
-                sent_f[to : to + 1, :] = att_f[pl.ds(i, 1), :]
-                sent_f[to + per_pair : to + per_pair + 1, :] = ffn_f[pl.ds(i, 1), :]
-        sent_ref[...] = sent_f[...].astype(BF16)
 
         row = lax.broadcasted_iota(I32, (requests, 128), 0)
         long_row = lax.broadcasted_iota(I32, (rows, 128), 0)
@@ -133,13 +152,11 @@
         arr = jnp.zeros((requests, 128), I32)
         inv = jnp.zeros((requests, 128), I32)
         num = jnp.zeros((requests, 128), I32)
-        got = jnp.zeros((requests, 128), I32)
         back = jnp.zeros((rows, 128), I32)
         lane_row = lax.broadcasted_iota(I32, (8, 128), 1)
         sub_row = lax.broadcasted_iota(I32, (8, 128), 0)
         lane_counts = jnp.zeros((8, 128), I32)
         half = requests // 2
-        partners = positions(groups)
         for q in range(requests):
             at = row == q
             a = arriving[q]
@@ -147,14 +164,14 @@
             arr = jnp.where(at, a, arr)
             num = jnp.where(at, n, num)
             inv = jnp.where(at, inverse[q], inv)
-            got = jnp.where(
-                at, (me ^ partners[q // per_pair]) * 2 * per_pair + q % per_pair, got
-            )
             back = jnp.where(long_row // slots == q, inverse[q], back)
             lane_counts = jnp.where(
                 (lane_row % half == q % half) & (sub_row == q // half), n, lane_counts
             )
         lanes_ref[...] = lane_counts
+        spot = row // per_pair
+        partner = (spot % (groups // 2)) * 2 + spot // (groups // 2)
+        got = (me ^ partner) * (2 * per_pair) + row % per_pair
         blocks = []
         for t in range(slots):
             block = jnp.where(lane == SOURCE, arr * slots + t, 0)
@@ -166,27 +183,94 @@
             blocks.append(block)
         table = jnp.concatenate(blocks, axis=0)
         cols[...] = jnp.where(long_lane == BACK, back + (long_row % slots) * requests, table)
+        for q in range(requests):
+            copies[q].wait()
+            packed[q // per_pair][q % per_pair] = stage[q].astype(BF16)
 
     return run(
         body,
-        "make_plan",
-        (rank, new_owner, counts),
-        (att, ffn),
+        "plan_and_pack",
+        (rank,),
+        (new_owner, counts, wkv_state),
         [
-            pltpu.SMEM((requests,), I32),
-            pltpu.SMEM((requests,), I32),
+            pltpu.SMEM((requests + 1,), I32),
             vmem((rows, 128), I32),
             vmem((8, 128), I32),
-            vmem((sent_rows, width), BF16),
-        ],
+        ]
+        + [vmem((per_pair, heads, cells), BF16) for _ in range(groups)],
         scratch=[
+            pltpu.SMEM(new_owner.shape, I32),
+            pltpu.SMEM(counts.shape, I32),
             pltpu.SMEM((groups,), I32),
             pltpu.SMEM((requests,), I32),
-            vmem((requests, width), F32),
-            vmem((requests, width), F32),
-            vmem((sent_rows, width), F32),
+            pltpu.SMEM((requests + 1,), I32),
+            vmem(wkv_state.shape, F32),
+            pltpu.SemaphoreType.DMA((requests,)),
+            pltpu.SemaphoreType.DMA((2,)),
         ],
-    )
+        in_hbm=(0, 1, 2),
+    )
+
+
+def pack_shifts(rank, new_owner, att, ffn, groups, parts):
+    requests, width = att.shape
+    per_pair = requests // groups
+
+    def body(rank_ref, owner_far, att_far, ffn_far, sent_ref, owner, turn, order, att_ref, ffn_ref, wide, sent_f, sems):
+        me = rank_ref[0]
+        copies = [
+            pltpu.make_async_copy(
+                owner_far, owner, sems.at[0]
+            ),
+            pltpu.make_async_copy(att_far, att_ref, sems.at[1]),
+            pltpu.make_async_copy(ffn_far, ffn_ref, sems.at[2]),
+        ]
+        for c in copies:
+            c.start()
+        for g in range(groups):
+            turn[g] = 0
+        copies[0].wait()
+
+        def own(i, _):
+            target = owner[me * requests + i] // requests
+            order[target * per_pair + turn[target]] = i
+            turn[target] = turn[target] + 1
+            return 0
+
+        lax.fori_loop(0, requests, own, 0, unroll=4)
+        copies[1].wait()
+        copies[2].wait()
+        wide[0] = att_ref[...].astype(F32)
+        wide[1] = ffn_ref[...].astype(F32)
+        for d in range(groups):
+            for j in range(per_pair):
+                at = pl.ds(order[d * per_pair + j], 1)
+                to = d * 2 * per_pair + j
+                sent_f[to : to + 1, :] = wide[0, at, :]
+                sent_f[to + per_pair : to + per_pair + 1, :] = wide[1, at, :]
+        for d in range(groups):
+            piece = sent_f[d * 2 * per_pair : (d + 1) * 2 * per_pair, :].astype(BF16)
+            for m in range(parts):
+                sent_ref[d, m] = piece
+
+    return run(
+        body,
+        "pack_shifts",
+        (rank,),
+        (new_owner, att, ffn),
+        [vmem((groups, parts, 2 * per_pair, width), BF16)],
+        scratch=[
+            pltpu.SMEM(new_owner.shape, I32),
+            pltpu.SMEM((groups,), I32),
+            pltpu.SMEM((requests,), I32),
+            vmem(att.shape, BF16),
+            vmem(ffn.shape, BF16),
+            vmem((2, requests, width), F32),
+            vmem((2 * requests, width), F32),
+            pltpu.SemaphoreType.DMA((3,)),
+        ],
+        in_hbm=(0, 1, 2),
+    )[0]
 
 
 def chooser(cols, lane, rows, columns):
@@ -196,40 +280,18 @@
 
 
 def sort_shifts(cols, got):
-    sent_rows, width = got.shape
-    requests = sent_rows // 2
+    groups, parts, twice, width = got.shape
+    requests = groups * twice // 2
 
     def body(cols_ref, got_ref, att, ffn):
-        for lane, out in ((ATT, att), (FFN, ffn)):
-            out[...] = dot32(chooser(cols_ref, lane, requests, sent_rows), got_ref[...]).astype(BF16)
-
-    return run(body, "sort_shifts", (), (cols, got), [vmem((requests, width), BF16)] * 2)
-
-
-def pack_states(order, wkv_state, groups):
-    requests, heads, cells = wkv_state.shape
-    per_pair = requests // groups
-
-    def body(order_ref, src, *refs):
-        outs, (stage, sems) = refs[:groups], refs[groups:]
-        copies = [
-            pltpu.make_async_copy(src.at[order_ref[q]], stage.at[q], sems.at[q])
-            for q in range(requests)
-        ]
-        for c in copies:
-            c.start()
-        for q in range(requests):
-            copies[q].wait()
-            outs[q // per_pair][q % per_pair] = stage[q].astype(BF16)
+        picks = [chooser(cols_ref, lane, requests, 2 * requests) for lane in (ATT, FFN)]
+        for m in range(parts):
+            rows = got_ref[:, m].astype(F32).reshape(2 * requests, width).astype(BF16)
+            for pick, out in zip(picks, (att, ffn)):
+                out[m] = dot32(pick, rows).astype(BF16)
 
     return run(
-        body,
-        "pack_states",
-        (order,),
-        (wkv_state,),
-        [vmem((per_pair, heads, cells), BF16) for _ in range(groups)],
-        scratch=[vmem(wkv_state.shape, F32), pltpu.SemaphoreType.DMA((requests,))],
-        in_hbm=(0,),
+        body, "sort_shifts", (), (cols, got), [vmem((parts, requests, width), BF16)] * 2
     )
 
 
@@ -275,16 +337,17 @@
     rows, width = toks[0].shape
     parts = len(toks)
     total = parts * width
-    requests = att.shape[0]
+    requests = att.shape[1]
     slots = rows // requests
     small = down_d.shape[0]
     rank_g = down_g.shape[1]
     low_width = rank_g + 2 * small
 
-    def body(place_ref, *refs):
+    def body(ready, place_ref, *refs):
         tok = refs[:parts]
         att_ref, col, nrm, mx, dd, da, dg, normed, low, low_send, shift = refs[parts:]
         pick = chooser(col, SOURCE, rows, rows)
+        ready()
         xs = [dot32(pick, t[...]) for t in tok]
         mean = sum(jnp.sum(x, axis=1, keepdims=True) for x in xs) / total
         cs = [x - mean for x in xs]
@@ -295,7 +358,7 @@
             normed[k] = cs[k] * scale * nrm[0:1, at] + nrm[1:2, at]
         at = pl.ds(pl.multiple_of(place_ref[0] * width, 128), width)
         now = normed[0]
-        before = jnp.concatenate([att_ref[...].astype(F32), now[: rows - requests]], axis=0)
+        before = jnp.concatenate([att_ref[place_ref[0]].astype(F32), now[: rows - requests]], axis=0)
         delta = before - now
         mixed = lambda c: (now + delta * mx[c : c + 1, at]).astype(BF16)
         nothing = jnp.zeros((small, width), BF16)
@@ -322,34 +385,38 @@
             vmem((rows, low_width), BF16),
             vmem((requests, width), BF16),
         ],
-    )
-
-
-def projections(place, normed, atts, mix, weights):
+        fetch=(*range(1, parts), *range(parts + 2, parts + 7)),
+    )
+
+
+def projections(place, normed, att, mix, weights):
     parts, rows, width = normed.shape
-    requests = atts[0].shape[0]
+    requests = att.shape[1]
     out_width = weights[0].shape[1]
 
-    def body(place_ref, n_ref, *refs):
-        att, mx, w, outs = refs[:parts], refs[parts], refs[parts + 1 : parts + 4], refs[parts + 4 :]
-        sums = [None] * 3
-        for k in range(parts):
-            at = pl.ds(pl.multiple_of((place_ref[0] ^ k) * width, 128), width)
-            now = n_ref[k]
-            before = jnp.concatenate([att[k][...].astype(F32), now[: rows - requests]], axis=0)
-            delta = before - now
-            for which, c in enumerate((0, 2, 3)):
-                term = dot32((now + delta * mx[c : c + 1, at]).astype(BF16), w[which][at, :])
-                sums[which] = term if k == 0 else sums[which] + term
-        for out, value in zip(outs, sums):
-            out[...] = value
+    def body(ready, place_ref, n_ref, *refs):
+        att_ref, mx, w, outs = refs[0], refs[1], refs[2:5], refs[5:]
+        ready(0)
+        for which, c in enumerate((0, 2, 3)):
+            ready(1 + which)
+            for k in range(parts):
+                at = pl.ds(pl.multiple_of((place_ref[0] ^ k) * width, 128), width)
+                now = n_ref[k]
+                before = jnp.concatenate(
+                    [att_ref[place_ref[0] ^ k].astype(F32), now[: rows - requests]], axis=0
+                )
+                mixed = (now + (before - now) * mx[c : c + 1, at]).astype(BF16)
+                term = dot32(mixed, w[which][at, :])
+                total = term if k == 0 else total + term
+            outs[which][...] = total
 
     return run(
         body,
         "projections",
         (place,),
-        (normed, *atts, mix, *weights),
+        (normed, att, mix, *weights),
         [vmem((rows, out_width), F32) for _ in weights],
+        fetch=(2, 3, 4, 5),
     )
 
 
@@ -395,7 +462,7 @@
     n_others = len(low_others)
     pairs = [(t, b) for t in range(slots) for b in range(t + 1)]
 
-    def body(low, *refs):
+    def body(ready, low, *refs):
         others = refs[:n_others]
         (r_ref, k_ref, v_ref, hp, du, au, gu, cnt) = refs[n_others : n_others + 8]
         (w_out, c_out, v_out, kq_out, uq_out, d_out, g_out, b_out, vec) = refs[n_others + 8 :]
@@ -405,6 +472,7 @@
         glow = jax.nn.sigmoid(total[:, 0:rank_g]).astype(BF16)
         pair = total[:, rank_g : rank_g + 2 * small]
         nothing = jnp.zeros((small, width), BF16)
+        ready()
         decay_in = dot32(
             jnp.tanh(pair).astype(BF16), jnp.concatenate([du[...], nothing], axis=0)
         )
@@ -483,6 +551,7 @@
             vmem((rows, width), F32),
         ],
         scratch=[vmem((6, halves, slots, size, lanes), F32)],
+        fetch=tuple(range(n_others + 4, n_others + 8)),
     )
 
 
@@ -496,7 +565,7 @@
     pairs = [(t, b) for t in range(slots) for b in range(t + 1)]
     quad = 4
 
-    def body(place_ref, *refs):
+    def body(ready, place_ref, *refs):
         st = refs[:halves]
         w_ref, c_ref, v_ref, gate_ref, bonus_ref, hp, wo = refs[halves : halves + 7]
         outs = refs[halves + 7 : halves + 7 + parts]
@@ -540,6 +609,7 @@
                 spread = jnp.mean(center * center, axis=0, keepdims=True)
                 by_group[t * halves + g] = center * lax.rsqrt(spread + 0.00064)
         backs = swap_groups(by_group, group)
+        ready()
         each = 128 // size
         for g in range(n_groups):
             at = slice(g * 128, (g + 1) * 128)
@@ -559,6 +629,7 @@
         + [vmem((rows, width), BF16) for _ in range(parts - 1)]
         + [vmem(values.shape, F32)],
         scratch=[vmem(weights.shape, F32), vmem((rows, width), BF16)],
+        fetch=(halves + 5, halves + 6),
     )
 
 
@@ -566,8 +637,8 @@
     halves = len(states)
     size, _, lanes = states[0].shape
     slots = removed.shape[1]
-    requests = arriving.shape[0]
-    half = requests // halves
+    half = lanes // heads
+    requests = half * halves
     step_chunks = 4
     per_chunk = 128 // size
     steps = size // (per_chunk * step_chunks)
@@ -646,27 +717,28 @@
     return run(body, "middle", (), (tok, cols, own, *others), [vmem((rows, width), BF16)])[0]
 
 
-def channel_mix(place, mids, prevs, cols, norm, mix, key_weight, value_weight):
+def channel_mix(place, mids, prev, cols, norm, mix, key_weight, value_weight):
     parts = len(mids)
     rows, width = mids[0].shape
     total = parts * width
-    requests = prevs[0].shape[0]
+    requests = prev.shape[1]
     slots = rows // requests
 
-    def body(place_ref, *refs):
-        mid, prev = refs[:parts], refs[parts : 2 * parts]
-        col, nrm, mx, kw, vw = refs[2 * parts : 2 * parts + 5]
-        outs, shift = refs[2 * parts + 5 : 3 * parts + 5], refs[3 * parts + 5]
+    def body(ready, place_ref, *refs):
+        mid = refs[:parts]
+        prev_ref, col, nrm, mx, kw, vw = refs[parts : parts + 6]
+        outs, shift = refs[parts + 6 : 2 * parts + 6], refs[2 * parts + 6]
         xs = [m[...].astype(F32) for m in mid]
         mean = sum(jnp.sum(x, axis=1, keepdims=True) for x in xs) / total
         cs = [x - mean for x in xs]
         var = sum(jnp.sum(c * c, axis=1, keepdims=True) for c in cs) / total
         scale = lax.rsqrt(var + 1e-05)
+        ready()
         acc = None
         for k in range(parts):
             at = pl.ds(pl.multiple_of((place_ref[0] ^ k) * width, 128), width)
             now = cs[k] * scale * nrm[2:3, at] + nrm[3:4, at]
-            before = jnp.concatenate([prev[k][...].astype(F32), now[: rows - requests]], axis=0)
+            before = jnp.concatenate([prev_ref[place_ref[0] ^ k].astype(F32), now[: rows - requests]], axis=0)
             term = dot32((now + (before - now) * mx[6:7, at]).astype(BF16), kw[at, :])
             acc = term if k == 0 else acc + term
             if k == 0:
@@ -688,10 +760,11 @@
         body,
         "channel_mix",
         (place,),
-        (*mids, *prevs, cols, norm, mix, key_weight, value_weight),
+        (*mids, prev, cols, norm, mix, key_weight, value_weight),
         [vmem((rows, width), F32)]
         + [vmem((rows, width), BF16) for _ in range(parts - 1)]
         + [vmem((requests, width), BF16)],
+        fetch=(parts + 2, parts + 3),
     )
 
 
@@ -745,25 +818,25 @@
     scatter = lambda xs: [xor_permute(xs[k], "mdl", parts, k) for k in range(1, parts)]
 
     toks = gather(tokens.reshape(rows, width))
-    order, arriving, cols, lane_counts, sent = make_plan(
-        rank, new_owner, counts, att_shift, ffn_shift, groups, slots
-    )
-    got = lax.all_to_all(
-        sent.reshape(groups, -1, width), "req", split_axis=0, concat_axis=0, tiled=True
-    )
-    att, ffn = sort_shifts(cols, got.reshape(2 * requests, width))
-    atts = gather(att)
-
-    first = toks[1]
-    order, first = lax.optimization_barrier((order, first))
-    toks = [toks[0], first] + toks[2:]
-    packed = pack_states(order, wkv_state, groups)
+    sent = pack_shifts(rank, new_owner, att_shift, ffn_shift, groups, parts)
+    later, *toks = lax.optimization_barrier((rank, *toks))
+    arriving, cols, lane_counts, *packed = plan_and_pack(
+        later, new_owner, counts, wkv_state, groups, slots
+    )
     payloads = [
         packed[at] if k == 0 else xor_permute(packed[at], "req", groups, k)
         for at, k in enumerate(positions(groups))
     ]
     split = groups // 2
     states = [states_to_lanes(payloads[:split], size), states_to_lanes(payloads[split:], size)]
+    got = lax.all_to_all(
+        sent.reshape(groups * parts, -1, width),
+        ("req", "mdl"),
+        split_axis=0,
+        concat_axis=0,
+        tiled=True,
+    )
+    att, ffn = sort_shifts(cols, got.reshape(groups, parts, -1, width))
 
     normed, low, low_send, new_att = first_norm(
         place,
@@ -777,9 +850,8 @@
         gate_down,
     )
     low_others = gather(low_send)[1:]
-    ffns = gather(ffn)
     recept, key, value = projections(
-        place, normed, atts, mix_coeffs, (recept_weight, key_weight, value_weight)
+        place, normed, att, mix_coeffs, (recept_weight, key_weight, value_weight)
     )
     weights, coefs, vals, keys, units, decay, gate, bonus = head_vectors(
         low,
@@ -801,7 +873,7 @@
     results = channel_mix(
         place,
         gather(mid),
-        ffns,
+        ffn,
         cols,
         norm_params,
         mix_coeffs,

time: 131 us -> 109 us (0.83)
  local copies, waits for them, and re-layouts: 15.9 us -> 3.54 us
  blocking collectives: 7.39 us -> 0 us
  waiting for transfers between devices: 28.6 us -> 32.3 us
  starting transfers between devices: 41.7 us -> 39 us
  Pallas kernels: 35.7 us -> 33.2 us
    unnamed x56 -> x10, local copies, waits for them, and re-layouts: 14.3 us -> 1.9 us
    ppermute x28 -> x22, starting transfers between devices: 41.7 us -> 32.9 us  [xor_permute(): return lax.ppermute(x, axis, [(a, a ^ k) for a in range(size)])]
    all_to_all x1 -> x0, blocking collectives: 7.39 us -> none  [per_device(): lax.all_to_all(sent.reshape(groups, -1, width), 'req', split_axis=0, conc...]
    all_to_all x0 -> x1, starting transfers between devices: none -> 6.07 us  [per_device(): lax.all_to_all(sent.reshape(groups * parts, -1, width), ('req', 'mdl'), s...]
    ppermute x28 -> x22, waiting for transfers between devices: 28.6 us -> 32.2 us  [xor_permute(): return lax.ppermute(x, axis, [(a, a ^ k) for a in range(size)])]
    pallas_call x12, Pallas kernels: 28.8 us -> 26.3 us  [run(): pl.pallas_call(whole, grid_spec=pltpu.PrefetchScalarGridSpec(num_scalar_p...]
  transfers between devices with their start and end apart: 28 -> 23, of which waited for: 8 -> 10; matrix products, arithmetic and copies ran while one was open for 1% -> 1% of each run, Pallas kernels for 22% -> 21%
where the time goes in v3:
time: 109 us
  starting transfers between devices  39 us (36%)
  Pallas kernels  33.2 us (30%)
  waiting for transfers between devices  32.3 us (30%)
  local copies, waits for them, and re-layouts  3.54 us (3%)
    ppermute x22, starting transfers between devices, xor_permute(): return lax.ppermute(x, axis, [(a, a ^ k) for a in range(size)])  32.9 us
    ppermute x22, waiting for transfers between devices, xor_permute(): return lax.ppermute(x, axis, [(a, a ^ k) for a in range(size)])  32.2 us
    pallas_call x12, Pallas kernels, run(): pl.pallas_call(whole, grid_spec=pltpu.PrefetchScalarGridSpec(num_scalar_p...  26.3 us
    pallas_call x1, Pallas kernels, final_states(): pl.pallas_call(body, grid_spec=pltpu.PrefetchScalarGridSpec(num_scalar_pr...  6.96 us
    all_to_all x1, starting transfers between devices, per_device(): lax.all_to_all(sent.reshape(groups * parts, -1, width), ('req', 'mdl'), s...  6.07 us
  transfers between devices with their start and end apart: 23, of which 10 were waited for; matrix products, arithmetic and copies ran while one was open for 1% of the time, Pallas kernels for 21%

profile of v3, /device:TPU:0, one launch (start us, length us, event | category | flops | bytes accessed | tf_op | source)
XLA Modules:
  0.0 108.8 jit_solution(12167231384210906926)
XLA Ops:
  0.6 0.9 reshape.27.refs_1_.refs_0_
  1.6 3.1 %collective-permute-start = (bf16[128,512]{1,0:T(8,128)(2,1)S(1)}, bf16[128,512]{1,0:T(8,128)(2,1)S(1)}, u32[]{:S(2)}, u32[]{:S(2)}) collective-permute-start(bf16[128,512]{1,0:T(8,128)(2,1)S(1)} %reshape.27.refs_1_.refs_0_), channel_id=1, source_target_pairs={{0,1},{1,0},{2,3},{3,2},{4,5},{5,4},{6,7},{7,6},{8,9},{9,8},{10,11... | collective-permute-start | bytes 393224 | tf_op jit(solution)/shard_map/ppermute | solution.py:17
  4.7 2.6 %collective-permute-start.1 = (bf16[128,512]{1,0:T(8,128)(2,1)S(1)}, bf16[128,512]{1,0:T(8,128)(2,1)S(1)}, u32[]{:S(2)}, u32[]{:S(2)}) collective-permute-start(bf16[128,512]{1,0:T(8,128)(2,1)S(1)} %reshape.27.refs_1_.refs_0_), channel_id=1, source_target_pairs={{0,2},{1,3},{2,0},{3,1},{4,6},{5,7},{6,4},{7,5},{8,10},{9,11},{10,... | collective-permute-start | bytes 393224 | tf_op jit(solution)/shard_map/ppermute | solution.py:17
  7.3 0.0 collective-permute-start.2
  7.3 1.8 %pack_shifts.1 = bf16[8,4,8,512]{3,2,1,0:T(8,128)(2,1)} custom-call(s32[1]{0:T(128)} %bitcast.refs_0_, s32[256]{0:T(256)} %refs_1_.3, bf16[32,512]{1,0:T(8,128)(2,1)} %refs_2_.3, bf16[32,512]{1,0:T(8,128)(2,1)} %refs_3_.4), custom_call_target="tpu_custom_call" | custom-call | tf_op jit(solution)/shard_map/pack_shifts/pallas_call | solution.py:62
  9.0 6.1 %all-to-all-start = ((bf16[32,8,512]{2,1,0:T(8,128)(2,1)}), bf16[32,8,512]{2,1,0:T(8,128)(2,1)S(1)}, u32[]{:S(2)}, u32[]{:S(2)}) async-start(bf16[32,8,512]{2,1,0:T(8,128)(2,1)} %bitcast.2), calls=%async_computation | async-start | bytes 524288 | tf_op jit(solution)/shard_map/all_to_all | solution.py:832
  15.1 0.0 collective-permute-done.refs_2_
  15.1 0.0 copy-start.2
  15.2 2.4 %collective-permute-done.1.refs_3_ = bf16[128,512]{1,0:T(8,128)(2,1)S(1)} collective-permute-done((bf16[128,512]{1,0:T(8,128)(2,1)S(1)}, bf16[128,512]{1,0:T(8,128)(2,1)S(1)}, u32[]{:S(2)}, u32[]{:S(2)}) %collective-permute-start.1) | collective-permute-done | bytes 131104 | tf_op jit(solution)/shard_map/ppermute | solution.py:17
  17.6 0.7 copy-done.3
  18.2 0.0 collective-permute-done.2.refs_4_
  18.2 5.3 %plan_and_pack.1 = (s32[33]{0:T(128)S(1)}, s32[128,128]{1,0:T(8,128)S(1)}, s32[8,128]{1,0:T(8,128)S(1)}, bf16[4,8,4096]{2,1,0:T(8,128)(2,1)S(1)}, bf16[4,8,4096]...) custom-call(s32[1]{0:T(128)} %bitcast.refs_0_, ...), custom_call_target="tpu_custom_call" | custom-call | tf_op jit(solution)/shard_map/plan_and_pack/pallas_call | solution.py:62
  23.6 1.6 %collective-permute-start.3 = (bf16[4,8,4096]{2,1,0:T(8,128)(2,1)S(1)}, bf16[4,8,4096]{2,1,0:T(8,128)(2,1)S(1)}, u32[]{:S(2)}, u32[]{:S(2)}) collective-permute-start(bf16[4,8,4096]{2,1,0:T(8,128)(2,1)S(1)} %get-tuple-element.51), channel_id=1, source_target_pairs={{0,8},{4,12},{8,0},{12,4},{16,24},{20,28},{24,16},{28,20},{1,9},{5... | collective-permute-start | bytes 786440 | tf_op jit(solution)/shard_map/ppermute | solution.py:17
  25.1 1.5 %collective-permute-start.4 = (bf16[4,8,4096]{2,1,0:T(8,128)(2,1)S(1)}, bf16[4,8,4096]{2,1,0:T(8,128)(2,1)S(1)}, u32[]{:S(2)}, u32[]{:S(2)}) collective-permute-start(bf16[4,8,4096]{2,1,0:T(8,128)(2,1)S(1)} %get-tuple-element.52), channel_id=1, source_target_pairs={{0,16},{4,20},{8,24},{12,28},{16,0},{20,4},{24,8},{28,12},{1,17},{... | collective-permute-start | bytes 786440 | tf_op jit(solution)/shard_map/ppermute | solution.py:17
  26.7 0.5 collective-permute-start.5
  27.1 0.0 collective-permute-start.6
  27.1 1.6 %collective-permute-start.7 = (bf16[4,8,4096]{2,1,0:T(8,128)(2,1)S(1)}, bf16[4,8,4096]{2,1,0:T(8,128)(2,1)S(1)}, u32[]{:S(2)}, u32[]{:S(2)}) collective-permute-start(bf16[4,8,4096]{2,1,0:T(8,128)(2,1)S(1)} %get-tuple-element.55), channel_id=1, source_target_pairs={{0,12},{4,8},{8,4},{12,0},{16,28},{20,24},{24,20},{28,16},{1,13},{... | collective-permute-start | bytes 786440 | tf_op jit(solution)/shard_map/ppermute | solution.py:17
  28.7 4.1 %collective-permute-done.3.refs_1_ = bf16[4,8,4096]{2,1,0:T(8,128)(2,1)S(1)} collective-permute-done((bf16[4,8,4096]{2,1,0:T(8,128)(2,1)S(1)}, bf16[4,8,4096]{2,1,0:T(8,128)(2,1)S(1)}, u32[]{:S(2)}, u32[]{:S(2)}) %collective-permute-start.3) | collective-permute-done | bytes 262176 | tf_op jit(solution)/shard_map/ppermute | solution.py:17
  32.9 0.0 collective-permute-start.8
  32.9 1.7 %collective-permute-done.4.refs_2_ = bf16[4,8,4096]{2,1,0:T(8,128)(2,1)S(1)} collective-permute-done((bf16[4,8,4096]{2,1,0:T(8,128)(2,1)S(1)}, bf16[4,8,4096]{2,1,0:T(8,128)(2,1)S(1)}, u32[]{:S(2)}, u32[]{:S(2)}) %collective-permute-start.4) | collective-permute-done | bytes 262176 | tf_op jit(solution)/shard_map/ppermute | solution.py:17
  34.6 1.0 collective-permute-start.9
  35.6 0.0 all-to-all-done
  35.6 0.3 sort_shifts.1
  35.8 2.3 %first_norm.1 = (f32[4,128,512]{2,1,0:T(8,128)S(1)}, f32[128,448]{1,0:T(8,128)S(1)}, bf16[128,448]{1,0:T(8,128)(2,1)S(1)}, bf16[32,512]{1,0:T(8,128)(2,1)S(1)}) custom-call(s32[1]{0:T(128)} %bitcast.1.refs_0_, bf16[128,512]{1,0:T(8,128)(2,1)S(1)} %reshape.27.refs_1_.refs_0_, bf16[128,512]{1,0:T(8,128)(2,1)} %copy-done.2, bf16[128,512]{1,0:T(8,128)(2,1)} %copy-done.3, ...), custom_call_target="tpu_custom_call" | custom-call | tf_op jit(solution)/shard_map/first_norm/pallas_call | solution.py:62
  38.2 1.3 %collective-permute-done.5.refs_3_ = bf16[4,8,4096]{2,1,0:T(8,128)(2,1)S(1)} collective-permute-done((bf16[4,8,4096]{2,1,0:T(8,128)(2,1)}, bf16[4,8,4096]{2,1,0:T(8,128)(2,1)S(1)}, u32[]{:S(2)}, u32[]{:S(2)}) %collective-permute-start.5) | collective-permute-done | bytes 262176 | tf_op jit(solution)/shard_map/ppermute | solution.py:17
  39.5 1.9 %collective-permute-start.10 = (bf16[128,448]{1,0:T(8,128)(2,1)S(1)}, bf16[128,448]{1,0:T(8,128)(2,1)S(1)}, u32[]{:S(2)}, u32[]{:S(2)}) collective-permute-start(bf16[128,448]{1,0:T(8,128)(2,1)S(1)} %get-tuple-element.63), channel_id=1, source_target_pairs={{0,1},{1,0},{2,3},{3,2},{4,5},{5,4},{6,7},{7,6},{8,9},{9,8},{10,11... | collective-permute-start | bytes 344072 | tf_op jit(solution)/shard_map/ppermute | solution.py:17
  41.4 0.0 collective-permute-done.6.refs_0_
  41.4 2.0 %collective-permute-start.11 = (bf16[128,448]{1,0:T(8,128)(2,1)S(1)}, bf16[128,448]{1,0:T(8,128)(2,1)S(1)}, u32[]{:S(2)}, u32[]{:S(2)}) collective-permute-start(bf16[128,448]{1,0:T(8,128)(2,1)S(1)} %get-tuple-element.63), channel_id=1, source_target_pairs={{0,2},{1,3},{2,0},{3,1},{4,6},{5,7},{6,4},{7,5},{8,10},{9,11},{10,... | collective-permute-start | bytes 344072 | tf_op jit(solution)/shard_map/ppermute | solution.py:17
  43.4 0.0 collective-permute-done.7.refs_1_
  43.4 2.1 %collective-permute-start.12 = (bf16[128,448]{1,0:T(8,128)(2,1)S(1)}, bf16[128,448]{1,0:T(8,128)(2,1)S(1)}, u32[]{:S(2)}, u32[]{:S(2)}) collective-permute-start(bf16[128,448]{1,0:T(8,128)(2,1)S(1)} %get-tuple-element.63), channel_id=1, source_target_pairs={{0,3},{1,2},{2,1},{3,0},{4,7},{5,6},{6,5},{7,4},{8,11},{9,10},{10,... | collective-permute-start | bytes 344072 | tf_op jit(solution)/shard_map/ppermute | solution.py:17
  45.5 1.3 %states_to_lanes.2.refs_1_.refs_0_ = f32[64,64,128]{2,1,0:T(8,128)S(1)} custom-call(bf16[4,8,4096]{2,1,0:T(8,128)(2,1)S(1)} %get-tuple-element.50.refs_0_, bf16[4,8,4096]{2,1,0:T(8,128)(2,1)S(1)} %collective-permute-done.3.refs_1_, bf16[4,8,4096]{2,1,0:T(8,128)(2,1)S(1)} %collective-permute-done.4.refs_2_, bf16[4,8,4096]{2,1,0:T(8,128)(2,1)S(1)} %collective-permute-done.5.refs_3_), custom_call_target="tpu_custom_call" | custom-call | tf_op jit(solution)/shard_map/states_to_lanes/pallas_call | solution.py:62
  46.8 2.1 %collective-permute-done.8.refs_2_ = bf16[4,8,4096]{2,1,0:T(8,128)(2,1)S(1)} collective-permute-done((bf16[4,8,4096]{2,1,0:T(8,128)(2,1)S(1)}, bf16[4,8,4096]{2,1,0:T(8,128)(2,1)S(1)}, u32[]{:S(2)}, u32[]{:S(2)}) %collective-permute-start.8) | collective-permute-done | bytes 262176 | tf_op jit(solution)/shard_map/ppermute | solution.py:17
  48.9 0.0 collective-permute-done.9.refs_3_
  48.9 1.3 %states_to_lanes.3.refs_2_.refs_1_ = f32[64,64,128]{2,1,0:T(8,128)S(1)} custom-call(bf16[4,8,4096]{2,1,0:T(8,128)(2,1)S(1)} %collective-permute-done.6.refs_0_, bf16[4,8,4096]{2,1,0:T(8,128)(2,1)S(1)} %collective-permute-done.7.refs_1_, bf16[4,8,4096]{2,1,0:T(8,128)(2,1)S(1)} %collective-permute-done.8.refs_2_, ...), custom_call_target="tpu_custom_call" | custom-call | tf_op jit(solution)/shard_map/states_to_lanes/pallas_call | solution.py:62
  50.2 3.4 %projections.1 = (f32[128,512]{1,0:T(8,128)S(1)}, f32[128,512]{1,0:T(8,128)S(1)}, f32[128,512]{1,0:T(8,128)S(1)}) custom-call(s32[1]{0:T(128)} %bitcast.1.refs_0_, f32[4,128,512]{2,1,0:T(8,128)S(1)} %get-tuple-element.64.refs_1_, bf16[4,32,512]{2,1,0:T(8,128)(2,1)S(1)} %get-tuple-element.61.refs_5_.refs_2_, f32[7,2048]{1,0:T(8,128)} %refs_8_.7, ...), custom_call_target="tpu_custom_call" | custom-call | tf_op jit(solution)/shard_map/projections/pallas_call | solution.py:62
  53.7 0.0 collective-permute-done.11.refs_2_
  53.7 0.0 collective-permute-done.12.refs_3_
  53.7 3.6 %head_vectors.1 = (f32[2,8,64,128]{3,2,1,0:T(8,128)S(1)}, f32[2,20,128]{2,1,0:T(8,128)S(1)}, f32[2,4,64,128]{3,2,1,0:T(8,128)S(1)}, f32[2,4,64,128]{3,2,1,0:T(8,...) custom-call(f32[128,448]{1,0:T(8,128)S(1)} %get-tuple-element.62.ref, ...), custom_call_target="tpu_custom_call" | custom-call | tf_op jit(solution)/shard_map/head_vectors/pallas_call | solution.py:62
  57.3 0.0 copy-start
  57.3 0.0 copy-start.1
  57.3 4.0 %head_outputs.1 = (f32[128,512]{1,0:T(8,128)S(1)}, bf16[128,512]{1,0:T(8,128)(2,1)S(1)}, bf16[128,512]{1,0:T(8,128)(2,1)S(1)}, bf16[128,512]{1,0:T(8,128)(2,1)S(1)}, f32[2,4,64,128]{3,2,1,0:T(8,128)S(1)}) custom-call(s32[1]{0:T(128)} %bitcast.1.refs_0_, f32[64,64,128]{2,1,0:T(8,128)S(1)} %states_to_lanes.2.refs_1_.refs_0_, ...), custom_call_target="tpu_custom_call" | custom-call | tf_op jit(solution)/shard_map/head_outputs/pallas_call | solution.py:62
  61.3 2.6 %collective-permute-start.13 = (bf16[128,512]{1,0:T(8,128)(2,1)S(1)}, bf16[128,512]{1,0:T(8,128)(2,1)S(1)}, u32[]{:S(2)}, u32[]{:S(2)}) collective-permute-start(bf16[128,512]{1,0:T(8,128)(2,1)S(1)} %get-tuple-element.75), channel_id=1, source_target_pairs={{0,1},{1,0},{2,3},{3,2},{4,5},{5,4},{6,7},{7,6},{8,9},{9,8},{10,11... | collective-permute-start | bytes 393224 | tf_op jit(solution)/shard_map/ppermute | solution.py:17
  63.9 1.6 %collective-permute-start.14 = (bf16[128,512]{1,0:T(8,128)(2,1)S(1)}, bf16[128,512]{1,0:T(8,128)(2,1)S(1)}, u32[]{:S(2)}, u32[]{:S(2)}) collective-permute-start(bf16[128,512]{1,0:T(8,128)(2,1)S(1)} %get-tuple-element.76), channel_id=1, source_target_pairs={{0,2},{1,3},{2,0},{3,1},{4,6},{5,7},{6,4},{7,5},{8,10},{9,11},{10,... | collective-permute-start | bytes 393224 | tf_op jit(solution)/shard_map/ppermute | solution.py:17
  65.5 1.4 %collective-permute-start.15 = (bf16[128,512]{1,0:T(8,128)(2,1)S(1)}, bf16[128,512]{1,0:T(8,128)(2,1)S(1)}, u32[]{:S(2)}, u32[]{:S(2)}) collective-permute-start(bf16[128,512]{1,0:T(8,128)(2,1)S(1)} %get-tuple-element.77), channel_id=1, source_target_pairs={{0,3},{1,2},{2,1},{3,0},{4,7},{5,6},{6,5},{7,4},{8,11},{9,10},{10,... | collective-permute-start | bytes 393224 | tf_op jit(solution)/shard_map/ppermute | solution.py:17
  66.9 2.2 %collective-permute-done.13.refs_3_ = bf16[128,512]{1,0:T(8,128)(2,1)S(1)} collective-permute-done((bf16[128,512]{1,0:T(8,128)(2,1)S(1)}, bf16[128,512]{1,0:T(8,128)(2,1)S(1)}, u32[]{:S(2)}, u32[]{:S(2)}) %collective-permute-start.13) | collective-permute-done | bytes 131104 | tf_op jit(solution)/shard_map/ppermute | solution.py:17
  69.1 7.5 %collective-permute-done.14.refs_4_ = bf16[128,512]{1,0:T(8,128)(2,1)S(1)} collective-permute-done((bf16[128,512]{1,0:T(8,128)(2,1)S(1)}, bf16[128,512]{1,0:T(8,128)(2,1)S(1)}, u32[]{:S(2)}, u32[]{:S(2)}) %collective-permute-start.14) | collective-permute-done | bytes 131104 | tf_op jit(solution)/shard_map/ppermute | solution.py:17
  76.6 0.0 collective-permute-done.15.refs_5_
  76.6 0.3 middle.1.refs_1_.refs_0_
  76.9 2.2 %collective-permute-start.16 = (bf16[128,512]{1,0:T(8,128)(2,1)S(1)}, bf16[128,512]{1,0:T(8,128)(2,1)S(1)}, u32[]{:S(2)}, u32[]{:S(2)}) collective-permute-start(bf16[128,512]{1,0:T(8,128)(2,1)S(1)} %middle.1.refs_1_.refs_0_), channel_id=1, source_target_pairs={{0,1},{1,0},{2,3},{3,2},{4,5},{5,4},{6,7},{7,6},{8,9},{9,8},{10,11... | collective-permute-start | bytes 393224 | tf_op jit(solution)/shard_map/ppermute | solution.py:17
  79.1 1.4 %collective-permute-start.17 = (bf16[128,512]{1,0:T(8,128)(2,1)S(1)}, bf16[128,512]{1,0:T(8,128)(2,1)S(1)}, u32[]{:S(2)}, u32[]{:S(2)}) collective-permute-start(bf16[128,512]{1,0:T(8,128)(2,1)S(1)} %middle.1.refs_1_.refs_0_), channel_id=1, source_target_pairs={{0,2},{1,3},{2,0},{3,1},{4,6},{5,7},{6,4},{7,5},{8,10},{9,11},{10,... | collective-permute-start | bytes 393224 | tf_op jit(solution)/shard_map/ppermute | solution.py:17
  80.5 1.4 %collective-permute-start.18 = (bf16[128,512]{1,0:T(8,128)(2,1)S(1)}, bf16[128,512]{1,0:T(8,128)(2,1)S(1)}, u32[]{:S(2)}, u32[]{:S(2)}) collective-permute-start(bf16[128,512]{1,0:T(8,128)(2,1)S(1)} %middle.1.refs_1_.refs_0_), channel_id=1, source_target_pairs={{0,3},{1,2},{2,1},{3,0},{4,7},{5,6},{6,5},{7,4},{8,11},{9,10},{10,... | collective-permute-start | bytes 393224 | tf_op jit(solution)/shard_map/ppermute | solution.py:17
  81.9 1.6 %collective-permute-done.16.refs_2_ = bf16[128,512]{1,0:T(8,128)(2,1)S(1)} collective-permute-done((bf16[128,512]{1,0:T(8,128)(2,1)S(1)}, bf16[128,512]{1,0:T(8,128)(2,1)S(1)}, u32[]{:S(2)}, u32[]{:S(2)}) %collective-permute-start.16) | collective-permute-done | bytes 131104 | tf_op jit(solution)/shard_map/ppermute | solution.py:17
  83.5 8.0 %collective-permute-done.17.refs_3_ = bf16[128,512]{1,0:T(8,128)(2,1)S(1)} collective-permute-done((bf16[128,512]{1,0:T(8,128)(2,1)S(1)}, bf16[128,512]{1,0:T(8,128)(2,1)S(1)}, u32[]{:S(2)}, u32[]{:S(2)}) %collective-permute-start.17) | collective-permute-done | bytes 131104 | tf_op jit(solution)/shard_map/ppermute | solution.py:17
  91.5 0.0 collective-permute-done.18.refs_4_
  91.5 2.4 %channel_mix.1 = (f32[128,512]{1,0:T(8,128)S(1)}, bf16[128,512]{1,0:T(8,128)(2,1)S(1)}, bf16[128,512]{1,0:T(8,128)(2,1)S(1)}, bf16[128,512]{1,0:T(8,128)(2,1)S(1)}, bf16[32,512]{1,0:T(8,128)(2,1)S(1)}) custom-call(s32[1]{0:T(128)} %bitcast.1.refs_0_, bf16[128,512]{1,0:T(8,128)(2,1)S(1)} %middle.1.refs_1_.refs_0_, ...), custom_call_target="tpu_custom_call" | custom-call | tf_op jit(solution)/shard_map/channel_mix/pallas_call | solution.py:62
  93.9 2.0 %collective-permute-start.19 = (bf16[128,512]{1,0:T(8,128)(2,1)S(1)}, bf16[128,512]{1,0:T(8,128)(2,1)S(1)}, u32[]{:S(2)}, u32[]{:S(2)}) collective-permute-start(bf16[128,512]{1,0:T(8,128)(2,1)S(1)} %get-tuple-element.80), channel_id=1, source_target_pairs={{0,1},{1,0},{2,3},{3,2},{4,5},{5,4},{6,7},{7,6},{8,9},{9,8},{10,11... | collective-permute-start | bytes 393224 | tf_op jit(solution)/shard_map/ppermute | solution.py:17
  96.0 1.1 collective-permute-start.20
  97.0 1.4 %collective-permute-start.21 = (bf16[128,512]{1,0:T(8,128)(2,1)S(1)}, bf16[128,512]{1,0:T(8,128)(2,1)S(1)}, u32[]{:S(2)}, u32[]{:S(2)}) collective-permute-start(bf16[128,512]{1,0:T(8,128)(2,1)S(1)} %get-tuple-element.82), channel_id=1, source_target_pairs={{0,3},{1,2},{2,1},{3,0},{4,7},{5,6},{6,5},{7,4},{8,11},{9,10},{10,... | collective-permute-start | bytes 393224 | tf_op jit(solution)/shard_map/ppermute | solution.py:17
  98.4 0.6 copy.25
  99.0 7.0 %final_states.1 = f32[32,8,4096]{2,1,0:T(8,128)} custom-call(s32[33]{0:T(128)S(1)} %get-tuple-element.83.arr_ref, f32[64,64,128]{2,1,0:T(8,128)S(1)} %states_to_lanes.2.refs_1_.refs_0_, f32[64,64,128]{2,1,0:T(8,128)S(1)} %states_to_lanes.3.refs_2_.refs_1_, f32[2,4,64,128]{3,2,1,0:T(8,128)S(1)} %get-tuple-element.84.refs_2_, ...), custom_call_target="tpu_custom_call" | custom-call | tf_op jit(solution)/shard_map/final_states/pallas_call | solution.py:689
  106.0 0.6 copy.26
  106.6 1.3 %collective-permute-done.20.refs_3_ = bf16[128,512]{1,0:T(8,128)(2,1)S(1)} collective-permute-done((bf16[128,512]{1,0:T(8,128)(2,1)S(1)}, bf16[128,512]{1,0:T(8,128)(2,1)S(1)}, u32[]{:S(2)}, u32[]{:S(2)}) %collective-permute-start.20) | collective-permute-done | bytes 131104 | tf_op jit(solution)/shard_map/ppermute | solution.py:17
  107.9 0.2 finish.1
  108.1 0.7 reshape.31
  (7 shorter events, 0.0 us)
Async XLA Ops:
  1.6 13.6 %collective-permute-start = (bf16[128,512]{1,0:T(8,128)(2,1)S(1)}, bf16[128,512]{1,0:T(8,128)(2,1)S(1)}, u32[]{:S(2)}, u32[]{:S(2)}) collective-permute-start(bf16[128,512]{1,0:T(8,128)(2,1)S(1)} %reshape.27.refs_1_.refs_0_), channel_id=1, source_target_pairs={{0,1},{1,0},{2,3},{3,2},{4,5},{5,4},{6,7},{7,6},{8,9},{9,8},{10,11... | collective-permute-start | bytes 393224 | tf_op jit(solution)/shard_map/ppermute | solution.py:17
  4.7 12.9 %collective-permute-start.1 = (bf16[128,512]{1,0:T(8,128)(2,1)S(1)}, bf16[128,512]{1,0:T(8,128)(2,1)S(1)}, u32[]{:S(2)}, u32[]{:S(2)}) collective-permute-start(bf16[128,512]{1,0:T(8,128)(2,1)S(1)} %reshape.27.refs_1_.refs_0_), channel_id=1, source_target_pairs={{0,2},{1,3},{2,0},{3,1},{4,6},{5,7},{6,4},{7,5},{8,10},{9,11},{10,... | collective-permute-start | bytes 393224 | tf_op jit(solution)/shard_map/ppermute | solution.py:17
  7.3 11.0 %collective-permute-start.2 = (bf16[128,512]{1,0:T(8,128)(2,1)S(1)}, bf16[128,512]{1,0:T(8,128)(2,1)}, u32[]{:S(2)}, u32[]{:S(2)}) collective-permute-start(bf16[128,512]{1,0:T(8,128)(2,1)S(1)} %reshape.27.refs_1_.refs_0_), channel_id=1, source_target_pairs={{0,3},{1,2},{2,1},{3,0},{4,7},{5,6},{6,5},{7,4},{8,11},{9,10},{10,... | collective-permute-start | bytes 393224 | tf_op jit(solution)/shard_map/ppermute | solution.py:17
  9.0 26.5 %all-to-all-start = ((bf16[32,8,512]{2,1,0:T(8,128)(2,1)}), bf16[32,8,512]{2,1,0:T(8,128)(2,1)S(1)}, u32[]{:S(2)}, u32[]{:S(2)}) async-start(bf16[32,8,512]{2,1,0:T(8,128)(2,1)} %bitcast.2), calls=%async_computation | async-start | bytes 524288 | tf_op jit(solution)/shard_map/all_to_all | solution.py:832
  15.1 8.4 %copy-start.2 = (bf16[128,512]{1,0:T(8,128)(2,1)}, bf16[128,512]{1,0:T(8,128)(2,1)S(1)}, u32[]{:S(2)}) copy-start(bf16[128,512]{1,0:T(8,128)(2,1)S(1)} %collective-permute-done.refs_2_) | copy-start | bytes 393220
  17.6 0.7 copy-start.3
  23.6 9.3 %collective-permute-start.3 = (bf16[4,8,4096]{2,1,0:T(8,128)(2,1)S(1)}, bf16[4,8,4096]{2,1,0:T(8,128)(2,1)S(1)}, u32[]{:S(2)}, u32[]{:S(2)}) collective-permute-start(bf16[4,8,4096]{2,1,0:T(8,128)(2,1)S(1)} %get-tuple-element.51), channel_id=1, source_target_pairs={{0,8},{4,12},{8,0},{12,4},{16,24},{20,28},{24,16},{28,20},{1,9},{5... | collective-permute-start | bytes 786440 | tf_op jit(solution)/shard_map/ppermute | solution.py:17
  25.1 9.4 %collective-permute-start.4 = (bf16[4,8,4096]{2,1,0:T(8,128)(2,1)S(1)}, bf16[4,8,4096]{2,1,0:T(8,128)(2,1)S(1)}, u32[]{:S(2)}, u32[]{:S(2)}) collective-permute-start(bf16[4,8,4096]{2,1,0:T(8,128)(2,1)S(1)} %get-tuple-element.52), channel_id=1, source_target_pairs={{0,16},{4,20},{8,24},{12,28},{16,0},{20,4},{24,8},{28,12},{1,17},{... | collective-permute-start | bytes 786440 | tf_op jit(solution)/shard_map/ppermute | solution.py:17
  26.7 12.8 %collective-permute-start.5 = (bf16[4,8,4096]{2,1,0:T(8,128)(2,1)}, bf16[4,8,4096]{2,1,0:T(8,128)(2,1)S(1)}, u32[]{:S(2)}, u32[]{:S(2)}) collective-permute-start(bf16[4,8,4096]{2,1,0:T(8,128)(2,1)} %get-tuple-element.53), channel_id=1, source_target_pairs={{0,24},{4,28},{8,16},{12,20},{16,8},{20,12},{24,0},{28,4},{1,25},{... | collective-permute-start | bytes 786440 | tf_op jit(solution)/shard_map/ppermute | solution.py:17
  27.1 14.2 %collective-permute-start.6 = (bf16[4,8,4096]{2,1,0:T(8,128)(2,1)}, bf16[4,8,4096]{2,1,0:T(8,128)(2,1)S(1)}, u32[]{:S(2)}, u32[]{:S(2)}) collective-permute-start(bf16[4,8,4096]{2,1,0:T(8,128)(2,1)} %get-tuple-element.54), channel_id=1, source_target_pairs={{0,4},{4,0},{8,12},{12,8},{16,20},{20,16},{24,28},{28,24},{1,5},{5... | collective-permute-start | bytes 786440 | tf_op jit(solution)/shard_map/ppermute | solution.py:17
  27.1 16.3 %collective-permute-start.7 = (bf16[4,8,4096]{2,1,0:T(8,128)(2,1)S(1)}, bf16[4,8,4096]{2,1,0:T(8,128)(2,1)S(1)}, u32[]{:S(2)}, u32[]{:S(2)}) collective-permute-start(bf16[4,8,4096]{2,1,0:T(8,128)(2,1)S(1)} %get-tuple-element.55), channel_id=1, source_target_pairs={{0,12},{4,8},{8,4},{12,0},{16,28},{20,24},{24,20},{28,16},{1,13},{... | collective-permute-start | bytes 786440 | tf_op jit(solution)/shard_map/ppermute | solution.py:17
  32.9 16.0 %collective-permute-start.8 = (bf16[4,8,4096]{2,1,0:T(8,128)(2,1)S(1)}, bf16[4,8,4096]{2,1,0:T(8,128)(2,1)S(1)}, u32[]{:S(2)}, u32[]{:S(2)}) collective-permute-start(bf16[4,8,4096]{2,1,0:T(8,128)(2,1)S(1)} %get-tuple-element.56), channel_id=1, source_target_pairs={{0,20},{4,16},{8,28},{12,24},{16,4},{20,0},{24,12},{28,8},{1,21},{... | collective-permute-start | bytes 786440 | tf_op jit(solution)/shard_map/ppermute | solution.py:17
  34.6 14.3 %collective-permute-start.9 = (bf16[4,8,4096]{2,1,0:T(8,128)(2,1)S(1)}, bf16[4,8,4096]{2,1,0:T(8,128)(2,1)S(1)}, u32[]{:S(2)}, u32[]{:S(2)}) collective-permute-start(bf16[4,8,4096]{2,1,0:T(8,128)(2,1)S(1)} %get-tuple-element.57), channel_id=1, source_target_pairs={{0,28},{4,24},{8,20},{12,16},{16,12},{20,8},{24,4},{28,0},{1,29},{... | collective-permute-start | bytes 786440 | tf_op jit(solution)/shard_map/ppermute | solution.py:17
  39.5 14.2 %collective-permute-start.10 = (bf16[128,448]{1,0:T(8,128)(2,1)S(1)}, bf16[128,448]{1,0:T(8,128)(2,1)S(1)}, u32[]{:S(2)}, u32[]{:S(2)}) collective-permute-start(bf16[128,448]{1,0:T(8,128)(2,1)S(1)} %get-tuple-element.63), channel_id=1, source_target_pairs={{0,1},{1,0},{2,3},{3,2},{4,5},{5,4},{6,7},{7,6},{8,9},{9,8},{10,11... | collective-permute-start | bytes 344072 | tf_op jit(solution)/shard_map/ppermute | solution.py:17
  41.4 12.3 %collective-permute-start.11 = (bf16[128,448]{1,0:T(8,128)(2,1)S(1)}, bf16[128,448]{1,0:T(8,128)(2,1)S(1)}, u32[]{:S(2)}, u32[]{:S(2)}) collective-permute-start(bf16[128,448]{1,0:T(8,128)(2,1)S(1)} %get-tuple-element.63), channel_id=1, source_target_pairs={{0,2},{1,3},{2,0},{3,1},{4,6},{5,7},{6,4},{7,5},{8,10},{9,11},{10,... | collective-permute-start | bytes 344072 | tf_op jit(solution)/shard_map/ppermute | solution.py:17
  43.4 10.3 %collective-permute-start.12 = (bf16[128,448]{1,0:T(8,128)(2,1)S(1)}, bf16[128,448]{1,0:T(8,128)(2,1)S(1)}, u32[]{:S(2)}, u32[]{:S(2)}) collective-permute-start(bf16[128,448]{1,0:T(8,128)(2,1)S(1)} %get-tuple-element.63), channel_id=1, source_target_pairs={{0,3},{1,2},{2,1},{3,0},{4,7},{5,6},{6,5},{7,4},{8,11},{9,10},{10,... | collective-permute-start | bytes 344072 | tf_op jit(solution)/shard_map/ppermute | solution.py:17
  57.3 34.2 %copy-start = (bf16[2048,1024]{1,0:T(8,128)(2,1)S(1)}, bf16[2048,1024]{1,0:T(8,128)(2,1)}, u32[]{:S(2)}) copy-start(bf16[2048,1024]{1,0:T(8,128)(2,1)} %refs_9_.5) | copy-start | bytes 12582916
  57.3 34.2 %copy-start.1 = (bf16[1024,2048]{1,0:T(8,128)(2,1)S(1)}, bf16[1024,2048]{1,0:T(8,128)(2,1)}, u32[]{:S(2)}) copy-start(bf16[1024,2048]{1,0:T(8,128)(2,1)} %refs_10_.3) | copy-start | bytes 12582916
  61.3 7.8 %collective-permute-start.13 = (bf16[128,512]{1,0:T(8,128)(2,1)S(1)}, bf16[128,512]{1,0:T(8,128)(2,1)S(1)}, u32[]{:S(2)}, u32[]{:S(2)}) collective-permute-start(bf16[128,512]{1,0:T(8,128)(2,1)S(1)} %get-tuple-element.75), channel_id=1, source_target_pairs={{0,1},{1,0},{2,3},{3,2},{4,5},{5,4},{6,7},{7,6},{8,9},{9,8},{10,11... | collective-permute-start | bytes 393224 | tf_op jit(solution)/shard_map/ppermute | solution.py:17
  63.9 12.7 %collective-permute-start.14 = (bf16[128,512]{1,0:T(8,128)(2,1)S(1)}, bf16[128,512]{1,0:T(8,128)(2,1)S(1)}, u32[]{:S(2)}, u32[]{:S(2)}) collective-permute-start(bf16[128,512]{1,0:T(8,128)(2,1)S(1)} %get-tuple-element.76), channel_id=1, source_target_pairs={{0,2},{1,3},{2,0},{3,1},{4,6},{5,7},{6,4},{7,5},{8,10},{9,11},{10,... | collective-permute-start | bytes 393224 | tf_op jit(solution)/shard_map/ppermute | solution.py:17
  65.5 11.1 %collective-permute-start.15 = (bf16[128,512]{1,0:T(8,128)(2,1)S(1)}, bf16[128,512]{1,0:T(8,128)(2,1)S(1)}, u32[]{:S(2)}, u32[]{:S(2)}) collective-permute-start(bf16[128,512]{1,0:T(8,128)(2,1)S(1)} %get-tuple-element.77), channel_id=1, source_target_pairs={{0,3},{1,2},{2,1},{3,0},{4,7},{5,6},{6,5},{7,4},{8,11},{9,10},{10,... | collective-permute-start | bytes 393224 | tf_op jit(solution)/shard_map/ppermute | solution.py:17
  76.9 6.6 %collective-permute-start.16 = (bf16[128,512]{1,0:T(8,128)(2,1)S(1)}, bf16[128,512]{1,0:T(8,128)(2,1)S(1)}, u32[]{:S(2)}, u32[]{:S(2)}) collective-permute-start(bf16[128,512]{1,0:T(8,128)(2,1)S(1)} %middle.1.refs_1_.refs_0_), channel_id=1, source_target_pairs={{0,1},{1,0},{2,3},{3,2},{4,5},{5,4},{6,7},{7,6},{8,9},{9,8},{10,11... | collective-permute-start | bytes 393224 | tf_op jit(solution)/shard_map/ppermute | solution.py:17
  79.1 12.4 %collective-permute-start.17 = (bf16[128,512]{1,0:T(8,128)(2,1)S(1)}, bf16[128,512]{1,0:T(8,128)(2,1)S(1)}, u32[]{:S(2)}, u32[]{:S(2)}) collective-permute-start(bf16[128,512]{1,0:T(8,128)(2,1)S(1)} %middle.1.refs_1_.refs_0_), channel_id=1, source_target_pairs={{0,2},{1,3},{2,0},{3,1},{4,6},{5,7},{6,4},{7,5},{8,10},{9,11},{10,... | collective-permute-start | bytes 393224 | tf_op jit(solution)/shard_map/ppermute | solution.py:17
  80.5 11.0 %collective-permute-start.18 = (bf16[128,512]{1,0:T(8,128)(2,1)S(1)}, bf16[128,512]{1,0:T(8,128)(2,1)S(1)}, u32[]{:S(2)}, u32[]{:S(2)}) collective-permute-start(bf16[128,512]{1,0:T(8,128)(2,1)S(1)} %middle.1.refs_1_.refs_0_), channel_id=1, source_target_pairs={{0,3},{1,2},{2,1},{3,0},{4,7},{5,6},{6,5},{7,4},{8,11},{9,10},{10,... | collective-permute-start | bytes 393224 | tf_op jit(solution)/shard_map/ppermute | solution.py:17
  93.9 12.7 %collective-permute-start.19 = (bf16[128,512]{1,0:T(8,128)(2,1)S(1)}, bf16[128,512]{1,0:T(8,128)(2,1)S(1)}, u32[]{:S(2)}, u32[]{:S(2)}) collective-permute-start(bf16[128,512]{1,0:T(8,128)(2,1)S(1)} %get-tuple-element.80), channel_id=1, source_target_pairs={{0,1},{1,0},{2,3},{3,2},{4,5},{5,4},{6,7},{7,6},{8,9},{9,8},{10,11... | collective-permute-start | bytes 393224 | tf_op jit(solution)/shard_map/ppermute | solution.py:17
  96.0 11.9 %collective-permute-start.20 = (bf16[128,512]{1,0:T(8,128)(2,1)S(1)}, bf16[128,512]{1,0:T(8,128)(2,1)S(1)}, u32[]{:S(2)}, u32[]{:S(2)}) collective-permute-start(bf16[128,512]{1,0:T(8,128)(2,1)S(1)} %get-tuple-element.81), channel_id=1, source_target_pairs={{0,2},{1,3},{2,0},{3,1},{4,6},{5,7},{6,4},{7,5},{8,10},{9,11},{10,... | collective-permute-start | bytes 393224 | tf_op jit(solution)/shard_map/ppermute | solution.py:17
  97.0 10.9 %collective-permute-start.21 = (bf16[128,512]{1,0:T(8,128)(2,1)S(1)}, bf16[128,512]{1,0:T(8,128)(2,1)S(1)}, u32[]{:S(2)}, u32[]{:S(2)}) collective-permute-start(bf16[128,512]{1,0:T(8,128)(2,1)S(1)} %get-tuple-element.82), channel_id=1, source_target_pairs={{0,3},{1,2},{2,1},{3,0},{4,7},{5,6},{6,5},{7,4},{8,11},{9,10},{10,... | collective-permute-start | bytes 393224 | tf_op jit(solution)/shard_map/ppermute | solution.py:17

commit v4 on v3

--- a/solution.py
+++ b/solution.py
@@ -29,13 +29,37 @@
     return pltpu.VMEM(shape, dtype)
 
 
-def run(body, name, scalars, args, outs, scratch=(), fetch=(), in_hbm=()):
-    far = set(fetch) | set(in_hbm)
+def run(body, name, scalars, args, outs, scratch=(), fetch=(), in_hbm=(), bring=()):
+    n_own, n_made = len(args), len(outs)
+    args = (*args, *bring)
+    outs = [*outs, *[vmem(b.shape, b.dtype) for b in bring]]
+    far = set(fetch) | set(in_hbm) | set(range(n_own, len(args)))
     anywhere = pl.BlockSpec(memory_space=pltpu.HBM)
     near = pl.BlockSpec(memory_space=pltpu.VMEM)
     n_scalars, n_args, n_outs = len(scalars), len(args), len(outs)
 
     def whole(*refs):
+        if not bring:
+            return inner(*refs)
+        refs = list(refs)
+        sems = refs.pop()
+        first = n_scalars + n_own
+        sources = refs[first : first + len(bring)]
+        del refs[first : first + len(bring)]
+        first += n_made
+        targets = refs[first : first + len(bring)]
+        del refs[first : first + len(bring)]
+        copies = [
+            pltpu.make_async_copy(a, b, sems.at[i])
+            for i, (a, b) in enumerate(zip(sources, targets))
+        ]
+        for c in copies:
+            c.start()
+        inner(*refs)
+        for c in copies:
+            c.wait()
+
+    def inner(*refs):
         refs = list(refs)
         if not fetch:
             return body(*refs)
@@ -59,6 +83,8 @@
     extra = [pltpu.VMEM(args[i].shape, args[i].dtype) for i in fetch]
     if fetch:
         extra.append(pltpu.SemaphoreType.DMA((len(fetch),)))
+    if bring:
+        extra.append(pltpu.SemaphoreType.DMA((len(bring),)))
     return pl.pallas_call(
         whole,
         grid_spec=pltpu.PrefetchScalarGridSpec(
@@ -97,25 +123,28 @@
 SOURCE, BACK, LIVE, COUNT, UNSORT, ATT, FFN = range(7)
 
 
-def plan_and_pack(rank, new_owner, counts, wkv_state, groups, slots):
-    requests, heads, cells = wkv_state.shape
+def make_plan(rank, new_owner, counts, att, ffn, groups, parts, slots):
+    requests, width = att.shape
     per_pair = requests // groups
     rows = requests * slots
 
     def body(
-        rank_ref, owner_far, cnt_far, wkv, arriving, cols, lanes_ref, *rest
+        rank_ref, owner_far, cnt_far, att_far, ffn_far,
+        order, arriving, cols, lanes_ref, sent_ref,
+        owner, cnt, turn, inverse, att_ref, ffn_ref, wide, sent_f, sems,
     ):
-        packed = rest[:groups]
-        owner, cnt, turn, order, inverse, stage, sems, small = rest[groups:]
         me = rank_ref[0]
-        get_owner = pltpu.make_async_copy(owner_far, owner, small.at[0])
-        get_counts = pltpu.make_async_copy(cnt_far, cnt, small.at[1])
-        get_owner.start()
-        get_counts.start()
-        get_owner.wait()
-        get_counts.wait()
+        copies = [
+            pltpu.make_async_copy(owner_far, owner, sems.at[0]),
+            pltpu.make_async_copy(cnt_far, cnt, sems.at[1]),
+            pltpu.make_async_copy(att_far, att_ref, sems.at[2]),
+            pltpu.make_async_copy(ffn_far, ffn_ref, sems.at[3]),
+        ]
+        for c in copies:
+            c.start()
         for g in range(groups):
             turn[g] = 0
+        copies[0].wait()
 
         def own(i, _):
             spot = place_of((owner[me * requests + i] // requests) ^ me, groups)
@@ -124,10 +153,21 @@
             return 0
 
         lax.fori_loop(0, requests, own, 0, unroll=4)
-        copies = []
-        for q in range(requests):
-            copies.append(pltpu.make_async_copy(wkv.at[order[q]], stage.at[q], sems.at[q]))
-            copies[q].start()
+        for c in copies[1:]:
+            c.wait()
+        wide[0] = att_ref[...].astype(F32)
+        wide[1] = ffn_ref[...].astype(F32)
+        for d in range(groups):
+            base = place_of(me ^ d, groups) * per_pair
+            for j in range(per_pair):
+                at = pl.ds(order[base + j], 1)
+                to = d * 2 * per_pair + j
+                sent_f[to : to + 1, :] = wide[0, at, :]
+                sent_f[to + per_pair : to + per_pair + 1, :] = wide[1, at, :]
+        for d in range(groups):
+            piece = sent_f[d * 2 * per_pair : (d + 1) * 2 * per_pair, :].astype(BF16)
+            for m in range(parts):
+                sent_ref[d, m] = piece
 
         def source(s, _):
             base = place_of(s ^ me, groups) * per_pair
@@ -144,7 +184,6 @@
             return 0
 
         lax.fori_loop(0, groups, source, 0)
-
         row = lax.broadcasted_iota(I32, (requests, 128), 0)
         long_row = lax.broadcasted_iota(I32, (rows, 128), 0)
         lane = lax.broadcasted_iota(I32, (requests, 128), 1)
@@ -183,94 +222,58 @@
             blocks.append(block)
         table = jnp.concatenate(blocks, axis=0)
         cols[...] = jnp.where(long_lane == BACK, back + (long_row % slots) * requests, table)
-        for q in range(requests):
-            copies[q].wait()
-            packed[q // per_pair][q % per_pair] = stage[q].astype(BF16)
 
     return run(
         body,
-        "plan_and_pack",
+        "make_plan",
         (rank,),
-        (new_owner, counts, wkv_state),
+        (new_owner, counts, att, ffn),
         [
+            pltpu.SMEM((requests,), I32),
             pltpu.SMEM((requests + 1,), I32),
             vmem((rows, 128), I32),
             vmem((8, 128), I32),
-        ]
-        + [vmem((per_pair, heads, cells), BF16) for _ in range(groups)],
+            vmem((groups, parts, 2 * per_pair, width), BF16),
+        ],
         scratch=[
             pltpu.SMEM(new_owner.shape, I32),
             pltpu.SMEM(counts.shape, I32),
             pltpu.SMEM((groups,), I32),
-            pltpu.SMEM((requests,), I32),
             pltpu.SMEM((requests + 1,), I32),
-            vmem(wkv_state.shape, F32),
-            pltpu.SemaphoreType.DMA((requests,)),
-            pltpu.SemaphoreType.DMA((2,)),
-        ],
-        in_hbm=(0, 1, 2),
-    )
-
-
-def pack_shifts(rank, new_owner, att, ffn, groups, parts):
-    requests, width = att.shape
-    per_pair = requests // groups
-
-    def body(rank_ref, owner_far, att_far, ffn_far, sent_ref, owner, turn, order, att_ref, ffn_ref, wide, sent_f, sems):
-        me = rank_ref[0]
-        copies = [
-            pltpu.make_async_copy(
-                owner_far, owner, sems.at[0]
-            ),
-            pltpu.make_async_copy(att_far, att_ref, sems.at[1]),
-            pltpu.make_async_copy(ffn_far, ffn_ref, sems.at[2]),
-        ]
-        for c in copies:
-            c.start()
-        for g in range(groups):
-            turn[g] = 0
-        copies[0].wait()
-
-        def own(i, _):
-            target = owner[me * requests + i] // requests
-            order[target * per_pair + turn[target]] = i
-            turn[target] = turn[target] + 1
-            return 0
-
-        lax.fori_loop(0, requests, own, 0, unroll=4)
-        copies[1].wait()
-        copies[2].wait()
-        wide[0] = att_ref[...].astype(F32)
-        wide[1] = ffn_ref[...].astype(F32)
-        for d in range(groups):
-            for j in range(per_pair):
-                at = pl.ds(order[d * per_pair + j], 1)
-                to = d * 2 * per_pair + j
-                sent_f[to : to + 1, :] = wide[0, at, :]
-                sent_f[to + per_pair : to + per_pair + 1, :] = wide[1, at, :]
-        for d in range(groups):
-            piece = sent_f[d * 2 * per_pair : (d + 1) * 2 * per_pair, :].astype(BF16)
-            for m in range(parts):
-                sent_ref[d, m] = piece
-
-    return run(
-        body,
-        "pack_shifts",
-        (rank,),
-        (new_owner, att, ffn),
-        [vmem((groups, parts, 2 * per_pair, width), BF16)],
-        scratch=[
-            pltpu.SMEM(new_owner.shape, I32),
-            pltpu.SMEM((groups,), I32),
-            pltpu.SMEM((requests,), I32),
             vmem(att.shape, BF16),
             vmem(ffn.shape, BF16),
             vmem((2, requests, width), F32),
             vmem((2 * requests, width), F32),
-            pltpu.SemaphoreType.DMA((3,)),
+            pltpu.SemaphoreType.DMA((4,)),
         ],
-        in_hbm=(0, 1, 2),
-    )[0]
+        in_hbm=(0, 1, 2, 3),
+    )
+
+
+def pack_states(order, wkv_state, groups):
+    requests, heads, cells = wkv_state.shape
+    per_pair = requests // groups
+
+    def body(order_ref, wkv, *rest):
+        packed = rest[:groups]
+        stage, sems = rest[groups:]
+        copies = []
+        for q in range(requests):
+            copies.append(pltpu.make_async_copy(wkv.at[order_ref[q]], stage.at[q], sems.at[q]))
+            copies[q].start()
+        for q in range(requests):
+            copies[q].wait()
+            packed[q // per_pair][q % per_pair] = stage[q].astype(BF16)
+
+    return run(
+        body,
+        "pack_states",
+        (order,),
+        (wkv_state,),
+        [vmem((per_pair, heads, cells), BF16) for _ in range(groups)],
+        scratch=[vmem(wkv_state.shape, F32), pltpu.SemaphoreType.DMA((requests,))],
+        in_hbm=(0,),
+    )
 
 
 def chooser(cols, lane, rows, columns):
@@ -283,7 +286,8 @@
     groups, parts, twice, width = got.shape
     requests = groups * twice // 2
 
-    def body(cols_ref, got_ref, att, ffn):
+    def body(ready, cols_ref, got_ref, att, ffn):
+        ready()
         picks = [chooser(cols_ref, lane, requests, 2 * requests) for lane in (ATT, FFN)]
         for m in range(parts):
             rows = got_ref[:, m].astype(F32).reshape(2 * requests, width).astype(BF16)
@@ -291,11 +295,16 @@
                 out[m] = dot32(pick, rows).astype(BF16)
 
     return run(
-        body, "sort_shifts", (), (cols, got), [vmem((parts, requests, width), BF16)] * 2
-    )
-
-
-def states_to_lanes(payloads, size):
+        body,
+        "sort_shifts",
+        (),
+        (cols, got),
+        [vmem((parts, requests, width), BF16)] * 2,
+        fetch=(0, 1),
+    )
+
+
+def states_to_lanes(payloads, size, bring):
     per_pair, heads, cells = payloads[0].shape
     requests = per_pair * len(payloads)
     lanes = heads * requests
@@ -330,7 +339,8 @@
         payloads,
         [vmem((cells // size, size, lanes), F32)],
         scratch=[vmem((together, requests * heads, 128), F32)],
-    )[0]
+        bring=bring,
+    )
 
 
 def first_norm(place, toks, att, cols, norm, mix, down_d, down_a, down_g):
@@ -346,8 +356,8 @@
     def body(ready, place_ref, *refs):
         tok = refs[:parts]
         att_ref, col, nrm, mx, dd, da, dg, normed, low, low_send, shift = refs[parts:]
+        ready()
         pick = chooser(col, SOURCE, rows, rows)
-        ready()
         xs = [dot32(pick, t[...]) for t in tok]
         mean = sum(jnp.sum(x, axis=1, keepdims=True) for x in xs) / total
         cs = [x - mean for x in xs]
@@ -385,7 +395,7 @@
             vmem((rows, low_width), BF16),
             vmem((requests, width), BF16),
         ],
-        fetch=(*range(1, parts), *range(parts + 2, parts + 7)),
+        fetch=(*range(1, parts), *range(parts + 1, parts + 7)),
     )
 
 
@@ -394,11 +404,9 @@
     requests = att.shape[1]
     out_width = weights[0].shape[1]
 
-    def body(ready, place_ref, n_ref, *refs):
+    def body(place_ref, n_ref, *refs):
         att_ref, mx, w, outs = refs[0], refs[1], refs[2:5], refs[5:]
-        ready(0)
         for which, c in enumerate((0, 2, 3)):
-            ready(1 + which)
             for k in range(parts):
                 at = pl.ds(pl.multiple_of((place_ref[0] ^ k) * width, 128), width)
                 now = n_ref[k]
@@ -416,7 +424,6 @@
         (place,),
         (normed, att, mix, *weights),
         [vmem((rows, out_width), F32) for _ in weights],
-        fetch=(2, 3, 4, 5),
     )
 
 
@@ -462,7 +469,7 @@
     n_others = len(low_others)
     pairs = [(t, b) for t in range(slots) for b in range(t + 1)]
 
-    def body(ready, low, *refs):
+    def body(low, *refs):
         others = refs[:n_others]
         (r_ref, k_ref, v_ref, hp, du, au, gu, cnt) = refs[n_others : n_others + 8]
         (w_out, c_out, v_out, kq_out, uq_out, d_out, g_out, b_out, vec) = refs[n_others + 8 :]
@@ -472,7 +479,6 @@
         glow = jax.nn.sigmoid(total[:, 0:rank_g]).astype(BF16)
         pair = total[:, rank_g : rank_g + 2 * small]
         nothing = jnp.zeros((small, width), BF16)
-        ready()
         decay_in = dot32(
             jnp.tanh(pair).astype(BF16), jnp.concatenate([du[...], nothing], axis=0)
         )
@@ -551,7 +557,6 @@
             vmem((rows, width), F32),
         ],
         scratch=[vmem((6, halves, slots, size, lanes), F32)],
-        fetch=tuple(range(n_others + 4, n_others + 8)),
     )
 
 
@@ -565,7 +570,7 @@
     pairs = [(t, b) for t in range(slots) for b in range(t + 1)]
     quad = 4
 
-    def body(ready, place_ref, *refs):
+    def body(place_ref, *refs):
         st = refs[:halves]
         w_ref, c_ref, v_ref, gate_ref, bonus_ref, hp, wo = refs[halves : halves + 7]
         outs = refs[halves + 7 : halves + 7 + parts]
@@ -609,7 +614,6 @@
                 spread = jnp.mean(center * center, axis=0, keepdims=True)
                 by_group[t * halves + g] = center * lax.rsqrt(spread + 0.00064)
         backs = swap_groups(by_group, group)
-        ready()
         each = 128 // size
         for g in range(n_groups):
             at = slice(g * 128, (g + 1) * 128)
@@ -629,7 +633,6 @@
         + [vmem((rows, width), BF16) for _ in range(parts - 1)]
         + [vmem(values.shape, F32)],
         scratch=[vmem(weights.shape, F32), vmem((rows, width), BF16)],
-        fetch=(halves + 5, halves + 6),
     )
 
 
@@ -818,17 +821,11 @@
     scatter = lambda xs: [xor_permute(xs[k], "mdl", parts, k) for k in range(1, parts)]
 
     toks = gather(tokens.reshape(rows, width))
-    sent = pack_shifts(rank, new_owner, att_shift, ffn_shift, groups, parts)
-    later, *toks = lax.optimization_barrier((rank, *toks))
-    arriving, cols, lane_counts, *packed = plan_and_pack(
-        later, new_owner, counts, wkv_state, groups, slots
-    )
-    payloads = [
-        packed[at] if k == 0 else xor_permute(packed[at], "req", groups, k)
-        for at, k in enumerate(positions(groups))
-    ]
-    split = groups // 2
-    states = [states_to_lanes(payloads[:split], size), states_to_lanes(payloads[split:], size)]
+    order, arriving, cols, lane_counts, sent = make_plan(
+        rank, new_owner, counts, att_shift, ffn_shift, groups, parts, slots
+    )
+    order, toks[1], toks[2] = lax.optimization_barrier((order, toks[1], toks[2]))
+    packed = pack_states(order, wkv_state, groups)
     got = lax.all_to_all(
         sent.reshape(groups * parts, -1, width),
         ("req", "mdl"),
@@ -849,9 +846,24 @@
         alpha_down.T,
         gate_down,
     )
+    partners = positions(groups)
+    issue = [1] + [k for k in partners if k > 1]
+    moved = {k: xor_permute(packed[partners.index(k)], "req", groups, k) for k in issue}
+    moved[0] = packed[0]
+    payloads = [moved[k] for k in partners]
+    split = groups // 2
+    first_half, recept_near, key_near, mix_near = states_to_lanes(
+        payloads[:split], size, (recept_weight, key_weight, mix_coeffs)
+    )
+    second_half, value_near, out_near, head_near, *ups = states_to_lanes(
+        payloads[split:],
+        size,
+        (value_weight, output_weight, head_params, decay_up, alpha_up, gate_up),
+    )
+    states = [first_half, second_half]
     low_others = gather(low_send)[1:]
     recept, key, value = projections(
-        place, normed, att, mix_coeffs, (recept_weight, key_weight, value_weight)
+        place, normed, att, mix_near, (recept_near, key_near, value_near)
     )
     weights, coefs, vals, keys, units, decay, gate, bonus = head_vectors(
         low,
@@ -859,13 +871,13 @@
         recept,
         key,
         value,
-        head_params,
-        (decay_up, alpha_up, gate_up),
+        head_near,
+        ups,
         lane_counts,
         size,
     )
     results = head_outputs(
-        place, states, weights, coefs, vals, gate, bonus, head_params, output_weight, parts
+        place, states, weights, coefs, vals, gate, bonus, head_near, out_near, parts
     )
     outs, removed = results[:parts], results[parts]
     mid = middle(toks[0], cols, outs[0], scatter(outs))

time: 109 us -> 108 us (level)
  waiting for transfers between devices: 32.3 us -> 25.9 us
  starting transfers between devices: 39 us -> 43.6 us
    ppermute x22, starting transfers between devices: 32.9 us -> 40.3 us  [xor_permute(): return lax.ppermute(x, axis, [(a, a ^ k) for a in range(size)])]
    ppermute x22, waiting for transfers between devices: 32.2 us -> 25.9 us  [xor_permute(): return lax.ppermute(x, axis, [(a, a ^ k) for a in range(size)])]
    all_to_all x1, starting transfers between devices: 6.07 us -> 3.31 us  [per_device(): lax.all_to_all(sent.reshape(groups * parts, -1, width), ('req', 'mdl'), s...]
    unnamed x10 -> x16, local copies, waits for them, and re-layouts: 1.9 us -> 2.52 us
  transfers between devices with their start and end apart: 23 -> 23, of which waited for: 10 -> 8; matrix products, arithmetic and copies ran while one was open for 1% -> 1% of each run, Pallas kernels for 21% -> 22%
where the time goes in v4:
time: 108 us
  starting transfers between devices  43.6 us (40%)
  Pallas kernels  33.3 us (31%)
  waiting for transfers between devices  25.9 us (24%)
  local copies, waits for them, and re-layouts  4.16 us (4%)
    ppermute x22, starting transfers between devices, xor_permute(): return lax.ppermute(x, axis, [(a, a ^ k) for a in range(size)])  40.3 us
    pallas_call x12, Pallas kernels, run(): pl.pallas_call(whole, grid_spec=pltpu.PrefetchScalarGridSpec(num_scalar_p...  26.4 us
    ppermute x22, waiting for transfers between devices, xor_permute(): return lax.ppermute(x, axis, [(a, a ^ k) for a in range(size)])  25.9 us
    pallas_call x1, Pallas kernels, final_states(): pl.pallas_call(body, grid_spec=pltpu.PrefetchScalarGridSpec(num_scalar_pr...  6.94 us
    all_to_all x1, starting transfers between devices, per_device(): lax.all_to_all(sent.reshape(groups * parts, -1, width), ('req', 'mdl'), s...  3.31 us
    unnamed x16, local copies, waits for them, and re-layouts  2.52 us
  transfers between devices with their start and end apart: 23, of which 8 were waited for; matrix products, arithmetic and copies ran while one was open for 1% of the time, Pallas kernels for 22%

profile of v4, /device:TPU:0, one launch (start us, length us, event | category | flops | bytes accessed | tf_op | source)
XLA Modules:
  0.0 107.8 jit_solution(12807963248777675641)
XLA Ops:
  0.6 0.9 reshape.26.refs_1_.refs_0_
  1.6 3.1 %collective-permute-start = (bf16[128,512]{1,0:T(8,128)(2,1)S(1)}, bf16[128,512]{1,0:T(8,128)(2,1)S(1)}, u32[]{:S(2)}, u32[]{:S(2)}) collective-permute-start(bf16[128,512]{1,0:T(8,128)(2,1)S(1)} %reshape.26.refs_1_.refs_0_), channel_id=1, source_target_pairs={{0,1},{1,0},{2,3},{3,2},{4,5},{5,4},{6,7},{7,6},{8,9},{9,8},{10,11... | collective-permute-start | bytes 393224 | tf_op jit(solution)/shard_map/ppermute | solution.py:17
  4.7 2.6 %collective-permute-start.1 = (bf16[128,512]{1,0:T(8,128)(2,1)S(1)}, bf16[128,512]{1,0:T(8,128)(2,1)S(1)}, u32[]{:S(2)}, u32[]{:S(2)}) collective-permute-start(bf16[128,512]{1,0:T(8,128)(2,1)S(1)} %reshape.26.refs_1_.refs_0_), channel_id=1, source_target_pairs={{0,2},{1,3},{2,0},{3,1},{4,6},{5,7},{6,4},{7,5},{8,10},{9,11},{10,... | collective-permute-start | bytes 393224 | tf_op jit(solution)/shard_map/ppermute | solution.py:17
  7.3 4.7 %make_plan.1 = (s32[32]{0:T(128)S(1)}, s32[33]{0:T(128)S(1)}, s32[128,128]{1,0:T(8,128)S(1)}, s32[8,128]{1,0:T(8,128)S(1)}, bf16[8,4,8,512]{3,2,1,0:T(8,128)(2,1)}) custom-call(s32[1]{0:T(128)} %bitcast.refs_0_, s32[256]{0:T(256)} %refs_1_.2, s32[32]{0:T(128)} %refs_2_.1, bf16[32,512]{1,0:T(8,128)(2,1)} %refs_3_.1, bf16[32,512]{1,0:T(8,128)(2,1)} %refs_4_.3), custom_call_target="tpu_custom_call" | custom-call | tf_op jit(solution)/shard_map/make_plan/pallas_call | solution.py:88
  11.9 0.6 copy-done.2
  12.6 3.3 %all-to-all-start = ((bf16[32,8,512]{2,1,0:T(8,128)(2,1)}), bf16[32,8,512]{2,1,0:T(8,128)(2,1)}, u32[]{:S(2)}, u32[]{:S(2)}) async-start(bf16[32,8,512]{2,1,0:T(8,128)(2,1)} %bitcast.2), calls=%async_computation | async-start | bytes 524288 | tf_op jit(solution)/shard_map/all_to_all | solution.py:829
  15.9 0.0 collective-permute-done.refs_2_
  15.9 0.0 copy-start.4
  15.9 0.0 collective-permute-done.1.refs_3_
  15.9 3.1 %pack_states.1 = (bf16[4,8,4096]{2,1,0:T(8,128)(2,1)S(1)}, bf16[4,8,4096]{2,1,0:T(8,128)(2,1)S(1)}, bf16[4,8,4096]{2,1,0:T(8,128)(2,1)S(1)}, bf16[4,8,4096]{2,1,...) custom-call(s32[32]{0:T(128)S(1)} %get-tuple-element.60.refs_0_, ...), custom_call_target="tpu_custom_call" | custom-call | tf_op jit(solution)/shard_map/pack_states/pallas_call | solution.py:88
  19.0 0.1 collective-permute-start.5
  19.1 1.6 %collective-permute-start.6 = (bf16[4,8,4096]{2,1,0:T(8,128)(2,1)S(1)}, bf16[4,8,4096]{2,1,0:T(8,128)(2,1)S(1)}, u32[]{:S(2)}, u32[]{:S(2)}) collective-permute-start(bf16[4,8,4096]{2,1,0:T(8,128)(2,1)S(1)} %get-tuple-element.67), channel_id=1, source_target_pairs={{0,12},{4,8},{8,4},{12,0},{16,28},{20,24},{24,20},{28,16},{1,13},{... | collective-permute-start | bytes 786440 | tf_op jit(solution)/shard_map/ppermute | solution.py:17
  20.7 3.5 %collective-permute-start.9 = (bf16[128,512]{1,0:T(8,128)(2,1)S(1)}, bf16[128,512]{1,0:T(8,128)(2,1)S(1)}, u32[]{:S(2)}, u32[]{:S(2)}) collective-permute-start(bf16[128,512]{1,0:T(8,128)(2,1)S(1)} %reshape.26.refs_1_.refs_0_), channel_id=1, source_target_pairs={{0,3},{1,2},{2,1},{3,0},{4,7},{5,6},{6,5},{7,4},{8,11},{9,10},{10,... | collective-permute-start | bytes 393224 | tf_op jit(solution)/shard_map/ppermute | solution.py:17
  24.2 0.5 collective-permute-start.2
  24.8 1.5 %collective-permute-start.3 = (bf16[4,8,4096]{2,1,0:T(8,128)(2,1)S(1)}, bf16[4,8,4096]{2,1,0:T(8,128)(2,1)S(1)}, u32[]{:S(2)}, u32[]{:S(2)}) collective-permute-start(bf16[4,8,4096]{2,1,0:T(8,128)(2,1)S(1)} %get-tuple-element.63), channel_id=1, source_target_pairs={{0,16},{4,20},{8,24},{12,28},{16,0},{20,4},{24,8},{28,12},{1,17},{... | collective-permute-start | bytes 786440 | tf_op jit(solution)/shard_map/ppermute | solution.py:17
  26.3 2.0 %collective-permute-done.9.refs_4_ = bf16[128,512]{1,0:T(8,128)(2,1)S(1)} collective-permute-done((bf16[128,512]{1,0:T(8,128)(2,1)S(1)}, bf16[128,512]{1,0:T(8,128)(2,1)S(1)}, u32[]{:S(2)}, u32[]{:S(2)}) %collective-permute-start.9) | collective-permute-done | bytes 131104 | tf_op jit(solution)/shard_map/ppermute | solution.py:17
  28.2 0.6 copy-done.6
  28.9 1.7 %collective-permute-start.4 = (bf16[4,8,4096]{2,1,0:T(8,128)(2,1)S(1)}, bf16[4,8,4096]{2,1,0:T(8,128)(2,1)S(1)}, u32[]{:S(2)}, u32[]{:S(2)}) collective-permute-start(bf16[4,8,4096]{2,1,0:T(8,128)(2,1)S(1)} %get-tuple-element.64), channel_id=1, source_target_pairs={{0,24},{4,28},{8,16},{12,20},{16,8},{20,12},{24,0},{28,4},{1,25},{... | collective-permute-start | bytes 786440 | tf_op jit(solution)/shard_map/ppermute | solution.py:17
  30.5 0.0 collective-permute-done.5.refs_0_
  30.5 0.0 collective-permute-start.7
  30.6 0.0 collective-permute-done.6.refs_1_
  30.6 2.5 %collective-permute-start.8 = (bf16[4,8,4096]{2,1,0:T(8,128)(2,1)S(1)}, bf16[4,8,4096]{2,1,0:T(8,128)(2,1)S(1)}, u32[]{:S(2)}, u32[]{:S(2)}) collective-permute-start(bf16[4,8,4096]{2,1,0:T(8,128)(2,1)S(1)} %get-tuple-element.69), channel_id=1, source_target_pairs={{0,28},{4,24},{8,20},{12,16},{16,12},{20,8},{24,4},{28,0},{1,29},{... | collective-permute-start | bytes 786440 | tf_op jit(solution)/shard_map/ppermute | solution.py:17
  33.0 0.0 all-to-all-done
  33.0 1.3 %sort_shifts.1 = (bf16[4,32,512]{2,1,0:T(8,128)(2,1)S(1)}, bf16[4,32,512]{2,1,0:T(8,128)(2,1)S(1)}) custom-call(s32[128,128]{1,0:T(8,128)} %copy-done.2, bf16[8,4,8,512]{3,2,1,0:T(8,128)(2,1)} %bitcast.3.refs_1_), custom_call_target="tpu_custom_call" | custom-call | tf_op jit(solution)/shard_map/sort_shifts/pallas_call | solution.py:88
  34.3 2.4 %first_norm.1 = (f32[4,128,512]{2,1,0:T(8,128)S(1)}, f32[128,448]{1,0:T(8,128)S(1)}, bf16[128,448]{1,0:T(8,128)(2,1)S(1)}, bf16[32,512]{1,0:T(8,128)(2,1)S(1)}) custom-call(s32[1]{0:T(128)} %bitcast.1.refs_0_, bf16[128,512]{1,0:T(8,128)(2,1)S(1)} %reshape.26.refs_1_.refs_0_, bf16[128,512]{1,0:T(8,128)(2,1)} %copy-done.4, bf16[128,512]{1,0:T(8,128)(2,1)} %copy-done.5, ...), custom_call_target="tpu_custom_call" | custom-call | tf_op jit(solution)/shard_map/first_norm/pallas_call | solution.py:88
  36.7 0.0 collective-permute-done.2.refs_1_
  36.7 3.1 %collective-permute-start.10 = (bf16[128,448]{1,0:T(8,128)(2,1)S(1)}, bf16[128,448]{1,0:T(8,128)(2,1)S(1)}, u32[]{:S(2)}, u32[]{:S(2)}) collective-permute-start(bf16[128,448]{1,0:T(8,128)(2,1)S(1)} %get-tuple-element.76), channel_id=1, source_target_pairs={{0,1},{1,0},{2,3},{3,2},{4,5},{5,4},{6,7},{7,6},{8,9},{9,8},{10,11... | collective-permute-start | bytes 344072 | tf_op jit(solution)/shard_map/ppermute | solution.py:17
  39.9 0.0 collective-permute-done.3.refs_2_
  39.9 1.0 collective-permute-start.11
  40.8 0.7 collective-permute-done.4.refs_3_
  41.5 2.9 %collective-permute-start.12 = (bf16[128,448]{1,0:T(8,128)(2,1)S(1)}, bf16[128,448]{1,0:T(8,128)(2,1)S(1)}, u32[]{:S(2)}, u32[]{:S(2)}) collective-permute-start(bf16[128,448]{1,0:T(8,128)(2,1)S(1)} %get-tuple-element.76), channel_id=1, source_target_pairs={{0,3},{1,2},{2,1},{3,0},{4,7},{5,6},{6,5},{7,4},{8,11},{9,10},{10,... | collective-permute-start | bytes 344072 | tf_op jit(solution)/shard_map/ppermute | solution.py:17
  44.4 2.2 %states_to_lanes.2 = (f32[64,64,128]{2,1,0:T(8,128)S(1)}, bf16[2048,512]{1,0:T(8,128)(2,1)S(1)}, bf16[2048,512]{1,0:T(8,128)(2,1)S(1)}, f32[7,2048]{1,0:T(8,128)S(1)}) custom-call(bf16[4,8,4096]{2,1,0:T(8,128)(2,1)S(1)} %get-tuple-element.61.refs_0_, bf16[4,8,4096]{2,1,0:T(8,128)(2,1)S(1)} %collective-permute-done.2.refs_1_, ...), custom_call_target="tpu_custom_call" | custom-call | tf_op jit(solution)/shard_map/states_to_lanes/pallas_call | solution.py:88
  46.7 3.2 %collective-permute-done.7.refs_2_ = bf16[4,8,4096]{2,1,0:T(8,128)(2,1)S(1)} collective-permute-done((bf16[4,8,4096]{2,1,0:T(8,128)(2,1)S(1)}, bf16[4,8,4096]{2,1,0:T(8,128)(2,1)S(1)}, u32[]{:S(2)}, u32[]{:S(2)}) %collective-permute-start.7) | collective-permute-done | bytes 262176 | tf_op jit(solution)/shard_map/ppermute | solution.py:17
  49.9 0.0 collective-permute-done.8.refs_3_
  49.9 2.3 %states_to_lanes.3 = (f32[64,64,128]{2,1,0:T(8,128)S(1)}, bf16[2048,512]{1,0:T(8,128)(2,1)S(1)}, bf16[512,2048]{1,0:T(8,128)(2,1)S(1)}, f32[7,512]{1,0:T(8,128)S...) custom-call(bf16[4,8,4096]{2,1,0:T(8,128)(2,1)S(1)} %collective-permute-done.5.refs_0_, ...), custom_call_target="tpu_custom_call" | custom-call | tf_op jit(solution)/shard_map/states_to_lanes/pallas_call | solution.py:88
  52.3 1.0 projections.1
  53.3 0.0 collective-permute-done.12.refs_3_
  53.4 2.5 %head_vectors.1 = (f32[2,8,64,128]{3,2,1,0:T(8,128)S(1)}, f32[2,20,128]{2,1,0:T(8,128)S(1)}, f32[2,4,64,128]{3,2,1,0:T(8,128)S(1)}, f32[2,4,64,128]{3,2,1,0:T(8,...) custom-call(f32[128,448]{1,0:T(8,128)S(1)} %get-tuple-element.75.ref, ...), custom_call_target="tpu_custom_call" | custom-call | tf_op jit(solution)/shard_map/head_vectors/pallas_call | solution.py:88
  55.8 0.0 copy-start
  55.9 0.0 copy-start.1
  55.9 3.9 %head_outputs.1 = (f32[128,512]{1,0:T(8,128)S(1)}, bf16[128,512]{1,0:T(8,128)(2,1)S(1)}, bf16[128,512]{1,0:T(8,128)(2,1)S(1)}, bf16[128,512]{1,0:T(8,128)(2,1)S(1)}, f32[2,4,64,128]{3,2,1,0:T(8,128)S(1)}) custom-call(s32[1]{0:T(128)} %bitcast.1.refs_0_, f32[64,64,128]{2,1,0:T(8,128)S(1)} %get-tuple-element.65.refs_1_.refs_0_, ...), custom_call_target="tpu_custom_call" | custom-call | tf_op jit(solution)/shard_map/head_outputs/pallas_call | solution.py:88
  59.8 3.7 %collective-permute-start.13 = (bf16[128,512]{1,0:T(8,128)(2,1)S(1)}, bf16[128,512]{1,0:T(8,128)(2,1)S(1)}, u32[]{:S(2)}, u32[]{:S(2)}) collective-permute-start(bf16[128,512]{1,0:T(8,128)(2,1)S(1)} %get-tuple-element.97), channel_id=1, source_target_pairs={{0,1},{1,0},{2,3},{3,2},{4,5},{5,4},{6,7},{7,6},{8,9},{9,8},{10,11... | collective-permute-start | bytes 393224 | tf_op jit(solution)/shard_map/ppermute | solution.py:17
  63.5 0.4 collective-permute-start.14
  63.8 2.1 %collective-permute-start.15 = (bf16[128,512]{1,0:T(8,128)(2,1)S(1)}, bf16[128,512]{1,0:T(8,128)(2,1)S(1)}, u32[]{:S(2)}, u32[]{:S(2)}) collective-permute-start(bf16[128,512]{1,0:T(8,128)(2,1)S(1)} %get-tuple-element.99), channel_id=1, source_target_pairs={{0,3},{1,2},{2,1},{3,0},{4,7},{5,6},{6,5},{7,4},{8,11},{9,10},{10,... | collective-permute-start | bytes 393224 | tf_op jit(solution)/shard_map/ppermute | solution.py:17
  65.9 2.1 %collective-permute-done.13.refs_3_ = bf16[128,512]{1,0:T(8,128)(2,1)S(1)} collective-permute-done((bf16[128,512]{1,0:T(8,128)(2,1)S(1)}, bf16[128,512]{1,0:T(8,128)(2,1)S(1)}, u32[]{:S(2)}, u32[]{:S(2)}) %collective-permute-start.13) | collective-permute-done | bytes 131104 | tf_op jit(solution)/shard_map/ppermute | solution.py:17
  68.0 8.0 %collective-permute-done.14.refs_4_ = bf16[128,512]{1,0:T(8,128)(2,1)S(1)} collective-permute-done((bf16[128,512]{1,0:T(8,128)(2,1)S(1)}, bf16[128,512]{1,0:T(8,128)(2,1)S(1)}, u32[]{:S(2)}, u32[]{:S(2)}) %collective-permute-start.14) | collective-permute-done | bytes 131104 | tf_op jit(solution)/shard_map/ppermute | solution.py:17
  76.0 0.0 collective-permute-done.15.refs_5_
  76.0 0.3 middle.1.refs_1_.refs_0_
  76.3 2.5 %collective-permute-start.16 = (bf16[128,512]{1,0:T(8,128)(2,1)S(1)}, bf16[128,512]{1,0:T(8,128)(2,1)S(1)}, u32[]{:S(2)}, u32[]{:S(2)}) collective-permute-start(bf16[128,512]{1,0:T(8,128)(2,1)S(1)} %middle.1.refs_1_.refs_0_), channel_id=1, source_target_pairs={{0,1},{1,0},{2,3},{3,2},{4,5},{5,4},{6,7},{7,6},{8,9},{9,8},{10,11... | collective-permute-start | bytes 393224 | tf_op jit(solution)/shard_map/ppermute | solution.py:17
  78.8 0.3 collective-permute-start.17
  79.0 2.2 %collective-permute-start.18 = (bf16[128,512]{1,0:T(8,128)(2,1)S(1)}, bf16[128,512]{1,0:T(8,128)(2,1)S(1)}, u32[]{:S(2)}, u32[]{:S(2)}) collective-permute-start(bf16[128,512]{1,0:T(8,128)(2,1)S(1)} %middle.1.refs_1_.refs_0_), channel_id=1, source_target_pairs={{0,3},{1,2},{2,1},{3,0},{4,7},{5,6},{6,5},{7,4},{8,11},{9,10},{10,... | collective-permute-start | bytes 393224 | tf_op jit(solution)/shard_map/ppermute | solution.py:17
  81.2 1.5 %collective-permute-done.16.refs_2_ = bf16[128,512]{1,0:T(8,128)(2,1)S(1)} collective-permute-done((bf16[128,512]{1,0:T(8,128)(2,1)S(1)}, bf16[128,512]{1,0:T(8,128)(2,1)S(1)}, u32[]{:S(2)}, u32[]{:S(2)}) %collective-permute-start.16) | collective-permute-done | bytes 131104 | tf_op jit(solution)/shard_map/ppermute | solution.py:17
  82.7 7.3 %collective-permute-done.17.refs_3_ = bf16[128,512]{1,0:T(8,128)(2,1)S(1)} collective-permute-done((bf16[128,512]{1,0:T(8,128)(2,1)S(1)}, bf16[128,512]{1,0:T(8,128)(2,1)S(1)}, u32[]{:S(2)}, u32[]{:S(2)}) %collective-permute-start.17) | collective-permute-done | bytes 131104 | tf_op jit(solution)/shard_map/ppermute | solution.py:17
  90.1 2.4 %channel_mix.1 = (f32[128,512]{1,0:T(8,128)S(1)}, bf16[128,512]{1,0:T(8,128)(2,1)S(1)}, bf16[128,512]{1,0:T(8,128)(2,1)S(1)}, bf16[128,512]{1,0:T(8,128)(2,1)S(1)}, bf16[32,512]{1,0:T(8,128)(2,1)S(1)}) custom-call(s32[1]{0:T(128)} %bitcast.1.refs_0_, bf16[128,512]{1,0:T(8,128)(2,1)S(1)} %middle.1.refs_1_.refs_0_, ...), custom_call_target="tpu_custom_call" | custom-call | tf_op jit(solution)/shard_map/channel_mix/pallas_call | solution.py:88
  92.5 2.7 %collective-permute-start.19 = (bf16[128,512]{1,0:T(8,128)(2,1)S(1)}, bf16[128,512]{1,0:T(8,128)(2,1)S(1)}, u32[]{:S(2)}, u32[]{:S(2)}) collective-permute-start(bf16[128,512]{1,0:T(8,128)(2,1)S(1)} %get-tuple-element.102), channel_id=1, source_target_pairs={{0,1},{1,0},{2,3},{3,2},{4,5},{5,4},{6,7},{7,6},{8,9},{9,8},{10,11... | collective-permute-start | bytes 393224 | tf_op jit(solution)/shard_map/ppermute | solution.py:17
  95.2 2.4 %collective-permute-start.21 = (bf16[128,512]{1,0:T(8,128)(2,1)S(1)}, bf16[128,512]{1,0:T(8,128)(2,1)S(1)}, u32[]{:S(2)}, u32[]{:S(2)}) collective-permute-start(bf16[128,512]{1,0:T(8,128)(2,1)S(1)} %get-tuple-element.104), channel_id=1, source_target_pairs={{0,3},{1,2},{2,1},{3,0},{4,7},{5,6},{6,5},{7,4},{8,11},{9,10},{10,... | collective-permute-start | bytes 393224 | tf_op jit(solution)/shard_map/ppermute | solution.py:17
  97.6 0.6 copy.25
  98.2 6.9 %final_states.1 = f32[32,8,4096]{2,1,0:T(8,128)} custom-call(s32[33]{0:T(128)S(1)} %get-tuple-element.105.arr_ref, f32[64,64,128]{2,1,0:T(8,128)S(1)} %get-tuple-element.65.refs_1_.refs_0_, f32[64,64,128]{2,1,0:T(8,128)S(1)} %get-tuple-element.70.refs_2_.refs_1_, f32[2,4,64,128]{3,2,1,0:T(8,128)S(1)} %get-tuple-element.106.refs_2_, ...), custom_call_target="tpu_custom_call" | custom-call | tf_op jit(solution)/shard_map/final_states/pallas_call | solution.py:692
  105.2 0.6 copy.26
  105.8 0.0 collective-permute-done.19.refs_2_
  105.8 1.1 %collective-permute-done.20.refs_3_ = bf16[128,512]{1,0:T(8,128)(2,1)S(1)} collective-permute-done((bf16[128,512]{1,0:T(8,128)(2,1)S(1)}, bf16[128,512]{1,0:T(8,128)(2,1)S(1)}, u32[]{:S(2)}, u32[]{:S(2)}) %collective-permute-start.20) | collective-permute-done | bytes 131104 | tf_op jit(solution)/shard_map/ppermute | solution.py:17
  106.9 0.0 collective-permute-done.21.refs_4_
  106.9 0.2 finish.1
  107.1 0.7 reshape.31
  (13 shorter events, 0.0 us)
Async XLA Ops:
  1.6 14.3 %collective-permute-start = (bf16[128,512]{1,0:T(8,128)(2,1)S(1)}, bf16[128,512]{1,0:T(8,128)(2,1)S(1)}, u32[]{:S(2)}, u32[]{:S(2)}) collective-permute-start(bf16[128,512]{1,0:T(8,128)(2,1)S(1)} %reshape.26.refs_1_.refs_0_), channel_id=1, source_target_pairs={{0,1},{1,0},{2,3},{3,2},{4,5},{5,4},{6,7},{7,6},{8,9},{9,8},{10,11... | collective-permute-start | bytes 393224 | tf_op jit(solution)/shard_map/ppermute | solution.py:17
  4.7 11.2 %collective-permute-start.1 = (bf16[128,512]{1,0:T(8,128)(2,1)S(1)}, bf16[128,512]{1,0:T(8,128)(2,1)S(1)}, u32[]{:S(2)}, u32[]{:S(2)}) collective-permute-start(bf16[128,512]{1,0:T(8,128)(2,1)S(1)} %reshape.26.refs_1_.refs_0_), channel_id=1, source_target_pairs={{0,2},{1,3},{2,0},{3,1},{4,6},{5,7},{6,4},{7,5},{8,10},{9,11},{10,... | collective-permute-start | bytes 393224 | tf_op jit(solution)/shard_map/ppermute | solution.py:17
  11.9 0.6 copy-start.2
  12.6 20.5 %all-to-all-start = ((bf16[32,8,512]{2,1,0:T(8,128)(2,1)}), bf16[32,8,512]{2,1,0:T(8,128)(2,1)}, u32[]{:S(2)}, u32[]{:S(2)}) async-start(bf16[32,8,512]{2,1,0:T(8,128)(2,1)} %bitcast.2), calls=%async_computation | async-start | bytes 524288 | tf_op jit(solution)/shard_map/all_to_all | solution.py:829
  15.9 3.1 %copy-start.4 = (bf16[128,512]{1,0:T(8,128)(2,1)}, bf16[128,512]{1,0:T(8,128)(2,1)S(1)}, u32[]{:S(2)}) copy-start(bf16[128,512]{1,0:T(8,128)(2,1)S(1)} %collective-permute-done.refs_2_) | copy-start | bytes 393220
  15.9 3.1 %copy-start.5 = (bf16[128,512]{1,0:T(8,128)(2,1)}, bf16[128,512]{1,0:T(8,128)(2,1)S(1)}, u32[]{:S(2)}) copy-start(bf16[128,512]{1,0:T(8,128)(2,1)S(1)} %collective-permute-done.1.refs_3_) | copy-start | bytes 393220
  19.0 11.5 %collective-permute-start.5 = (bf16[4,8,4096]{2,1,0:T(8,128)(2,1)S(1)}, bf16[4,8,4096]{2,1,0:T(8,128)(2,1)S(1)}, u32[]{:S(2)}, u32[]{:S(2)}) collective-permute-start(bf16[4,8,4096]{2,1,0:T(8,128)(2,1)S(1)} %get-tuple-element.66), channel_id=1, source_target_pairs={{0,4},{4,0},{8,12},{12,8},{16,20},{20,16},{24,28},{28,24},{1,5},{5... | collective-permute-start | bytes 786440 | tf_op jit(solution)/shard_map/ppermute | solution.py:17
  19.1 11.4 %collective-permute-start.6 = (bf16[4,8,4096]{2,1,0:T(8,128)(2,1)S(1)}, bf16[4,8,4096]{2,1,0:T(8,128)(2,1)S(1)}, u32[]{:S(2)}, u32[]{:S(2)}) collective-permute-start(bf16[4,8,4096]{2,1,0:T(8,128)(2,1)S(1)} %get-tuple-element.67), channel_id=1, source_target_pairs={{0,12},{4,8},{8,4},{12,0},{16,28},{20,24},{24,20},{28,16},{1,13},{... | collective-permute-start | bytes 786440 | tf_op jit(solution)/shard_map/ppermute | solution.py:17
  20.7 7.5 %collective-permute-start.9 = (bf16[128,512]{1,0:T(8,128)(2,1)S(1)}, bf16[128,512]{1,0:T(8,128)(2,1)S(1)}, u32[]{:S(2)}, u32[]{:S(2)}) collective-permute-start(bf16[128,512]{1,0:T(8,128)(2,1)S(1)} %reshape.26.refs_1_.refs_0_), channel_id=1, source_target_pairs={{0,3},{1,2},{2,1},{3,0},{4,7},{5,6},{6,5},{7,4},{8,11},{9,10},{10,... | collective-permute-start | bytes 393224 | tf_op jit(solution)/shard_map/ppermute | solution.py:17
  24.2 12.5 %collective-permute-start.2 = (bf16[4,8,4096]{2,1,0:T(8,128)(2,1)S(1)}, bf16[4,8,4096]{2,1,0:T(8,128)(2,1)S(1)}, u32[]{:S(2)}, u32[]{:S(2)}) collective-permute-start(bf16[4,8,4096]{2,1,0:T(8,128)(2,1)S(1)} %get-tuple-element.62), channel_id=1, source_target_pairs={{0,8},{4,12},{8,0},{12,4},{16,24},{20,28},{24,16},{28,20},{1,9},{5... | collective-permute-start | bytes 786440 | tf_op jit(solution)/shard_map/ppermute | solution.py:17
  24.8 15.1 %collective-permute-start.3 = (bf16[4,8,4096]{2,1,0:T(8,128)(2,1)S(1)}, bf16[4,8,4096]{2,1,0:T(8,128)(2,1)S(1)}, u32[]{:S(2)}, u32[]{:S(2)}) collective-permute-start(bf16[4,8,4096]{2,1,0:T(8,128)(2,1)S(1)} %get-tuple-element.63), channel_id=1, source_target_pairs={{0,16},{4,20},{8,24},{12,28},{16,0},{20,4},{24,8},{28,12},{1,17},{... | collective-permute-start | bytes 786440 | tf_op jit(solution)/shard_map/ppermute | solution.py:17
  28.2 0.7 copy-start.6
  28.9 12.6 %collective-permute-start.4 = (bf16[4,8,4096]{2,1,0:T(8,128)(2,1)S(1)}, bf16[4,8,4096]{2,1,0:T(8,128)(2,1)S(1)}, u32[]{:S(2)}, u32[]{:S(2)}) collective-permute-start(bf16[4,8,4096]{2,1,0:T(8,128)(2,1)S(1)} %get-tuple-element.64), channel_id=1, source_target_pairs={{0,24},{4,28},{8,16},{12,20},{16,8},{20,12},{24,0},{28,4},{1,25},{... | collective-permute-start | bytes 786440 | tf_op jit(solution)/shard_map/ppermute | solution.py:17
  30.5 19.4 %collective-permute-start.7 = (bf16[4,8,4096]{2,1,0:T(8,128)(2,1)S(1)}, bf16[4,8,4096]{2,1,0:T(8,128)(2,1)S(1)}, u32[]{:S(2)}, u32[]{:S(2)}) collective-permute-start(bf16[4,8,4096]{2,1,0:T(8,128)(2,1)S(1)} %get-tuple-element.68), channel_id=1, source_target_pairs={{0,20},{4,16},{8,28},{12,24},{16,4},{20,0},{24,12},{28,8},{1,21},{... | collective-permute-start | bytes 786440 | tf_op jit(solution)/shard_map/ppermute | solution.py:17
  30.6 19.4 %collective-permute-start.8 = (bf16[4,8,4096]{2,1,0:T(8,128)(2,1)S(1)}, bf16[4,8,4096]{2,1,0:T(8,128)(2,1)S(1)}, u32[]{:S(2)}, u32[]{:S(2)}) collective-permute-start(bf16[4,8,4096]{2,1,0:T(8,128)(2,1)S(1)} %get-tuple-element.69), channel_id=1, source_target_pairs={{0,28},{4,24},{8,20},{12,16},{16,12},{20,8},{24,4},{28,0},{1,29},{... | collective-permute-start | bytes 786440 | tf_op jit(solution)/shard_map/ppermute | solution.py:17
  36.7 16.6 %collective-permute-start.10 = (bf16[128,448]{1,0:T(8,128)(2,1)S(1)}, bf16[128,448]{1,0:T(8,128)(2,1)S(1)}, u32[]{:S(2)}, u32[]{:S(2)}) collective-permute-start(bf16[128,448]{1,0:T(8,128)(2,1)S(1)} %get-tuple-element.76), channel_id=1, source_target_pairs={{0,1},{1,0},{2,3},{3,2},{4,5},{5,4},{6,7},{7,6},{8,9},{9,8},{10,11... | collective-permute-start | bytes 344072 | tf_op jit(solution)/shard_map/ppermute | solution.py:17
  39.9 13.5 %collective-permute-start.11 = (bf16[128,448]{1,0:T(8,128)(2,1)S(1)}, bf16[128,448]{1,0:T(8,128)(2,1)S(1)}, u32[]{:S(2)}, u32[]{:S(2)}) collective-permute-start(bf16[128,448]{1,0:T(8,128)(2,1)S(1)} %get-tuple-element.76), channel_id=1, source_target_pairs={{0,2},{1,3},{2,0},{3,1},{4,6},{5,7},{6,4},{7,5},{8,10},{9,11},{10,... | collective-permute-start | bytes 344072 | tf_op jit(solution)/shard_map/ppermute | solution.py:17
  41.5 11.8 %collective-permute-start.12 = (bf16[128,448]{1,0:T(8,128)(2,1)S(1)}, bf16[128,448]{1,0:T(8,128)(2,1)S(1)}, u32[]{:S(2)}, u32[]{:S(2)}) collective-permute-start(bf16[128,448]{1,0:T(8,128)(2,1)S(1)} %get-tuple-element.76), channel_id=1, source_target_pairs={{0,3},{1,2},{2,1},{3,0},{4,7},{5,6},{6,5},{7,4},{8,11},{9,10},{10,... | collective-permute-start | bytes 344072 | tf_op jit(solution)/shard_map/ppermute | solution.py:17
  53.3 22.7 %copy-start.3 = (s32[128,128]{1,0:T(8,128)S(1)}, s32[128,128]{1,0:T(8,128)}, u32[]{:S(2)}) copy-start(s32[128,128]{1,0:T(8,128)} %copy-done.2) | copy-start | bytes 196612
  55.8 34.2 %copy-start = (bf16[2048,1024]{1,0:T(8,128)(2,1)S(1)}, bf16[2048,1024]{1,0:T(8,128)(2,1)}, u32[]{:S(2)}) copy-start(bf16[2048,1024]{1,0:T(8,128)(2,1)} %refs_9_.3) | copy-start | bytes 12582916
  55.9 34.2 %copy-start.1 = (bf16[1024,2048]{1,0:T(8,128)(2,1)S(1)}, bf16[1024,2048]{1,0:T(8,128)(2,1)}, u32[]{:S(2)}) copy-start(bf16[1024,2048]{1,0:T(8,128)(2,1)} %refs_10_.1) | copy-start | bytes 12582916
  59.8 8.2 %collective-permute-start.13 = (bf16[128,512]{1,0:T(8,128)(2,1)S(1)}, bf16[128,512]{1,0:T(8,128)(2,1)S(1)}, u32[]{:S(2)}, u32[]{:S(2)}) collective-permute-start(bf16[128,512]{1,0:T(8,128)(2,1)S(1)} %get-tuple-element.97), channel_id=1, source_target_pairs={{0,1},{1,0},{2,3},{3,2},{4,5},{5,4},{6,7},{7,6},{8,9},{9,8},{10,11... | collective-permute-start | bytes 393224 | tf_op jit(solution)/shard_map/ppermute | solution.py:17
  63.5 12.5 %collective-permute-start.14 = (bf16[128,512]{1,0:T(8,128)(2,1)S(1)}, bf16[128,512]{1,0:T(8,128)(2,1)S(1)}, u32[]{:S(2)}, u32[]{:S(2)}) collective-permute-start(bf16[128,512]{1,0:T(8,128)(2,1)S(1)} %get-tuple-element.98), channel_id=1, source_target_pairs={{0,2},{1,3},{2,0},{3,1},{4,6},{5,7},{6,4},{7,5},{8,10},{9,11},{10,... | collective-permute-start | bytes 393224 | tf_op jit(solution)/shard_map/ppermute | solution.py:17
  63.8 12.2 %collective-permute-start.15 = (bf16[128,512]{1,0:T(8,128)(2,1)S(1)}, bf16[128,512]{1,0:T(8,128)(2,1)S(1)}, u32[]{:S(2)}, u32[]{:S(2)}) collective-permute-start(bf16[128,512]{1,0:T(8,128)(2,1)S(1)} %get-tuple-element.99), channel_id=1, source_target_pairs={{0,3},{1,2},{2,1},{3,0},{4,7},{5,6},{6,5},{7,4},{8,11},{9,10},{10,... | collective-permute-start | bytes 393224 | tf_op jit(solution)/shard_map/ppermute | solution.py:17
  76.3 6.4 %collective-permute-start.16 = (bf16[128,512]{1,0:T(8,128)(2,1)S(1)}, bf16[128,512]{1,0:T(8,128)(2,1)S(1)}, u32[]{:S(2)}, u32[]{:S(2)}) collective-permute-start(bf16[128,512]{1,0:T(8,128)(2,1)S(1)} %middle.1.refs_1_.refs_0_), channel_id=1, source_target_pairs={{0,1},{1,0},{2,3},{3,2},{4,5},{5,4},{6,7},{7,6},{8,9},{9,8},{10,11... | collective-permute-start | bytes 393224 | tf_op jit(solution)/shard_map/ppermute | solution.py:17
  78.8 11.3 %collective-permute-start.17 = (bf16[128,512]{1,0:T(8,128)(2,1)S(1)}, bf16[128,512]{1,0:T(8,128)(2,1)S(1)}, u32[]{:S(2)}, u32[]{:S(2)}) collective-permute-start(bf16[128,512]{1,0:T(8,128)(2,1)S(1)} %middle.1.refs_1_.refs_0_), channel_id=1, source_target_pairs={{0,2},{1,3},{2,0},{3,1},{4,6},{5,7},{6,4},{7,5},{8,10},{9,11},{10,... | collective-permute-start | bytes 393224 | tf_op jit(solution)/shard_map/ppermute | solution.py:17
  79.0 11.0 %collective-permute-start.18 = (bf16[128,512]{1,0:T(8,128)(2,1)S(1)}, bf16[128,512]{1,0:T(8,128)(2,1)S(1)}, u32[]{:S(2)}, u32[]{:S(2)}) collective-permute-start(bf16[128,512]{1,0:T(8,128)(2,1)S(1)} %middle.1.refs_1_.refs_0_), channel_id=1, source_target_pairs={{0,3},{1,2},{2,1},{3,0},{4,7},{5,6},{6,5},{7,4},{8,11},{9,10},{10,... | collective-permute-start | bytes 393224 | tf_op jit(solution)/shard_map/ppermute | solution.py:17
  92.5 13.3 %collective-permute-start.19 = (bf16[128,512]{1,0:T(8,128)(2,1)S(1)}, bf16[128,512]{1,0:T(8,128)(2,1)S(1)}, u32[]{:S(2)}, u32[]{:S(2)}) collective-permute-start(bf16[128,512]{1,0:T(8,128)(2,1)S(1)} %get-tuple-element.102), channel_id=1, source_target_pairs={{0,1},{1,0},{2,3},{3,2},{4,5},{5,4},{6,7},{7,6},{8,9},{9,8},{10,11... | collective-permute-start | bytes 393224 | tf_op jit(solution)/shard_map/ppermute | solution.py:17
  95.2 11.7 %collective-permute-start.20 = (bf16[128,512]{1,0:T(8,128)(2,1)S(1)}, bf16[128,512]{1,0:T(8,128)(2,1)S(1)}, u32[]{:S(2)}, u32[]{:S(2)}) collective-permute-start(bf16[128,512]{1,0:T(8,128)(2,1)S(1)} %get-tuple-element.103), channel_id=1, source_target_pairs={{0,2},{1,3},{2,0},{3,1},{4,6},{5,7},{6,4},{7,5},{8,10},{9,11},{10,... | collective-permute-start | bytes 393224 | tf_op jit(solution)/shard_map/ppermute | solution.py:17
  95.2 11.7 %collective-permute-start.21 = (bf16[128,512]{1,0:T(8,128)(2,1)S(1)}, bf16[128,512]{1,0:T(8,128)(2,1)S(1)}, u32[]{:S(2)}, u32[]{:S(2)}) collective-permute-start(bf16[128,512]{1,0:T(8,128)(2,1)S(1)} %get-tuple-element.104), channel_id=1, source_target_pairs={{0,3},{1,2},{2,1},{3,0},{4,7},{5,6},{6,5},{7,4},{8,11},{9,10},{10,... | collective-permute-start | bytes 393224 | tf_op jit(solution)/shard_map/ppermute | solution.py:17

commit v5 on v4

--- a/solution.py
+++ b/solution.py
@@ -824,7 +824,7 @@
     order, arriving, cols, lane_counts, sent = make_plan(
         rank, new_owner, counts, att_shift, ffn_shift, groups, parts, slots
     )
-    order, toks[1], toks[2] = lax.optimization_barrier((order, toks[1], toks[2]))
+    order, toks[2], toks[3] = lax.optimization_barrier((order, toks[2], toks[3]))
     packed = pack_states(order, wkv_state, groups)
     got = lax.all_to_all(
         sent.reshape(groups * parts, -1, width),

time: 108 us -> 105 us (0.972)
  starting transfers between devices: 43.6 us -> 39.7 us
  waiting for transfers between devices: 25.9 us -> 27 us
    ppermute x22, starting transfers between devices: 40.3 us -> 34.9 us  [xor_permute(): return lax.ppermute(x, axis, [(a, a ^ k) for a in range(size)])]
    all_to_all x1, starting transfers between devices: 3.31 us -> 4.85 us  [per_device(): lax.all_to_all(sent.reshape(groups * parts, -1, width), ('req', 'mdl'), s...]
    ppermute x22, waiting for transfers between devices: 25.9 us -> 27 us  [xor_permute(): return lax.ppermute(x, axis, [(a, a ^ k) for a in range(size)])]
  transfers between devices with their start and end apart: 23 -> 23, of which waited for: 8 -> 8; matrix products, arithmetic and copies ran while one was open for 1% -> 1% of each run, Pallas kernels for 22% -> 23%
where the time goes in v5:
time: 105 us
  starting transfers between devices  39.7 us (38%)
  Pallas kernels  33.3 us (32%)
  waiting for transfers between devices  27 us (26%)
  local copies, waits for them, and re-layouts  4.16 us (4%)
    ppermute x22, starting transfers between devices, xor_permute(): return lax.ppermute(x, axis, [(a, a ^ k) for a in range(size)])  34.9 us
    ppermute x22, waiting for transfers between devices, xor_permute(): return lax.ppermute(x, axis, [(a, a ^ k) for a in range(size)])  27 us
    pallas_call x12, Pallas kernels, run(): pl.pallas_call(whole, grid_spec=pltpu.PrefetchScalarGridSpec(num_scalar_p...  26.4 us
    pallas_call x1, Pallas kernels, final_states(): pl.pallas_call(body, grid_spec=pltpu.PrefetchScalarGridSpec(num_scalar_pr...  6.95 us
    all_to_all x1, starting transfers between devices, per_device(): lax.all_to_all(sent.reshape(groups * parts, -1, width), ('req', 'mdl'), s...  4.85 us
    unnamed x16, local copies, waits for them, and re-layouts  2.52 us
  transfers between devices with their start and end apart: 23, of which 8 were waited for; matrix products, arithmetic and copies ran while one was open for 1% of the time, Pallas kernels for 23%

profile of v5, /device:TPU:0, one launch (start us, length us, event | category | flops | bytes accessed | tf_op | source)
XLA Modules:
  0.0 105.1 jit_solution(15018084845981605998)
XLA Ops:
  0.6 0.9 reshape.26.refs_1_.refs_0_
  1.6 4.1 %collective-permute-start = (bf16[128,512]{1,0:T(8,128)(2,1)S(1)}, bf16[128,512]{1,0:T(8,128)(2,1)S(1)}, u32[]{:S(2)}, u32[]{:S(2)}) collective-permute-start(bf16[128,512]{1,0:T(8,128)(2,1)S(1)} %reshape.26.refs_1_.refs_0_), channel_id=1, source_target_pairs={{0,2},{1,3},{2,0},{3,1},{4,6},{5,7},{6,4},{7,5},{8,10},{9,11},{10,... | collective-permute-start | bytes 393224 | tf_op jit(solution)/shard_map/ppermute | solution.py:17
  5.7 1.3 %collective-permute-start.1 = (bf16[128,512]{1,0:T(8,128)(2,1)S(1)}, bf16[128,512]{1,0:T(8,128)(2,1)S(1)}, u32[]{:S(2)}, u32[]{:S(2)}) collective-permute-start(bf16[128,512]{1,0:T(8,128)(2,1)S(1)} %reshape.26.refs_1_.refs_0_), channel_id=1, source_target_pairs={{0,3},{1,2},{2,1},{3,0},{4,7},{5,6},{6,5},{7,4},{8,11},{9,10},{10,... | collective-permute-start | bytes 393224 | tf_op jit(solution)/shard_map/ppermute | solution.py:17
  7.0 4.7 %make_plan.1 = (s32[32]{0:T(128)S(1)}, s32[33]{0:T(128)S(1)}, s32[128,128]{1,0:T(8,128)S(1)}, s32[8,128]{1,0:T(8,128)S(1)}, bf16[8,4,8,512]{3,2,1,0:T(8,128)(2,1)}) custom-call(s32[1]{0:T(128)} %bitcast.refs_0_, s32[256]{0:T(256)} %refs_1_.2, s32[32]{0:T(128)} %refs_2_.1, bf16[32,512]{1,0:T(8,128)(2,1)} %refs_3_.1, bf16[32,512]{1,0:T(8,128)(2,1)} %refs_4_.3), custom_call_target="tpu_custom_call" | custom-call | tf_op jit(solution)/shard_map/make_plan/pallas_call | solution.py:88
  11.7 0.6 copy-done.2
  12.3 4.9 %all-to-all-start = ((bf16[32,8,512]{2,1,0:T(8,128)(2,1)}), bf16[32,8,512]{2,1,0:T(8,128)(2,1)}, u32[]{:S(2)}, u32[]{:S(2)}) async-start(bf16[32,8,512]{2,1,0:T(8,128)(2,1)} %bitcast.2), calls=%async_computation | async-start | bytes 524288 | tf_op jit(solution)/shard_map/all_to_all | solution.py:829
  17.2 0.0 collective-permute-done.refs_3_
  17.2 0.0 collective-permute-done.1.refs_4_
  17.2 3.1 %pack_states.1 = (bf16[4,8,4096]{2,1,0:T(8,128)(2,1)S(1)}, bf16[4,8,4096]{2,1,0:T(8,128)(2,1)S(1)}, bf16[4,8,4096]{2,1,0:T(8,128)(2,1)S(1)}, bf16[4,8,4096]{2,1,...) custom-call(s32[32]{0:T(128)S(1)} %get-tuple-element.60.refs_0_, ...), custom_call_target="tpu_custom_call" | custom-call | tf_op jit(solution)/shard_map/pack_states/pallas_call | solution.py:88
  20.3 0.2 collective-permute-start.5
  20.6 1.6 %collective-permute-start.6 = (bf16[4,8,4096]{2,1,0:T(8,128)(2,1)S(1)}, bf16[4,8,4096]{2,1,0:T(8,128)(2,1)S(1)}, u32[]{:S(2)}, u32[]{:S(2)}) collective-permute-start(bf16[4,8,4096]{2,1,0:T(8,128)(2,1)S(1)} %get-tuple-element.67), channel_id=1, source_target_pairs={{0,12},{4,8},{8,4},{12,0},{16,28},{20,24},{24,20},{28,16},{1,13},{... | collective-permute-start | bytes 786440 | tf_op jit(solution)/shard_map/ppermute | solution.py:17
  22.2 1.5 %collective-permute-start.9 = (bf16[128,512]{1,0:T(8,128)(2,1)S(1)}, bf16[128,512]{1,0:T(8,128)(2,1)S(1)}, u32[]{:S(2)}, u32[]{:S(2)}) collective-permute-start(bf16[128,512]{1,0:T(8,128)(2,1)S(1)} %reshape.26.refs_1_.refs_0_), channel_id=1, source_target_pairs={{0,1},{1,0},{2,3},{3,2},{4,5},{5,4},{6,7},{7,6},{8,9},{9,8},{10,11... | collective-permute-start | bytes 393224 | tf_op jit(solution)/shard_map/ppermute | solution.py:17
  23.7 0.6 collective-permute-start.2
  24.2 1.5 %collective-permute-start.3 = (bf16[4,8,4096]{2,1,0:T(8,128)(2,1)S(1)}, bf16[4,8,4096]{2,1,0:T(8,128)(2,1)S(1)}, u32[]{:S(2)}, u32[]{:S(2)}) collective-permute-start(bf16[4,8,4096]{2,1,0:T(8,128)(2,1)S(1)} %get-tuple-element.63), channel_id=1, source_target_pairs={{0,16},{4,20},{8,24},{12,28},{16,0},{20,4},{24,8},{28,12},{1,17},{... | collective-permute-start | bytes 786440 | tf_op jit(solution)/shard_map/ppermute | solution.py:17
  25.7 2.8 %collective-permute-done.9.refs_2_ = bf16[128,512]{1,0:T(8,128)(2,1)S(1)} collective-permute-done((bf16[128,512]{1,0:T(8,128)(2,1)S(1)}, bf16[128,512]{1,0:T(8,128)(2,1)S(1)}, u32[]{:S(2)}, u32[]{:S(2)}) %collective-permute-start.9) | collective-permute-done | bytes 131104 | tf_op jit(solution)/shard_map/ppermute | solution.py:17
  28.5 0.7 copy-done.6
  29.2 1.9 %collective-permute-start.4 = (bf16[4,8,4096]{2,1,0:T(8,128)(2,1)S(1)}, bf16[4,8,4096]{2,1,0:T(8,128)(2,1)S(1)}, u32[]{:S(2)}, u32[]{:S(2)}) collective-permute-start(bf16[4,8,4096]{2,1,0:T(8,128)(2,1)S(1)} %get-tuple-element.64), channel_id=1, source_target_pairs={{0,24},{4,28},{8,16},{12,20},{16,8},{20,12},{24,0},{28,4},{1,25},{... | collective-permute-start | bytes 786440 | tf_op jit(solution)/shard_map/ppermute | solution.py:17
  31.0 0.0 collective-permute-done.5.refs_0_
  31.0 0.0 collective-permute-start.7
  31.0 0.0 collective-permute-done.6.refs_1_
  31.0 2.2 %collective-permute-start.8 = (bf16[4,8,4096]{2,1,0:T(8,128)(2,1)S(1)}, bf16[4,8,4096]{2,1,0:T(8,128)(2,1)S(1)}, u32[]{:S(2)}, u32[]{:S(2)}) collective-permute-start(bf16[4,8,4096]{2,1,0:T(8,128)(2,1)S(1)} %get-tuple-element.69), channel_id=1, source_target_pairs={{0,28},{4,24},{8,20},{12,16},{16,12},{20,8},{24,4},{28,0},{1,29},{... | collective-permute-start | bytes 786440 | tf_op jit(solution)/shard_map/ppermute | solution.py:17
  33.3 0.0 all-to-all-done
  33.3 1.3 %sort_shifts.1 = (bf16[4,32,512]{2,1,0:T(8,128)(2,1)S(1)}, bf16[4,32,512]{2,1,0:T(8,128)(2,1)S(1)}) custom-call(s32[128,128]{1,0:T(8,128)} %copy-done.2, bf16[8,4,8,512]{3,2,1,0:T(8,128)(2,1)} %bitcast.3.refs_1_), custom_call_target="tpu_custom_call" | custom-call | tf_op jit(solution)/shard_map/sort_shifts/pallas_call | solution.py:88
  34.6 2.4 %first_norm.1 = (f32[4,128,512]{2,1,0:T(8,128)S(1)}, f32[128,448]{1,0:T(8,128)S(1)}, bf16[128,448]{1,0:T(8,128)(2,1)S(1)}, bf16[32,512]{1,0:T(8,128)(2,1)S(1)}) custom-call(s32[1]{0:T(128)} %bitcast.1.refs_0_, bf16[128,512]{1,0:T(8,128)(2,1)S(1)} %reshape.26.refs_1_.refs_0_, bf16[128,512]{1,0:T(8,128)(2,1)} %copy-done.6, bf16[128,512]{1,0:T(8,128)(2,1)} %copy-done.4, ...), custom_call_target="tpu_custom_call" | custom-call | tf_op jit(solution)/shard_map/first_norm/pallas_call | solution.py:88
  36.9 0.0 collective-permute-done.2.refs_1_
  37.0 0.8 collective-permute-start.10
  37.8 0.0 collective-permute-done.3.refs_2_
  37.8 2.5 %collective-permute-start.11 = (bf16[128,448]{1,0:T(8,128)(2,1)S(1)}, bf16[128,448]{1,0:T(8,128)(2,1)S(1)}, u32[]{:S(2)}, u32[]{:S(2)}) collective-permute-start(bf16[128,448]{1,0:T(8,128)(2,1)S(1)} %get-tuple-element.76), channel_id=1, source_target_pairs={{0,2},{1,3},{2,0},{3,1},{4,6},{5,7},{6,4},{7,5},{8,10},{9,11},{10,... | collective-permute-start | bytes 344072 | tf_op jit(solution)/shard_map/ppermute | solution.py:17
  40.2 2.7 %collective-permute-done.4.refs_3_ = bf16[4,8,4096]{2,1,0:T(8,128)(2,1)S(1)} collective-permute-done((bf16[4,8,4096]{2,1,0:T(8,128)(2,1)S(1)}, bf16[4,8,4096]{2,1,0:T(8,128)(2,1)S(1)}, u32[]{:S(2)}, u32[]{:S(2)}) %collective-permute-start.4) | collective-permute-done | bytes 262176 | tf_op jit(solution)/shard_map/ppermute | solution.py:17
  42.9 2.9 %collective-permute-start.12 = (bf16[128,448]{1,0:T(8,128)(2,1)S(1)}, bf16[128,448]{1,0:T(8,128)(2,1)S(1)}, u32[]{:S(2)}, u32[]{:S(2)}) collective-permute-start(bf16[128,448]{1,0:T(8,128)(2,1)S(1)} %get-tuple-element.76), channel_id=1, source_target_pairs={{0,3},{1,2},{2,1},{3,0},{4,7},{5,6},{6,5},{7,4},{8,11},{9,10},{10,... | collective-permute-start | bytes 344072 | tf_op jit(solution)/shard_map/ppermute | solution.py:17
  45.8 2.2 %states_to_lanes.2 = (f32[64,64,128]{2,1,0:T(8,128)S(1)}, bf16[2048,512]{1,0:T(8,128)(2,1)S(1)}, bf16[2048,512]{1,0:T(8,128)(2,1)S(1)}, f32[7,2048]{1,0:T(8,128)S(1)}) custom-call(bf16[4,8,4096]{2,1,0:T(8,128)(2,1)S(1)} %get-tuple-element.61.refs_0_, bf16[4,8,4096]{2,1,0:T(8,128)(2,1)S(1)} %collective-permute-done.2.refs_1_, ...), custom_call_target="tpu_custom_call" | custom-call | tf_op jit(solution)/shard_map/states_to_lanes/pallas_call | solution.py:88
  48.0 2.4 %collective-permute-done.7.refs_2_ = bf16[4,8,4096]{2,1,0:T(8,128)(2,1)S(1)} collective-permute-done((bf16[4,8,4096]{2,1,0:T(8,128)(2,1)S(1)}, bf16[4,8,4096]{2,1,0:T(8,128)(2,1)S(1)}, u32[]{:S(2)}, u32[]{:S(2)}) %collective-permute-start.7) | collective-permute-done | bytes 262176 | tf_op jit(solution)/shard_map/ppermute | solution.py:17
  50.4 0.0 collective-permute-done.8.refs_3_
  50.4 2.3 %states_to_lanes.3 = (f32[64,64,128]{2,1,0:T(8,128)S(1)}, bf16[2048,512]{1,0:T(8,128)(2,1)S(1)}, bf16[512,2048]{1,0:T(8,128)(2,1)S(1)}, f32[7,512]{1,0:T(8,128)S...) custom-call(bf16[4,8,4096]{2,1,0:T(8,128)(2,1)S(1)} %collective-permute-done.5.refs_0_, ...), custom_call_target="tpu_custom_call" | custom-call | tf_op jit(solution)/shard_map/states_to_lanes/pallas_call | solution.py:88
  52.8 1.1 %projections.1 = (f32[128,512]{1,0:T(8,128)S(1)}, f32[128,512]{1,0:T(8,128)S(1)}, f32[128,512]{1,0:T(8,128)S(1)}) custom-call(s32[1]{0:T(128)} %bitcast.1.refs_0_, f32[4,128,512]{2,1,0:T(8,128)S(1)} %get-tuple-element.77.refs_1_, bf16[4,32,512]{2,1,0:T(8,128)(2,1)S(1)} %get-tuple-element.74.refs_5_.refs_2_, f32[7,2048]{1,0:T(8,128)S(1)} %get-tuple-element.78.refs_3_, ...), custom_call_target="tpu_custom_call" | custom-call | tf_op jit(solution)/shard_map/projections/pallas_call | solution.py:88
  53.8 0.0 collective-permute-done.10.refs_1_
  53.8 0.0 collective-permute-done.12.refs_3_
  53.9 2.5 %head_vectors.1 = (f32[2,8,64,128]{3,2,1,0:T(8,128)S(1)}, f32[2,20,128]{2,1,0:T(8,128)S(1)}, f32[2,4,64,128]{3,2,1,0:T(8,128)S(1)}, f32[2,4,64,128]{3,2,1,0:T(8,...) custom-call(f32[128,448]{1,0:T(8,128)S(1)} %get-tuple-element.75.ref, ...), custom_call_target="tpu_custom_call" | custom-call | tf_op jit(solution)/shard_map/head_vectors/pallas_call | solution.py:88
  56.4 0.0 copy-start
  56.4 0.0 copy-start.1
  56.4 3.9 %head_outputs.1 = (f32[128,512]{1,0:T(8,128)S(1)}, bf16[128,512]{1,0:T(8,128)(2,1)S(1)}, bf16[128,512]{1,0:T(8,128)(2,1)S(1)}, bf16[128,512]{1,0:T(8,128)(2,1)S(1)}, f32[2,4,64,128]{3,2,1,0:T(8,128)S(1)}) custom-call(s32[1]{0:T(128)} %bitcast.1.refs_0_, f32[64,64,128]{2,1,0:T(8,128)S(1)} %get-tuple-element.65.refs_1_.refs_0_, ...), custom_call_target="tpu_custom_call" | custom-call | tf_op jit(solution)/shard_map/head_outputs/pallas_call | solution.py:88
  60.3 0.1 collective-permute-start.13
  60.4 2.9 %collective-permute-start.14 = (bf16[128,512]{1,0:T(8,128)(2,1)S(1)}, bf16[128,512]{1,0:T(8,128)(2,1)S(1)}, u32[]{:S(2)}, u32[]{:S(2)}) collective-permute-start(bf16[128,512]{1,0:T(8,128)(2,1)S(1)} %get-tuple-element.98), channel_id=1, source_target_pairs={{0,2},{1,3},{2,0},{3,1},{4,6},{5,7},{6,4},{7,5},{8,10},{9,11},{10,... | collective-permute-start | bytes 393224 | tf_op jit(solution)/shard_map/ppermute | solution.py:17
  63.3 1.5 %collective-permute-start.15 = (bf16[128,512]{1,0:T(8,128)(2,1)S(1)}, bf16[128,512]{1,0:T(8,128)(2,1)S(1)}, u32[]{:S(2)}, u32[]{:S(2)}) collective-permute-start(bf16[128,512]{1,0:T(8,128)(2,1)S(1)} %get-tuple-element.99), channel_id=1, source_target_pairs={{0,3},{1,2},{2,1},{3,0},{4,7},{5,6},{6,5},{7,4},{8,11},{9,10},{10,... | collective-permute-start | bytes 393224 | tf_op jit(solution)/shard_map/ppermute | solution.py:17
  64.8 2.8 %collective-permute-done.13.refs_3_ = bf16[128,512]{1,0:T(8,128)(2,1)S(1)} collective-permute-done((bf16[128,512]{1,0:T(8,128)(2,1)S(1)}, bf16[128,512]{1,0:T(8,128)(2,1)S(1)}, u32[]{:S(2)}, u32[]{:S(2)}) %collective-permute-start.13) | collective-permute-done | bytes 131104 | tf_op jit(solution)/shard_map/ppermute | solution.py:17
  67.5 5.8 %collective-permute-done.14.refs_4_ = bf16[128,512]{1,0:T(8,128)(2,1)S(1)} collective-permute-done((bf16[128,512]{1,0:T(8,128)(2,1)S(1)}, bf16[128,512]{1,0:T(8,128)(2,1)S(1)}, u32[]{:S(2)}, u32[]{:S(2)}) %collective-permute-start.14) | collective-permute-done | bytes 131104 | tf_op jit(solution)/shard_map/ppermute | solution.py:17
  73.3 0.0 collective-permute-done.15.refs_5_
  73.3 0.3 middle.1.refs_1_.refs_0_
  73.6 2.3 %collective-permute-start.16 = (bf16[128,512]{1,0:T(8,128)(2,1)S(1)}, bf16[128,512]{1,0:T(8,128)(2,1)S(1)}, u32[]{:S(2)}, u32[]{:S(2)}) collective-permute-start(bf16[128,512]{1,0:T(8,128)(2,1)S(1)} %middle.1.refs_1_.refs_0_), channel_id=1, source_target_pairs={{0,1},{1,0},{2,3},{3,2},{4,5},{5,4},{6,7},{7,6},{8,9},{9,8},{10,11... | collective-permute-start | bytes 393224 | tf_op jit(solution)/shard_map/ppermute | solution.py:17
  75.9 0.9 collective-permute-start.17
  76.8 1.5 %collective-permute-start.18 = (bf16[128,512]{1,0:T(8,128)(2,1)S(1)}, bf16[128,512]{1,0:T(8,128)(2,1)S(1)}, u32[]{:S(2)}, u32[]{:S(2)}) collective-permute-start(bf16[128,512]{1,0:T(8,128)(2,1)S(1)} %middle.1.refs_1_.refs_0_), channel_id=1, source_target_pairs={{0,3},{1,2},{2,1},{3,0},{4,7},{5,6},{6,5},{7,4},{8,11},{9,10},{10,... | collective-permute-start | bytes 393224 | tf_op jit(solution)/shard_map/ppermute | solution.py:17
  78.3 1.5 %collective-permute-done.16.refs_2_ = bf16[128,512]{1,0:T(8,128)(2,1)S(1)} collective-permute-done((bf16[128,512]{1,0:T(8,128)(2,1)S(1)}, bf16[128,512]{1,0:T(8,128)(2,1)S(1)}, u32[]{:S(2)}, u32[]{:S(2)}) %collective-permute-start.16) | collective-permute-done | bytes 131104 | tf_op jit(solution)/shard_map/ppermute | solution.py:17
  79.8 7.9 %collective-permute-done.17.refs_3_ = bf16[128,512]{1,0:T(8,128)(2,1)S(1)} collective-permute-done((bf16[128,512]{1,0:T(8,128)(2,1)S(1)}, bf16[128,512]{1,0:T(8,128)(2,1)S(1)}, u32[]{:S(2)}, u32[]{:S(2)}) %collective-permute-start.17) | collective-permute-done | bytes 131104 | tf_op jit(solution)/shard_map/ppermute | solution.py:17
  87.7 2.4 %channel_mix.1 = (f32[128,512]{1,0:T(8,128)S(1)}, bf16[128,512]{1,0:T(8,128)(2,1)S(1)}, bf16[128,512]{1,0:T(8,128)(2,1)S(1)}, bf16[128,512]{1,0:T(8,128)(2,1)S(1)}, bf16[32,512]{1,0:T(8,128)(2,1)S(1)}) custom-call(s32[1]{0:T(128)} %bitcast.1.refs_0_, bf16[128,512]{1,0:T(8,128)(2,1)S(1)} %middle.1.refs_1_.refs_0_, ...), custom_call_target="tpu_custom_call" | custom-call | tf_op jit(solution)/shard_map/channel_mix/pallas_call | solution.py:88
  90.1 2.2 %collective-permute-start.19 = (bf16[128,512]{1,0:T(8,128)(2,1)S(1)}, bf16[128,512]{1,0:T(8,128)(2,1)S(1)}, u32[]{:S(2)}, u32[]{:S(2)}) collective-permute-start(bf16[128,512]{1,0:T(8,128)(2,1)S(1)} %get-tuple-element.102), channel_id=1, source_target_pairs={{0,1},{1,0},{2,3},{3,2},{4,5},{5,4},{6,7},{7,6},{8,9},{9,8},{10,11... | collective-permute-start | bytes 393224 | tf_op jit(solution)/shard_map/ppermute | solution.py:17
  92.3 0.7 collective-permute-start.20
  93.0 1.7 %collective-permute-start.21 = (bf16[128,512]{1,0:T(8,128)(2,1)S(1)}, bf16[128,512]{1,0:T(8,128)(2,1)S(1)}, u32[]{:S(2)}, u32[]{:S(2)}) collective-permute-start(bf16[128,512]{1,0:T(8,128)(2,1)S(1)} %get-tuple-element.104), channel_id=1, source_target_pairs={{0,3},{1,2},{2,1},{3,0},{4,7},{5,6},{6,5},{7,4},{8,11},{9,10},{10,... | collective-permute-start | bytes 393224 | tf_op jit(solution)/shard_map/ppermute | solution.py:17
  94.7 0.6 copy.25
  95.4 6.9 %final_states.1 = f32[32,8,4096]{2,1,0:T(8,128)} custom-call(s32[33]{0:T(128)S(1)} %get-tuple-element.105.arr_ref, f32[64,64,128]{2,1,0:T(8,128)S(1)} %get-tuple-element.65.refs_1_.refs_0_, f32[64,64,128]{2,1,0:T(8,128)S(1)} %get-tuple-element.70.refs_2_.refs_1_, f32[2,4,64,128]{3,2,1,0:T(8,128)S(1)} %get-tuple-element.106.refs_2_, ...), custom_call_target="tpu_custom_call" | custom-call | tf_op jit(solution)/shard_map/final_states/pallas_call | solution.py:692
  102.3 0.6 copy.26
  102.9 0.0 collective-permute-done.19.refs_2_
  102.9 1.2 %collective-permute-done.20.refs_3_ = bf16[128,512]{1,0:T(8,128)(2,1)S(1)} collective-permute-done((bf16[128,512]{1,0:T(8,128)(2,1)S(1)}, bf16[128,512]{1,0:T(8,128)(2,1)S(1)}, u32[]{:S(2)}, u32[]{:S(2)}) %collective-permute-start.20) | collective-permute-done | bytes 131104 | tf_op jit(solution)/shard_map/ppermute | solution.py:17
  104.2 0.2 finish.1
  104.4 0.7 reshape.31
  (13 shorter events, 0.0 us)
Async XLA Ops:
  1.6 15.6 %collective-permute-start = (bf16[128,512]{1,0:T(8,128)(2,1)S(1)}, bf16[128,512]{1,0:T(8,128)(2,1)S(1)}, u32[]{:S(2)}, u32[]{:S(2)}) collective-permute-start(bf16[128,512]{1,0:T(8,128)(2,1)S(1)} %reshape.26.refs_1_.refs_0_), channel_id=1, source_target_pairs={{0,2},{1,3},{2,0},{3,1},{4,6},{5,7},{6,4},{7,5},{8,10},{9,11},{10,... | collective-permute-start | bytes 393224 | tf_op jit(solution)/shard_map/ppermute | solution.py:17
  5.7 11.5 %collective-permute-start.1 = (bf16[128,512]{1,0:T(8,128)(2,1)S(1)}, bf16[128,512]{1,0:T(8,128)(2,1)S(1)}, u32[]{:S(2)}, u32[]{:S(2)}) collective-permute-start(bf16[128,512]{1,0:T(8,128)(2,1)S(1)} %reshape.26.refs_1_.refs_0_), channel_id=1, source_target_pairs={{0,3},{1,2},{2,1},{3,0},{4,7},{5,6},{6,5},{7,4},{8,11},{9,10},{10,... | collective-permute-start | bytes 393224 | tf_op jit(solution)/shard_map/ppermute | solution.py:17
  11.7 0.6 copy-start.2
  12.3 20.9 %all-to-all-start = ((bf16[32,8,512]{2,1,0:T(8,128)(2,1)}), bf16[32,8,512]{2,1,0:T(8,128)(2,1)}, u32[]{:S(2)}, u32[]{:S(2)}) async-start(bf16[32,8,512]{2,1,0:T(8,128)(2,1)} %bitcast.2), calls=%async_computation | async-start | bytes 524288 | tf_op jit(solution)/shard_map/all_to_all | solution.py:829
  17.2 3.1 %copy-start.4 = (bf16[128,512]{1,0:T(8,128)(2,1)}, bf16[128,512]{1,0:T(8,128)(2,1)S(1)}, u32[]{:S(2)}) copy-start(bf16[128,512]{1,0:T(8,128)(2,1)S(1)} %collective-permute-done.refs_3_) | copy-start | bytes 393220
  17.2 3.1 %copy-start.5 = (bf16[128,512]{1,0:T(8,128)(2,1)}, bf16[128,512]{1,0:T(8,128)(2,1)S(1)}, u32[]{:S(2)}) copy-start(bf16[128,512]{1,0:T(8,128)(2,1)S(1)} %collective-permute-done.1.refs_4_) | copy-start | bytes 393220
  20.3 10.7 %collective-permute-start.5 = (bf16[4,8,4096]{2,1,0:T(8,128)(2,1)S(1)}, bf16[4,8,4096]{2,1,0:T(8,128)(2,1)S(1)}, u32[]{:S(2)}, u32[]{:S(2)}) collective-permute-start(bf16[4,8,4096]{2,1,0:T(8,128)(2,1)S(1)} %get-tuple-element.66), channel_id=1, source_target_pairs={{0,4},{4,0},{8,12},{12,8},{16,20},{20,16},{24,28},{28,24},{1,5},{5... | collective-permute-start | bytes 786440 | tf_op jit(solution)/shard_map/ppermute | solution.py:17
  20.6 10.5 %collective-permute-start.6 = (bf16[4,8,4096]{2,1,0:T(8,128)(2,1)S(1)}, bf16[4,8,4096]{2,1,0:T(8,128)(2,1)S(1)}, u32[]{:S(2)}, u32[]{:S(2)}) collective-permute-start(bf16[4,8,4096]{2,1,0:T(8,128)(2,1)S(1)} %get-tuple-element.67), channel_id=1, source_target_pairs={{0,12},{4,8},{8,4},{12,0},{16,28},{20,24},{24,20},{28,16},{1,13},{... | collective-permute-start | bytes 786440 | tf_op jit(solution)/shard_map/ppermute | solution.py:17
  22.2 6.3 %collective-permute-start.9 = (bf16[128,512]{1,0:T(8,128)(2,1)S(1)}, bf16[128,512]{1,0:T(8,128)(2,1)S(1)}, u32[]{:S(2)}, u32[]{:S(2)}) collective-permute-start(bf16[128,512]{1,0:T(8,128)(2,1)S(1)} %reshape.26.refs_1_.refs_0_), channel_id=1, source_target_pairs={{0,1},{1,0},{2,3},{3,2},{4,5},{5,4},{6,7},{7,6},{8,9},{9,8},{10,11... | collective-permute-start | bytes 393224 | tf_op jit(solution)/shard_map/ppermute | solution.py:17
  23.7 13.3 %collective-permute-start.2 = (bf16[4,8,4096]{2,1,0:T(8,128)(2,1)S(1)}, bf16[4,8,4096]{2,1,0:T(8,128)(2,1)S(1)}, u32[]{:S(2)}, u32[]{:S(2)}) collective-permute-start(bf16[4,8,4096]{2,1,0:T(8,128)(2,1)S(1)} %get-tuple-element.62), channel_id=1, source_target_pairs={{0,8},{4,12},{8,0},{12,4},{16,24},{20,28},{24,16},{28,20},{1,9},{5... | collective-permute-start | bytes 786440 | tf_op jit(solution)/shard_map/ppermute | solution.py:17
  24.2 13.5 %collective-permute-start.3 = (bf16[4,8,4096]{2,1,0:T(8,128)(2,1)S(1)}, bf16[4,8,4096]{2,1,0:T(8,128)(2,1)S(1)}, u32[]{:S(2)}, u32[]{:S(2)}) collective-permute-start(bf16[4,8,4096]{2,1,0:T(8,128)(2,1)S(1)} %get-tuple-element.63), channel_id=1, source_target_pairs={{0,16},{4,20},{8,24},{12,28},{16,0},{20,4},{24,8},{28,12},{1,17},{... | collective-permute-start | bytes 786440 | tf_op jit(solution)/shard_map/ppermute | solution.py:17
  28.5 0.7 copy-start.6
  29.2 13.8 %collective-permute-start.4 = (bf16[4,8,4096]{2,1,0:T(8,128)(2,1)S(1)}, bf16[4,8,4096]{2,1,0:T(8,128)(2,1)S(1)}, u32[]{:S(2)}, u32[]{:S(2)}) collective-permute-start(bf16[4,8,4096]{2,1,0:T(8,128)(2,1)S(1)} %get-tuple-element.64), channel_id=1, source_target_pairs={{0,24},{4,28},{8,16},{12,20},{16,8},{20,12},{24,0},{28,4},{1,25},{... | collective-permute-start | bytes 786440 | tf_op jit(solution)/shard_map/ppermute | solution.py:17
  31.0 19.4 %collective-permute-start.7 = (bf16[4,8,4096]{2,1,0:T(8,128)(2,1)S(1)}, bf16[4,8,4096]{2,1,0:T(8,128)(2,1)S(1)}, u32[]{:S(2)}, u32[]{:S(2)}) collective-permute-start(bf16[4,8,4096]{2,1,0:T(8,128)(2,1)S(1)} %get-tuple-element.68), channel_id=1, source_target_pairs={{0,20},{4,16},{8,28},{12,24},{16,4},{20,0},{24,12},{28,8},{1,21},{... | collective-permute-start | bytes 786440 | tf_op jit(solution)/shard_map/ppermute | solution.py:17
  31.0 19.4 %collective-permute-start.8 = (bf16[4,8,4096]{2,1,0:T(8,128)(2,1)S(1)}, bf16[4,8,4096]{2,1,0:T(8,128)(2,1)S(1)}, u32[]{:S(2)}, u32[]{:S(2)}) collective-permute-start(bf16[4,8,4096]{2,1,0:T(8,128)(2,1)S(1)} %get-tuple-element.69), channel_id=1, source_target_pairs={{0,28},{4,24},{8,20},{12,16},{16,12},{20,8},{24,4},{28,0},{1,29},{... | collective-permute-start | bytes 786440 | tf_op jit(solution)/shard_map/ppermute | solution.py:17
  37.0 16.9 %collective-permute-start.10 = (bf16[128,448]{1,0:T(8,128)(2,1)S(1)}, bf16[128,448]{1,0:T(8,128)(2,1)S(1)}, u32[]{:S(2)}, u32[]{:S(2)}) collective-permute-start(bf16[128,448]{1,0:T(8,128)(2,1)S(1)} %get-tuple-element.76), channel_id=1, source_target_pairs={{0,1},{1,0},{2,3},{3,2},{4,5},{5,4},{6,7},{7,6},{8,9},{9,8},{10,11... | collective-permute-start | bytes 344072 | tf_op jit(solution)/shard_map/ppermute | solution.py:17
  37.8 16.1 %collective-permute-start.11 = (bf16[128,448]{1,0:T(8,128)(2,1)S(1)}, bf16[128,448]{1,0:T(8,128)(2,1)S(1)}, u32[]{:S(2)}, u32[]{:S(2)}) collective-permute-start(bf16[128,448]{1,0:T(8,128)(2,1)S(1)} %get-tuple-element.76), channel_id=1, source_target_pairs={{0,2},{1,3},{2,0},{3,1},{4,6},{5,7},{6,4},{7,5},{8,10},{9,11},{10,... | collective-permute-start | bytes 344072 | tf_op jit(solution)/shard_map/ppermute | solution.py:17
  42.9 10.9 %collective-permute-start.12 = (bf16[128,448]{1,0:T(8,128)(2,1)S(1)}, bf16[128,448]{1,0:T(8,128)(2,1)S(1)}, u32[]{:S(2)}, u32[]{:S(2)}) collective-permute-start(bf16[128,448]{1,0:T(8,128)(2,1)S(1)} %get-tuple-element.76), channel_id=1, source_target_pairs={{0,3},{1,2},{2,1},{3,0},{4,7},{5,6},{6,5},{7,4},{8,11},{9,10},{10,... | collective-permute-start | bytes 344072 | tf_op jit(solution)/shard_map/ppermute | solution.py:17
  53.9 19.5 %copy-start.3 = (s32[128,128]{1,0:T(8,128)S(1)}, s32[128,128]{1,0:T(8,128)}, u32[]{:S(2)}) copy-start(s32[128,128]{1,0:T(8,128)} %copy-done.2) | copy-start | bytes 196612
  56.4 31.3 %copy-start = (bf16[2048,1024]{1,0:T(8,128)(2,1)S(1)}, bf16[2048,1024]{1,0:T(8,128)(2,1)}, u32[]{:S(2)}) copy-start(bf16[2048,1024]{1,0:T(8,128)(2,1)} %refs_9_.3) | copy-start | bytes 12582916
  56.4 31.3 %copy-start.1 = (bf16[1024,2048]{1,0:T(8,128)(2,1)S(1)}, bf16[1024,2048]{1,0:T(8,128)(2,1)}, u32[]{:S(2)}) copy-start(bf16[1024,2048]{1,0:T(8,128)(2,1)} %refs_10_.1) | copy-start | bytes 12582916
  60.3 7.2 %collective-permute-start.13 = (bf16[128,512]{1,0:T(8,128)(2,1)S(1)}, bf16[128,512]{1,0:T(8,128)(2,1)S(1)}, u32[]{:S(2)}, u32[]{:S(2)}) collective-permute-start(bf16[128,512]{1,0:T(8,128)(2,1)S(1)} %get-tuple-element.97), channel_id=1, source_target_pairs={{0,1},{1,0},{2,3},{3,2},{4,5},{5,4},{6,7},{7,6},{8,9},{9,8},{10,11... | collective-permute-start | bytes 393224 | tf_op jit(solution)/shard_map/ppermute | solution.py:17
  60.4 12.9 %collective-permute-start.14 = (bf16[128,512]{1,0:T(8,128)(2,1)S(1)}, bf16[128,512]{1,0:T(8,128)(2,1)S(1)}, u32[]{:S(2)}, u32[]{:S(2)}) collective-permute-start(bf16[128,512]{1,0:T(8,128)(2,1)S(1)} %get-tuple-element.98), channel_id=1, source_target_pairs={{0,2},{1,3},{2,0},{3,1},{4,6},{5,7},{6,4},{7,5},{8,10},{9,11},{10,... | collective-permute-start | bytes 393224 | tf_op jit(solution)/shard_map/ppermute | solution.py:17
  63.3 10.0 %collective-permute-start.15 = (bf16[128,512]{1,0:T(8,128)(2,1)S(1)}, bf16[128,512]{1,0:T(8,128)(2,1)S(1)}, u32[]{:S(2)}, u32[]{:S(2)}) collective-permute-start(bf16[128,512]{1,0:T(8,128)(2,1)S(1)} %get-tuple-element.99), channel_id=1, source_target_pairs={{0,3},{1,2},{2,1},{3,0},{4,7},{5,6},{6,5},{7,4},{8,11},{9,10},{10,... | collective-permute-start | bytes 393224 | tf_op jit(solution)/shard_map/ppermute | solution.py:17
  73.6 6.2 %collective-permute-start.16 = (bf16[128,512]{1,0:T(8,128)(2,1)S(1)}, bf16[128,512]{1,0:T(8,128)(2,1)S(1)}, u32[]{:S(2)}, u32[]{:S(2)}) collective-permute-start(bf16[128,512]{1,0:T(8,128)(2,1)S(1)} %middle.1.refs_1_.refs_0_), channel_id=1, source_target_pairs={{0,1},{1,0},{2,3},{3,2},{4,5},{5,4},{6,7},{7,6},{8,9},{9,8},{10,11... | collective-permute-start | bytes 393224 | tf_op jit(solution)/shard_map/ppermute | solution.py:17
  75.9 11.8 %collective-permute-start.17 = (bf16[128,512]{1,0:T(8,128)(2,1)S(1)}, bf16[128,512]{1,0:T(8,128)(2,1)S(1)}, u32[]{:S(2)}, u32[]{:S(2)}) collective-permute-start(bf16[128,512]{1,0:T(8,128)(2,1)S(1)} %middle.1.refs_1_.refs_0_), channel_id=1, source_target_pairs={{0,2},{1,3},{2,0},{3,1},{4,6},{5,7},{6,4},{7,5},{8,10},{9,11},{10,... | collective-permute-start | bytes 393224 | tf_op jit(solution)/shard_map/ppermute | solution.py:17
  76.8 10.9 %collective-permute-start.18 = (bf16[128,512]{1,0:T(8,128)(2,1)S(1)}, bf16[128,512]{1,0:T(8,128)(2,1)S(1)}, u32[]{:S(2)}, u32[]{:S(2)}) collective-permute-start(bf16[128,512]{1,0:T(8,128)(2,1)S(1)} %middle.1.refs_1_.refs_0_), channel_id=1, source_target_pairs={{0,3},{1,2},{2,1},{3,0},{4,7},{5,6},{6,5},{7,4},{8,11},{9,10},{10,... | collective-permute-start | bytes 393224 | tf_op jit(solution)/shard_map/ppermute | solution.py:17
  90.1 12.8 %collective-permute-start.19 = (bf16[128,512]{1,0:T(8,128)(2,1)S(1)}, bf16[128,512]{1,0:T(8,128)(2,1)S(1)}, u32[]{:S(2)}, u32[]{:S(2)}) collective-permute-start(bf16[128,512]{1,0:T(8,128)(2,1)S(1)} %get-tuple-element.102), channel_id=1, source_target_pairs={{0,1},{1,0},{2,3},{3,2},{4,5},{5,4},{6,7},{7,6},{8,9},{9,8},{10,11... | collective-permute-start | bytes 393224 | tf_op jit(solution)/shard_map/ppermute | solution.py:17
  92.3 11.9 %collective-permute-start.20 = (bf16[128,512]{1,0:T(8,128)(2,1)S(1)}, bf16[128,512]{1,0:T(8,128)(2,1)S(1)}, u32[]{:S(2)}, u32[]{:S(2)}) collective-permute-start(bf16[128,512]{1,0:T(8,128)(2,1)S(1)} %get-tuple-element.103), channel_id=1, source_target_pairs={{0,2},{1,3},{2,0},{3,1},{4,6},{5,7},{6,4},{7,5},{8,10},{9,11},{10,... | collective-permute-start | bytes 393224 | tf_op jit(solution)/shard_map/ppermute | solution.py:17
  93.0 11.1 %collective-permute-start.21 = (bf16[128,512]{1,0:T(8,128)(2,1)S(1)}, bf16[128,512]{1,0:T(8,128)(2,1)S(1)}, u32[]{:S(2)}, u32[]{:S(2)}) collective-permute-start(bf16[128,512]{1,0:T(8,128)(2,1)S(1)} %get-tuple-element.104), channel_id=1, source_target_pairs={{0,3},{1,2},{2,1},{3,0},{4,7},{5,6},{6,5},{7,4},{8,11},{9,10},{10,... | collective-permute-start | bytes 393224 | tf_op jit(solution)/shard_map/ppermute | solution.py:17

commit v6 on v5

--- a/solution.py
+++ b/solution.py
@@ -23,6 +23,10 @@
 
 def dot32_turned(a, b):
     return lax.dot_general(a, b, (((1,), (1,)), ((), ())), preferred_element_type=F32)
+
+
+def full_spec(shape):
+    return pl.BlockSpec(shape, lambda *_: (0,) * len(shape))
 
 
 def vmem(shape, dtype):
@@ -92,13 +96,19 @@
             grid=(1,),
             in_specs=[anywhere if i in far else near for i in range(n_args)],
             out_specs=[
-                pl.BlockSpec(memory_space=pltpu.SMEM) if o.memory_space == pltpu.SMEM else near
+                full_spec(o.shape)
+                if isinstance(o, jax.ShapeDtypeStruct)
+                else pl.BlockSpec(memory_space=pltpu.SMEM)
+                if o.memory_space == pltpu.SMEM
+                else near
                 for o in outs
             ],
             scratch_shapes=list(scratch) + extra,
         ),
         out_shape=[
-            jax.ShapeDtypeStruct(o.shape, o.dtype) if o.memory_space == pltpu.SMEM else o
+            o
+            if isinstance(o, jax.ShapeDtypeStruct) or o.memory_space != pltpu.SMEM
+            else jax.ShapeDtypeStruct(o.shape, o.dtype)
             for o in outs
         ],
         compiler_params=pltpu.CompilerParams(vmem_limit_bytes=SCRATCH_LIMIT),
@@ -771,7 +781,7 @@
     )
 
 
-def finish(mid, own, others, cols):
+def finish(mid, own, others, cols, slots):
     rows, width = mid.shape
 
     def body(mid_ref, own_ref, *refs):
@@ -781,9 +791,11 @@
             total = total + o[...].astype(F32)
         live = col[:, LIVE : LIVE + 1] > 0
         total = jnp.where(live, mid_ref[...].astype(F32) + total, 0.0).astype(BF16)
-        out[...] = dot32(chooser(col, BACK, rows, rows), total).astype(BF16)
-
-    return run(body, "finish", (), (mid, own, *others, cols), [vmem((rows, width), BF16)])[0]
+        done = dot32(chooser(col, BACK, rows, rows), total)
+        out[...] = done.reshape(rows // slots, slots, width).astype(BF16)
+
+    whole = jax.ShapeDtypeStruct((rows // slots, slots, width), BF16)
+    return run(body, "finish", (), (mid, own, *others, cols), [whole])[0]
 
 
 def per_device(
@@ -893,8 +905,8 @@
         ffn_value_weight,
     )
     outs, new_ffn = results[:parts], results[parts]
-    block = finish(mid, outs[0], scatter(outs), cols)
-    return (block.reshape(requests, slots, width), new_state, new_att, new_ffn)
+    block = finish(mid, outs[0], scatter(outs), cols, slots)
+    return (block, new_state, new_att, new_ffn)
 
 
 def solution(mesh):

time: 105 us -> 105 us (level)
  no operation moved by 1% of the time
where the time goes in v6:
time: 105 us
  starting transfers between devices  39.7 us (38%)
  Pallas kernels  34 us (32%)
  waiting for transfers between devices  27 us (26%)
  local copies, waits for them, and re-layouts  3.46 us (3%)
    ppermute x22, starting transfers between devices, xor_permute(): return lax.ppermute(x, axis, [(a, a ^ k) for a in range(size)])  34.9 us
    ppermute x22, waiting for transfers between devices, xor_permute(): return lax.ppermute(x, axis, [(a, a ^ k) for a in range(size)])  27 us
    pallas_call x12, Pallas kernels, run(): pl.pallas_call(whole, grid_spec=pltpu.PrefetchScalarGridSpec(num_scalar_p...  27 us
    pallas_call x1, Pallas kernels, final_states(): pl.pallas_call(body, grid_spec=pltpu.PrefetchScalarGridSpec(num_scalar_pr...  6.94 us
    all_to_all x1, starting transfers between devices, per_device(): lax.all_to_all(sent.reshape(groups * parts, -1, width), ('req', 'mdl'), s...  4.85 us
    unnamed x16, local copies, waits for them, and re-layouts  2.52 us
  transfers between devices with their start and end apart: 23, of which 8 were waited for; matrix products, arithmetic and copies ran while one was open for 1% of the time, Pallas kernels for 23%

profile of v6, /device:TPU:0, one launch (start us, length us, event | category | flops | bytes accessed | tf_op | source)
XLA Modules:
  0.0 105.1 jit_solution(15576867177320757866)
XLA Ops:
  0.6 0.9 reshape.23.refs_1_.refs_0_
  1.6 4.1 %collective-permute-start = (bf16[128,512]{1,0:T(8,128)(2,1)S(1)}, bf16[128,512]{1,0:T(8,128)(2,1)S(1)}, u32[]{:S(2)}, u32[]{:S(2)}) collective-permute-start(bf16[128,512]{1,0:T(8,128)(2,1)S(1)} %reshape.23.refs_1_.refs_0_), channel_id=1, source_target_pairs={{0,2},{1,3},{2,0},{3,1},{4,6},{5,7},{6,4},{7,5},{8,10},{9,11},{10,... | collective-permute-start | bytes 393224 | tf_op jit(solution)/shard_map/ppermute | solution.py:17
  5.7 1.3 %collective-permute-start.1 = (bf16[128,512]{1,0:T(8,128)(2,1)S(1)}, bf16[128,512]{1,0:T(8,128)(2,1)S(1)}, u32[]{:S(2)}, u32[]{:S(2)}) collective-permute-start(bf16[128,512]{1,0:T(8,128)(2,1)S(1)} %reshape.23.refs_1_.refs_0_), channel_id=1, source_target_pairs={{0,3},{1,2},{2,1},{3,0},{4,7},{5,6},{6,5},{7,4},{8,11},{9,10},{10,... | collective-permute-start | bytes 393224 | tf_op jit(solution)/shard_map/ppermute | solution.py:17
  7.0 4.7 %make_plan.1 = (s32[32]{0:T(128)S(1)}, s32[33]{0:T(128)S(1)}, s32[128,128]{1,0:T(8,128)S(1)}, s32[8,128]{1,0:T(8,128)S(1)}, bf16[8,4,8,512]{3,2,1,0:T(8,128)(2,1)}) custom-call(s32[1]{0:T(128)} %bitcast.refs_0_, s32[256]{0:T(256)} %refs_1_.2, s32[32]{0:T(128)} %refs_2_.1, bf16[32,512]{1,0:T(8,128)(2,1)} %refs_3_.1, bf16[32,512]{1,0:T(8,128)(2,1)} %refs_4_.3), custom_call_target="tpu_custom_call" | custom-call | tf_op jit(solution)/shard_map/make_plan/pallas_call | solution.py:92
  11.7 0.6 copy-done.2
  12.3 4.9 %all-to-all-start = ((bf16[32,8,512]{2,1,0:T(8,128)(2,1)}), bf16[32,8,512]{2,1,0:T(8,128)(2,1)}, u32[]{:S(2)}, u32[]{:S(2)}) async-start(bf16[32,8,512]{2,1,0:T(8,128)(2,1)} %bitcast.2), calls=%async_computation | async-start | bytes 524288 | tf_op jit(solution)/shard_map/all_to_all | solution.py:841
  17.2 0.0 collective-permute-done.refs_3_
  17.2 0.0 collective-permute-done.1.refs_4_
  17.2 3.1 %pack_states.1 = (bf16[4,8,4096]{2,1,0:T(8,128)(2,1)S(1)}, bf16[4,8,4096]{2,1,0:T(8,128)(2,1)S(1)}, bf16[4,8,4096]{2,1,0:T(8,128)(2,1)S(1)}, bf16[4,8,4096]{2,1,...) custom-call(s32[32]{0:T(128)S(1)} %get-tuple-element.60.refs_0_, ...), custom_call_target="tpu_custom_call" | custom-call | tf_op jit(solution)/shard_map/pack_states/pallas_call | solution.py:92
  20.3 0.2 collective-permute-start.5
  20.6 1.6 %collective-permute-start.6 = (bf16[4,8,4096]{2,1,0:T(8,128)(2,1)S(1)}, bf16[4,8,4096]{2,1,0:T(8,128)(2,1)S(1)}, u32[]{:S(2)}, u32[]{:S(2)}) collective-permute-start(bf16[4,8,4096]{2,1,0:T(8,128)(2,1)S(1)} %get-tuple-element.67), channel_id=1, source_target_pairs={{0,12},{4,8},{8,4},{12,0},{16,28},{20,24},{24,20},{28,16},{1,13},{... | collective-permute-start | bytes 786440 | tf_op jit(solution)/shard_map/ppermute | solution.py:17
  22.2 1.5 %collective-permute-start.9 = (bf16[128,512]{1,0:T(8,128)(2,1)S(1)}, bf16[128,512]{1,0:T(8,128)(2,1)S(1)}, u32[]{:S(2)}, u32[]{:S(2)}) collective-permute-start(bf16[128,512]{1,0:T(8,128)(2,1)S(1)} %reshape.23.refs_1_.refs_0_), channel_id=1, source_target_pairs={{0,1},{1,0},{2,3},{3,2},{4,5},{5,4},{6,7},{7,6},{8,9},{9,8},{10,11... | collective-permute-start | bytes 393224 | tf_op jit(solution)/shard_map/ppermute | solution.py:17
  23.7 0.6 collective-permute-start.2
  24.2 1.5 %collective-permute-start.3 = (bf16[4,8,4096]{2,1,0:T(8,128)(2,1)S(1)}, bf16[4,8,4096]{2,1,0:T(8,128)(2,1)S(1)}, u32[]{:S(2)}, u32[]{:S(2)}) collective-permute-start(bf16[4,8,4096]{2,1,0:T(8,128)(2,1)S(1)} %get-tuple-element.63), channel_id=1, source_target_pairs={{0,16},{4,20},{8,24},{12,28},{16,0},{20,4},{24,8},{28,12},{1,17},{... | collective-permute-start | bytes 786440 | tf_op jit(solution)/shard_map/ppermute | solution.py:17
  25.7 2.8 %collective-permute-done.9.refs_2_ = bf16[128,512]{1,0:T(8,128)(2,1)S(1)} collective-permute-done((bf16[128,512]{1,0:T(8,128)(2,1)S(1)}, bf16[128,512]{1,0:T(8,128)(2,1)S(1)}, u32[]{:S(2)}, u32[]{:S(2)}) %collective-permute-start.9) | collective-permute-done | bytes 131104 | tf_op jit(solution)/shard_map/ppermute | solution.py:17
  28.5 0.7 copy-done.6
  29.2 1.9 %collective-permute-start.4 = (bf16[4,8,4096]{2,1,0:T(8,128)(2,1)S(1)}, bf16[4,8,4096]{2,1,0:T(8,128)(2,1)S(1)}, u32[]{:S(2)}, u32[]{:S(2)}) collective-permute-start(bf16[4,8,4096]{2,1,0:T(8,128)(2,1)S(1)} %get-tuple-element.64), channel_id=1, source_target_pairs={{0,24},{4,28},{8,16},{12,20},{16,8},{20,12},{24,0},{28,4},{1,25},{... | collective-permute-start | bytes 786440 | tf_op jit(solution)/shard_map/ppermute | solution.py:17
  31.0 0.0 collective-permute-done.5.refs_0_
  31.0 0.0 collective-permute-start.7
  31.0 0.0 collective-permute-done.6.refs_1_
  31.0 2.2 %collective-permute-start.8 = (bf16[4,8,4096]{2,1,0:T(8,128)(2,1)S(1)}, bf16[4,8,4096]{2,1,0:T(8,128)(2,1)S(1)}, u32[]{:S(2)}, u32[]{:S(2)}) collective-permute-start(bf16[4,8,4096]{2,1,0:T(8,128)(2,1)S(1)} %get-tuple-element.69), channel_id=1, source_target_pairs={{0,28},{4,24},{8,20},{12,16},{16,12},{20,8},{24,4},{28,0},{1,29},{... | collective-permute-start | bytes 786440 | tf_op jit(solution)/shard_map/ppermute | solution.py:17
  33.3 0.0 all-to-all-done
  33.3 1.3 %sort_shifts.1 = (bf16[4,32,512]{2,1,0:T(8,128)(2,1)S(1)}, bf16[4,32,512]{2,1,0:T(8,128)(2,1)S(1)}) custom-call(s32[128,128]{1,0:T(8,128)} %copy-done.2, bf16[8,4,8,512]{3,2,1,0:T(8,128)(2,1)} %bitcast.3.refs_1_), custom_call_target="tpu_custom_call" | custom-call | tf_op jit(solution)/shard_map/sort_shifts/pallas_call | solution.py:92
  34.6 2.4 %first_norm.1 = (f32[4,128,512]{2,1,0:T(8,128)S(1)}, f32[128,448]{1,0:T(8,128)S(1)}, bf16[128,448]{1,0:T(8,128)(2,1)S(1)}, bf16[32,512]{1,0:T(8,128)(2,1)S(1)}) custom-call(s32[1]{0:T(128)} %bitcast.1.refs_0_, bf16[128,512]{1,0:T(8,128)(2,1)S(1)} %reshape.23.refs_1_.refs_0_, bf16[128,512]{1,0:T(8,128)(2,1)} %copy-done.6, bf16[128,512]{1,0:T(8,128)(2,1)} %copy-done.4, ...), custom_call_target="tpu_custom_call" | custom-call | tf_op jit(solution)/shard_map/first_norm/pallas_call | solution.py:92
  36.9 0.0 collective-permute-done.2.refs_1_
  37.0 0.8 collective-permute-start.10
  37.8 0.0 collective-permute-done.3.refs_2_
  37.8 2.5 %collective-permute-start.11 = (bf16[128,448]{1,0:T(8,128)(2,1)S(1)}, bf16[128,448]{1,0:T(8,128)(2,1)S(1)}, u32[]{:S(2)}, u32[]{:S(2)}) collective-permute-start(bf16[128,448]{1,0:T(8,128)(2,1)S(1)} %get-tuple-element.76), channel_id=1, source_target_pairs={{0,2},{1,3},{2,0},{3,1},{4,6},{5,7},{6,4},{7,5},{8,10},{9,11},{10,... | collective-permute-start | bytes 344072 | tf_op jit(solution)/shard_map/ppermute | solution.py:17
  40.2 2.7 %collective-permute-done.4.refs_3_ = bf16[4,8,4096]{2,1,0:T(8,128)(2,1)S(1)} collective-permute-done((bf16[4,8,4096]{2,1,0:T(8,128)(2,1)S(1)}, bf16[4,8,4096]{2,1,0:T(8,128)(2,1)S(1)}, u32[]{:S(2)}, u32[]{:S(2)}) %collective-permute-start.4) | collective-permute-done | bytes 262176 | tf_op jit(solution)/shard_map/ppermute | solution.py:17
  42.9 2.9 %collective-permute-start.12 = (bf16[128,448]{1,0:T(8,128)(2,1)S(1)}, bf16[128,448]{1,0:T(8,128)(2,1)S(1)}, u32[]{:S(2)}, u32[]{:S(2)}) collective-permute-start(bf16[128,448]{1,0:T(8,128)(2,1)S(1)} %get-tuple-element.76), channel_id=1, source_target_pairs={{0,3},{1,2},{2,1},{3,0},{4,7},{5,6},{6,5},{7,4},{8,11},{9,10},{10,... | collective-permute-start | bytes 344072 | tf_op jit(solution)/shard_map/ppermute | solution.py:17
  45.8 2.2 %states_to_lanes.2 = (f32[64,64,128]{2,1,0:T(8,128)S(1)}, bf16[2048,512]{1,0:T(8,128)(2,1)S(1)}, bf16[2048,512]{1,0:T(8,128)(2,1)S(1)}, f32[7,2048]{1,0:T(8,128)S(1)}) custom-call(bf16[4,8,4096]{2,1,0:T(8,128)(2,1)S(1)} %get-tuple-element.61.refs_0_, bf16[4,8,4096]{2,1,0:T(8,128)(2,1)S(1)} %collective-permute-done.2.refs_1_, ...), custom_call_target="tpu_custom_call" | custom-call | tf_op jit(solution)/shard_map/states_to_lanes/pallas_call | solution.py:92
  48.0 2.4 %collective-permute-done.7.refs_2_ = bf16[4,8,4096]{2,1,0:T(8,128)(2,1)S(1)} collective-permute-done((bf16[4,8,4096]{2,1,0:T(8,128)(2,1)S(1)}, bf16[4,8,4096]{2,1,0:T(8,128)(2,1)S(1)}, u32[]{:S(2)}, u32[]{:S(2)}) %collective-permute-start.7) | collective-permute-done | bytes 262176 | tf_op jit(solution)/shard_map/ppermute | solution.py:17
  50.4 0.0 collective-permute-done.8.refs_3_
  50.4 2.3 %states_to_lanes.3 = (f32[64,64,128]{2,1,0:T(8,128)S(1)}, bf16[2048,512]{1,0:T(8,128)(2,1)S(1)}, bf16[512,2048]{1,0:T(8,128)(2,1)S(1)}, f32[7,512]{1,0:T(8,128)S...) custom-call(bf16[4,8,4096]{2,1,0:T(8,128)(2,1)S(1)} %collective-permute-done.5.refs_0_, ...), custom_call_target="tpu_custom_call" | custom-call | tf_op jit(solution)/shard_map/states_to_lanes/pallas_call | solution.py:92
  52.8 1.1 %projections.1 = (f32[128,512]{1,0:T(8,128)S(1)}, f32[128,512]{1,0:T(8,128)S(1)}, f32[128,512]{1,0:T(8,128)S(1)}) custom-call(s32[1]{0:T(128)} %bitcast.1.refs_0_, f32[4,128,512]{2,1,0:T(8,128)S(1)} %get-tuple-element.77.refs_1_, bf16[4,32,512]{2,1,0:T(8,128)(2,1)S(1)} %get-tuple-element.74.refs_5_.refs_2_, f32[7,2048]{1,0:T(8,128)S(1)} %get-tuple-element.78.refs_3_, ...), custom_call_target="tpu_custom_call" | custom-call | tf_op jit(solution)/shard_map/projections/pallas_call | solution.py:92
  53.8 0.0 collective-permute-done.10.refs_1_
  53.8 0.0 collective-permute-done.11.refs_2_
  53.8 0.0 collective-permute-done.12.refs_3_
  53.9 2.5 %head_vectors.1 = (f32[2,8,64,128]{3,2,1,0:T(8,128)S(1)}, f32[2,20,128]{2,1,0:T(8,128)S(1)}, f32[2,4,64,128]{3,2,1,0:T(8,128)S(1)}, f32[2,4,64,128]{3,2,1,0:T(8,...) custom-call(f32[128,448]{1,0:T(8,128)S(1)} %get-tuple-element.75.ref, ...), custom_call_target="tpu_custom_call" | custom-call | tf_op jit(solution)/shard_map/head_vectors/pallas_call | solution.py:92
  56.4 0.0 copy-start
  56.4 0.0 copy-start.1
  56.4 3.9 %head_outputs.1 = (f32[128,512]{1,0:T(8,128)S(1)}, bf16[128,512]{1,0:T(8,128)(2,1)S(1)}, bf16[128,512]{1,0:T(8,128)(2,1)S(1)}, bf16[128,512]{1,0:T(8,128)(2,1)S(1)}, f32[2,4,64,128]{3,2,1,0:T(8,128)S(1)}) custom-call(s32[1]{0:T(128)} %bitcast.1.refs_0_, f32[64,64,128]{2,1,0:T(8,128)S(1)} %get-tuple-element.65.refs_1_.refs_0_, ...), custom_call_target="tpu_custom_call" | custom-call | tf_op jit(solution)/shard_map/head_outputs/pallas_call | solution.py:92
  60.3 0.1 collective-permute-start.13
  60.4 2.9 %collective-permute-start.14 = (bf16[128,512]{1,0:T(8,128)(2,1)S(1)}, bf16[128,512]{1,0:T(8,128)(2,1)S(1)}, u32[]{:S(2)}, u32[]{:S(2)}) collective-permute-start(bf16[128,512]{1,0:T(8,128)(2,1)S(1)} %get-tuple-element.98), channel_id=1, source_target_pairs={{0,2},{1,3},{2,0},{3,1},{4,6},{5,7},{6,4},{7,5},{8,10},{9,11},{10,... | collective-permute-start | bytes 393224 | tf_op jit(solution)/shard_map/ppermute | solution.py:17
  63.3 1.5 %collective-permute-start.15 = (bf16[128,512]{1,0:T(8,128)(2,1)S(1)}, bf16[128,512]{1,0:T(8,128)(2,1)S(1)}, u32[]{:S(2)}, u32[]{:S(2)}) collective-permute-start(bf16[128,512]{1,0:T(8,128)(2,1)S(1)} %get-tuple-element.99), channel_id=1, source_target_pairs={{0,3},{1,2},{2,1},{3,0},{4,7},{5,6},{6,5},{7,4},{8,11},{9,10},{10,... | collective-permute-start | bytes 393224 | tf_op jit(solution)/shard_map/ppermute | solution.py:17
  64.8 2.8 %collective-permute-done.13.refs_3_ = bf16[128,512]{1,0:T(8,128)(2,1)S(1)} collective-permute-done((bf16[128,512]{1,0:T(8,128)(2,1)S(1)}, bf16[128,512]{1,0:T(8,128)(2,1)S(1)}, u32[]{:S(2)}, u32[]{:S(2)}) %collective-permute-start.13) | collective-permute-done | bytes 131104 | tf_op jit(solution)/shard_map/ppermute | solution.py:17
  67.5 5.8 %collective-permute-done.14.refs_4_ = bf16[128,512]{1,0:T(8,128)(2,1)S(1)} collective-permute-done((bf16[128,512]{1,0:T(8,128)(2,1)S(1)}, bf16[128,512]{1,0:T(8,128)(2,1)S(1)}, u32[]{:S(2)}, u32[]{:S(2)}) %collective-permute-start.14) | collective-permute-done | bytes 131104 | tf_op jit(solution)/shard_map/ppermute | solution.py:17
  73.3 0.0 collective-permute-done.15.refs_5_
  73.3 0.3 middle.1.refs_1_.refs_0_
  73.6 2.3 %collective-permute-start.16 = (bf16[128,512]{1,0:T(8,128)(2,1)S(1)}, bf16[128,512]{1,0:T(8,128)(2,1)S(1)}, u32[]{:S(2)}, u32[]{:S(2)}) collective-permute-start(bf16[128,512]{1,0:T(8,128)(2,1)S(1)} %middle.1.refs_1_.refs_0_), channel_id=1, source_target_pairs={{0,1},{1,0},{2,3},{3,2},{4,5},{5,4},{6,7},{7,6},{8,9},{9,8},{10,11... | collective-permute-start | bytes 393224 | tf_op jit(solution)/shard_map/ppermute | solution.py:17
  75.9 0.9 collective-permute-start.17
  76.8 1.5 %collective-permute-start.18 = (bf16[128,512]{1,0:T(8,128)(2,1)S(1)}, bf16[128,512]{1,0:T(8,128)(2,1)S(1)}, u32[]{:S(2)}, u32[]{:S(2)}) collective-permute-start(bf16[128,512]{1,0:T(8,128)(2,1)S(1)} %middle.1.refs_1_.refs_0_), channel_id=1, source_target_pairs={{0,3},{1,2},{2,1},{3,0},{4,7},{5,6},{6,5},{7,4},{8,11},{9,10},{10,... | collective-permute-start | bytes 393224 | tf_op jit(solution)/shard_map/ppermute | solution.py:17
  78.3 1.5 %collective-permute-done.16.refs_2_ = bf16[128,512]{1,0:T(8,128)(2,1)S(1)} collective-permute-done((bf16[128,512]{1,0:T(8,128)(2,1)S(1)}, bf16[128,512]{1,0:T(8,128)(2,1)S(1)}, u32[]{:S(2)}, u32[]{:S(2)}) %collective-permute-start.16) | collective-permute-done | bytes 131104 | tf_op jit(solution)/shard_map/ppermute | solution.py:17
  79.8 7.9 %collective-permute-done.17.refs_3_ = bf16[128,512]{1,0:T(8,128)(2,1)S(1)} collective-permute-done((bf16[128,512]{1,0:T(8,128)(2,1)S(1)}, bf16[128,512]{1,0:T(8,128)(2,1)S(1)}, u32[]{:S(2)}, u32[]{:S(2)}) %collective-permute-start.17) | collective-permute-done | bytes 131104 | tf_op jit(solution)/shard_map/ppermute | solution.py:17
  87.7 0.0 collective-permute-done.18.refs_4_
  87.7 2.4 %channel_mix.1 = (f32[128,512]{1,0:T(8,128)S(1)}, bf16[128,512]{1,0:T(8,128)(2,1)S(1)}, bf16[128,512]{1,0:T(8,128)(2,1)S(1)}, bf16[128,512]{1,0:T(8,128)(2,1)S(1)}, bf16[32,512]{1,0:T(8,128)(2,1)S(1)}) custom-call(s32[1]{0:T(128)} %bitcast.1.refs_0_, bf16[128,512]{1,0:T(8,128)(2,1)S(1)} %middle.1.refs_1_.refs_0_, ...), custom_call_target="tpu_custom_call" | custom-call | tf_op jit(solution)/shard_map/channel_mix/pallas_call | solution.py:92
  90.1 2.2 %collective-permute-start.19 = (bf16[128,512]{1,0:T(8,128)(2,1)S(1)}, bf16[128,512]{1,0:T(8,128)(2,1)S(1)}, u32[]{:S(2)}, u32[]{:S(2)}) collective-permute-start(bf16[128,512]{1,0:T(8,128)(2,1)S(1)} %get-tuple-element.102), channel_id=1, source_target_pairs={{0,1},{1,0},{2,3},{3,2},{4,5},{5,4},{6,7},{7,6},{8,9},{9,8},{10,11... | collective-permute-start | bytes 393224 | tf_op jit(solution)/shard_map/ppermute | solution.py:17
  92.3 0.7 collective-permute-start.20
  93.0 1.7 %collective-permute-start.21 = (bf16[128,512]{1,0:T(8,128)(2,1)S(1)}, bf16[128,512]{1,0:T(8,128)(2,1)S(1)}, u32[]{:S(2)}, u32[]{:S(2)}) collective-permute-start(bf16[128,512]{1,0:T(8,128)(2,1)S(1)} %get-tuple-element.104), channel_id=1, source_target_pairs={{0,3},{1,2},{2,1},{3,0},{4,7},{5,6},{6,5},{7,4},{8,11},{9,10},{10,... | collective-permute-start | bytes 393224 | tf_op jit(solution)/shard_map/ppermute | solution.py:17
  94.7 0.6 copy.25
  95.4 6.9 %final_states.1 = f32[32,8,4096]{2,1,0:T(8,128)} custom-call(s32[33]{0:T(128)S(1)} %get-tuple-element.105.arr_ref, f32[64,64,128]{2,1,0:T(8,128)S(1)} %get-tuple-element.65.refs_1_.refs_0_, f32[64,64,128]{2,1,0:T(8,128)S(1)} %get-tuple-element.70.refs_2_.refs_1_, f32[2,4,64,128]{3,2,1,0:T(8,128)S(1)} %get-tuple-element.106.refs_2_, ...), custom_call_target="tpu_custom_call" | custom-call | tf_op jit(solution)/shard_map/final_states/pallas_call | solution.py:702
  102.3 0.6 copy.26
  102.9 1.2 %collective-permute-done.20.refs_3_ = bf16[128,512]{1,0:T(8,128)(2,1)S(1)} collective-permute-done((bf16[128,512]{1,0:T(8,128)(2,1)S(1)}, bf16[128,512]{1,0:T(8,128)(2,1)S(1)}, u32[]{:S(2)}, u32[]{:S(2)}) %collective-permute-start.20) | collective-permute-done | bytes 131104 | tf_op jit(solution)/shard_map/ppermute | solution.py:17
  104.2 0.9 finish.1
  (12 shorter events, 0.0 us)
Async XLA Ops:
  1.6 15.6 %collective-permute-start = (bf16[128,512]{1,0:T(8,128)(2,1)S(1)}, bf16[128,512]{1,0:T(8,128)(2,1)S(1)}, u32[]{:S(2)}, u32[]{:S(2)}) collective-permute-start(bf16[128,512]{1,0:T(8,128)(2,1)S(1)} %reshape.23.refs_1_.refs_0_), channel_id=1, source_target_pairs={{0,2},{1,3},{2,0},{3,1},{4,6},{5,7},{6,4},{7,5},{8,10},{9,11},{10,... | collective-permute-start | bytes 393224 | tf_op jit(solution)/shard_map/ppermute | solution.py:17
  5.7 11.5 %collective-permute-start.1 = (bf16[128,512]{1,0:T(8,128)(2,1)S(1)}, bf16[128,512]{1,0:T(8,128)(2,1)S(1)}, u32[]{:S(2)}, u32[]{:S(2)}) collective-permute-start(bf16[128,512]{1,0:T(8,128)(2,1)S(1)} %reshape.23.refs_1_.refs_0_), channel_id=1, source_target_pairs={{0,3},{1,2},{2,1},{3,0},{4,7},{5,6},{6,5},{7,4},{8,11},{9,10},{10,... | collective-permute-start | bytes 393224 | tf_op jit(solution)/shard_map/ppermute | solution.py:17
  11.7 0.6 copy-start.2
  12.3 20.9 %all-to-all-start = ((bf16[32,8,512]{2,1,0:T(8,128)(2,1)}), bf16[32,8,512]{2,1,0:T(8,128)(2,1)}, u32[]{:S(2)}, u32[]{:S(2)}) async-start(bf16[32,8,512]{2,1,0:T(8,128)(2,1)} %bitcast.2), calls=%async_computation | async-start | bytes 524288 | tf_op jit(solution)/shard_map/all_to_all | solution.py:841
  17.2 3.1 %copy-start.4 = (bf16[128,512]{1,0:T(8,128)(2,1)}, bf16[128,512]{1,0:T(8,128)(2,1)S(1)}, u32[]{:S(2)}) copy-start(bf16[128,512]{1,0:T(8,128)(2,1)S(1)} %collective-permute-done.refs_3_) | copy-start | bytes 393220
  17.2 3.1 %copy-start.5 = (bf16[128,512]{1,0:T(8,128)(2,1)}, bf16[128,512]{1,0:T(8,128)(2,1)S(1)}, u32[]{:S(2)}) copy-start(bf16[128,512]{1,0:T(8,128)(2,1)S(1)} %collective-permute-done.1.refs_4_) | copy-start | bytes 393220
  20.3 10.7 %collective-permute-start.5 = (bf16[4,8,4096]{2,1,0:T(8,128)(2,1)S(1)}, bf16[4,8,4096]{2,1,0:T(8,128)(2,1)S(1)}, u32[]{:S(2)}, u32[]{:S(2)}) collective-permute-start(bf16[4,8,4096]{2,1,0:T(8,128)(2,1)S(1)} %get-tuple-element.66), channel_id=1, source_target_pairs={{0,4},{4,0},{8,12},{12,8},{16,20},{20,16},{24,28},{28,24},{1,5},{5... | collective-permute-start | bytes 786440 | tf_op jit(solution)/shard_map/ppermute | solution.py:17
  20.6 10.5 %collective-permute-start.6 = (bf16[4,8,4096]{2,1,0:T(8,128)(2,1)S(1)}, bf16[4,8,4096]{2,1,0:T(8,128)(2,1)S(1)}, u32[]{:S(2)}, u32[]{:S(2)}) collective-permute-start(bf16[4,8,4096]{2,1,0:T(8,128)(2,1)S(1)} %get-tuple-element.67), channel_id=1, source_target_pairs={{0,12},{4,8},{8,4},{12,0},{16,28},{20,24},{24,20},{28,16},{1,13},{... | collective-permute-start | bytes 786440 | tf_op jit(solution)/shard_map/ppermute | solution.py:17
  22.2 6.3 %collective-permute-start.9 = (bf16[128,512]{1,0:T(8,128)(2,1)S(1)}, bf16[128,512]{1,0:T(8,128)(2,1)S(1)}, u32[]{:S(2)}, u32[]{:S(2)}) collective-permute-start(bf16[128,512]{1,0:T(8,128)(2,1)S(1)} %reshape.23.refs_1_.refs_0_), channel_id=1, source_target_pairs={{0,1},{1,0},{2,3},{3,2},{4,5},{5,4},{6,7},{7,6},{8,9},{9,8},{10,11... | collective-permute-start | bytes 393224 | tf_op jit(solution)/shard_map/ppermute | solution.py:17
  23.7 13.3 %collective-permute-start.2 = (bf16[4,8,4096]{2,1,0:T(8,128)(2,1)S(1)}, bf16[4,8,4096]{2,1,0:T(8,128)(2,1)S(1)}, u32[]{:S(2)}, u32[]{:S(2)}) collective-permute-start(bf16[4,8,4096]{2,1,0:T(8,128)(2,1)S(1)} %get-tuple-element.62), channel_id=1, source_target_pairs={{0,8},{4,12},{8,0},{12,4},{16,24},{20,28},{24,16},{28,20},{1,9},{5... | collective-permute-start | bytes 786440 | tf_op jit(solution)/shard_map/ppermute | solution.py:17
  24.2 13.5 %collective-permute-start.3 = (bf16[4,8,4096]{2,1,0:T(8,128)(2,1)S(1)}, bf16[4,8,4096]{2,1,0:T(8,128)(2,1)S(1)}, u32[]{:S(2)}, u32[]{:S(2)}) collective-permute-start(bf16[4,8,4096]{2,1,0:T(8,128)(2,1)S(1)} %get-tuple-element.63), channel_id=1, source_target_pairs={{0,16},{4,20},{8,24},{12,28},{16,0},{20,4},{24,8},{28,12},{1,17},{... | collective-permute-start | bytes 786440 | tf_op jit(solution)/shard_map/ppermute | solution.py:17
  28.5 0.7 copy-start.6
  29.2 13.8 %collective-permute-start.4 = (bf16[4,8,4096]{2,1,0:T(8,128)(2,1)S(1)}, bf16[4,8,4096]{2,1,0:T(8,128)(2,1)S(1)}, u32[]{:S(2)}, u32[]{:S(2)}) collective-permute-start(bf16[4,8,4096]{2,1,0:T(8,128)(2,1)S(1)} %get-tuple-element.64), channel_id=1, source_target_pairs={{0,24},{4,28},{8,16},{12,20},{16,8},{20,12},{24,0},{28,4},{1,25},{... | collective-permute-start | bytes 786440 | tf_op jit(solution)/shard_map/ppermute | solution.py:17
  31.0 19.4 %collective-permute-start.7 = (bf16[4,8,4096]{2,1,0:T(8,128)(2,1)S(1)}, bf16[4,8,4096]{2,1,0:T(8,128)(2,1)S(1)}, u32[]{:S(2)}, u32[]{:S(2)}) collective-permute-start(bf16[4,8,4096]{2,1,0:T(8,128)(2,1)S(1)} %get-tuple-element.68), channel_id=1, source_target_pairs={{0,20},{4,16},{8,28},{12,24},{16,4},{20,0},{24,12},{28,8},{1,21},{... | collective-permute-start | bytes 786440 | tf_op jit(solution)/shard_map/ppermute | solution.py:17
  31.0 19.4 %collective-permute-start.8 = (bf16[4,8,4096]{2,1,0:T(8,128)(2,1)S(1)}, bf16[4,8,4096]{2,1,0:T(8,128)(2,1)S(1)}, u32[]{:S(2)}, u32[]{:S(2)}) collective-permute-start(bf16[4,8,4096]{2,1,0:T(8,128)(2,1)S(1)} %get-tuple-element.69), channel_id=1, source_target_pairs={{0,28},{4,24},{8,20},{12,16},{16,12},{20,8},{24,4},{28,0},{1,29},{... | collective-permute-start | bytes 786440 | tf_op jit(solution)/shard_map/ppermute | solution.py:17
  37.0 16.9 %collective-permute-start.10 = (bf16[128,448]{1,0:T(8,128)(2,1)S(1)}, bf16[128,448]{1,0:T(8,128)(2,1)S(1)}, u32[]{:S(2)}, u32[]{:S(2)}) collective-permute-start(bf16[128,448]{1,0:T(8,128)(2,1)S(1)} %get-tuple-element.76), channel_id=1, source_target_pairs={{0,1},{1,0},{2,3},{3,2},{4,5},{5,4},{6,7},{7,6},{8,9},{9,8},{10,11... | collective-permute-start | bytes 344072 | tf_op jit(solution)/shard_map/ppermute | solution.py:17
  37.8 16.1 %collective-permute-start.11 = (bf16[128,448]{1,0:T(8,128)(2,1)S(1)}, bf16[128,448]{1,0:T(8,128)(2,1)S(1)}, u32[]{:S(2)}, u32[]{:S(2)}) collective-permute-start(bf16[128,448]{1,0:T(8,128)(2,1)S(1)} %get-tuple-element.76), channel_id=1, source_target_pairs={{0,2},{1,3},{2,0},{3,1},{4,6},{5,7},{6,4},{7,5},{8,10},{9,11},{10,... | collective-permute-start | bytes 344072 | tf_op jit(solution)/shard_map/ppermute | solution.py:17
  42.9 10.9 %collective-permute-start.12 = (bf16[128,448]{1,0:T(8,128)(2,1)S(1)}, bf16[128,448]{1,0:T(8,128)(2,1)S(1)}, u32[]{:S(2)}, u32[]{:S(2)}) collective-permute-start(bf16[128,448]{1,0:T(8,128)(2,1)S(1)} %get-tuple-element.76), channel_id=1, source_target_pairs={{0,3},{1,2},{2,1},{3,0},{4,7},{5,6},{6,5},{7,4},{8,11},{9,10},{10,... | collective-permute-start | bytes 344072 | tf_op jit(solution)/shard_map/ppermute | solution.py:17
  53.9 19.5 %copy-start.3 = (s32[128,128]{1,0:T(8,128)S(1)}, s32[128,128]{1,0:T(8,128)}, u32[]{:S(2)}) copy-start(s32[128,128]{1,0:T(8,128)} %copy-done.2) | copy-start | bytes 196612
  56.4 31.3 %copy-start = (bf16[2048,1024]{1,0:T(8,128)(2,1)S(1)}, bf16[2048,1024]{1,0:T(8,128)(2,1)}, u32[]{:S(2)}) copy-start(bf16[2048,1024]{1,0:T(8,128)(2,1)} %refs_9_.3) | copy-start | bytes 12582916
  56.4 31.3 %copy-start.1 = (bf16[1024,2048]{1,0:T(8,128)(2,1)S(1)}, bf16[1024,2048]{1,0:T(8,128)(2,1)}, u32[]{:S(2)}) copy-start(bf16[1024,2048]{1,0:T(8,128)(2,1)} %refs_10_.1) | copy-start | bytes 12582916
  60.3 7.2 %collective-permute-start.13 = (bf16[128,512]{1,0:T(8,128)(2,1)S(1)}, bf16[128,512]{1,0:T(8,128)(2,1)S(1)}, u32[]{:S(2)}, u32[]{:S(2)}) collective-permute-start(bf16[128,512]{1,0:T(8,128)(2,1)S(1)} %get-tuple-element.97), channel_id=1, source_target_pairs={{0,1},{1,0},{2,3},{3,2},{4,5},{5,4},{6,7},{7,6},{8,9},{9,8},{10,11... | collective-permute-start | bytes 393224 | tf_op jit(solution)/shard_map/ppermute | solution.py:17
  60.4 12.9 %collective-permute-start.14 = (bf16[128,512]{1,0:T(8,128)(2,1)S(1)}, bf16[128,512]{1,0:T(8,128)(2,1)S(1)}, u32[]{:S(2)}, u32[]{:S(2)}) collective-permute-start(bf16[128,512]{1,0:T(8,128)(2,1)S(1)} %get-tuple-element.98), channel_id=1, source_target_pairs={{0,2},{1,3},{2,0},{3,1},{4,6},{5,7},{6,4},{7,5},{8,10},{9,11},{10,... | collective-permute-start | bytes 393224 | tf_op jit(solution)/shard_map/ppermute | solution.py:17
  63.3 10.0 %collective-permute-start.15 = (bf16[128,512]{1,0:T(8,128)(2,1)S(1)}, bf16[128,512]{1,0:T(8,128)(2,1)S(1)}, u32[]{:S(2)}, u32[]{:S(2)}) collective-permute-start(bf16[128,512]{1,0:T(8,128)(2,1)S(1)} %get-tuple-element.99), channel_id=1, source_target_pairs={{0,3},{1,2},{2,1},{3,0},{4,7},{5,6},{6,5},{7,4},{8,11},{9,10},{10,... | collective-permute-start | bytes 393224 | tf_op jit(solution)/shard_map/ppermute | solution.py:17
  73.6 6.2 %collective-permute-start.16 = (bf16[128,512]{1,0:T(8,128)(2,1)S(1)}, bf16[128,512]{1,0:T(8,128)(2,1)S(1)}, u32[]{:S(2)}, u32[]{:S(2)}) collective-permute-start(bf16[128,512]{1,0:T(8,128)(2,1)S(1)} %middle.1.refs_1_.refs_0_), channel_id=1, source_target_pairs={{0,1},{1,0},{2,3},{3,2},{4,5},{5,4},{6,7},{7,6},{8,9},{9,8},{10,11... | collective-permute-start | bytes 393224 | tf_op jit(solution)/shard_map/ppermute | solution.py:17
  75.9 11.8 %collective-permute-start.17 = (bf16[128,512]{1,0:T(8,128)(2,1)S(1)}, bf16[128,512]{1,0:T(8,128)(2,1)S(1)}, u32[]{:S(2)}, u32[]{:S(2)}) collective-permute-start(bf16[128,512]{1,0:T(8,128)(2,1)S(1)} %middle.1.refs_1_.refs_0_), channel_id=1, source_target_pairs={{0,2},{1,3},{2,0},{3,1},{4,6},{5,7},{6,4},{7,5},{8,10},{9,11},{10,... | collective-permute-start | bytes 393224 | tf_op jit(solution)/shard_map/ppermute | solution.py:17
  76.8 10.9 %collective-permute-start.18 = (bf16[128,512]{1,0:T(8,128)(2,1)S(1)}, bf16[128,512]{1,0:T(8,128)(2,1)S(1)}, u32[]{:S(2)}, u32[]{:S(2)}) collective-permute-start(bf16[128,512]{1,0:T(8,128)(2,1)S(1)} %middle.1.refs_1_.refs_0_), channel_id=1, source_target_pairs={{0,3},{1,2},{2,1},{3,0},{4,7},{5,6},{6,5},{7,4},{8,11},{9,10},{10,... | collective-permute-start | bytes 393224 | tf_op jit(solution)/shard_map/ppermute | solution.py:17
  90.1 12.8 %collective-permute-start.19 = (bf16[128,512]{1,0:T(8,128)(2,1)S(1)}, bf16[128,512]{1,0:T(8,128)(2,1)S(1)}, u32[]{:S(2)}, u32[]{:S(2)}) collective-permute-start(bf16[128,512]{1,0:T(8,128)(2,1)S(1)} %get-tuple-element.102), channel_id=1, source_target_pairs={{0,1},{1,0},{2,3},{3,2},{4,5},{5,4},{6,7},{7,6},{8,9},{9,8},{10,11... | collective-permute-start | bytes 393224 | tf_op jit(solution)/shard_map/ppermute | solution.py:17
  92.3 11.9 %collective-permute-start.20 = (bf16[128,512]{1,0:T(8,128)(2,1)S(1)}, bf16[128,512]{1,0:T(8,128)(2,1)S(1)}, u32[]{:S(2)}, u32[]{:S(2)}) collective-permute-start(bf16[128,512]{1,0:T(8,128)(2,1)S(1)} %get-tuple-element.103), channel_id=1, source_target_pairs={{0,2},{1,3},{2,0},{3,1},{4,6},{5,7},{6,4},{7,5},{8,10},{9,11},{10,... | collective-permute-start | bytes 393224 | tf_op jit(solution)/shard_map/ppermute | solution.py:17
  93.0 11.1 %collective-permute-start.21 = (bf16[128,512]{1,0:T(8,128)(2,1)S(1)}, bf16[128,512]{1,0:T(8,128)(2,1)S(1)}, u32[]{:S(2)}, u32[]{:S(2)}) collective-permute-start(bf16[128,512]{1,0:T(8,128)(2,1)S(1)} %get-tuple-element.104), channel_id=1, source_target_pairs={{0,3},{1,2},{2,1},{3,0},{4,7},{5,6},{6,5},{7,4},{8,11},{9,10},{10,... | collective-permute-start | bytes 393224 | tf_op jit(solution)/shard_map/ppermute | solution.py:17
